TPU v7x, 512 devices: a whole 4x8x8 slice. The times are simulated.
512 devices in a mesh: wide: 64 (over y_hi, x, z), narrow: 8 (over y_lo, core).
Axes of the slice: x: 4, y: 8 (y_hi: 2, y_lo: 4; y = y_hi * 4 + y_lo), z: 8, core: 2. Of those that a mesh axis runs over, the one named last changes fastest.
Arguments:
- features: bfloat16 [65536, 1792], P(('wide', 'narrow')), may hold values from -6 to 6
- weight: bfloat16 [1792, 512], replicated, may hold values from -0.125 to 0.125
- bias: float32 [512], replicated, may hold values from -3 to 3
- tile_cols: int32 [512, 24], P(('wide', 'narrow')), may hold values from 0 to 511, as said below
- tile_count: int32 [512], P(('wide', 'narrow')), may hold values from 8 to 24, as said below
- nbr_slot: int32 [65536, 15], P(('wide', 'narrow')), may hold values from 0 to 23
- nbr_col: int32 [65536, 15], P(('wide', 'narrow')), may hold values from 0 to 127
- nbr_keep: int32 [65536, 15], P(('wide', 'narrow')), may hold values 0 or 1
- upstream: bfloat16 [65536, 512], P(('wide', 'narrow')), may hold values from -6 to 6
Outputs:
- hidden: bfloat16 [65536, 512], P(('wide', 'narrow'))
- grad_features: bfloat16 [65536, 1792], P(('wide', 'narrow'))
- grad_weight: bfloat16 [1792, 512], replicated
- grad_bias: float32 [512], replicated
Inputs may be any that keep to these rules, and one draw needn't show every extreme that they name: `tile_cols`: each block row lists 24 different column blocks, all in the wide group of the block row itself or in the two wide groups beside it, the first and last groups being beside each other. `tile_count`: some block row stores all 24 slots.
All inputs are finite; a program needn't handle non-finite values. No bound on the sum of `nbr_keep` on one device may be relied on, other than what follows from the above.
Results may differ from a plain program's by a relative error of at most 0.01.
Values may be sent and summed in bfloat16 or wider, within the bound.
No kernel may reach another device: no remote copies, remote signals or barrier semaphores. Data moves between devices by JAX's collectives and lax.ppermute only.
A program may use at most 64 MiB of HBM per device.

v0:
```python
import jax
import jax.numpy as jnp
from jax import lax
from jax.sharding import PartitionSpec as P

TILE = 128
KNN = 15


def extended(block, sides, width):
    for axis, dim in sides:
        count = lax.axis_size(axis)
        forward = [(i, i + 1) for i in range(count - 1)]
        forward.append((count - 1, 0))
        backward = [(target, source) for source, target in forward]
        low = lax.ppermute(
            lax.slice_in_dim(block, block.shape[dim] - width, None, axis=dim), axis, forward
        )
        high = lax.ppermute(lax.slice_in_dim(block, 0, width, axis=dim), axis, backward)
        block = jnp.concatenate([low, block, high], axis=dim)
    return block


def from_behind(shard, axis, by):
    peers = lax.axis_size(axis)
    return lax.ppermute(shard, axis, [(i, (i + by) % peers) for i in range(peers)])


def on_device(features, weight, bias, tile_cols, tile_count, nbr_slot, nbr_col, nbr_keep, upstream):
    local_rows = features.shape[0]
    wide_size = lax.axis_size("wide")
    narrow_size = lax.axis_size("narrow")
    group_rows = local_rows * narrow_size
    window = 3 * group_rows
    blocks_here = local_rows // TILE
    group_blocks = blocks_here * narrow_size
    block_total = group_blocks * wide_size
    slot_total = tile_cols.shape[1]
    start_block = (lax.axis_index("wide") - 1) * group_blocks
    projected = jnp.dot(features, weight, preferred_element_type=jnp.float32).astype(jnp.bfloat16)
    row_tiles = jnp.repeat(tile_cols, TILE, axis=0)
    row_count = jnp.repeat(tile_count, TILE)
    slot_hit = nbr_slot[:, :, None] == jnp.arange(slot_total, dtype=jnp.int32)
    chosen = jnp.sum(jnp.where(slot_hit, row_tiles[:, None, :], 0), axis=2)
    live_edges = nbr_keep * (nbr_slot < row_count[:, None]).astype(jnp.int32)
    live_float = live_edges.astype(jnp.float32)
    degree = 1.0 + jnp.sum(live_float, axis=1)
    position = (chosen - start_block) % block_total
    window_column = position * TILE + nbr_col
    columns = jnp.arange(window, dtype=jnp.int32)
    link_counts = jnp.zeros((local_rows, window), jnp.float32)
    for edge in range(KNN):
        link_counts = link_counts + jnp.where(
            window_column[:, edge : edge + 1] == columns, live_float[:, edge : edge + 1], 0.0
        )
    link_counts = link_counts.astype(jnp.bfloat16)
    group_panel = lax.all_gather(projected, "narrow", axis=0, tiled=True)
    window_panel = extended(group_panel, (("wide", 0),), group_rows)
    gathered_sum = jnp.dot(link_counts, window_panel, preferred_element_type=jnp.float32)
    pre_activation = (projected.astype(jnp.float32) + gathered_sum) / degree[:, None] + bias
    sigma_pre = jax.nn.sigmoid(pre_activation)
    hidden = (pre_activation * sigma_pre).astype(jnp.bfloat16)
    grad_pre = upstream.astype(jnp.float32) * sigma_pre * (1.0 + pre_activation * (1.0 - sigma_pre))
    scaled = (grad_pre / degree[:, None]).astype(jnp.bfloat16)
    spread = lax.dot_general(
        link_counts, scaled, (((0,), (0,)), ((), ())), preferred_element_type=jnp.float32
    )
    from_right = from_behind(spread[:group_rows], "wide", -1)
    from_left = from_behind(spread[2 * group_rows :], "wide", 1)
    group_terms = spread[group_rows : 2 * group_rows] + from_right + from_left
    grad_proj = scaled.astype(jnp.float32) + lax.psum_scatter(
        group_terms, "narrow", scatter_dimension=0, tiled=True
    )
    grad_round = grad_proj.astype(jnp.bfloat16)
    weight_part = lax.dot_general(
        features, grad_round, (((0,), (0,)), ((), ())), preferred_element_type=jnp.float32
    )
    weight_grad, bias_grad = lax.psum((weight_part, jnp.sum(grad_pre, axis=0)), ("wide", "narrow"))
    grad_features = lax.dot_general(
        grad_round, weight, (((1,), (1,)), ((), ())), preferred_element_type=jnp.float32
    ).astype(jnp.bfloat16)
    return (hidden, grad_features, weight_grad.astype(jnp.bfloat16), bias_grad)


def solution(mesh):
    in_specs = (
        P(("wide", "narrow"), None),
        P(),
        P(),
        P(("wide", "narrow"), None),
        P(("wide", "narrow")),
        P(("wide", "narrow"), None),
        P(("wide", "narrow"), None),
        P(("wide", "narrow"), None),
        P(("wide", "narrow"), None),
    )
    out_specs = (P(("wide", "narrow"), None), P(("wide", "narrow"), None), P(), P())
    return jax.shard_map(
        on_device, mesh=mesh, in_specs=in_specs, out_specs=out_specs, check_vma=False
    )
```

profile of v0, /device:TPU:1, one launch (start us, length us, event | category | flops | bytes accessed | tf_op | source)
XLA Modules:
  0.0 385.0 jit_solution(6524432697258899610)
XLA Ops:
  7.2 0.0 copy-start
  7.2 0.0 copy-start.3
  7.2 0.0 copy-start.4
  7.2 0.0 copy-start.6
  7.2 0.0 copy-start.5
  7.2 0.0 copy-start.7
  7.2 0.0 copy-start.8
  7.2 0.0 all-gather.2.cloned.1.call-start
  7.3 1.4 copy-done
  8.7 2.1 convolution_convert_fusion.1
  10.8 0.0 all-gather.2.cloned.1.call-update
  10.8 0.0 reduce-scatter.2.cloned.1.call-start
  11.5 42.6 %all-gather.2.cloned.1.call-done = bf16[1024,512]{1,0:T(8,128)(2,1)} async-done(((bf16[128,512]{1,0:T(8,128)(2,1)}), bf16[1024,512]{1,0:T(8,128)(2,1)}) %all-gather.2.cloned.1.call-update) | async-done | bytes 1048592 | tf_op jit(solution)/shard_map/all_gather | solution.py:57
  54.1 11.8 %collective-permute-start.1 = (bf16[1024,512]{1,0:T(8,128)(2,1)}, bf16[1024,512]{1,0:T(8,128)(2,1)S(1)}, u32[]{:S(2)}, u32[]{:S(2)}) collective-permute-start(bf16[1024,512]{1,0:T(8,128)(2,1)} %all-gather.2.cloned.1.call-done), channel_id=1, source_target_pairs={{8,0},{16,8},{24,16},{32,24},{40,32},{48,40},{56,48},{64,56},{72,6... | collective-permute-start | bytes 3145736 | tf_op jit(solution)/shard_map/ppermute | solution.py:19
  65.9 1.9 collective-permute-start
  67.8 0.0 copy-done.3
  67.8 0.0 copy-done.4
  67.9 0.0 copy-done.6
  67.9 0.1 select_reduce_fusion
  68.0 0.0 copy-done.5
  68.1 40.9 %collective-permute-done.1 = bf16[1024,512]{1,0:T(8,128)(2,1)S(1)} collective-permute-done((bf16[1024,512]{1,0:T(8,128)(2,1)}, bf16[1024,512]{1,0:T(8,128)(2,1)S(1)}, u32[]{:S(2)}, u32[]{:S(2)}) %collective-permute-start.1) | collective-permute-done | bytes 1048608 | tf_op jit(solution)/shard_map/ppermute | solution.py:19
  109.0 12.0 %collective-permute-done = bf16[1024,512]{1,0:T(8,128)(2,1)} collective-permute-done((bf16[1024,512]{1,0:T(8,128)(2,1)}, bf16[1024,512]{1,0:T(8,128)(2,1)}, u32[]{:S(2)}, u32[]{:S(2)}) %collective-permute-start) | collective-permute-done | bytes 1048608 | tf_op jit(solution)/shard_map/ppermute | solution.py:16
  121.1 0.0 copy-done.7
  121.1 0.0 copy-done.8
  121.1 5.6 %fusion.21 = (f32[512]{0:T(512)S(1)}, f32[128,512]{1,0:T(8,128)S(1)}, bf16[128,512]{1,0:T(8,128)(2,1)}) fusion(bf16[128,512]{1,0:T(8,128)(2,1)S(1)} %copy-done.7, f32[512]{0:T(512)S(1)} %copy-done.8, f32[128]{0:T(128)S(1)} %broadcast_add_fusion, bf16[1024,512]{1,0:T(8,128)(2,1)S(1)} %collective-permute-done.1, ...), kind=kOutput, calls=%fused_computation.77 | convolution fusion | flops 430833152 | bytes 3821056 | tf_op jit(solution)/shard_map/dot_general | solution.py:59
  126.6 4.0 %fusion.20 = f32[3072,512]{1,0:T(8,128)S(1)} fusion(f32[128,512]{1,0:T(8,128)S(1)} %get-tuple-element.15, f32[128]{0:T(128)S(1)} %broadcast_add_fusion, f32[128]{0:T(128)S(1)} %get-tuple-element.37, s32[128]{0:T(128)S(1)} %get-tuple-element.22, f32[128]{0:T(128)S(1)} %get-tuple-element.38, s32[128]{0:T(128)S(1)} %get-tuple-element.23, ...), kind=kOutput, calls=%fused_computation.76 | convolution fusion | flops 420478976 | bytes 6569472 | tf_op jit(solution)/shard_map/dot_general | solution.py:65
  130.7 0.4 fusion.23
  131.1 1.9 collective-permute-start.2
  133.1 3.4 collective-permute-start.3
  136.4 70.4 %collective-permute-done.2 = f32[1024,512]{1,0:T(8,128)S(1)} collective-permute-done((f32[1024,512]{1,0:T(8,128)S(1)}, f32[1024,512]{1,0:T(8,128)S(1)}, u32[]{:S(2)}, u32[]{:S(2)}) %collective-permute-start.2) | collective-permute-done | bytes 2097184 | tf_op jit(solution)/shard_map/ppermute | solution.py:26
  206.8 12.2 %collective-permute-done.3 = f32[1024,512]{1,0:T(8,128)S(1)} collective-permute-done((f32[1024,512]{1,0:T(8,128)S(1)}, f32[1024,512]{1,0:T(8,128)S(1)}, u32[]{:S(2)}, u32[]{:S(2)}) %collective-permute-start.3) | collective-permute-done | bytes 2097184 | tf_op jit(solution)/shard_map/ppermute | solution.py:26
  219.1 2.1 fusion.6
  221.2 0.0 copy-start.1
  221.2 0.0 reduce-scatter.2.cloned.1.call-update
  221.2 30.4 %reduce-scatter.2.cloned.1.call-done = f32[128,512]{1,0:T(8,128)} async-done(((f32[1024,512]{1,0:T(8,128)}), f32[128,512]{1,0:T(8,128)}) %reduce-scatter.2.cloned.1.call-update) | async-done | bytes 262160 | tf_op jit(solution)/shard_map/reduce_scatter | solution.py:71
  251.6 0.0 copy-done.1
  251.6 3.5 convolution_bitcast_fusion
  255.1 117.8 %all-reduce.2 = (bf16[1792,512]{0,1:T(8,128)(2,1)}, f32[512]{0:T(512)}) all-reduce(f32[1792,512]{0,1:T(8,128)} %convolution_bitcast_fusion, f32[512]{0:T(512)S(1)} %get-tuple-element.14), channel_id=1, replica_groups=mesh['wide'=64,'narrow'=8] {'wide','narrow'}, use_global_device_ids=true, to_apply=%region_3.4 | all-reduce | flops 918016 | bytes 5509120 | tf_op jit(solution)/shard_map/psum | solution.py:78
  372.8 0.0 copy-start.2
  372.8 3.9 %copy.15 = bf16[1792,512]{1,0:T(8,128)(2,1)} copy(bf16[1792,512]{0,1:T(8,128)(2,1)} %get-tuple-element.12) | data formatting | bytes 3670016
  376.7 0.0 copy-done.2
  376.7 1.5 convolution_convert_fusion
  (5 shorter events, 0.1 us)
Async XLA Ops:
  7.2 1.5 copy-start
  7.2 60.7 %copy-start.3 = (s32[128,15]{0,1:T(8,128)S(1)}, s32[128,15]{0,1:T(8,128)}, u32[]{:S(2)}) copy-start(s32[128,15]{0,1:T(8,128)} %param.14) | copy-start | bytes 23044
  7.2 60.7 %copy-start.4 = (s32[128,15]{0,1:T(8,128)S(1)}, s32[128,15]{0,1:T(8,128)}, u32[]{:S(2)}) copy-start(s32[128,15]{0,1:T(8,128)} %param.16) | copy-start | bytes 23044
  7.2 60.7 %copy-start.6 = (s32[1,24]{1,0:T(1,128)S(1)}, s32[1,24]{1,0:T(1,128)}, u32[]{:S(2)}) copy-start(s32[1,24]{1,0:T(1,128)} %param.12) | copy-start | bytes 292
  7.2 60.8 %copy-start.5 = (s32[128,15]{0,1:T(8,128)S(1)}, s32[128,15]{0,1:T(8,128)}, u32[]{:S(2)}) copy-start(s32[128,15]{0,1:T(8,128)} %param.15) | copy-start | bytes 23044
  7.2 113.8 %copy-start.7 = (bf16[128,512]{1,0:T(8,128)(2,1)S(1)}, bf16[128,512]{1,0:T(8,128)(2,1)}, u32[]{:S(2)}) copy-start(bf16[128,512]{1,0:T(8,128)(2,1)} %param.17) | copy-start | bytes 393220
  7.2 113.8 %copy-start.8 = (f32[512]{0:T(512)S(1)}, f32[512]{0:T(512)}, u32[]{:S(2)}) copy-start(f32[512]{0:T(512)} %param.11) | copy-start | bytes 6148
  7.2 46.8 %all-gather.2.cloned.1.call-start = ((), (), s32[]{:S(2)}) async-start(), calls=%async_computation.1 | async-start | bytes 1179648 | tf_op jit(solution)/shard_map/all_gather | solution.py:57
  10.8 240.8 %reduce-scatter.2.cloned.1.call-start = ((), (), s32[]{:S(2)}) async-start(), calls=%async_computation.2 | async-start | bytes 2359296 | tf_op jit(solution)/shard_map/reduce_scatter | solution.py:71
  54.1 54.9 %collective-permute-start.1 = (bf16[1024,512]{1,0:T(8,128)(2,1)}, bf16[1024,512]{1,0:T(8,128)(2,1)S(1)}, u32[]{:S(2)}, u32[]{:S(2)}) collective-permute-start(bf16[1024,512]{1,0:T(8,128)(2,1)} %all-gather.2.cloned.1.call-done), channel_id=1, source_target_pairs={{8,0},{16,8},{24,16},{32,24},{40,32},{48,40},{56,48},{64,56},{72,6... | collective-permute-start | bytes 3145736 | tf_op jit(solution)/shard_map/ppermute | solution.py:19
  65.9 55.1 %collective-permute-start = (bf16[1024,512]{1,0:T(8,128)(2,1)}, bf16[1024,512]{1,0:T(8,128)(2,1)}, u32[]{:S(2)}, u32[]{:S(2)}) collective-permute-start(bf16[1024,512]{1,0:T(8,128)(2,1)} %all-gather.2.cloned.1.call-done), channel_id=1, source_target_pairs={{0,8},{8,16},{16,24},{24,32},{32,40},{40,48},{48,56},{56,64},{64,7... | collective-permute-start | bytes 3145736 | tf_op jit(solution)/shard_map/ppermute | solution.py:16
  131.1 75.7 %collective-permute-start.2 = (f32[1024,512]{1,0:T(8,128)S(1)}, f32[1024,512]{1,0:T(8,128)S(1)}, u32[]{:S(2)}, u32[]{:S(2)}) collective-permute-start(f32[1024,512]{1,0:T(8,128)S(1)} %get-tuple-element.18), channel_id=1, source_target_pairs={{0,504},{8,0},{16,8},{24,16},{32,24},{40,32},{48,40},{56,48},{64,5... | collective-permute-start | bytes 6291464 | tf_op jit(solution)/shard_map/ppermute | solution.py:26
  133.1 86.0 %collective-permute-start.3 = (f32[1024,512]{1,0:T(8,128)S(1)}, f32[1024,512]{1,0:T(8,128)S(1)}, u32[]{:S(2)}, u32[]{:S(2)}) collective-permute-start(f32[1024,512]{1,0:T(8,128)S(1)} %get-tuple-element.19), channel_id=1, source_target_pairs={{0,8},{8,16},{16,24},{24,32},{32,40},{40,48},{48,56},{56,64},{64,7... | collective-permute-start | bytes 6291464 | tf_op jit(solution)/shard_map/ppermute | solution.py:26
  221.2 30.4 %copy-start.1 = (bf16[128,1792]{1,0:T(8,128)(2,1)S(1)}, bf16[128,1792]{1,0:T(8,128)(2,1)}, u32[]{:S(2)}) copy-start(bf16[128,1792]{1,0:T(8,128)(2,1)} %param.9) | copy-start | bytes 1376260
  372.8 3.9 %copy-start.2 = (f32[128,512]{1,0:T(8,128)S(1)}, f32[128,512]{1,0:T(8,128)}, u32[]{:S(2)}) copy-start(f32[128,512]{1,0:T(8,128)} %reduce-scatter.2.cloned.1.call-done) | copy-start | bytes 786436
Sparse Core Ops, SparseCore 0:
  10.9 43.1 all-gather.1
  221.3 30.2 reduce-scatter.1
where the time goes:
time: 386 us; the launch traced here: 385 us
  waiting for transfers between devices  209 us (54%)
  blocking collectives  118 us (31%)
  starting transfers between devices  19.1 us (5%)
  matrix products  16.7 us (4%)
  between operations  14.9 us (4%)
  local copies, waits for them, and re-layouts  5.76 us (1%)
    psum x1, blocking collectives, on_device(): lax.psum((weight_part, jnp.sum(grad_pre, axis=0)), ('wide', 'narrow'))  118 us
    ppermute x2, waiting for transfers between devices, from_behind(): lax.ppermute(shard, axis, [(i, (i + by) % peers) for i in range(peers)])  82.6 us
    all_gather x1, waiting for transfers between devices, on_device(): group_panel = lax.all_gather(projected, 'narrow', axis=0, tiled=True)  42.6 us
    ppermute x1, waiting for transfers between devices, extended(): lax.ppermute(lax.slice_in_dim(block, 0, width, axis=dim), axis, backward)  40.9 us
    reduce_scatter x1, waiting for transfers between devices, on_device(): lax.psum_scatter(group_terms, 'narrow', scatter_dimension=0, tiled=True)  30.4 us
    ppermute x1, waiting for transfers between devices, extended(): lax.ppermute(lax.slice_in_dim(block, block.shape[dim] - width, None, axis...  12 us
    ppermute x1, starting transfers between devices, extended(): lax.ppermute(lax.slice_in_dim(block, 0, width, axis=dim), axis, backward)  11.8 us
  transfers between devices with their start and end apart: 6, of which 6 were waited for; matrix products, arithmetic and copies ran while one was open for 0% of the time, Pallas kernels for 0%

commit v1 on v0

v1 whole, which is shorter than its diff:
```python
import jax
import jax.numpy as jnp
from jax import lax
from jax.experimental import pallas as pl
from jax.experimental.pallas import tpu as pltpu
from jax.sharding import Mesh
from jax.sharding import PartitionSpec as P

TILE = 128
KNN = 15
HID = 512
AXES = ("yh", "x", "z", "yl", "c")
SIZES = (2, 4, 8, 4, 2)
WIDE = ("yh", "x", "z")
RUN = 4
PARITY_ROWS = RUN * TILE
KEY_ROWS = 8
DEAD = 31
PIECES = 6
F_RUN = 448
SLABS = 128
BIAS_SLAB = 112

bf16 = jnp.bfloat16
f32 = jnp.float32


def spread_to(shard, axes, count):
    return lax.all_to_all(jnp.broadcast_to(shard[None], (count,) + shard.shape), axes, 0, 0)


def neighbours(block):
    count = 64
    forward = [(i, (i + 1) % count) for i in range(count)]
    backward = [((i + 1) % count, i) for i in range(count)]
    return lax.ppermute(block, WIDE, forward), lax.ppermute(block, WIDE, backward)


def swap_core(block):
    return lax.ppermute(block, "c", [(0, 1), (1, 0)])


def gather_window(shard):
    own = spread_to(shard, "yl", RUN)
    low, high = neighbours(own)
    own_other = swap_core(own)
    return low, swap_core(low), own, own_other, high, swap_core(high)


def forward_counts_kernel(key_ref, out_ref):
    def rows(step, carry):
        keys = key_ref[pl.ds(step * 16, 16), :]
        spread = [jnp.broadcast_to(keys[:, e : e + 1], (16, 128)) for e in range(KNN)]
        for tile in range(PIECES * RUN):
            lanes = lax.broadcasted_iota(jnp.int32, (16, 128), 1) + tile * 128
            total = jnp.zeros((16, 128), f32)
            for e in range(KNN):
                total = total + jnp.where(spread[e] == lanes, 1.0, 0.0)
            out_ref[pl.ds(step * 16, 16), tile * 128 : (tile + 1) * 128] = total.astype(bf16)
        return carry

    lax.fori_loop(0, TILE // 16, rows, 0)


def forward_counts(keys):
    return pl.pallas_call(
        forward_counts_kernel,
        out_shape=jax.ShapeDtypeStruct((TILE, PIECES * PARITY_ROWS), bf16),
        name="forward_counts",
    )(keys)


def backward_counts_kernel(core_ref, *refs):
    pieces, out_ref = refs[:PIECES], refs[PIECES]
    core = core_ref[0]
    for p in range(PIECES):
        wanted = 2 - p // 2
        for y in range(RUN):
            head = pieces[p][y, TILE : TILE + KEY_ROWS, :].astype(f32).astype(jnp.int32)
            targets = []
            for half in range(2):
                block = head[:, half * 128 : half * 128 + 128] - (8 * wanted + core)
                cell = head[:, 256 + half * 128 : 384 + half * 128]
                valid = jnp.logical_and(
                    jnp.logical_and(block >= 0, block < 8), jnp.bitwise_and(block, 1) == 0
                )
                found = lax.shift_right_arithmetic(block, 1) * TILE + cell
                targets.append(jnp.where(valid, found, -1))
            lane = (p * RUN + y) * 128
            for step in range(PARITY_ROWS // 16):
                rows = lax.broadcasted_iota(jnp.int32, (16, 128), 0) + step * 16
                total = jnp.zeros((16, 128), f32)
                for e in range(KNN):
                    key = targets[e // 8][e % 8 : e % 8 + 1, :]
                    total = total + jnp.where(key == rows, 1.0, 0.0)
                out_ref[step * 16 : step * 16 + 16, lane : lane + 128] = total.astype(bf16)


def backward_counts(core, pieces):
    return pl.pallas_call(
        backward_counts_kernel,
        in_specs=[pl.BlockSpec(memory_space=pltpu.SMEM)]
        + [pl.BlockSpec(memory_space=pltpu.VMEM)] * PIECES,
        out_shape=jax.ShapeDtypeStruct((PARITY_ROWS, PIECES * PARITY_ROWS), bf16),
        name="backward_counts",
    )(core, *pieces)


def forward_kernel(counts_ref, own_ref, degree_ref, bias_ref, up_ref, *refs):
    pieces, (hidden_ref, scaled_ref, bias_out_ref) = refs[:PIECES], refs[PIECES:]
    total = own_ref[...].astype(f32)
    for p in range(PIECES):
        for y in range(RUN):
            lane = (p * RUN + y) * 128
            total = total + jnp.dot(
                counts_ref[:, lane : lane + 128],
                pieces[p][y, :TILE, :],
                preferred_element_type=f32,
            )
    degree = degree_ref[...]
    pre = total / degree + bias_ref[...]
    sigma = jax.nn.sigmoid(pre)
    hidden_ref[...] = (pre * sigma).astype(bf16)
    grad_pre = up_ref[...].astype(f32) * sigma * (1.0 + pre * (1.0 - sigma))
    scaled_ref[...] = (grad_pre / degree).astype(bf16)
    bias_out_ref[...] = jnp.sum(grad_pre, axis=0, keepdims=True)


def forward_math(counts, own, degree, bias, upstream, pieces):
    return pl.pallas_call(
        forward_kernel,
        out_shape=(
            jax.ShapeDtypeStruct((TILE, HID), bf16),
            jax.ShapeDtypeStruct((TILE, HID), bf16),
            jax.ShapeDtypeStruct((1, HID), f32),
        ),
        name="forward_math",
    )(counts, own, degree, bias, upstream, *pieces)


def backward_kernel(run_ref, counts_ref, feats_ref, bias_ref, *refs):
    pieces, (own_ref, slab_ref, round_ref) = refs[:PIECES], refs[PIECES:]
    total = pieces[2][...].reshape(PARITY_ROWS, HID).astype(f32)
    for p in range(PIECES):
        total = total + jnp.dot(
            counts_ref[:, p * PARITY_ROWS : (p + 1) * PARITY_ROWS],
            pieces[p][...].reshape(PARITY_ROWS, HID),
            preferred_element_type=f32,
        )
    rounded = total.astype(bf16)
    round_ref[...] = rounded.reshape(RUN, TILE, HID)
    own_ref[...] = round_ref[run_ref[0]]
    part = lax.dot_general(
        feats_ref[...].reshape(PARITY_ROWS, F_RUN),
        rounded,
        (((0,), (0,)), ((), ())),
        preferred_element_type=f32,
    ).astype(bf16)
    for row in range(F_RUN // 16):
        for lane in range(HID // 128):
            slab_ref[row * 4 + lane] = part[row * 16 : row * 16 + 16, lane * 128 : lane * 128 + 128]
    slab_ref[BIAS_SLAB] = bias_ref[...]
    for rest in range(BIAS_SLAB + 1, SLABS):
        slab_ref[rest] = jnp.zeros((16, 128), bf16)


def backward_math(run, counts, feats, bias_rows, pieces):
    return pl.pallas_call(
        backward_kernel,
        in_specs=[pl.BlockSpec(memory_space=pltpu.SMEM)]
        + [pl.BlockSpec(memory_space=pltpu.VMEM)] * (3 + PIECES),
        out_shape=(
            jax.ShapeDtypeStruct((TILE, HID), bf16),
            jax.ShapeDtypeStruct((SLABS, 16, 128), bf16),
        ),
        scratch_shapes=[pltpu.VMEM((RUN, TILE, HID), bf16)],
        name="backward_math",
    )(run, counts, feats, bias_rows, *pieces)


def high_low(value):
    high = lax.reduce_precision(value, 8, 7)
    return jnp.concatenate([high, value - high, jnp.zeros((8, 128), f32)], axis=0).astype(bf16)


def on_device(features, weight, bias, tile_cols, tile_count, nbr_slot, nbr_col, nbr_keep, upstream):
    group = (lax.axis_index("yh") * 4 + lax.axis_index("x")) * 8 + lax.axis_index("z")
    run = lax.axis_index("yl")
    core = lax.axis_index("c")
    block_total = 512
    slot_total = tile_cols.shape[1]

    projected = jnp.dot(features, weight, preferred_element_type=f32).astype(bf16)

    live = nbr_keep * (nbr_slot < tile_count[0]).astype(jnp.int32)
    chosen = jnp.zeros_like(nbr_slot)
    for slot in range(slot_total):
        chosen = chosen + jnp.where(nbr_slot == slot, tile_cols[0, slot], 0)
    position = (chosen - (group - 1) * 8) % block_total
    key_block = jnp.where(live > 0, position, DEAD)
    degree = 1.0 + jnp.sum(live, axis=1, keepdims=True).astype(f32)
    pad = jnp.zeros((1, TILE), bf16)
    block_rows = jnp.concatenate([key_block.T.astype(bf16), pad], axis=0)
    cell_rows = jnp.concatenate([nbr_col.T.astype(bf16), pad], axis=0)
    key_rows = jnp.concatenate(
        [block_rows[:8], block_rows[8:], cell_rows[:8], cell_rows[8:]], axis=1
    )
    reach = position // 8
    member = position % 8
    other = (member % 2 != core).astype(jnp.int32)
    place = (reach * 2 + other) * PARITY_ROWS + (member // 2) * TILE + nbr_col
    counts = forward_counts(jnp.where(live > 0, place, -1))

    packed = jnp.concatenate([projected, key_rows], axis=0)
    first = gather_window(packed)
    feats = lax.all_to_all(features.reshape(TILE, RUN, F_RUN).transpose(1, 0, 2), "yl", 0, 0)
    hidden, scaled, bias_part = forward_math(
        counts, projected, degree, bias[None], upstream, first
    )
    counts_back = backward_counts(core.reshape(1), first)
    second = gather_window(scaled)
    own_round, slabs = backward_math(
        run.reshape(1), counts_back, feats, high_low(bias_part.reshape(4, 128)), second
    )
    reduced = jnp.sum(lax.all_to_all(slabs, WIDE + ("c",), 0, 0).astype(f32), axis=0)
    is_bias = (group * 2 + core) == BIAS_SLAB
    piece = jnp.where(is_bias, high_low(reduced[:4] + reduced[4:8]), reduced.astype(bf16))
    column = spread_to(piece, ("yh", "yl"), 8)
    plane = spread_to(column, ("x", "z"), 32)
    plane_other = swap_core(plane)
    both = jnp.stack([plane, plane_other])
    both = jnp.where(core == 0, both, both[::-1])
    both = both.reshape(2, 4, 8, 2, RUN, 16, 128)
    ordered = both.transpose(4, 3, 1, 2, 0, 5, 6).reshape(RUN, SLABS, 16, 128)
    weight_grad = (
        ordered[:, :BIAS_SLAB]
        .reshape(RUN, F_RUN // 16, 4, 16, 128)
        .transpose(0, 1, 3, 2, 4)
        .reshape(RUN * F_RUN, HID)
    )
    bias_rows = ordered[:, BIAS_SLAB].astype(f32)
    bias_grad = jnp.sum(bias_rows[:, :4] + bias_rows[:, 4:8], axis=0).reshape(HID)
    grad_features = lax.dot_general(
        own_round, weight, (((1,), (1,)), ((), ())), preferred_element_type=f32
    ).astype(bf16)
    return hidden, grad_features, weight_grad, bias_grad


def solution(mesh):
    split = Mesh(mesh.devices.reshape(SIZES), AXES)
    rows = P(AXES, None)
    in_specs = (rows, P(), P(), rows, P(AXES), rows, rows, rows, rows)
    out_specs = (rows, rows, P(), P())
    return jax.shard_map(
        on_device, mesh=split, in_specs=in_specs, out_specs=out_specs, check_vma=False
    )
```

time: 386 us -> 280 us (0.73)
  waiting for transfers between devices: 209 us -> 81.9 us
  blocking collectives: 118 us -> 58.7 us
  starting transfers between devices: 19.1 us -> 70.3 us
  Pallas kernels: 0 us -> 29.6 us
  other arithmetic: 2.23 us -> 20.1 us
  matrix products: 16.7 us -> 2.91 us
  between operations: 14.9 us -> 1.67 us
  local copies, waits for them, and re-layouts: 5.76 us -> 13.6 us
    psum x1 -> x0, blocking collectives: 118 us -> none  [on_device(): lax.psum((weight_part, jnp.sum(grad_pre, axis=0)), ('wide', 'narrow'))]
    ppermute x4 -> x11, waiting for transfers between devices: 136 us -> 49.7 us  [the longest x2 39.5 us: neighbours(): lax.ppermute(block, WIDE, backward)]
    all_to_all x0 -> x3, blocking collectives: none -> 58.7 us  [spread_to(): lax.all_to_all(jnp.broadcast_to(shard[None], (count,) + shard.shape), axe...]
    all_gather x1 -> x0, waiting for transfers between devices: 42.6 us -> none  [on_device(): group_panel = lax.all_gather(projected, 'narrow', axis=0, tiled=True)]
    all_to_all x0 -> x3, waiting for transfers between devices: none -> 32.1 us  [the longest x1 19.5 us: on_device(): lax.all_to_all(slabs, WIDE + ('c',), 0, 0).astype(f32)]
    ppermute x4 -> x11, starting transfers between devices: 19 us -> 49.6 us  [the longest x7 25.1 us: swap_core(): return lax.ppermute(block, 'c', [(0, 1), (1, 0)])]
    reduce_scatter x1 -> x0, waiting for transfers between devices: 30.4 us -> none  [on_device(): lax.psum_scatter(group_terms, 'narrow', scatter_dimension=0, tiled=True)]
    pallas_call x0 -> x4, Pallas kernels: none -> 29.6 us  [the longest x1 14.2 us: backward_counts(): pl.pallas_call(backward_counts_kernel, in_specs=[pl.BlockSpec(memory_spac...]
  transfers between devices with their start and end apart: 6 -> 14, of which waited for: 6 -> 6; matrix products, arithmetic and copies ran while one was open for 0% -> 2% of each run, Pallas kernels for 0% -> 7%
where the time goes in v1:
time: 280 us; the launch traced here: 279 us
  waiting for transfers between devices  81.9 us (29%)
  starting transfers between devices  70.3 us (25%)
  blocking collectives  58.7 us (21%)
  Pallas kernels  29.6 us (11%)
  other arithmetic  20.1 us (7%)
  local copies, waits for them, and re-layouts  13.6 us (5%)
  matrix products  2.91 us (1%)
    all_to_all x3, blocking collectives, spread_to(): lax.all_to_all(jnp.broadcast_to(shard[None], (count,) + shard.shape), axe...  58.7 us
    ppermute x2, waiting for transfers between devices, neighbours(): lax.ppermute(block, WIDE, backward)  39.5 us
    ppermute x7, starting transfers between devices, swap_core(): return lax.ppermute(block, 'c', [(0, 1), (1, 0)])  25.1 us
    all_to_all x1, waiting for transfers between devices, on_device(): lax.all_to_all(slabs, WIDE + ('c',), 0, 0).astype(f32)  19.5 us
    ppermute x2, starting transfers between devices, neighbours(): lax.ppermute(block, WIDE, backward)  19.2 us
    convert_element_type x1, other arithmetic, on_device(): block_rows = jnp.concatenate([key_block.T.astype(bf16), pad], axis=0)  15.7 us
    pallas_call x1, Pallas kernels, backward_counts(): pl.pallas_call(backward_counts_kernel, in_specs=[pl.BlockSpec(memory_spac...  14.2 us
    all_to_all x1, starting transfers between devices, on_device(): lax.all_to_all(slabs, WIDE + ('c',), 0, 0).astype(f32)  13.8 us
  transfers between devices with their start and end apart: 14, of which 6 were waited for; matrix products, arithmetic and copies ran while one was open for 2% of the time, Pallas kernels for 7%

profile of v1, /device:TPU:1, one launch (start us, length us, event | category | flops | bytes accessed | tf_op | source)
XLA Modules:
  0.0 278.9 jit_solution(15920974227639677465)
XLA Ops:
  0.6 0.0 copy-start
  0.6 1.5 fusion.22
  2.1 2.0 fusion.21
  4.8 15.7 %fusion.15 = (bf16[15,128]{1,0:T(8,128)(2,1)S(1)}, s32[128,15]{0,1:T(8,128)S(1)}, pred[128,15]{0,1:T(8,128)(4,1)S(1)}) fusion(s32[]{:T(128)S(6)} %mul.31, s32[]{:T(128)} %bitcast.24, s32[128,15]{0,1:T(8,128)} %param.14, s32[]{:T(128)} %bitcast.23, s32[]{:T(128)} %bitcast.22, s32[]{:T(128)} %bitcast.21, s32[]{:T(128)} %bitcast.20, s32[]{:T(128)} %bitcast.19, ...), kind=kLoop, calls=%fused_computation.41 | loop fusion | flops 168960 | bytes 28904 | tf_op jit(solution)/shard_map/convert_element_type | solution.py:203
  20.5 0.8 convert_bitcast_fusion
  21.3 0.0 copy-done
  21.3 0.0 copy-start.8
  21.3 0.0 copy-start.9
  21.3 1.4 convolution_convert_fusion.1.own_ref
  22.8 0.0 copy-start.5
  22.9 18.7 %all_to_all.30.refs_2_ = bf16[4,136,512]{2,1,0:T(8,128)(2,1)S(1)} all-to-all(bf16[4,136,512]{2,1,0:T(8,128)(2,1)S(1)} %broadcast_in_dim.158), channel_id=1, replica_groups=mesh['yh'=2,'x'=4,'z'=8,'yl'=4,'c'=2] {'yl'}, dimensions={0} | all-to-all | bytes 1114112 | tf_op jit(solution)/shard_map/all_to_all | solution.py:29
  41.6 17.3 %collective-permute-start.3 = (bf16[4,136,512]{2,1,0:T(8,128)(2,1)S(1)}, bf16[4,136,512]{2,1,0:T(8,128)(2,1)S(1)}, u32[]{:S(2)}, u32[]{:S(2)}) collective-permute-start(bf16[4,136,512]{2,1,0:T(8,128)(2,1)S(1)} %all_to_all.30.refs_2_), channel_id=1, source_target_pairs={{8,0},{16,8},{24,16},{32,24},{40,32},{48,40},{56,48},{64,56},{72,6... | collective-permute-start | bytes 1671176 | tf_op jit(solution)/shard_map/ppermute | solution.py:36
  58.9 1.9 collective-permute-start
  60.8 3.6 %collective-permute-start.2 = (bf16[4,136,512]{2,1,0:T(8,128)(2,1)S(1)}, bf16[4,136,512]{2,1,0:T(8,128)(2,1)}, u32[]{:S(2)}, u32[]{:S(2)}) collective-permute-start(bf16[4,136,512]{2,1,0:T(8,128)(2,1)S(1)} %all_to_all.30.refs_2_), channel_id=1, source_target_pairs={{0,1},{1,0},{2,3},{3,2},{4,5},{5,4},{6,7},{7,6},{8,9},{9,8},{10,11... | collective-permute-start | bytes 1671176 | tf_op jit(solution)/shard_map/ppermute | solution.py:40
  64.5 18.4 %collective-permute-done.3.refs_4_ = bf16[4,136,512]{2,1,0:T(8,128)(2,1)S(1)} collective-permute-done((bf16[4,136,512]{2,1,0:T(8,128)(2,1)S(1)}, bf16[4,136,512]{2,1,0:T(8,128)(2,1)S(1)}, u32[]{:S(2)}, u32[]{:S(2)}) %collective-permute-start.3) | collective-permute-done | bytes 557088 | tf_op jit(solution)/shard_map/ppermute | solution.py:36
  82.9 2.6 collective-permute-start.4
  85.5 9.4 %collective-permute-done.refs_0_ = bf16[4,136,512]{2,1,0:T(8,128)(2,1)S(1)} collective-permute-done((bf16[4,136,512]{2,1,0:T(8,128)(2,1)S(1)}, bf16[4,136,512]{2,1,0:T(8,128)(2,1)S(1)}, u32[]{:S(2)}, u32[]{:S(2)}) %collective-permute-start) | collective-permute-done | bytes 557088 | tf_op jit(solution)/shard_map/ppermute | solution.py:36
  94.8 3.0 %collective-permute-start.1 = (bf16[4,136,512]{2,1,0:T(8,128)(2,1)S(1)}, bf16[4,136,512]{2,1,0:T(8,128)(2,1)}, u32[]{:S(2)}, u32[]{:S(2)}) collective-permute-start(bf16[4,136,512]{2,1,0:T(8,128)(2,1)S(1)} %collective-permute-done.refs_0_), channel_id=1, source_target_pairs={{0,1},{1,0},{2,3},{3,2},{4,5},{5,4},{6,7},{7,6},{8,9},{9,8},{10,11... | collective-permute-start | bytes 1671176 | tf_op jit(solution)/shard_map/ppermute | solution.py:40
  97.9 0.7 copy.26.degree_ref
  98.6 0.7 copy.25.key_ref
  99.4 5.3 %forward_counts.1.counts_ref = bf16[128,3072]{1,0:T(8,128)(2,1)} custom-call(s32[128,15]{1,0:T(8,128)} %copy.25.key_ref), custom_call_target="tpu_custom_call" | custom-call | tf_op jit(solution)/shard_map/forward_counts/pallas_call | solution.py:66
  104.7 0.0 collective-permute-done.2.refs_3_
  104.7 0.0 collective-permute-done.4.refs_5_
  104.7 0.0 collective-permute-done.1.refs_1_
  104.7 4.1 %forward_math.1 = (bf16[128,512]{1,0:T(8,128)(2,1)}, bf16[128,512]{1,0:T(8,128)(2,1)}, f32[1,512]{1,0:T(1,128)}) custom-call(bf16[128,3072]{1,0:T(8,128)(2,1)} %forward_counts.1.counts_ref, bf16[128,512]{1,0:T(8,128)(2,1)} %copy-done.5, f32[128,1]{1,0:T(8,128)} %copy.26.degree_ref, f32[1,512]{1,0:T(1,128)} %bitcast.71, bf16[128,512]{1,0:T(8,128)(2,1)} %up_ref.1, ...), custom_call_target="tpu_custom_call" | custom-call | tf_op jit(solution)/shard_map/forward_math/pallas_call | solution.py:130
  108.8 1.7 broadcast_in_dim.159
  110.5 3.5 %all-to-all-start.2 = ((bf16[4,128,512]{2,1,0:T(8,128)(2,1)}), bf16[4,128,512]{2,1,0:T(8,128)(2,1)S(1)}, u32[]{:S(2)}, u32[]{:S(2)}) async-start(bf16[4,128,512]{2,1,0:T(8,128)(2,1)} %broadcast_in_dim.159), calls=%async_computation.2 | async-start | bytes 1048576 | tf_op jit(solution)/shard_map/all_to_all | solution.py:29
  114.0 2.0 copy.27
  116.0 12.6 %all-to-all-done.2.refs_2_ = bf16[4,128,512]{2,1,0:T(8,128)(2,1)S(1)} async-done(((bf16[4,128,512]{2,1,0:T(8,128)(2,1)}), bf16[4,128,512]{2,1,0:T(8,128)(2,1)S(1)}, u32[]{:S(2)}, u32[]{:S(2)}) %all-to-all-start.2) | async-done | bytes 524320 | tf_op jit(solution)/shard_map/all_to_all | solution.py:29
  128.6 3.5 %all-to-all-start.1 = ((bf16[4,128,448]{1,2,0:T(8,128)(2,1)}), bf16[4,128,448]{1,2,0:T(8,128)(2,1)S(1)}, u32[]{:S(2)}, u32[]{:S(2)}) async-start(bf16[4,128,448]{1,2,0:T(8,128)(2,1)} %bitcast.32), calls=%async_computation.1 | async-start | bytes 917504 | tf_op jit(solution)/shard_map/all_to_all | solution.py:216
  132.1 1.9 collective-permute-start.8
  134.0 3.4 %collective-permute-start.5 = (bf16[4,128,512]{2,1,0:T(8,128)(2,1)S(1)}, bf16[4,128,512]{2,1,0:T(8,128)(2,1)}, u32[]{:S(2)}, u32[]{:S(2)}) collective-permute-start(bf16[4,128,512]{2,1,0:T(8,128)(2,1)S(1)} %all-to-all-done.2.refs_2_), channel_id=1, source_target_pairs={{0,8},{8,16},{16,24},{24,32},{32,40},{40,48},{48,56},{56,64},{64,7... | collective-permute-start | bytes 1572872 | tf_op jit(solution)/shard_map/ppermute | solution.py:36
  137.4 3.3 %collective-permute-start.7 = (bf16[4,128,512]{2,1,0:T(8,128)(2,1)S(1)}, bf16[4,128,512]{2,1,0:T(8,128)(2,1)}, u32[]{:S(2)}, u32[]{:S(2)}) collective-permute-start(bf16[4,128,512]{2,1,0:T(8,128)(2,1)S(1)} %all-to-all-done.2.refs_2_), channel_id=1, source_target_pairs={{0,1},{1,0},{2,3},{3,2},{4,5},{5,4},{6,7},{7,6},{8,9},{9,8},{10,11... | collective-permute-start | bytes 1572872 | tf_op jit(solution)/shard_map/ppermute | solution.py:40
  140.6 21.0 %collective-permute-done.8.refs_4_ = bf16[4,128,512]{2,1,0:T(8,128)(2,1)S(1)} collective-permute-done((bf16[4,128,512]{2,1,0:T(8,128)(2,1)S(1)}, bf16[4,128,512]{2,1,0:T(8,128)(2,1)S(1)}, u32[]{:S(2)}, u32[]{:S(2)}) %collective-permute-start.8) | collective-permute-done | bytes 524320 | tf_op jit(solution)/shard_map/ppermute | solution.py:36
  161.7 3.3 %collective-permute-start.9 = (bf16[4,128,512]{2,1,0:T(8,128)(2,1)S(1)}, bf16[4,128,512]{2,1,0:T(8,128)(2,1)}, u32[]{:S(2)}, u32[]{:S(2)}) collective-permute-start(bf16[4,128,512]{2,1,0:T(8,128)(2,1)S(1)} %collective-permute-done.8.refs_4_), channel_id=1, source_target_pairs={{0,1},{1,0},{2,3},{3,2},{4,5},{5,4},{6,7},{7,6},{8,9},{9,8},{10,11... | collective-permute-start | bytes 1572872 | tf_op jit(solution)/shard_map/ppermute | solution.py:40
  164.9 0.0 collective-permute-done.5.refs_0_
  165.0 2.1 collective-permute-start.6
  167.1 0.1 pad.9.clone
  167.2 0.0 all-to-all-done.1
  167.2 1.0 copy.28.feats_ref
  168.2 14.2 %backward_counts.1.counts_ref = bf16[512,3072]{1,0:T(8,128)(2,1)} custom-call(s32[1]{0:T(128)} %bitcast.30.core_ref, bf16[4,136,512]{2,1,0:T(8,128)(2,1)} %copy-done.3, bf16[4,136,512]{2,1,0:T(8,128)(2,1)} %collective-permute-done.1.refs_1_, bf16[4,136,512]{2,1,0:T(8,128)(2,1)} %copy-done.1, bf16[4,136,512]{2,1,0:T(8,128)(2,1)} %collective-permute-done.2.refs_3_, ...), custom_call_target="tpu_custom_call" | custom-call | tf_op jit(solution)/shard_map/backward_counts/pallas_call | solution.py:100
  182.4 0.7 maximum_maximum_fusion.1.bias_ref
  183.1 0.0 collective-permute-done.7.refs_3_
  183.1 0.0 collective-permute-done.9.refs_5_
  183.1 0.0 collective-permute-done.6.refs_1_
  183.1 6.1 %backward_math.1 = (bf16[128,512]{1,0:T(8,128)(2,1)}, bf16[128,16,128]{2,1,0:T(8,128)(2,1)}) custom-call(s32[1]{0:T(128)} %bitcast.29.run_ref, bf16[512,3072]{1,0:T(8,128)(2,1)} %backward_counts.1.counts_ref, bf16[4,128,448]{2,1,0:T(8,128)(2,1)} %copy.28.feats_ref, bf16[16,128]{1,0:T(8,128)(2,1)} %maximum_maximum_fusion.1.bias_ref, ...), custom_call_target="tpu_custom_call" | custom-call | tf_op jit(solution)/shard_map/backward_math/pallas_call | solution.py:168
  189.2 13.8 %all-to-all-start.3 = ((bf16[128,16,128]{2,1,0:T(8,128)(2,1)}), bf16[128,16,128]{2,1,0:T(8,128)(2,1)S(1)}, u32[]{:S(2)}, u32[]{:S(2)}) async-start(bf16[128,16,128]{2,1,0:T(8,128)(2,1)} %get-tuple-element.13), calls=%async_computation.3 | async-start | bytes 1048576 | tf_op jit(solution)/shard_map/all_to_all | solution.py:225
  203.0 0.0 copy-start.7
  203.0 19.5 %all-to-all-done.3 = bf16[128,16,128]{2,1,0:T(8,128)(2,1)S(1)} async-done(((bf16[128,16,128]{2,1,0:T(8,128)(2,1)}), bf16[128,16,128]{2,1,0:T(8,128)(2,1)S(1)}, u32[]{:S(2)}, u32[]{:S(2)}) %all-to-all-start.3) | async-done | bytes 524320 | tf_op jit(solution)/shard_map/all_to_all | solution.py:225
  222.5 0.1 convert_reduce_fusion
  222.6 0.1 maximum_select_fusion
  222.7 11.6 %all_to_all.31 = bf16[8,16,128]{2,1,0:T(8,128)(2,1)S(1)} all-to-all(bf16[8,16,128]{2,1,0:T(8,128)(2,1)S(1)} %broadcast_in_dim.160), channel_id=1, replica_groups=mesh['yh'=2,'x'=4,'z'=8,'yl'=4,'c'=2] {'yh','yl'}, dimensions={0} | all-to-all | bytes 65536 | tf_op jit(solution)/shard_map/all_to_all | solution.py:29
  234.3 0.2 broadcast_in_dim.161
  234.5 28.4 %all_to_all.32 = bf16[32,8,16,128]{3,2,1,0:T(8,128)(2,1)S(1)} all-to-all(bf16[32,8,16,128]{3,2,1,0:T(8,128)(2,1)S(1)} %broadcast_in_dim.161), channel_id=1, replica_groups=mesh['yh'=2,'x'=4,'z'=8,'yl'=4,'c'=2] {'x','z'}, dimensions={0} | all-to-all | bytes 2097152 | tf_op jit(solution)/shard_map/all_to_all | solution.py:29
  262.9 7.3 %collective-permute-start.10 = (bf16[32,8,16,128]{3,2,1,0:T(8,128)(2,1)S(1)}, bf16[32,8,16,128]{3,2,1,0:T(8,128)(2,1)}, u32[]{:S(2)}, u32[]{:S(2)}) collective-permute-start(bf16[32,8,16,128]{3,2,1,0:T(8,128)(2,1)S(1)} %all_to_all.32), channel_id=1, source_target_pairs={{0,1},{1,0},{2,3},{3,2},{4,5},{5,4},{6,7},{7,6},{8,9},{9,8},{10,11... | collective-permute-start | bytes 3145736 | tf_op jit(solution)/shard_map/ppermute | solution.py:40
  270.2 1.5 convolution_convert_fusion
  271.7 0.9 collective-permute-done.10
  272.6 1.4 pad_maximum_fusion
  274.0 0.7 reverse_select_fusion
  274.8 0.6 copy.29
  275.4 0.3 slice.140
  275.7 0.6 fusion.10
  276.3 1.0 copy.30
  277.3 1.6 copy.33
  (26 shorter events, 0.2 us)
Async XLA Ops:
  0.6 20.7 %copy-start = (bf16[1792,512]{1,0:T(8,128)(2,1)S(1)}, bf16[1792,512]{1,0:T(8,128)(2,1)}, u32[]{:S(2)}) copy-start(bf16[1792,512]{1,0:T(8,128)(2,1)} %param.10) | copy-start | bytes 5505028
  21.3 76.5 %copy-start.8 = (s32[128,15]{0,1:T(8,128)S(1)}, s32[128,15]{0,1:T(8,128)}, u32[]{:S(2)}) copy-start(s32[128,15]{0,1:T(8,128)} %param.14) | copy-start | bytes 23044
  21.3 76.5 %copy-start.9 = (s32[128,15]{0,1:T(8,128)S(1)}, s32[128,15]{0,1:T(8,128)}, u32[]{:S(2)}) copy-start(s32[128,15]{0,1:T(8,128)} %param.16) | copy-start | bytes 23044
  22.8 72.1 %copy-start.5 = (bf16[128,512]{1,0:T(8,128)(2,1)}, bf16[128,512]{1,0:T(8,128)(2,1)S(1)}, u32[]{:S(2)}) copy-start(bf16[128,512]{1,0:T(8,128)(2,1)S(1)} %convolution_convert_fusion.1.own_ref) | copy-start | bytes 393220
  41.6 63.1 %copy-start.1 = (bf16[4,136,512]{2,1,0:T(8,128)(2,1)}, bf16[4,136,512]{2,1,0:T(8,128)(2,1)S(1)}, u32[]{:S(2)}) copy-start(bf16[4,136,512]{2,1,0:T(8,128)(2,1)S(1)} %all_to_all.30.refs_2_) | copy-start | bytes 1671172
  41.6 41.3 %collective-permute-start.3 = (bf16[4,136,512]{2,1,0:T(8,128)(2,1)S(1)}, bf16[4,136,512]{2,1,0:T(8,128)(2,1)S(1)}, u32[]{:S(2)}, u32[]{:S(2)}) collective-permute-start(bf16[4,136,512]{2,1,0:T(8,128)(2,1)S(1)} %all_to_all.30.refs_2_), channel_id=1, source_target_pairs={{8,0},{16,8},{24,16},{32,24},{40,32},{48,40},{56,48},{64,56},{72,6... | collective-permute-start | bytes 1671176 | tf_op jit(solution)/shard_map/ppermute | solution.py:36
  58.9 35.9 %collective-permute-start = (bf16[4,136,512]{2,1,0:T(8,128)(2,1)S(1)}, bf16[4,136,512]{2,1,0:T(8,128)(2,1)S(1)}, u32[]{:S(2)}, u32[]{:S(2)}) collective-permute-start(bf16[4,136,512]{2,1,0:T(8,128)(2,1)S(1)} %all_to_all.30.refs_2_), channel_id=1, source_target_pairs={{0,8},{8,16},{16,24},{24,32},{32,40},{40,48},{48,56},{56,64},{64,7... | collective-permute-start | bytes 1671176 | tf_op jit(solution)/shard_map/ppermute | solution.py:36
  60.8 43.8 %collective-permute-start.2 = (bf16[4,136,512]{2,1,0:T(8,128)(2,1)S(1)}, bf16[4,136,512]{2,1,0:T(8,128)(2,1)}, u32[]{:S(2)}, u32[]{:S(2)}) collective-permute-start(bf16[4,136,512]{2,1,0:T(8,128)(2,1)S(1)} %all_to_all.30.refs_2_), channel_id=1, source_target_pairs={{0,1},{1,0},{2,3},{3,2},{4,5},{5,4},{6,7},{7,6},{8,9},{9,8},{10,11... | collective-permute-start | bytes 1671176 | tf_op jit(solution)/shard_map/ppermute | solution.py:40
  82.9 21.8 %copy-start.2 = (bf16[4,136,512]{2,1,0:T(8,128)(2,1)}, bf16[4,136,512]{2,1,0:T(8,128)(2,1)S(1)}, u32[]{:S(2)}) copy-start(bf16[4,136,512]{2,1,0:T(8,128)(2,1)S(1)} %collective-permute-done.3.refs_4_) | copy-start | bytes 1671172
  82.9 21.8 %collective-permute-start.4 = (bf16[4,136,512]{2,1,0:T(8,128)(2,1)S(1)}, bf16[4,136,512]{2,1,0:T(8,128)(2,1)}, u32[]{:S(2)}, u32[]{:S(2)}) collective-permute-start(bf16[4,136,512]{2,1,0:T(8,128)(2,1)S(1)} %collective-permute-done.3.refs_4_), channel_id=1, source_target_pairs={{0,1},{1,0},{2,3},{3,2},{4,5},{5,4},{6,7},{7,6},{8,9},{9,8},{10,11... | collective-permute-start | bytes 1671176 | tf_op jit(solution)/shard_map/ppermute | solution.py:40
  94.8 9.8 %copy-start.3 = (bf16[4,136,512]{2,1,0:T(8,128)(2,1)}, bf16[4,136,512]{2,1,0:T(8,128)(2,1)S(1)}, u32[]{:S(2)}) copy-start(bf16[4,136,512]{2,1,0:T(8,128)(2,1)S(1)} %collective-permute-done.refs_0_) | copy-start | bytes 1671172
  94.8 9.8 %collective-permute-start.1 = (bf16[4,136,512]{2,1,0:T(8,128)(2,1)S(1)}, bf16[4,136,512]{2,1,0:T(8,128)(2,1)}, u32[]{:S(2)}, u32[]{:S(2)}) collective-permute-start(bf16[4,136,512]{2,1,0:T(8,128)(2,1)S(1)} %collective-permute-done.refs_0_), channel_id=1, source_target_pairs={{0,1},{1,0},{2,3},{3,2},{4,5},{5,4},{6,7},{7,6},{8,9},{9,8},{10,11... | collective-permute-start | bytes 1671176 | tf_op jit(solution)/shard_map/ppermute | solution.py:40
  110.5 18.1 %all-to-all-start.2 = ((bf16[4,128,512]{2,1,0:T(8,128)(2,1)}), bf16[4,128,512]{2,1,0:T(8,128)(2,1)S(1)}, u32[]{:S(2)}, u32[]{:S(2)}) async-start(bf16[4,128,512]{2,1,0:T(8,128)(2,1)} %broadcast_in_dim.159), calls=%async_computation.2 | async-start | bytes 1048576 | tf_op jit(solution)/shard_map/all_to_all | solution.py:29
  128.6 53.8 %copy-start.4 = (bf16[4,128,512]{2,1,0:T(8,128)(2,1)}, bf16[4,128,512]{2,1,0:T(8,128)(2,1)S(1)}, u32[]{:S(2)}) copy-start(bf16[4,128,512]{2,1,0:T(8,128)(2,1)S(1)} %all-to-all-done.2.refs_2_) | copy-start | bytes 1572868
  128.6 38.6 %all-to-all-start.1 = ((bf16[4,128,448]{1,2,0:T(8,128)(2,1)}), bf16[4,128,448]{1,2,0:T(8,128)(2,1)S(1)}, u32[]{:S(2)}, u32[]{:S(2)}) async-start(bf16[4,128,448]{1,2,0:T(8,128)(2,1)} %bitcast.32), calls=%async_computation.1 | async-start | bytes 917504 | tf_op jit(solution)/shard_map/all_to_all | solution.py:216
  132.1 29.6 %collective-permute-start.8 = (bf16[4,128,512]{2,1,0:T(8,128)(2,1)S(1)}, bf16[4,128,512]{2,1,0:T(8,128)(2,1)S(1)}, u32[]{:S(2)}, u32[]{:S(2)}) collective-permute-start(bf16[4,128,512]{2,1,0:T(8,128)(2,1)S(1)} %all-to-all-done.2.refs_2_), channel_id=1, source_target_pairs={{8,0},{16,8},{24,16},{32,24},{40,32},{48,40},{56,48},{64,56},{72,6... | collective-permute-start | bytes 1572872 | tf_op jit(solution)/shard_map/ppermute | solution.py:36
  134.0 31.0 %collective-permute-start.5 = (bf16[4,128,512]{2,1,0:T(8,128)(2,1)S(1)}, bf16[4,128,512]{2,1,0:T(8,128)(2,1)}, u32[]{:S(2)}, u32[]{:S(2)}) collective-permute-start(bf16[4,128,512]{2,1,0:T(8,128)(2,1)S(1)} %all-to-all-done.2.refs_2_), channel_id=1, source_target_pairs={{0,8},{8,16},{16,24},{24,32},{32,40},{40,48},{48,56},{56,64},{64,7... | collective-permute-start | bytes 1572872 | tf_op jit(solution)/shard_map/ppermute | solution.py:36
  137.4 45.7 %collective-permute-start.7 = (bf16[4,128,512]{2,1,0:T(8,128)(2,1)S(1)}, bf16[4,128,512]{2,1,0:T(8,128)(2,1)}, u32[]{:S(2)}, u32[]{:S(2)}) collective-permute-start(bf16[4,128,512]{2,1,0:T(8,128)(2,1)S(1)} %all-to-all-done.2.refs_2_), channel_id=1, source_target_pairs={{0,1},{1,0},{2,3},{3,2},{4,5},{5,4},{6,7},{7,6},{8,9},{9,8},{10,11... | collective-permute-start | bytes 1572872 | tf_op jit(solution)/shard_map/ppermute | solution.py:40
  161.7 20.7 %copy-start.6 = (bf16[4,128,512]{2,1,0:T(8,128)(2,1)}, bf16[4,128,512]{2,1,0:T(8,128)(2,1)S(1)}, u32[]{:S(2)}) copy-start(bf16[4,128,512]{2,1,0:T(8,128)(2,1)S(1)} %collective-permute-done.8.refs_4_) | copy-start | bytes 1572868
  161.7 21.4 %collective-permute-start.9 = (bf16[4,128,512]{2,1,0:T(8,128)(2,1)S(1)}, bf16[4,128,512]{2,1,0:T(8,128)(2,1)}, u32[]{:S(2)}, u32[]{:S(2)}) collective-permute-start(bf16[4,128,512]{2,1,0:T(8,128)(2,1)S(1)} %collective-permute-done.8.refs_4_), channel_id=1, source_target_pairs={{0,1},{1,0},{2,3},{3,2},{4,5},{5,4},{6,7},{7,6},{8,9},{9,8},{10,11... | collective-permute-start | bytes 1572872 | tf_op jit(solution)/shard_map/ppermute | solution.py:40
  165.0 18.1 %collective-permute-start.6 = (bf16[4,128,512]{2,1,0:T(8,128)(2,1)}, bf16[4,128,512]{2,1,0:T(8,128)(2,1)}, u32[]{:S(2)}, u32[]{:S(2)}) collective-permute-start(bf16[4,128,512]{2,1,0:T(8,128)(2,1)} %collective-permute-done.5.refs_0_), channel_id=1, source_target_pairs={{0,1},{1,0},{2,3},{3,2},{4,5},{5,4},{6,7},{7,6},{8,9},{9,8},{10,11... | collective-permute-start | bytes 1572872 | tf_op jit(solution)/shard_map/ppermute | solution.py:40
  168.2 14.2 %copy-start.10 = (f32[1,512]{1,0:T(1,128)S(1)}, f32[1,512]{1,0:T(1,128)}, u32[]{:S(2)}) copy-start(f32[1,512]{1,0:T(1,128)} %get-tuple-element.10) | copy-start | bytes 6148
  189.2 33.3 %all-to-all-start.3 = ((bf16[128,16,128]{2,1,0:T(8,128)(2,1)}), bf16[128,16,128]{2,1,0:T(8,128)(2,1)S(1)}, u32[]{:S(2)}, u32[]{:S(2)}) async-start(bf16[128,16,128]{2,1,0:T(8,128)(2,1)} %get-tuple-element.13), calls=%async_computation.3 | async-start | bytes 1048576 | tf_op jit(solution)/shard_map/all_to_all | solution.py:225
  203.0 67.3 %copy-start.7 = (bf16[128,512]{1,0:T(8,128)(2,1)S(1)}, bf16[128,512]{1,0:T(8,128)(2,1)}, u32[]{:S(2)}) copy-start(bf16[128,512]{1,0:T(8,128)(2,1)} %get-tuple-element.12) | copy-start | bytes 393220
  262.9 9.7 %collective-permute-start.10 = (bf16[32,8,16,128]{3,2,1,0:T(8,128)(2,1)S(1)}, bf16[32,8,16,128]{3,2,1,0:T(8,128)(2,1)}, u32[]{:S(2)}, u32[]{:S(2)}) collective-permute-start(bf16[32,8,16,128]{3,2,1,0:T(8,128)(2,1)S(1)} %all_to_all.32), channel_id=1, source_target_pairs={{0,1},{1,0},{2,3},{3,2},{4,5},{5,4},{6,7},{7,6},{8,9},{9,8},{10,11... | collective-permute-start | bytes 3145736 | tf_op jit(solution)/shard_map/ppermute | solution.py:40

commit v2 on v1

v2 whole, which is shorter than its diff:
```python
import jax
import jax.numpy as jnp
from jax import lax
from jax.experimental import pallas as pl
from jax.experimental.pallas import tpu as pltpu
from jax.sharding import Mesh
from jax.sharding import PartitionSpec as P

TILE = 128
KNN = 15
HID = 512
AXES = ("yh", "x", "z", "yl", "c")
SIZES = (2, 4, 8, 4, 2)
WIDE = ("yh", "x", "z")
RUN = 4
PARITY_ROWS = RUN * TILE
KEY_ROWS = 8
DEAD = 31
KEYS = 16
PIECES = 6
F_RUN = 448
SLABS = 128
BIAS_SLAB = 112

i32 = jnp.int32
bf16 = jnp.bfloat16
f32 = jnp.float32


EAGER = pl.CostEstimate(flops=4_000_000_000, transcendentals=0, bytes_accessed=8_000_000)
SMEM_SPEC = pl.BlockSpec(memory_space=pltpu.SMEM)
VMEM_SPEC = pl.BlockSpec(memory_space=pltpu.VMEM)


def spread_to(shard, axes, count):
    return lax.all_to_all(jnp.broadcast_to(shard[None], (count,) + shard.shape), axes, 0, 0)


FAR = ((31, 32), (63, 0))


def neighbours(block):
    count = 64
    forward = [(i, (i + 1) % count) for i in range(count) if i % 32 != 31]
    backward = [(target, source) for source, target in forward]
    return lax.ppermute(block, WIDE, forward), lax.ppermute(block, WIDE, backward)


def across(shard):
    pairs = list(FAR) + [(b, a) for a, b in FAR]
    return lax.ppermute(shard, WIDE, pairs)


def across_run(received):
    parts = [received]
    for step in range(1, RUN):
        pairs = []
        for group in (0, 31, 32, 63):
            for run in range(RUN):
                for core in range(2):
                    source = (group * RUN + run) * 2 + core
                    pairs.append((source, (group * RUN + (run ^ step)) * 2 + core))
        parts.append(lax.ppermute(received, AXES, pairs))
    return jnp.stack(parts)


def swap_core(block):
    return lax.ppermute(block, "c", [(0, 1), (1, 0)])


def gather_window(shard, copies, far_low, far_high, work):
    received = across(shard)
    own = lax.all_to_all(copies, "yl", 0, 0)
    low, high = neighbours(own)
    own_other = swap_core(own)
    remote = across_run(received)
    result = work(own)
    low, high, result = lax.optimization_barrier((low, high, result))
    low = jnp.where(far_low, remote, low)
    high = jnp.where(far_high, remote, high)
    return (low, swap_core(low), own, own_other, high, swap_core(high)), result


def project_kernel(ids_ref, count_ref, tiles_ref, slot_ref, col_ref, keep_ref, features_ref, weight_ref,
                   shard_ref, copies_ref, cells_ref, digits_ref, degree_ref):
    group, run, core = ids_ref[0], ids_ref[1], ids_ref[2]
    far_low, far_high = ids_ref[3], ids_ref[4]
    slot = slot_ref[...]
    live = keep_ref[...] * (slot < count_ref[0]).astype(i32)
    position = jnp.zeros_like(slot)
    for k in range(tiles_ref.shape[1]):
        block = tiles_ref[0, k] - (group - 1) * 8
        block = jnp.where(block < 0, block + 512, block)
        block = jnp.where(block >= 512, block - 512, block)
        position = position + jnp.where(slot == k, block, 0)
    alive = live > 0
    reach = lax.shift_right_logical(position, 3)
    member = jnp.bitwise_and(position, 7)
    other = jnp.bitwise_xor(jnp.bitwise_and(member, 1), core)
    step = lax.shift_right_logical(member, 1)
    twist = jnp.where(reach == 0, far_low * run, jnp.where(reach == 2, far_high * run, 0))
    place = (reach * 2 + other) * RUN + jnp.bitwise_xor(step, twist)
    pad = jnp.zeros((KEYS - KNN, TILE), i32)

    def rows(value):
        return jnp.concatenate([value, pad], axis=0)

    cells_ref[...] = rows(col_ref[...]).T
    digit = lax.shift_left(jnp.ones_like(place), 4 * jnp.bitwise_and(place, 7))
    for third in range(3):
        chosen = jnp.logical_and(alive, lax.shift_right_logical(place, 3) == third)
        digits_ref[third] = rows(jnp.where(chosen, digit, 0)).T
    degree_ref[...] = 1.0 + jnp.sum(rows(live).T.astype(f32), axis=1, keepdims=True)
    blocks = rows(jnp.where(alive, position, DEAD)).astype(f32).astype(bf16)
    cells = rows(col_ref[...]).astype(f32).astype(bf16)
    keys = jnp.concatenate([blocks[:8], blocks[8:], cells[:8], cells[8:]], axis=1)
    projected = jnp.dot(features_ref[...], weight_ref[...], preferred_element_type=f32).astype(bf16)
    shard_ref[:TILE, :] = projected
    shard_ref[TILE:, :] = keys
    for k in range(RUN):
        copies_ref[k, :TILE, :] = projected
        copies_ref[k, TILE:, :] = keys


def project(ids, tile_count, tile_cols, slot, col, keep, features, weight):
    rows = TILE + KEY_ROWS
    return pl.pallas_call(
        project_kernel,
        in_specs=[SMEM_SPEC] * 3 + [VMEM_SPEC] * 5,
        out_shape=(
            jax.ShapeDtypeStruct((rows, HID), bf16),
            jax.ShapeDtypeStruct((RUN, rows, HID), bf16),
            jax.ShapeDtypeStruct((TILE, KEYS), i32),
            jax.ShapeDtypeStruct((3, TILE, KEYS), i32),
            jax.ShapeDtypeStruct((TILE, 1), f32),
        ),
        name="project",
    )(ids, tile_count, tile_cols, slot, col, keep, features, weight)


def forward_counts_kernel(cells_ref, digits_ref, features_ref, out_ref, feats_ref):
    def rows(step, carry):
        here = pl.ds(step * 16, 16)
        lanes = lax.broadcasted_iota(i32, (16, 128), 1)
        cells = cells_ref[here, :]
        digits = [digits_ref[third, here, :] for third in range(3)]
        totals = [jnp.zeros((16, 128), i32) for _ in range(3)]
        for e in range(KNN):
            hit = cells[:, e : e + 1] == lanes
            for third in range(3):
                totals[third] = totals[third] + jnp.where(hit, digits[third][:, e : e + 1], 0)
        for tile in range(PIECES * RUN):
            digit = lax.shift_right_logical(totals[tile // 8], 4 * (tile % 8))
            count = jnp.bitwise_and(digit, 15).astype(f32).astype(bf16)
            out_ref[here, tile * 128 : (tile + 1) * 128] = count
        return carry

    lax.fori_loop(0, TILE // 16, rows, 0)
    for k in range(RUN):
        feats_ref[k] = features_ref[:, k * F_RUN : (k + 1) * F_RUN]


def forward_counts(cells, digits, features):
    return pl.pallas_call(
        forward_counts_kernel,
        in_specs=[VMEM_SPEC] * 3,
        out_shape=(
            jax.ShapeDtypeStruct((TILE, PIECES * PARITY_ROWS), bf16),
            jax.ShapeDtypeStruct((RUN, TILE, F_RUN), bf16),
        ),
        cost_estimate=EAGER,
        name="forward_counts",
    )(cells, digits, features)


def backward_counts_kernel(core_ref, *refs):
    pieces, out_ref = refs[:PIECES], refs[PIECES]
    core = core_ref[0]
    for p in range(PIECES):
        wanted = 2 - p // 2
        for y in range(RUN):
            head = pieces[p][y, TILE : TILE + KEY_ROWS, :].astype(f32).astype(i32)
            cells, digits = [], []
            for half in range(2):
                block = head[:, half * 128 : half * 128 + 128] - (8 * wanted + core)
                valid = jnp.logical_and(
                    jnp.logical_and(block >= 0, block < 8), jnp.bitwise_and(block, 1) == 0
                )
                shift = 2 * jnp.where(valid, block, 0)
                digits.append(jnp.where(valid, lax.shift_left(jnp.ones_like(shift), shift), 0))
                cells.append(head[:, 256 + half * 128 : 384 + half * 128])
            lane = (p * RUN + y) * 128
            for step in range(TILE // 16):
                rows = lax.broadcasted_iota(i32, (16, 128), 0) + step * 16
                total = jnp.zeros((16, 128), i32)
                for e in range(KNN):
                    cell = cells[e // 8][e % 8 : e % 8 + 1, :]
                    digit = digits[e // 8][e % 8 : e % 8 + 1, :]
                    total = total + jnp.where(cell == rows, digit, 0)
                for k in range(RUN):
                    count = jnp.bitwise_and(lax.shift_right_logical(total, 4 * k), 15)
                    at = k * TILE + step * 16
                    out_ref[at : at + 16, lane : lane + 128] = count.astype(f32).astype(bf16)


def backward_counts(core, pieces):
    return pl.pallas_call(
        backward_counts_kernel,
        in_specs=[SMEM_SPEC] + [VMEM_SPEC] * PIECES,
        out_shape=jax.ShapeDtypeStruct((PARITY_ROWS, PIECES * PARITY_ROWS), bf16),
        cost_estimate=EAGER,
        name="backward_counts",
    )(core, *pieces)


def forward_kernel(counts_ref, shard_ref, degree_ref, bias_ref, up_ref, *refs):
    pieces, (hidden_ref, scaled_ref, copies_ref, bias_out_ref) = refs[:PIECES], refs[PIECES:]
    total = shard_ref[:TILE, :].astype(f32)
    for p in range(PIECES):
        for y in range(RUN):
            lane = (p * RUN + y) * 128
            total = total + jnp.dot(
                counts_ref[:, lane : lane + 128],
                pieces[p][y, :TILE, :],
                preferred_element_type=f32,
            )
    degree = degree_ref[...]
    pre = total / degree + bias_ref[...]
    sigma = jax.nn.sigmoid(pre)
    hidden_ref[...] = (pre * sigma).astype(bf16)
    grad_pre = up_ref[...].astype(f32) * sigma * (1.0 + pre * (1.0 - sigma))
    scaled = (grad_pre / degree).astype(bf16)
    scaled_ref[...] = scaled
    for k in range(RUN):
        copies_ref[k] = scaled
    bias_out_ref[...] = jnp.sum(grad_pre, axis=0, keepdims=True)


def forward_math(counts, shard, degree, bias, upstream, pieces):
    return pl.pallas_call(
        forward_kernel,
        in_specs=[VMEM_SPEC] * (5 + PIECES),
        out_shape=(
            jax.ShapeDtypeStruct((TILE, HID), bf16),
            jax.ShapeDtypeStruct((TILE, HID), bf16),
            jax.ShapeDtypeStruct((RUN, TILE, HID), bf16),
            jax.ShapeDtypeStruct((1, HID), f32),
        ),
        name="forward_math",
    )(counts, shard, degree, bias, upstream, *pieces)


def backward_kernel(run_ref, counts_ref, feats_ref, bias_ref, *refs):
    pieces, (own_ref, slab_ref, round_ref) = refs[:PIECES], refs[PIECES:]
    total = pieces[2][...].reshape(PARITY_ROWS, HID).astype(f32)
    for p in range(PIECES):
        total = total + jnp.dot(
            counts_ref[:, p * PARITY_ROWS : (p + 1) * PARITY_ROWS],
            pieces[p][...].reshape(PARITY_ROWS, HID),
            preferred_element_type=f32,
        )
    rounded = total.astype(bf16)
    round_ref[...] = rounded.reshape(RUN, TILE, HID)
    own_ref[...] = round_ref[run_ref[0]]
    part = lax.dot_general(
        feats_ref[...].reshape(PARITY_ROWS, F_RUN),
        rounded,
        (((0,), (0,)), ((), ())),
        preferred_element_type=f32,
    ).astype(bf16)
    for row in range(F_RUN // 16):
        for lane in range(HID // 128):
            slab_ref[row * 4 + lane] = part[row * 16 : row * 16 + 16, lane * 128 : lane * 128 + 128]
    slab_ref[BIAS_SLAB] = bias_ref[...]
    for rest in range(BIAS_SLAB + 1, SLABS):
        slab_ref[rest] = jnp.zeros((16, 128), bf16)


def backward_math(run, counts, feats, bias_rows, pieces):
    return pl.pallas_call(
        backward_kernel,
        in_specs=[SMEM_SPEC] + [VMEM_SPEC] * (3 + PIECES),
        out_shape=(
            jax.ShapeDtypeStruct((TILE, HID), bf16),
            jax.ShapeDtypeStruct((SLABS, 16, 128), bf16),
        ),
        scratch_shapes=[pltpu.VMEM((RUN, TILE, HID), bf16)],
        name="backward_math",
    )(run, counts, feats, bias_rows, *pieces)


def high_low(value):
    high = lax.reduce_precision(value, 8, 7)
    return jnp.concatenate([high, value - high, jnp.zeros((8, 128), f32)], axis=0).astype(bf16)


def assemble_kernel(core_ref, mine_ref, other_ref, weight_ref, bias_ref):
    first = core_ref[0] == 0
    bias = jnp.zeros((4, 128), f32)
    for plane in range(32):
        x, z = plane // 8, plane % 8
        for column in range(8):
            yh, run = column // 4, column % 4
            mine, other = mine_ref[plane, column], other_ref[plane, column]
            for core in range(2):
                slab = ((yh * 4 + x) * 8 + z) * 2 + core
                if slab > BIAS_SLAB:
                    continue
                keep = first if core == 0 else jnp.logical_not(first)
                value = jnp.where(keep, mine, other)
                if slab == BIAS_SLAB:
                    rows = value.astype(f32)
                    bias = bias + (rows[:4] + rows[4:8])
                    continue
                row, lane = run * F_RUN + (slab // 4) * 16, (slab % 4) * 128
                weight_ref[row : row + 16, lane : lane + 128] = value
    bias_ref[...] = bias


def assemble(core, mine, other):
    return pl.pallas_call(
        assemble_kernel,
        in_specs=[SMEM_SPEC] + [VMEM_SPEC] * 2,
        out_shape=(
            jax.ShapeDtypeStruct((RUN * F_RUN, HID), bf16),
            jax.ShapeDtypeStruct((4, 128), f32),
        ),
        name="assemble",
    )(core, mine, other)


def on_device(features, weight, bias, tile_cols, tile_count, nbr_slot, nbr_col, nbr_keep, upstream):
    group = (lax.axis_index("yh") * 4 + lax.axis_index("x")) * 8 + lax.axis_index("z")
    run = lax.axis_index("yl")
    core = lax.axis_index("c")
    core_id = core.reshape(1).astype(i32)
    far_low = group % 32 == 0
    far_high = group % 32 == 31
    ids = jnp.stack([group, run, core, far_low.astype(i32), far_high.astype(i32)]).astype(i32)

    shard, copies, cells, digits, degree = project(
        ids, tile_count, tile_cols, nbr_slot.T, nbr_col.T, nbr_keep.T, features, weight
    )

    def count_forward(own):
        tied, _ = lax.optimization_barrier((cells, own))
        return forward_counts(tied, digits, features)

    first, (counts, slices) = gather_window(shard, copies, far_low, far_high, count_forward)
    feats = lax.all_to_all(slices, "yl", 0, 0)
    hidden, scaled, scaled_copies, bias_part = forward_math(
        counts, shard, degree, bias[None], upstream, first
    )

    def count_backward(own):
        tied, _ = lax.optimization_barrier((core_id, own))
        return backward_counts(tied, first)

    second, counts_back = gather_window(
        scaled, scaled_copies, far_low, far_high, count_backward
    )
    own_round, slabs = backward_math(
        run.reshape(1), counts_back, feats, high_low(bias_part.reshape(4, 128)), second
    )
    reduced = jnp.sum(lax.all_to_all(slabs, WIDE + ("c",), 0, 0).astype(f32), axis=0)
    is_bias = (group * 2 + core) == BIAS_SLAB
    piece = jnp.where(is_bias, high_low(reduced[:4] + reduced[4:8]), reduced.astype(bf16))
    column = spread_to(piece, ("yh", "yl"), 8)
    plane = spread_to(column, ("x", "z"), 32)
    weight_grad, bias_grad = assemble(core_id, plane, swap_core(plane))
    grad_features = lax.dot_general(
        own_round, weight, (((1,), (1,)), ((), ())), preferred_element_type=f32
    ).astype(bf16)
    return hidden, grad_features, weight_grad, bias_grad.reshape(HID)


def solution(mesh):
    split = Mesh(mesh.devices.reshape(SIZES), AXES)
    rows = P(AXES, None)
    in_specs = (rows, P(), P(), rows, P(AXES), rows, rows, rows, rows)
    out_specs = (rows, rows, P(), P())
    return jax.shard_map(
        on_device, mesh=split, in_specs=in_specs, out_specs=out_specs, check_vma=False
    )
```

time: 280 us -> 242 us (0.86)
  waiting for transfers between devices: 81.9 us -> 26.2 us
  starting transfers between devices: 70.3 us -> 101 us
  other arithmetic: 20.1 us -> 3.08 us
  blocking collectives: 58.7 us -> 72.5 us
  local copies, waits for them, and re-layouts: 13.6 us -> 7.31 us
    ppermute x0 -> x8, starting transfers between devices: none -> 44.5 us  [the longest x2 26 us: across(): return lax.ppermute(shard, WIDE, pairs)]
    ppermute x2, waiting for transfers between devices: 39.5 us -> 0.01 us  [neighbours(): lax.ppermute(block, WIDE, backward)]
    all_to_all x0 -> x2, blocking collectives: none -> 33.8 us  [gather_window(): own = lax.all_to_all(copies, 'yl', 0, 0)]
    all_to_all x3 -> x2, blocking collectives: 58.7 us -> 38.7 us  [spread_to(): lax.all_to_all(jnp.broadcast_to(shard[None], (count,) + shard.shape), axe...]
    ppermute x2, starting transfers between devices: 19.2 us -> 2.57 us  [neighbours(): lax.ppermute(block, WIDE, backward)]
    convert_element_type x3 -> x0, other arithmetic: 16.5 us -> none  [the longest x1 15.7 us: on_device(): block_rows = jnp.concatenate([key_block.T.astype(bf16), pad], axis=0)]
    all_to_all x2 -> x1, waiting for transfers between devices: 12.6 us -> 0.01 us  [on_device(): feats = lax.all_to_all(slices, 'yl', 0, 0)]
    ppermute x2, waiting for transfers between devices: 9.37 us -> 0.01 us  [neighbours(): lax.ppermute(block, WIDE, forward)]
  transfers between devices with their start and end apart: 14 -> 21, of which waited for: 6 -> 4; matrix products, arithmetic and copies ran while one was open for 2% -> 3% of each run, Pallas kernels for 7% -> 5%
where the time goes in v2:
time: 242 us; the launch traced here: 241 us
  starting transfers between devices  101 us (42%)
  blocking collectives  72.5 us (30%)
  Pallas kernels  27.4 us (11%)
  waiting for transfers between devices  26.2 us (11%)
  local copies, waits for them, and re-layouts  7.31 us (3%)
  other arithmetic  3.08 us (1%)
    all_to_all x2, blocking collectives, spread_to(): lax.all_to_all(jnp.broadcast_to(shard[None], (count,) + shard.shape), axe...  38.7 us
    all_to_all x2, blocking collectives, gather_window(): own = lax.all_to_all(copies, 'yl', 0, 0)  33.8 us
    ppermute x7, starting transfers between devices, swap_core(): return lax.ppermute(block, 'c', [(0, 1), (1, 0)])  29 us
    ppermute x2, starting transfers between devices, across(): return lax.ppermute(shard, WIDE, pairs)  26 us
    all_to_all x1, waiting for transfers between devices, on_device(): lax.all_to_all(slabs, WIDE + ('c',), 0, 0).astype(f32)  20.5 us
    ppermute x6, starting transfers between devices, across_run(): parts.append(lax.ppermute(received, AXES, pairs))  18.5 us
    ppermute x2, starting transfers between devices, neighbours(): lax.ppermute(block, WIDE, forward)  12 us
    all_to_all x1, starting transfers between devices, on_device(): lax.all_to_all(slabs, WIDE + ('c',), 0, 0).astype(f32)  9.68 us
  transfers between devices with their start and end apart: 21, of which 4 were waited for; matrix products, arithmetic and copies ran while one was open for 3% of the time, Pallas kernels for 5%

profile of v2, /device:TPU:1, one launch (start us, length us, event | category | flops | bytes accessed | tf_op | source)
XLA Modules:
  0.0 240.9 jit_solution(569340399063567562)
XLA Ops:
  1.3 0.7 stack.61.ids_ref
  2.0 3.0 %project.1 = (bf16[136,512]{1,0:T(8,128)(2,1)}, bf16[4,136,512]{2,1,0:T(8,128)(2,1)}, s32[128,16]{1,0:T(8,128)}, s32[3,128,16]{2,1,0:T(8,128)}, f32[128,1]{1,0:T(8,128)}) custom-call(s32[5]{0:T(128)} %stack.61.ids_ref, s32[1]{0:T(128)S(6)} %copy.15.count_ref, s32[1,24]{1,0:T(1,128)} %tiles_ref.1, s32[15,128]{1,0:T(8,128)} %bitcast.29, s32[15,128]{1,0:T(8,128)} %bitcast.30, ...), custom_call_target="tpu_custom_call" | custom-call | tf_op jit(solution)/shard_map/project/pallas_call | solution.py:127
  5.0 16.1 %all_to_all.30.refs_2_ = bf16[4,136,512]{2,1,0:T(8,128)(2,1)S(1)} all-to-all(bf16[4,136,512]{2,1,0:T(8,128)(2,1)} %get-tuple-element.28), channel_id=1, replica_groups=mesh['yh'=2,'x'=4,'z'=8,'yl'=4,'c'=2] {'yl'}, dimensions={0} | all-to-all | bytes 1114112 | tf_op jit(solution)/shard_map/all_to_all | solution.py:73
  21.1 8.0 %collective-permute-start = (bf16[4,136,512]{2,1,0:T(8,128)(2,1)S(1)}, bf16[4,136,512]{2,1,0:T(8,128)(2,1)S(1)}, u32[]{:S(2)}, u32[]{:S(2)}) collective-permute-start(bf16[4,136,512]{2,1,0:T(8,128)(2,1)S(1)} %all_to_all.30.refs_2_), channel_id=1, source_target_pairs={{0,8},{8,16},{16,24},{24,32},{32,40},{40,48},{48,56},{56,64},{64,7... | collective-permute-start | bytes 1671176 | tf_op jit(solution)/shard_map/ppermute | solution.py:46
  29.1 1.3 collective-permute-start.1
  30.4 17.1 %collective-permute-start.2 = (bf16[136,512]{1,0:T(8,128)(2,1)}, bf16[136,512]{1,0:T(8,128)(2,1)S(1)}, u32[]{:S(2)}, u32[]{:S(2)}) collective-permute-start(bf16[136,512]{1,0:T(8,128)(2,1)} %get-tuple-element.35.shard_ref), channel_id=1, source_target_pairs={{248,256},{504,0},{256,248},{0,504},{249,257},{505,1},{257,249},{1... | collective-permute-start | bytes 417800 | tf_op jit(solution)/shard_map/ppermute | solution.py:51
  47.4 3.2 %collective-permute-done.2 = bf16[136,512]{1,0:T(8,128)(2,1)S(1)} collective-permute-done((bf16[136,512]{1,0:T(8,128)(2,1)}, bf16[136,512]{1,0:T(8,128)(2,1)S(1)}, u32[]{:S(2)}, u32[]{:S(2)}) %collective-permute-start.2) | collective-permute-done | bytes 139296 | tf_op jit(solution)/shard_map/ppermute | solution.py:51
  50.7 1.9 collective-permute-start.3
  52.6 4.0 %collective-permute-start.4 = (bf16[136,512]{1,0:T(8,128)(2,1)S(1)}, bf16[136,512]{1,0:T(8,128)(2,1)S(1)}, u32[]{:S(2)}, u32[]{:S(2)}) collective-permute-start(bf16[136,512]{1,0:T(8,128)(2,1)S(1)} %collective-permute-done.2), channel_id=1, source_target_pairs={{0,4},{1,5},{2,6},{3,7},{4,0},{5,1},{6,2},{7,3},{248,252},{249,253... | collective-permute-start | bytes 417800 | tf_op jit(solution)/shard_map/ppermute | solution.py:63
  56.6 3.4 %collective-permute-start.5 = (bf16[136,512]{1,0:T(8,128)(2,1)S(1)}, bf16[136,512]{1,0:T(8,128)(2,1)S(1)}, u32[]{:S(2)}, u32[]{:S(2)}) collective-permute-start(bf16[136,512]{1,0:T(8,128)(2,1)S(1)} %collective-permute-done.2), channel_id=1, source_target_pairs={{0,6},{1,7},{2,4},{3,5},{4,2},{5,3},{6,0},{7,1},{248,254},{249,255... | collective-permute-start | bytes 417800 | tf_op jit(solution)/shard_map/ppermute | solution.py:63
  59.9 4.1 %forward_counts.1 = (bf16[128,3072]{1,0:T(8,128)(2,1)}, bf16[4,128,448]{2,1,0:T(8,128)(2,1)}) custom-call(s32[128,16]{1,0:T(8,128)} %get-tuple-element.30.cells_ref, s32[3,128,16]{2,1,0:T(8,128)} %get-tuple-element.31.digits_ref, bf16[128,1792]{1,0:T(8,128)(2,1)} %features_ref.3), custom_call_target="tpu_custom_call" | custom-call | flops 4000000000 | bytes 8000000 | tf_op jit(solution)/shard_map/forward_counts/pallas_call | solution.py:164
  64.1 0.0 collective-permute-done
  64.1 6.4 %collective-permute-start.7 = (bf16[4,136,512]{2,1,0:T(8,128)(2,1)S(1)}, bf16[4,136,512]{2,1,0:T(8,128)(2,1)S(1)}, u32[]{:S(2)}, u32[]{:S(2)}) collective-permute-start(bf16[4,136,512]{2,1,0:T(8,128)(2,1)S(1)} %all_to_all.30.refs_2_), channel_id=1, source_target_pairs={{0,1},{1,0},{2,3},{3,2},{4,5},{5,4},{6,7},{7,6},{8,9},{9,8},{10,11... | collective-permute-start | bytes 1671176 | tf_op jit(solution)/shard_map/ppermute | solution.py:68
  70.5 0.0 collective-permute-done.1
  70.5 0.0 collective-permute-done.4
  70.5 0.0 collective-permute-done.5
  70.5 0.0 copy-start.16
  70.5 0.6 copy-done.14
  71.1 0.1 copy-done.15
  71.2 0.0 copy-done.16
  71.2 1.2 broadcast_select_fusion
  72.4 1.9 collective-permute-start.6
  74.4 2.4 collective-permute-start.8
  76.8 0.0 collective-permute-done.6.refs_1_
  76.8 1.5 collective-permute-done.8.refs_5_
  78.3 0.8 copy-done.10
  79.2 4.3 %forward_math.1 = (bf16[128,512]{1,0:T(8,128)(2,1)}, bf16[128,512]{1,0:T(8,128)(2,1)}, bf16[4,128,512]{2,1,0:T(8,128)(2,1)}, f32[1,512]{1,0:T(1,128)}) custom-call(bf16[128,3072]{1,0:T(8,128)(2,1)} %get-tuple-element.34.counts_ref, bf16[136,512]{1,0:T(8,128)(2,1)} %get-tuple-element.35.shard_ref, f32[128,1]{1,0:T(8,128)} %get-tuple-element.36.degree_ref, ...), custom_call_target="tpu_custom_call" | custom-call | tf_op jit(solution)/shard_map/forward_math/pallas_call | solution.py:240
  83.4 17.7 %all_to_all.31.refs_2_ = bf16[4,128,512]{2,1,0:T(8,128)(2,1)S(1)} all-to-all(bf16[4,128,512]{2,1,0:T(8,128)(2,1)} %get-tuple-element.40), channel_id=1, replica_groups=mesh['yh'=2,'x'=4,'z'=8,'yl'=4,'c'=2] {'yl'}, dimensions={0} | all-to-all | bytes 1048576 | tf_op jit(solution)/shard_map/all_to_all | solution.py:73
  101.1 1.3 collective-permute-start.10
  102.4 4.0 %collective-permute-start.9 = (bf16[4,128,512]{2,1,0:T(8,128)(2,1)S(1)}, bf16[4,128,512]{2,1,0:T(8,128)(2,1)S(1)}, u32[]{:S(2)}, u32[]{:S(2)}) collective-permute-start(bf16[4,128,512]{2,1,0:T(8,128)(2,1)S(1)} %all_to_all.31.refs_2_), channel_id=1, source_target_pairs={{0,8},{8,16},{16,24},{24,32},{32,40},{40,48},{48,56},{56,64},{64,7... | collective-permute-start | bytes 1572872 | tf_op jit(solution)/shard_map/ppermute | solution.py:46
  106.5 8.9 %collective-permute-start.11 = (bf16[128,512]{1,0:T(8,128)(2,1)}, bf16[128,512]{1,0:T(8,128)(2,1)S(1)}, u32[]{:S(2)}, u32[]{:S(2)}) collective-permute-start(bf16[128,512]{1,0:T(8,128)(2,1)} %get-tuple-element.45), channel_id=1, source_target_pairs={{248,256},{504,0},{256,248},{0,504},{249,257},{505,1},{257,249},{1... | collective-permute-start | bytes 393224 | tf_op jit(solution)/shard_map/ppermute | solution.py:51
  115.4 2.0 copy.13
  117.4 3.5 %all-to-all-start.2 = ((bf16[4,128,448]{1,2,0:T(8,128)(2,1)}), bf16[4,128,448]{1,2,0:T(8,128)(2,1)S(1)}, u32[]{:S(2)}, u32[]{:S(2)}) async-start(bf16[4,128,448]{1,2,0:T(8,128)(2,1)} %copy.13), calls=%async_computation.2 | async-start | bytes 917504 | tf_op jit(solution)/shard_map/all_to_all | solution.py:350
  120.8 0.0 collective-permute-done.11
  120.9 3.3 %collective-permute-start.12 = (bf16[128,512]{1,0:T(8,128)(2,1)S(1)}, bf16[128,512]{1,0:T(8,128)(2,1)S(1)}, u32[]{:S(2)}, u32[]{:S(2)}) collective-permute-start(bf16[128,512]{1,0:T(8,128)(2,1)S(1)} %collective-permute-done.11), channel_id=1, source_target_pairs={{0,2},{1,3},{2,0},{3,1},{4,6},{5,7},{6,4},{7,5},{248,250},{249,251... | collective-permute-start | bytes 393224 | tf_op jit(solution)/shard_map/ppermute | solution.py:63
  124.2 4.0 %collective-permute-start.13 = (bf16[128,512]{1,0:T(8,128)(2,1)S(1)}, bf16[128,512]{1,0:T(8,128)(2,1)S(1)}, u32[]{:S(2)}, u32[]{:S(2)}) collective-permute-start(bf16[128,512]{1,0:T(8,128)(2,1)S(1)} %collective-permute-done.11), channel_id=1, source_target_pairs={{0,4},{1,5},{2,6},{3,7},{4,0},{5,1},{6,2},{7,3},{248,252},{249,253... | collective-permute-start | bytes 393224 | tf_op jit(solution)/shard_map/ppermute | solution.py:63
  128.2 2.0 collective-permute-start.14
  130.1 7.1 %backward_counts.1.counts_ref = bf16[512,3072]{1,0:T(8,128)(2,1)} custom-call(s32[1]{0:T(128)} %bitcast.2.core_ref, bf16[4,136,512]{2,1,0:T(8,128)(2,1)} %copy-done.3, bf16[4,136,512]{2,1,0:T(8,128)(2,1)} %copy-done.9, bf16[4,136,512]{2,1,0:T(8,128)(2,1)} %copy-done.4, bf16[4,136,512]{2,1,0:T(8,128)(2,1)} %copy-done.8, bf16[4,136,512]{2,1,0:T(8,128)(2,1)} %copy-done.2, ...), custom_call_target="tpu_custom_call" | custom-call | flops 4000000000 | bytes 8000000 | tf_op jit(solution)/shard_map/backward_counts/pallas_call | solution.py:207
  137.3 6.6 %collective-permute-start.16 = (bf16[4,128,512]{2,1,0:T(8,128)(2,1)S(1)}, bf16[4,128,512]{2,1,0:T(8,128)(2,1)S(1)}, u32[]{:S(2)}, u32[]{:S(2)}) collective-permute-start(bf16[4,128,512]{2,1,0:T(8,128)(2,1)S(1)} %all_to_all.31.refs_2_), channel_id=1, source_target_pairs={{0,1},{1,0},{2,3},{3,2},{4,5},{5,4},{6,7},{7,6},{8,9},{9,8},{10,11... | collective-permute-start | bytes 1572872 | tf_op jit(solution)/shard_map/ppermute | solution.py:68
  143.9 0.0 copy-start.12
  143.9 0.7 copy-done.12
  144.7 0.0 copy-done.18
  144.7 1.0 broadcast_select_fusion.2
  145.8 2.2 collective-permute-start.15
  147.9 2.1 collective-permute-start.17
  150.1 0.1 pad.9.clone
  150.2 0.7 maximum_maximum_fusion.bias_ref
  150.9 1.0 copy.14.feats_ref
  151.9 0.8 copy-done.11
  152.7 0.2 copy-done.13
  152.9 5.8 %backward_math.1 = (bf16[128,512]{1,0:T(8,128)(2,1)}, bf16[128,16,128]{2,1,0:T(8,128)(2,1)}) custom-call(s32[1]{0:T(128)} %bitcast.1.run_ref, bf16[512,3072]{1,0:T(8,128)(2,1)} %backward_counts.1.counts_ref, bf16[4,128,448]{2,1,0:T(8,128)(2,1)} %copy.14.feats_ref, bf16[16,128]{1,0:T(8,128)(2,1)} %maximum_maximum_fusion.bias_ref, ...), custom_call_target="tpu_custom_call" | custom-call | tf_op jit(solution)/shard_map/backward_math/pallas_call | solution.py:280
  158.7 9.7 %all-to-all-start.3 = ((bf16[128,16,128]{2,1,0:T(8,128)(2,1)}), bf16[128,16,128]{2,1,0:T(8,128)(2,1)S(1)}, u32[]{:S(2)}, u32[]{:S(2)}) async-start(bf16[128,16,128]{2,1,0:T(8,128)(2,1)} %get-tuple-element.49), calls=%async_computation.3 | async-start | bytes 1048576 | tf_op jit(solution)/shard_map/all_to_all | solution.py:365
  168.4 0.0 copy-start
  168.4 0.0 copy-start.17
  168.4 20.5 %all-to-all-done.3 = bf16[128,16,128]{2,1,0:T(8,128)(2,1)S(1)} async-done(((bf16[128,16,128]{2,1,0:T(8,128)(2,1)}), bf16[128,16,128]{2,1,0:T(8,128)(2,1)S(1)}, u32[]{:S(2)}, u32[]{:S(2)}) %all-to-all-start.3) | async-done | bytes 524320 | tf_op jit(solution)/shard_map/all_to_all | solution.py:365
  188.9 0.1 convert_reduce_fusion
  189.1 0.1 maximum_select_fusion
  189.1 10.4 %all_to_all.32 = bf16[8,16,128]{2,1,0:T(8,128)(2,1)S(1)} all-to-all(bf16[8,16,128]{2,1,0:T(8,128)(2,1)S(1)} %broadcast_in_dim.7), channel_id=1, replica_groups=mesh['yh'=2,'x'=4,'z'=8,'yl'=4,'c'=2] {'yh','yl'}, dimensions={0} | all-to-all | bytes 65536 | tf_op jit(solution)/shard_map/all_to_all | solution.py:36
  199.5 0.2 broadcast_in_dim.8
  199.8 28.3 %all_to_all.33.mine_ref = bf16[32,8,16,128]{3,2,1,0:T(8,128)(2,1)S(1)} all-to-all(bf16[32,8,16,128]{3,2,1,0:T(8,128)(2,1)S(1)} %broadcast_in_dim.8), channel_id=1, replica_groups=mesh['yh'=2,'x'=4,'z'=8,'yl'=4,'c'=2] {'x','z'}, dimensions={0} | all-to-all | bytes 2097152 | tf_op jit(solution)/shard_map/all_to_all | solution.py:36
  228.1 7.3 %collective-permute-start.18 = (bf16[32,8,16,128]{3,2,1,0:T(8,128)(2,1)S(1)}, bf16[32,8,16,128]{3,2,1,0:T(8,128)(2,1)}, u32[]{:S(2)}, u32[]{:S(2)}) collective-permute-start(bf16[32,8,16,128]{3,2,1,0:T(8,128)(2,1)S(1)} %all_to_all.33.mine_ref), channel_id=1, source_target_pairs={{0,1},{1,0},{2,3},{3,2},{4,5},{5,4},{6,7},{7,6},{8,9},{9,8},{10,11... | collective-permute-start | bytes 3145736 | tf_op jit(solution)/shard_map/ppermute | solution.py:68
  235.4 1.5 convolution_convert_fusion
  236.9 0.9 collective-permute-done.18.other_ref
  237.8 3.1 %assemble.1 = (bf16[1792,512]{1,0:T(8,128)(2,1)}, f32[4,128]{1,0:T(4,128)}) custom-call(s32[1]{0:T(128)} %bitcast.2.core_ref, bf16[32,8,16,128]{3,2,1,0:T(8,128)(2,1)} %copy-done.1, bf16[32,8,16,128]{3,2,1,0:T(8,128)(2,1)} %collective-permute-done.18.other_ref), custom_call_target="tpu_custom_call" | custom-call | tf_op jit(solution)/shard_map/assemble/pallas_call | solution.py:321
  (43 shorter events, 0.1 us)
Async XLA Ops:
  21.0 43.0 %copy-start.4 = (bf16[4,136,512]{2,1,0:T(8,128)(2,1)}, bf16[4,136,512]{2,1,0:T(8,128)(2,1)S(1)}, u32[]{:S(2)}) copy-start(bf16[4,136,512]{2,1,0:T(8,128)(2,1)S(1)} %all_to_all.30.refs_2_) | copy-start | bytes 1671172
  21.1 43.0 %collective-permute-start = (bf16[4,136,512]{2,1,0:T(8,128)(2,1)S(1)}, bf16[4,136,512]{2,1,0:T(8,128)(2,1)S(1)}, u32[]{:S(2)}, u32[]{:S(2)}) collective-permute-start(bf16[4,136,512]{2,1,0:T(8,128)(2,1)S(1)} %all_to_all.30.refs_2_), channel_id=1, source_target_pairs={{0,8},{8,16},{16,24},{24,32},{32,40},{40,48},{48,56},{56,64},{64,7... | collective-permute-start | bytes 1671176 | tf_op jit(solution)/shard_map/ppermute | solution.py:46
  29.1 41.4 %collective-permute-start.1 = (bf16[4,136,512]{2,1,0:T(8,128)(2,1)S(1)}, bf16[4,136,512]{2,1,0:T(8,128)(2,1)S(1)}, u32[]{:S(2)}, u32[]{:S(2)}) collective-permute-start(bf16[4,136,512]{2,1,0:T(8,128)(2,1)S(1)} %all_to_all.30.refs_2_), channel_id=1, source_target_pairs={{8,0},{16,8},{24,16},{32,24},{40,32},{48,40},{56,48},{64,56},{72,6... | collective-permute-start | bytes 1671176 | tf_op jit(solution)/shard_map/ppermute | solution.py:46
  30.4 20.3 %collective-permute-start.2 = (bf16[136,512]{1,0:T(8,128)(2,1)}, bf16[136,512]{1,0:T(8,128)(2,1)S(1)}, u32[]{:S(2)}, u32[]{:S(2)}) collective-permute-start(bf16[136,512]{1,0:T(8,128)(2,1)} %get-tuple-element.35.shard_ref), channel_id=1, source_target_pairs={{248,256},{504,0},{256,248},{0,504},{249,257},{505,1},{257,249},{1... | collective-permute-start | bytes 417800 | tf_op jit(solution)/shard_map/ppermute | solution.py:51
  50.7 19.8 %collective-permute-start.3 = (bf16[136,512]{1,0:T(8,128)(2,1)S(1)}, bf16[136,512]{1,0:T(8,128)(2,1)S(1)}, u32[]{:S(2)}, u32[]{:S(2)}) collective-permute-start(bf16[136,512]{1,0:T(8,128)(2,1)S(1)} %collective-permute-done.2), channel_id=1, source_target_pairs={{0,2},{1,3},{2,0},{3,1},{4,6},{5,7},{6,4},{7,5},{248,250},{249,251... | collective-permute-start | bytes 417800 | tf_op jit(solution)/shard_map/ppermute | solution.py:63
  52.6 17.9 %collective-permute-start.4 = (bf16[136,512]{1,0:T(8,128)(2,1)S(1)}, bf16[136,512]{1,0:T(8,128)(2,1)S(1)}, u32[]{:S(2)}, u32[]{:S(2)}) collective-permute-start(bf16[136,512]{1,0:T(8,128)(2,1)S(1)} %collective-permute-done.2), channel_id=1, source_target_pairs={{0,4},{1,5},{2,6},{3,7},{4,0},{5,1},{6,2},{7,3},{248,252},{249,253... | collective-permute-start | bytes 417800 | tf_op jit(solution)/shard_map/ppermute | solution.py:63
  56.6 14.0 %collective-permute-start.5 = (bf16[136,512]{1,0:T(8,128)(2,1)S(1)}, bf16[136,512]{1,0:T(8,128)(2,1)S(1)}, u32[]{:S(2)}, u32[]{:S(2)}) collective-permute-start(bf16[136,512]{1,0:T(8,128)(2,1)S(1)} %collective-permute-done.2), channel_id=1, source_target_pairs={{0,6},{1,7},{2,4},{3,5},{4,2},{5,3},{6,0},{7,1},{248,254},{249,255... | collective-permute-start | bytes 417800 | tf_op jit(solution)/shard_map/ppermute | solution.py:63
  64.1 12.7 %collective-permute-start.7 = (bf16[4,136,512]{2,1,0:T(8,128)(2,1)S(1)}, bf16[4,136,512]{2,1,0:T(8,128)(2,1)S(1)}, u32[]{:S(2)}, u32[]{:S(2)}) collective-permute-start(bf16[4,136,512]{2,1,0:T(8,128)(2,1)S(1)} %all_to_all.30.refs_2_), channel_id=1, source_target_pairs={{0,1},{1,0},{2,3},{3,2},{4,5},{5,4},{6,7},{7,6},{8,9},{9,8},{10,11... | collective-permute-start | bytes 1671176 | tf_op jit(solution)/shard_map/ppermute | solution.py:68
  70.5 0.6 copy-start.14
  70.5 0.7 copy-start.15
  70.5 0.7 copy-start.16
  72.4 6.7 %copy-start.2 = (bf16[4,136,512]{2,1,0:T(8,128)(2,1)}, bf16[4,136,512]{2,1,0:T(8,128)(2,1)S(1)}, u32[]{:S(2)}) copy-start(bf16[4,136,512]{2,1,0:T(8,128)(2,1)S(1)} %get-tuple-element.52.refs_4_) | copy-start | bytes 1671172
  72.4 6.7 %copy-start.3 = (bf16[4,136,512]{2,1,0:T(8,128)(2,1)}, bf16[4,136,512]{2,1,0:T(8,128)(2,1)S(1)}, u32[]{:S(2)}) copy-start(bf16[4,136,512]{2,1,0:T(8,128)(2,1)S(1)} %get-tuple-element.53.refs_0_) | copy-start | bytes 1671172
  72.4 4.4 %collective-permute-start.6 = (bf16[4,136,512]{2,1,0:T(8,128)(2,1)S(1)}, bf16[4,136,512]{2,1,0:T(8,128)(2,1)S(1)}, u32[]{:S(2)}, u32[]{:S(2)}) collective-permute-start(bf16[4,136,512]{2,1,0:T(8,128)(2,1)S(1)} %get-tuple-element.53.refs_0_), channel_id=1, source_target_pairs={{0,1},{1,0},{2,3},{3,2},{4,5},{5,4},{6,7},{7,6},{8,9},{9,8},{10,11... | collective-permute-start | bytes 1671176 | tf_op jit(solution)/shard_map/ppermute | solution.py:68
  74.4 4.0 %collective-permute-start.8 = (bf16[4,136,512]{2,1,0:T(8,128)(2,1)S(1)}, bf16[4,136,512]{2,1,0:T(8,128)(2,1)S(1)}, u32[]{:S(2)}, u32[]{:S(2)}) collective-permute-start(bf16[4,136,512]{2,1,0:T(8,128)(2,1)S(1)} %get-tuple-element.52.refs_4_), channel_id=1, source_target_pairs={{0,1},{1,0},{2,3},{3,2},{4,5},{5,4},{6,7},{7,6},{8,9},{9,8},{10,11... | collective-permute-start | bytes 1671176 | tf_op jit(solution)/shard_map/ppermute | solution.py:68
  76.8 2.4 copy-start.8
  76.8 2.4 copy-start.9
  78.3 0.8 copy-start.10
  101.1 36.1 %copy-start.7 = (bf16[4,128,512]{2,1,0:T(8,128)(2,1)}, bf16[4,128,512]{2,1,0:T(8,128)(2,1)S(1)}, u32[]{:S(2)}) copy-start(bf16[4,128,512]{2,1,0:T(8,128)(2,1)S(1)} %all_to_all.31.refs_2_) | copy-start | bytes 1572868
  101.1 36.1 %collective-permute-start.10 = (bf16[4,128,512]{2,1,0:T(8,128)(2,1)S(1)}, bf16[4,128,512]{2,1,0:T(8,128)(2,1)S(1)}, u32[]{:S(2)}, u32[]{:S(2)}) collective-permute-start(bf16[4,128,512]{2,1,0:T(8,128)(2,1)S(1)} %all_to_all.31.refs_2_), channel_id=1, source_target_pairs={{8,0},{16,8},{24,16},{32,24},{40,32},{48,40},{56,48},{64,56},{72,6... | collective-permute-start | bytes 1572872 | tf_op jit(solution)/shard_map/ppermute | solution.py:46
  102.4 41.5 %collective-permute-start.9 = (bf16[4,128,512]{2,1,0:T(8,128)(2,1)S(1)}, bf16[4,128,512]{2,1,0:T(8,128)(2,1)S(1)}, u32[]{:S(2)}, u32[]{:S(2)}) collective-permute-start(bf16[4,128,512]{2,1,0:T(8,128)(2,1)S(1)} %all_to_all.31.refs_2_), channel_id=1, source_target_pairs={{0,8},{8,16},{16,24},{24,32},{32,40},{40,48},{48,56},{56,64},{64,7... | collective-permute-start | bytes 1572872 | tf_op jit(solution)/shard_map/ppermute | solution.py:46
  106.5 14.4 %collective-permute-start.11 = (bf16[128,512]{1,0:T(8,128)(2,1)}, bf16[128,512]{1,0:T(8,128)(2,1)S(1)}, u32[]{:S(2)}, u32[]{:S(2)}) collective-permute-start(bf16[128,512]{1,0:T(8,128)(2,1)} %get-tuple-element.45), channel_id=1, source_target_pairs={{248,256},{504,0},{256,248},{0,504},{249,257},{505,1},{257,249},{1... | collective-permute-start | bytes 393224 | tf_op jit(solution)/shard_map/ppermute | solution.py:51
  117.4 33.5 %all-to-all-start.2 = ((bf16[4,128,448]{1,2,0:T(8,128)(2,1)}), bf16[4,128,448]{1,2,0:T(8,128)(2,1)S(1)}, u32[]{:S(2)}, u32[]{:S(2)}) async-start(bf16[4,128,448]{1,2,0:T(8,128)(2,1)} %copy.13), calls=%async_computation.2 | async-start | bytes 917504 | tf_op jit(solution)/shard_map/all_to_all | solution.py:350
  120.9 23.1 %collective-permute-start.12 = (bf16[128,512]{1,0:T(8,128)(2,1)S(1)}, bf16[128,512]{1,0:T(8,128)(2,1)S(1)}, u32[]{:S(2)}, u32[]{:S(2)}) collective-permute-start(bf16[128,512]{1,0:T(8,128)(2,1)S(1)} %collective-permute-done.11), channel_id=1, source_target_pairs={{0,2},{1,3},{2,0},{3,1},{4,6},{5,7},{6,4},{7,5},{248,250},{249,251... | collective-permute-start | bytes 393224 | tf_op jit(solution)/shard_map/ppermute | solution.py:63
  124.2 19.7 %collective-permute-start.13 = (bf16[128,512]{1,0:T(8,128)(2,1)S(1)}, bf16[128,512]{1,0:T(8,128)(2,1)S(1)}, u32[]{:S(2)}, u32[]{:S(2)}) collective-permute-start(bf16[128,512]{1,0:T(8,128)(2,1)S(1)} %collective-permute-done.11), channel_id=1, source_target_pairs={{0,4},{1,5},{2,6},{3,7},{4,0},{5,1},{6,2},{7,3},{248,252},{249,253... | collective-permute-start | bytes 393224 | tf_op jit(solution)/shard_map/ppermute | solution.py:63
  128.2 15.8 %collective-permute-start.14 = (bf16[128,512]{1,0:T(8,128)(2,1)S(1)}, bf16[128,512]{1,0:T(8,128)(2,1)S(1)}, u32[]{:S(2)}, u32[]{:S(2)}) collective-permute-start(bf16[128,512]{1,0:T(8,128)(2,1)S(1)} %collective-permute-done.11), channel_id=1, source_target_pairs={{0,6},{1,7},{2,4},{3,5},{4,2},{5,3},{6,0},{7,1},{248,254},{249,255... | collective-permute-start | bytes 393224 | tf_op jit(solution)/shard_map/ppermute | solution.py:63
  137.3 12.9 %copy-start.19 = (f32[1,512]{1,0:T(1,128)S(1)}, f32[1,512]{1,0:T(1,128)}, u32[]{:S(2)}) copy-start(f32[1,512]{1,0:T(1,128)} %get-tuple-element.44) | copy-start | bytes 6148
  137.3 14.6 %collective-permute-start.16 = (bf16[4,128,512]{2,1,0:T(8,128)(2,1)S(1)}, bf16[4,128,512]{2,1,0:T(8,128)(2,1)S(1)}, u32[]{:S(2)}, u32[]{:S(2)}) collective-permute-start(bf16[4,128,512]{2,1,0:T(8,128)(2,1)S(1)} %all_to_all.31.refs_2_), channel_id=1, source_target_pairs={{0,1},{1,0},{2,3},{3,2},{4,5},{5,4},{6,7},{7,6},{8,9},{9,8},{10,11... | collective-permute-start | bytes 1572872 | tf_op jit(solution)/shard_map/ppermute | solution.py:68
  143.9 0.8 copy-start.12
  143.9 0.8 copy-start.18
  145.7 6.2 %copy-start.5 = (bf16[4,128,512]{2,1,0:T(8,128)(2,1)}, bf16[4,128,512]{2,1,0:T(8,128)(2,1)S(1)}, u32[]{:S(2)}) copy-start(bf16[4,128,512]{2,1,0:T(8,128)(2,1)S(1)} %get-tuple-element.54.refs_4_) | copy-start | bytes 1572868
  145.8 6.2 %copy-start.6 = (bf16[4,128,512]{2,1,0:T(8,128)(2,1)}, bf16[4,128,512]{2,1,0:T(8,128)(2,1)S(1)}, u32[]{:S(2)}) copy-start(bf16[4,128,512]{2,1,0:T(8,128)(2,1)S(1)} %get-tuple-element.55.refs_0_) | copy-start | bytes 1572868
  145.8 6.1 %collective-permute-start.15 = (bf16[4,128,512]{2,1,0:T(8,128)(2,1)S(1)}, bf16[4,128,512]{2,1,0:T(8,128)(2,1)S(1)}, u32[]{:S(2)}, u32[]{:S(2)}) collective-permute-start(bf16[4,128,512]{2,1,0:T(8,128)(2,1)S(1)} %get-tuple-element.55.refs_0_), channel_id=1, source_target_pairs={{0,1},{1,0},{2,3},{3,2},{4,5},{5,4},{6,7},{7,6},{8,9},{9,8},{10,11... | collective-permute-start | bytes 1572872 | tf_op jit(solution)/shard_map/ppermute | solution.py:68
  147.9 4.0 %collective-permute-start.17 = (bf16[4,128,512]{2,1,0:T(8,128)(2,1)S(1)}, bf16[4,128,512]{2,1,0:T(8,128)(2,1)}, u32[]{:S(2)}, u32[]{:S(2)}) collective-permute-start(bf16[4,128,512]{2,1,0:T(8,128)(2,1)S(1)} %get-tuple-element.54.refs_4_), channel_id=1, source_target_pairs={{0,1},{1,0},{2,3},{3,2},{4,5},{5,4},{6,7},{7,6},{8,9},{9,8},{10,11... | collective-permute-start | bytes 1572872 | tf_op jit(solution)/shard_map/ppermute | solution.py:68
  151.9 0.8 copy-start.11
  151.9 1.0 copy-start.13
  158.7 30.2 %all-to-all-start.3 = ((bf16[128,16,128]{2,1,0:T(8,128)(2,1)}), bf16[128,16,128]{2,1,0:T(8,128)(2,1)S(1)}, u32[]{:S(2)}, u32[]{:S(2)}) async-start(bf16[128,16,128]{2,1,0:T(8,128)(2,1)} %get-tuple-element.49), calls=%async_computation.3 | async-start | bytes 1048576 | tf_op jit(solution)/shard_map/all_to_all | solution.py:365
  168.4 67.0 %copy-start = (bf16[1792,512]{1,0:T(8,128)(2,1)S(1)}, bf16[1792,512]{1,0:T(8,128)(2,1)}, u32[]{:S(2)}) copy-start(bf16[1792,512]{1,0:T(8,128)(2,1)} %weight_ref.1) | copy-start | bytes 5505028
  168.4 67.0 %copy-start.17 = (bf16[128,512]{1,0:T(8,128)(2,1)S(1)}, bf16[128,512]{1,0:T(8,128)(2,1)}, u32[]{:S(2)}) copy-start(bf16[128,512]{1,0:T(8,128)(2,1)} %get-tuple-element.48) | copy-start | bytes 393220
  228.1 9.8 %copy-start.1 = (bf16[32,8,16,128]{3,2,1,0:T(8,128)(2,1)}, bf16[32,8,16,128]{3,2,1,0:T(8,128)(2,1)S(1)}, u32[]{:S(2)}) copy-start(bf16[32,8,16,128]{3,2,1,0:T(8,128)(2,1)S(1)} %all_to_all.33.mine_ref) | copy-start | bytes 3145732
  228.1 9.8 %collective-permute-start.18 = (bf16[32,8,16,128]{3,2,1,0:T(8,128)(2,1)S(1)}, bf16[32,8,16,128]{3,2,1,0:T(8,128)(2,1)}, u32[]{:S(2)}, u32[]{:S(2)}) collective-permute-start(bf16[32,8,16,128]{3,2,1,0:T(8,128)(2,1)S(1)} %all_to_all.33.mine_ref), channel_id=1, source_target_pairs={{0,1},{1,0},{2,3},{3,2},{4,5},{5,4},{6,7},{7,6},{8,9},{9,8},{10,11... | collective-permute-start | bytes 3145736 | tf_op jit(solution)/shard_map/ppermute | solution.py:68

commit v3 on v0

v3 whole, which is shorter than its diff:
```python
import jax
import jax.numpy as jnp
from jax import lax
from jax.experimental import pallas as pl
from jax.experimental.pallas import tpu as pltpu
from jax.sharding import Mesh
from jax.sharding import PartitionSpec as P

TILE = 128
KNN = 15
KEYS = 16
HID = 512
HALF = 256
AXES = ("yh", "x", "z", "yl", "c")
SIZES = (2, 4, 8, 4, 2)
WIDE = ("yh", "x", "z")
GROUPS = 64
RUN = 4
MEMBERS = 8
REACH = 3
WINDOW = REACH * MEMBERS * TILE
BLOCKS = 512
DEAD = 31
F_RUN = 448
SLABS = 64
BIAS_SLAB = 56

i32 = jnp.int32
bf16 = jnp.bfloat16
f32 = jnp.float32

EAGER = pl.CostEstimate(flops=4_000_000_000, transcendentals=0, bytes_accessed=8_000_000)
SMEM_SPEC = pl.BlockSpec(memory_space=pltpu.SMEM)
VMEM_SPEC = pl.BlockSpec(memory_space=pltpu.VMEM)


def spread_to(shard, axes, count):
    return lax.all_to_all(jnp.broadcast_to(shard[None], (count,) + shard.shape), axes, 0, 0)


def neighbours(block):
    forward = [(i, (i + 1) % GROUPS) for i in range(GROUPS)]
    backward = [(target, source) for source, target in forward]
    return lax.ppermute(block, WIDE, forward), lax.ppermute(block, WIDE, backward)


def swap_core(block):
    return lax.ppermute(block, "c", [(0, 1), (1, 0)])


def project_kernel(ids_ref, count_ref, tiles_ref, slot_ref, col_ref, keep_ref, features_ref, weight_ref,
                   copies_ref):
    base = (ids_ref[0] - 1) * MEMBERS
    slot = slot_ref[...]
    live = keep_ref[...] * (slot < count_ref[0]).astype(i32)
    position = jnp.zeros_like(slot)
    for k in range(tiles_ref.shape[1]):
        block = tiles_ref[0, k] - base
        block = jnp.where(block < 0, block + BLOCKS, block)
        block = jnp.where(block >= BLOCKS, block - BLOCKS, block)
        position = position + jnp.where(slot == k, block, 0)
    pad = jnp.zeros((KEYS - KNN, TILE), i32)

    def rows(value):
        return jnp.concatenate([value, pad], axis=0)

    dead = rows(1 - live) + lax.broadcasted_iota(i32, (KEYS, TILE), 0) // KNN
    blocks = jnp.where(dead > 0, DEAD, rows(position))
    keys = jnp.concatenate([blocks, rows(col_ref[...])], axis=1).astype(f32).astype(bf16)
    projected = jnp.dot(features_ref[...], weight_ref[...], preferred_element_type=f32).astype(bf16)
    for k in range(MEMBERS):
        half = (k % 2) * HALF
        copies_ref[k, :TILE, :] = projected[:, half : half + HALF]
        copies_ref[k, TILE:, :] = keys


def project(ids, tile_count, tile_cols, slot, col, keep, features, weight):
    return pl.pallas_call(
        project_kernel,
        in_specs=[SMEM_SPEC] * 3 + [VMEM_SPEC] * 5,
        out_shape=jax.ShapeDtypeStruct((MEMBERS, TILE + KEYS, HALF), bf16),
        name="project",
    )(ids, tile_count, tile_cols, slot, col, keep, features, weight)


def digits_of(block, wanted):
    valid = lax.shift_right_arithmetic(block, 3) == wanted
    shift = 4 * jnp.bitwise_and(block, 7)
    return jnp.where(valid, lax.shift_left(jnp.ones_like(shift), shift), 0)


def forward_counts_kernel(ids_ref, own_ref, counts_ref, degree_ref):
    run = ids_ref[1]
    for core in range(2):
        keys = own_ref[run * 2 + core, TILE:, :].astype(f32).astype(i32).T
        block, cells = keys[:TILE, :], keys[TILE:, :]
        live = jnp.where(block < DEAD, 1.0, 0.0)
        degree_ref[core * TILE : core * TILE + TILE, :] = 1.0 + jnp.sum(live, axis=1, keepdims=True)
        digits = [digits_of(block, reach) for reach in range(REACH)]
        lanes = lax.broadcasted_iota(i32, (16, 128), 1)
        for step in range(TILE // 16):
            here = slice(step * 16, step * 16 + 16)
            totals = [jnp.zeros((16, 128), i32) for _ in range(REACH)]
            for e in range(KNN):
                hit = cells[here, e : e + 1] == lanes
                for reach in range(REACH):
                    totals[reach] = totals[reach] + jnp.where(hit, digits[reach][here, e : e + 1], 0)
            row = core * TILE + step * 16
            for tile in range(REACH * MEMBERS):
                digit = lax.shift_right_logical(totals[tile // 8], 4 * (tile % 8))
                count = jnp.bitwise_and(digit, 15).astype(f32).astype(bf16)
                counts_ref[row : row + 16, tile * 128 : tile * 128 + 128] = count


def forward_counts(ids, own):
    return pl.pallas_call(
        forward_counts_kernel,
        in_specs=[SMEM_SPEC, VMEM_SPEC],
        out_shape=(
            jax.ShapeDtypeStruct((2 * TILE, WINDOW), bf16),
            jax.ShapeDtypeStruct((2 * TILE, 1), f32),
        ),
        cost_estimate=EAGER,
        name="forward_counts",
    )(ids, own)


def backward_counts_kernel(*refs):
    pieces, out_ref = refs[:REACH], refs[REACH]

    def source(member, carry):
        for reach in range(REACH):
            keys = pieces[reach][member, TILE:, :].astype(f32).astype(i32)
            digits = digits_of(keys[:, :TILE], REACH - 1 - reach)
            cells = keys[:, TILE:]
            lanes = pl.ds(reach * MEMBERS * TILE + member * TILE, TILE)
            for step in range(TILE // 16):
                rows = lax.broadcasted_iota(i32, (16, 128), 0) + step * 16
                total = jnp.zeros((16, 128), i32)
                for e in range(KNN):
                    total = total + jnp.where(cells[e : e + 1, :] == rows, digits[e : e + 1, :], 0)
                for k in range(MEMBERS):
                    count = jnp.bitwise_and(lax.shift_right_logical(total, 4 * k), 15)
                    at = k * TILE + step * 16
                    out_ref[at : at + 16, lanes] = count.astype(f32).astype(bf16)
        return carry

    lax.fori_loop(0, MEMBERS, source, 0)


def backward_counts(pieces):
    return pl.pallas_call(
        backward_counts_kernel,
        in_specs=[VMEM_SPEC] * REACH,
        out_shape=jax.ShapeDtypeStruct((MEMBERS * TILE, WINDOW), bf16),
        cost_estimate=EAGER,
        name="backward_counts",
    )(*pieces)


def forward_kernel(ids_ref, counts_ref, degree_ref, bias_ref, up_ref, *refs):
    pieces, (hidden_ref, copies_ref, bias_out_ref) = refs[:REACH], refs[REACH:]
    run = ids_ref[1]
    total = jnp.concatenate(
        [pieces[1][run * 2 + core, :TILE, :].astype(f32) for core in range(2)], axis=0
    )
    for reach in range(REACH):
        for member in range(MEMBERS):
            lane = (reach * MEMBERS + member) * TILE
            total = total + jnp.dot(
                counts_ref[:, lane : lane + TILE],
                pieces[reach][member, :TILE, :],
                preferred_element_type=f32,
            )
    degree = degree_ref[...]
    pre = total / degree + bias_ref[...]
    sigma = jax.nn.sigmoid(pre)
    hidden_ref[...] = (pre * sigma).astype(bf16)
    grad_pre = up_ref[...].astype(f32) * sigma * (1.0 + pre * (1.0 - sigma))
    scaled = (grad_pre / degree).astype(bf16)
    for k in range(RUN):
        copies_ref[k] = scaled
    bias_out_ref[...] = jnp.sum(grad_pre, axis=0, keepdims=True)


def forward_math(ids, counts, degree, bias, upstream, pieces):
    return pl.pallas_call(
        forward_kernel,
        in_specs=[SMEM_SPEC] + [VMEM_SPEC] * (4 + REACH),
        out_shape=(
            jax.ShapeDtypeStruct((2 * TILE, HALF), bf16),
            jax.ShapeDtypeStruct((RUN, 2 * TILE, HALF), bf16),
            jax.ShapeDtypeStruct((1, HALF), f32),
        ),
        name="forward_math",
    )(ids, counts, degree, bias, upstream, *pieces)


def backward_kernel(ids_ref, counts_ref, bias_ref, feats_ref, feats_other_ref, *refs):
    pieces, (own_ref, slab_ref, round_ref) = refs[:REACH], refs[REACH:]
    run, core = ids_ref[1], ids_ref[2]
    group = MEMBERS * TILE
    total = pieces[1][...].reshape(group, HALF).astype(f32)
    for reach in range(REACH):
        total = total + jnp.dot(
            counts_ref[:, reach * group : reach * group + group],
            pieces[reach][...].reshape(group, HALF),
            preferred_element_type=f32,
        )
    round_ref[...] = total.astype(bf16).reshape(MEMBERS, TILE, HALF)
    for k in range(2):
        own_ref[k] = round_ref[run * 2 + k]
    part = jnp.zeros((F_RUN, HALF), f32)
    for feats, side in ((feats_ref, core), (feats_other_ref, 1 - core)):
        rows = jnp.concatenate([round_ref[k * 2 + side] for k in range(RUN)], axis=0)
        part = part + lax.dot_general(
            feats[...].reshape(RUN * TILE, F_RUN),
            rows,
            (((0,), (0,)), ((), ())),
            preferred_element_type=f32,
        )
    part = part.astype(bf16)
    for row in range(F_RUN // 16):
        for lane in range(2):
            slab_ref[row * 2 + lane] = part[row * 16 : row * 16 + 16, lane * 128 : lane * 128 + 128]
    slab_ref[BIAS_SLAB] = bias_ref[...]
    for rest in range(BIAS_SLAB + 1, SLABS):
        slab_ref[rest] = jnp.zeros((16, 128), bf16)


def backward_math(ids, counts, bias_rows, feats, feats_other, pieces):
    return pl.pallas_call(
        backward_kernel,
        in_specs=[SMEM_SPEC] + [VMEM_SPEC] * (4 + REACH),
        out_shape=(
            jax.ShapeDtypeStruct((2, TILE, HALF), bf16),
            jax.ShapeDtypeStruct((SLABS, 16, 128), bf16),
        ),
        scratch_shapes=[pltpu.VMEM((MEMBERS, TILE, HALF), bf16)],
        name="backward_math",
    )(ids, counts, bias_rows, feats, feats_other, *pieces)


def assemble_kernel(ids_ref, mine_ref, other_ref, weight_ref, bias_ref):
    first = ids_ref[2] == 0
    bias = [jnp.zeros((2, 128), f32), jnp.zeros((2, 128), f32)]
    for x in range(4):
        for column in range(64):
            yh, run, z = column // 32, (column // 8) % 4, column % 8
            slab = (yh * 4 + x) * 8 + z
            if slab > BIAS_SLAB:
                continue
            mine, other = mine_ref[x, column], other_ref[x, column]
            for core in range(2):
                keep = first if core == 0 else jnp.logical_not(first)
                value = jnp.where(keep, mine, other)
                if slab == BIAS_SLAB:
                    rows = value.astype(f32)
                    bias[core] = bias[core] + (rows[:2] + rows[2:4])
                else:
                    row, lane = run * F_RUN + (slab // 2) * 16, core * HALF + (slab % 2) * 128
                    weight_ref[row : row + 16, lane : lane + 128] = value
    bias_ref[:2, :] = bias[0]
    bias_ref[2:, :] = bias[1]


def assemble(ids, mine, other):
    return pl.pallas_call(
        assemble_kernel,
        in_specs=[SMEM_SPEC] + [VMEM_SPEC] * 2,
        out_shape=(
            jax.ShapeDtypeStruct((RUN * F_RUN, HID), bf16),
            jax.ShapeDtypeStruct((4, 128), f32),
        ),
        name="assemble",
    )(ids, mine, other)


def high_low(value):
    high = lax.reduce_precision(value, 8, 7)
    return jnp.concatenate([high, value - high, jnp.zeros((12, 128), f32)], axis=0).astype(bf16)


def on_device(features, weight, bias, tile_cols, tile_count, nbr_slot, nbr_col, nbr_keep, upstream):
    group = (lax.axis_index("yh") * 4 + lax.axis_index("x")) * 8 + lax.axis_index("z")
    core = lax.axis_index("c")
    ids = jnp.stack([group, lax.axis_index("yl"), core]).astype(i32)

    copies = project(
        ids, tile_count, tile_cols, nbr_slot.T, nbr_col.T, nbr_keep.T, features, weight
    )
    own = lax.all_to_all(copies, ("yl", "c"), 0, 0)
    up_halves = jnp.stack([upstream[:, :HALF], upstream[:, HALF:]])
    up_halves = lax.all_to_all(up_halves, "c", 0, 0).reshape(2 * TILE, HALF)
    low, high = neighbours(own)
    counts, degree = forward_counts(ids, own)
    low, high, counts, degree, up_halves = lax.optimization_barrier(
        (low, high, counts, degree, up_halves)
    )
    first = (low, own, high)
    slices = jnp.stack([features[:, k * F_RUN : (k + 1) * F_RUN] for k in range(RUN)])
    feats = lax.all_to_all(slices, "yl", 0, 0)
    feats_other = swap_core(feats)
    bias_half = lax.dynamic_slice(bias, (core * HALF,), (HALF,))[None]
    hidden_halves, scaled, bias_part = forward_math(
        ids, counts, degree, bias_half, up_halves, first
    )
    own = lax.all_to_all(scaled, "yl", 0, 0)
    counts_back = backward_counts(first)
    low, high = neighbours(own)
    rounds, slabs = backward_math(
        ids, counts_back, high_low(bias_part.reshape(2, 128)), feats, feats_other,
        tuple(block.reshape(MEMBERS, TILE, HALF) for block in (low, own, high)),
    )
    reduced = jnp.sum(lax.all_to_all(slabs, WIDE, 0, 0).astype(f32), axis=0)
    piece = jnp.where(
        group == BIAS_SLAB, high_low(reduced[:2] + reduced[2:4]), reduced.astype(bf16)
    )
    column = spread_to(piece, ("yh", "yl", "z"), 64)
    plane = spread_to(column, "x", 4)
    weight_grad, bias_grad = assemble(ids, plane, swap_core(plane))
    rows = jnp.concatenate([hidden_halves.reshape(2, TILE, HALF), rounds], axis=1)
    rows = lax.all_to_all(rows, "c", 0, 0)
    hidden = jnp.concatenate([rows[0, :TILE], rows[1, :TILE]], axis=1)
    own_round = jnp.concatenate([rows[0, TILE:], rows[1, TILE:]], axis=1)
    grad_features = lax.dot_general(
        own_round, weight, (((1,), (1,)), ((), ())), preferred_element_type=f32
    ).astype(bf16)
    return hidden, grad_features, weight_grad, bias_grad.reshape(HID)


def solution(mesh):
    split = Mesh(mesh.devices.reshape(SIZES), AXES)
    rows = P(AXES, None)
    in_specs = (rows, P(), P(), rows, P(AXES), rows, rows, rows, rows)
    out_specs = (rows, rows, P(), P())
    return jax.shard_map(
        on_device, mesh=split, in_specs=in_specs, out_specs=out_specs, check_vma=False
    )
```

time: 386 us -> 224 us (0.58)
  waiting for transfers between devices: 209 us -> 71.2 us
  blocking collectives: 118 us -> 35.9 us
  starting transfers between devices: 19.1 us -> 72.6 us
  Pallas kernels: 0 us -> 31.4 us
  matrix products: 16.7 us -> 1.48 us
  between operations: 14.9 us -> 1.52 us
    psum x1 -> x0, blocking collectives: 118 us -> none  [on_device(): lax.psum((weight_part, jnp.sum(grad_pre, axis=0)), ('wide', 'narrow'))]
    ppermute x4 -> x6, waiting for transfers between devices: 136 us -> 32.8 us  [the longest x2 31.9 us: neighbours(): lax.ppermute(block, WIDE, forward)]
    all_gather x1 -> x0, waiting for transfers between devices: 42.6 us -> none  [on_device(): group_panel = lax.all_gather(projected, 'narrow', axis=0, tiled=True)]
    all_to_all x0 -> x5, waiting for transfers between devices: none -> 38.3 us  [the longest x1 14.3 us: on_device(): own = lax.all_to_all(copies, ('yl', 'c'), 0, 0)]
    all_to_all x0 -> x3, blocking collectives: none -> 35.9 us  [the longest x2 32.3 us: spread_to(): lax.all_to_all(jnp.broadcast_to(shard[None], (count,) + shard.shape), axe...]
    all_to_all x0 -> x5, starting transfers between devices: none -> 34.3 us  [the longest x1 12.6 us: on_device(): reduced = jnp.sum(lax.all_to_all(slabs, WIDE, 0, 0).astype(f32), axis=0)]
    pallas_call x0 -> x6, Pallas kernels: none -> 31.4 us  [the longest x1 9.52 us: backward_counts(): pl.pallas_call(backward_counts_kernel, in_specs=[VMEM_SPEC] * REACH, out_...]
    reduce_scatter x1 -> x0, waiting for transfers between devices: 30.4 us -> none  [on_device(): lax.psum_scatter(group_terms, 'narrow', scatter_dimension=0, tiled=True)]
  transfers between devices with their start and end apart: 6 -> 11, of which waited for: 6 -> 6; matrix products, arithmetic and copies ran while one was open for 0% -> 3% of each run, Pallas kernels for 0% -> 10%
where the time goes in v3:
time: 224 us; the launch traced here: 223 us
  starting transfers between devices  72.6 us (32%)
  waiting for transfers between devices  71.2 us (32%)
  blocking collectives  35.9 us (16%)
  Pallas kernels  31.4 us (14%)
  local copies, waits for them, and re-layouts  5.63 us (3%)
  other arithmetic  3.67 us (2%)
    all_to_all x2, blocking collectives, spread_to(): lax.all_to_all(jnp.broadcast_to(shard[None], (count,) + shard.shape), axe...  32.3 us
    ppermute x2, waiting for transfers between devices, neighbours(): lax.ppermute(block, WIDE, forward)  31.9 us
    ppermute x2, starting transfers between devices, neighbours(): lax.ppermute(block, WIDE, backward)  24.2 us
    all_to_all x1, waiting for transfers between devices, on_device(): own = lax.all_to_all(copies, ('yl', 'c'), 0, 0)  14.3 us
    all_to_all x1, waiting for transfers between devices, on_device(): reduced = jnp.sum(lax.all_to_all(slabs, WIDE, 0, 0).astype(f32), axis=0)  14.1 us
    all_to_all x1, starting transfers between devices, on_device(): reduced = jnp.sum(lax.all_to_all(slabs, WIDE, 0, 0).astype(f32), axis=0)  12.6 us
    ppermute x2, starting transfers between devices, swap_core(): return lax.ppermute(block, 'c', [(0, 1), (1, 0)])  10.3 us
    all_to_all x1, starting transfers between devices, on_device(): up_halves = lax.all_to_all(up_halves, 'c', 0, 0).reshape(2 * TILE, HALF)  10.2 us
  transfers between devices with their start and end apart: 11, of which 6 were waited for; matrix products, arithmetic and copies ran while one was open for 3% of the time, Pallas kernels for 10%

profile of v3, /device:TPU:1, one launch (start us, length us, event | category | flops | bytes accessed | tf_op | source)
XLA Modules:
  0.0 223.4 jit_solution(13516063858041652987)
XLA Ops:
  0.6 0.9 slice_bitcast_fusion.5
  1.5 0.7 pad_maximum_fusion.2
  2.2 10.2 %all-to-all-start.1 = ((bf16[2,128,256]{2,1,0:T(8,128)(2,1)}), bf16[2,128,256]{2,1,0:T(8,128)(2,1)S(1)}, u32[]{:S(2)}, u32[]{:S(2)}) async-start(bf16[2,128,256]{2,1,0:T(8,128)(2,1)} %pad_maximum_fusion.2), calls=%async_computation.1 | async-start | bytes 262144 | tf_op jit(solution)/shard_map/all_to_all | solution.py:294
  13.1 0.6 pad_add_fusion.ids_ref
  13.7 3.0 %project.1 = bf16[8,144,256]{2,1,0:T(8,128)(2,1)} custom-call(s32[3]{0:T(128)} %pad_add_fusion.ids_ref, s32[1]{0:T(128)S(6)} %copy.23.count_ref, s32[1,24]{1,0:T(1,128)} %tiles_ref.1, s32[15,128]{1,0:T(8,128)} %bitcast.40, s32[15,128]{1,0:T(8,128)} %bitcast.41, s32[15,128]{1,0:T(8,128)} %bitcast.42, bf16[128,1792]{1,0:T(8,128)(2,1)} %features_ref.1, ...), custom_call_target="tpu_custom_call" | custom-call | tf_op jit(solution)/shard_map/project/pallas_call | solution.py:78
  16.7 0.0 all-to-all-done.1
  16.7 3.5 %all-to-all-start = ((bf16[8,144,256]{2,1,0:T(8,128)(2,1)}), bf16[8,144,256]{2,1,0:T(8,128)(2,1)S(1)}, u32[]{:S(2)}, u32[]{:S(2)}) async-start(bf16[8,144,256]{2,1,0:T(8,128)(2,1)} %project.1), calls=%async_computation | async-start | bytes 1179648 | tf_op jit(solution)/shard_map/all_to_all | solution.py:292
  20.2 0.0 copy-done.3
  20.2 0.0 copy-start.16
  20.2 0.1 fusion.6
  20.4 0.1 copy.19
  20.5 0.1 copy.20
  20.7 0.1 copy.21
  20.8 0.1 copy.22
  21.0 0.8 pad_maximum_fusion
  21.8 0.0 copy-done.12
  21.8 14.3 %all-to-all-done.own_ref.refs_1_ = bf16[8,144,256]{2,1,0:T(8,128)(2,1)S(1)} async-done(((bf16[8,144,256]{2,1,0:T(8,128)(2,1)}), bf16[8,144,256]{2,1,0:T(8,128)(2,1)S(1)}, u32[]{:S(2)}, u32[]{:S(2)}) %all-to-all-start) | async-done | bytes 589856 | tf_op jit(solution)/shard_map/all_to_all | solution.py:292
  36.1 3.5 %all-to-all-start.2 = ((bf16[4,128,448]{1,2,0:T(8,128)(2,1)}), bf16[4,128,448]{1,2,0:T(8,128)(2,1)S(1)}, u32[]{:S(2)}, u32[]{:S(2)}) async-start(bf16[4,128,448]{1,2,0:T(8,128)(2,1)} %pad_maximum_fusion), calls=%async_computation.2 | async-start | bytes 917504 | tf_op jit(solution)/shard_map/all_to_all | solution.py:302
  39.6 1.9 collective-permute-start
  41.5 12.7 %collective-permute-start.1 = (bf16[8,144,256]{2,1,0:T(8,128)(2,1)S(1)}, bf16[8,144,256]{2,1,0:T(8,128)(2,1)S(1)}, u32[]{:S(2)}, u32[]{:S(2)}) collective-permute-start(bf16[8,144,256]{2,1,0:T(8,128)(2,1)S(1)} %all-to-all-done.own_ref.refs_1_), channel_id=1, source_target_pairs={{8,0},{16,8},{24,16},{32,24},{40,32},{48,40},{56,48},{64,56},{72,6... | collective-permute-start | bytes 1769480 | tf_op jit(solution)/shard_map/ppermute | solution.py:44
  54.3 0.0 copy-done.16
  54.3 0.6 dynamic_slice.3
  54.9 0.0 copy-done.2
  54.9 5.1 %forward_counts.1 = (bf16[256,3072]{1,0:T(8,128)(2,1)}, f32[256,1]{1,0:T(8,128)}) custom-call(s32[3]{0:T(128)} %pad_add_fusion.ids_ref, bf16[8,144,256]{2,1,0:T(8,128)(2,1)} %copy-done.2), custom_call_target="tpu_custom_call" | custom-call | flops 4000000000 | bytes 8000000 | tf_op jit(solution)/shard_map/forward_counts/pallas_call | solution.py:116
  60.0 23.5 %collective-permute-done.refs_0_ = bf16[8,144,256]{2,1,0:T(8,128)(2,1)S(1)} collective-permute-done((bf16[8,144,256]{2,1,0:T(8,128)(2,1)S(1)}, bf16[8,144,256]{2,1,0:T(8,128)(2,1)S(1)}, u32[]{:S(2)}, u32[]{:S(2)}) %collective-permute-start) | collective-permute-done | bytes 589856 | tf_op jit(solution)/shard_map/ppermute | solution.py:44
  83.5 0.0 collective-permute-done.1.refs_2_
  83.5 0.8 copy-done.7
  84.3 0.2 copy-done.8
  84.5 3.9 %forward_math.1 = (bf16[256,256]{1,0:T(8,128)(2,1)}, bf16[4,256,256]{2,1,0:T(8,128)(2,1)}, f32[1,256]{1,0:T(1,128)}) custom-call(s32[3]{0:T(128)} %pad_add_fusion.ids_ref, bf16[256,3072]{1,0:T(8,128)(2,1)} %get-tuple-element.20.counts_ref, f32[256,1]{1,0:T(8,128)} %get-tuple-element.21.degree_ref, f32[1,256]{1,0:T(1,128)} %bitcast.43, ...), custom_call_target="tpu_custom_call" | custom-call | tf_op jit(solution)/shard_map/forward_math/pallas_call | solution.py:187
  88.4 0.0 all-to-all-done.2
  88.5 4.5 %all-to-all-start.3 = ((bf16[4,256,256]{2,1,0:T(8,128)(2,1)}), bf16[4,256,256]{2,1,0:T(8,128)(2,1)S(1)}, u32[]{:S(2)}, u32[]{:S(2)}) async-start(bf16[4,256,256]{2,1,0:T(8,128)(2,1)} %get-tuple-element.27), calls=%async_computation.3 | async-start | bytes 1048576 | tf_op jit(solution)/shard_map/all_to_all | solution.py:308
  92.9 0.1 pad.15.clone
  93.0 0.2 copy.18.feats_ref
  93.2 0.0 copy-start.5
  93.2 3.8 %collective-permute-start.2 = (bf16[4,128,448]{2,1,0:T(8,128)(2,1)S(1)}, bf16[4,128,448]{2,1,0:T(8,128)(2,1)S(1)}, u32[]{:S(2)}, u32[]{:S(2)}) collective-permute-start(bf16[4,128,448]{2,1,0:T(8,128)(2,1)S(1)} %copy.18.feats_ref), channel_id=1, source_target_pairs={{0,1},{1,0},{2,3},{3,2},{4,5},{5,4},{6,7},{7,6},{8,9},{9,8},{10,11... | collective-permute-start | bytes 1376264 | tf_op jit(solution)/shard_map/ppermute | solution.py:48
  97.0 0.0 copy-done.15
  97.0 9.9 %all-to-all-done.3 = bf16[4,256,256]{2,1,0:T(8,128)(2,1)S(1)} async-done(((bf16[4,256,256]{2,1,0:T(8,128)(2,1)}), bf16[4,256,256]{2,1,0:T(8,128)(2,1)S(1)}, u32[]{:S(2)}, u32[]{:S(2)}) %all-to-all-start.3) | async-done | bytes 524320 | tf_op jit(solution)/shard_map/all_to_all | solution.py:308
  106.9 1.9 collective-permute-start.3
  108.8 11.5 %collective-permute-start.4 = (bf16[4,256,256]{2,1,0:T(8,128)(2,1)S(1)}, bf16[4,256,256]{2,1,0:T(8,128)(2,1)S(1)}, u32[]{:S(2)}, u32[]{:S(2)}) collective-permute-start(bf16[4,256,256]{2,1,0:T(8,128)(2,1)S(1)} %all-to-all-done.3), channel_id=1, source_target_pairs={{8,0},{16,8},{24,16},{32,24},{40,32},{48,40},{56,48},{64,56},{72,6... | collective-permute-start | bytes 1572872 | tf_op jit(solution)/shard_map/ppermute | solution.py:44
  120.3 0.7 maximum_maximum_fusion.bias_ref
  121.0 9.5 %backward_counts.1.counts_ref = bf16[1024,3072]{1,0:T(8,128)(2,1)} custom-call(bf16[8,144,256]{2,1,0:T(8,128)(2,1)} %copy-done.7, bf16[8,144,256]{2,1,0:T(8,128)(2,1)} %copy-done.2, bf16[8,144,256]{2,1,0:T(8,128)(2,1)} %copy-done.8), custom_call_target="tpu_custom_call" | custom-call | flops 4000000000 | bytes 8000000 | tf_op jit(solution)/shard_map/backward_counts/pallas_call | solution.py:152
  130.5 0.0 copy-done.5
  130.5 0.0 collective-permute-done.2.feats_other_ref
  130.5 8.5 %collective-permute-done.3 = bf16[4,256,256]{2,1,0:T(8,128)(2,1)S(1)} collective-permute-done((bf16[4,256,256]{2,1,0:T(8,128)(2,1)S(1)}, bf16[4,256,256]{2,1,0:T(8,128)(2,1)S(1)}, u32[]{:S(2)}, u32[]{:S(2)}) %collective-permute-start.3) | collective-permute-done | bytes 524320 | tf_op jit(solution)/shard_map/ppermute | solution.py:44
  139.0 0.9 collective-permute-done.4
  139.9 0.0 copy-done.9
  139.9 0.8 copy-done.11
  140.7 6.8 %backward_math.1 = (bf16[2,128,256]{2,1,0:T(8,128)(2,1)}, bf16[64,16,128]{2,1,0:T(8,128)(2,1)}) custom-call(s32[3]{0:T(128)} %pad_add_fusion.ids_ref, bf16[1024,3072]{1,0:T(8,128)(2,1)} %backward_counts.1.counts_ref, bf16[16,128]{1,0:T(8,128)(2,1)} %maximum_maximum_fusion.bias_ref, bf16[4,128,448]{2,1,0:T(8,128)(2,1)} %copy-done.5, ...), custom_call_target="tpu_custom_call" | custom-call | tf_op jit(solution)/shard_map/backward_math/pallas_call | solution.py:232
  147.6 12.6 %all-to-all-start.5 = ((bf16[64,16,128]{2,1,0:T(8,128)(2,1)}), bf16[64,16,128]{2,1,0:T(8,128)(2,1)S(1)}, u32[]{:S(2)}, u32[]{:S(2)}) async-start(bf16[64,16,128]{2,1,0:T(8,128)(2,1)} %get-tuple-element.29), calls=%async_computation.5 | async-start | bytes 524288 | tf_op jit(solution)/shard_map/all_to_all | solution.py:315
  160.2 14.1 %all-to-all-done.5 = bf16[64,16,128]{2,1,0:T(8,128)(2,1)S(1)} async-done(((bf16[64,16,128]{2,1,0:T(8,128)(2,1)}), bf16[64,16,128]{2,1,0:T(8,128)(2,1)S(1)}, u32[]{:S(2)}, u32[]{:S(2)}) %all-to-all-start.5) | async-done | bytes 262176 | tf_op jit(solution)/shard_map/all_to_all | solution.py:315
  174.3 0.1 convert_reduce_fusion
  174.4 0.1 maximum_select_fusion
  174.5 18.3 %all_to_all.40 = bf16[64,16,128]{2,1,0:T(8,128)(2,1)S(1)} all-to-all(bf16[64,16,128]{2,1,0:T(8,128)(2,1)S(1)} %broadcast_in_dim.7), channel_id=1, replica_groups=mesh['yh'=2,'x'=4,'z'=8,'yl'=4,'c'=2] {'yh','yl','z'}, dimensions={0} | all-to-all | bytes 524288 | tf_op jit(solution)/shard_map/all_to_all | solution.py:38
  192.9 0.1 broadcast_in_dim.8
  193.0 0.0 copy-start
  193.0 14.0 %all_to_all.41.mine_ref = bf16[4,64,16,128]{3,2,1,0:T(8,128)(2,1)S(1)} all-to-all(bf16[4,64,16,128]{3,2,1,0:T(8,128)(2,1)S(1)} %broadcast_in_dim.8), channel_id=1, replica_groups=mesh['yh'=2,'x'=4,'z'=8,'yl'=4,'c'=2] {'x'}, dimensions={0} | all-to-all | bytes 2097152 | tf_op jit(solution)/shard_map/all_to_all | solution.py:38
  207.0 6.5 %collective-permute-start.5 = (bf16[4,64,16,128]{3,2,1,0:T(8,128)(2,1)S(1)}, bf16[4,64,16,128]{3,2,1,0:T(8,128)(2,1)S(1)}, u32[]{:S(2)}, u32[]{:S(2)}) collective-permute-start(bf16[4,64,16,128]{3,2,1,0:T(8,128)(2,1)S(1)} %all_to_all.41.mine_ref), channel_id=1, source_target_pairs={{0,1},{1,0},{2,3},{3,2},{4,5},{5,4},{6,7},{7,6},{8,9},{9,8},{10,11... | collective-permute-start | bytes 3145736 | tf_op jit(solution)/shard_map/ppermute | solution.py:48
  213.6 3.6 %all_to_all.42 = bf16[2,256,256]{2,1,0:T(8,128)(2,1)S(1)} all-to-all(bf16[2,256,256]{2,1,0:T(8,128)(2,1)S(1)} %pad_maximum_fusion.1), channel_id=1, replica_groups=mesh['yh'=2,'x'=4,'z'=8,'yl'=4,'c'=2] {'c'}, dimensions={0} | all-to-all | bytes 524288 | tf_op jit(solution)/shard_map/all_to_all | solution.py:323
  217.2 0.7 pad_maximum_fusion.3
  217.8 0.0 copy-done
  217.8 1.5 convolution_convert_fusion
  219.3 0.0 collective-permute-done.5.other_ref
  219.3 1.0 copy-done.6
  220.3 3.1 %assemble.1 = (bf16[1792,512]{1,0:T(8,128)(2,1)}, f32[4,128]{1,0:T(4,128)}) custom-call(s32[3]{0:T(128)} %pad_add_fusion.ids_ref, bf16[4,64,16,128]{3,2,1,0:T(8,128)(2,1)} %copy-done.1, bf16[4,64,16,128]{3,2,1,0:T(8,128)(2,1)} %copy-done.6), custom_call_target="tpu_custom_call" | custom-call | tf_op jit(solution)/shard_map/assemble/pallas_call | solution.py:268
  (25 shorter events, 0.1 us)
Async XLA Ops:
  2.2 14.5 %all-to-all-start.1 = ((bf16[2,128,256]{2,1,0:T(8,128)(2,1)}), bf16[2,128,256]{2,1,0:T(8,128)(2,1)S(1)}, u32[]{:S(2)}, u32[]{:S(2)}) async-start(bf16[2,128,256]{2,1,0:T(8,128)(2,1)} %pad_maximum_fusion.2), calls=%async_computation.1 | async-start | bytes 262144 | tf_op jit(solution)/shard_map/all_to_all | solution.py:294
  13.7 6.5 %copy-start.3 = (bf16[128,1792]{1,0:T(8,128)(2,1)S(1)}, bf16[128,1792]{1,0:T(8,128)(2,1)}, u32[]{:S(2)}) copy-start(bf16[128,1792]{1,0:T(8,128)(2,1)} %features_ref.1) | copy-start | bytes 1376260
  16.7 5.1 %copy-start.12 = (bf16[2,128,256]{2,1,0:T(8,128)(2,1)}, bf16[2,128,256]{2,1,0:T(8,128)(2,1)S(1)}, u32[]{:S(2)}) copy-start(bf16[2,128,256]{2,1,0:T(8,128)(2,1)S(1)} %all-to-all-done.1) | copy-start | bytes 393220
  16.7 19.4 %all-to-all-start = ((bf16[8,144,256]{2,1,0:T(8,128)(2,1)}), bf16[8,144,256]{2,1,0:T(8,128)(2,1)S(1)}, u32[]{:S(2)}, u32[]{:S(2)}) async-start(bf16[8,144,256]{2,1,0:T(8,128)(2,1)} %project.1), calls=%async_computation | async-start | bytes 1179648 | tf_op jit(solution)/shard_map/all_to_all | solution.py:292
  20.2 34.0 %copy-start.16 = (f32[512]{0:T(512)S(1)}, f32[512]{0:T(512)}, u32[]{:S(2)}) copy-start(f32[512]{0:T(512)} %param.11) | copy-start | bytes 6148
  36.1 18.8 %copy-start.2 = (bf16[8,144,256]{2,1,0:T(8,128)(2,1)}, bf16[8,144,256]{2,1,0:T(8,128)(2,1)S(1)}, u32[]{:S(2)}) copy-start(bf16[8,144,256]{2,1,0:T(8,128)(2,1)S(1)} %all-to-all-done.own_ref.refs_1_) | copy-start | bytes 1769476
  36.1 52.3 %all-to-all-start.2 = ((bf16[4,128,448]{1,2,0:T(8,128)(2,1)}), bf16[4,128,448]{1,2,0:T(8,128)(2,1)S(1)}, u32[]{:S(2)}, u32[]{:S(2)}) async-start(bf16[4,128,448]{1,2,0:T(8,128)(2,1)} %pad_maximum_fusion), calls=%async_computation.2 | async-start | bytes 917504 | tf_op jit(solution)/shard_map/all_to_all | solution.py:302
  39.6 43.9 %collective-permute-start = (bf16[8,144,256]{2,1,0:T(8,128)(2,1)S(1)}, bf16[8,144,256]{2,1,0:T(8,128)(2,1)S(1)}, u32[]{:S(2)}, u32[]{:S(2)}) collective-permute-start(bf16[8,144,256]{2,1,0:T(8,128)(2,1)S(1)} %all-to-all-done.own_ref.refs_1_), channel_id=1, source_target_pairs={{0,8},{8,16},{16,24},{24,32},{32,40},{40,48},{48,56},{56,64},{64,7... | collective-permute-start | bytes 1769480 | tf_op jit(solution)/shard_map/ppermute | solution.py:44
  41.5 41.9 %collective-permute-start.1 = (bf16[8,144,256]{2,1,0:T(8,128)(2,1)S(1)}, bf16[8,144,256]{2,1,0:T(8,128)(2,1)S(1)}, u32[]{:S(2)}, u32[]{:S(2)}) collective-permute-start(bf16[8,144,256]{2,1,0:T(8,128)(2,1)S(1)} %all-to-all-done.own_ref.refs_1_), channel_id=1, source_target_pairs={{8,0},{16,8},{24,16},{32,24},{40,32},{48,40},{56,48},{64,56},{72,6... | collective-permute-start | bytes 1769480 | tf_op jit(solution)/shard_map/ppermute | solution.py:44
  83.5 0.8 copy-start.7
  83.5 1.1 copy-start.8
  88.4 8.6 %copy-start.15 = (f32[1,256]{1,0:T(1,128)S(1)}, f32[1,256]{1,0:T(1,128)}, u32[]{:S(2)}) copy-start(f32[1,256]{1,0:T(1,128)} %get-tuple-element.26) | copy-start | bytes 3076
  88.5 18.5 %all-to-all-start.3 = ((bf16[4,256,256]{2,1,0:T(8,128)(2,1)}), bf16[4,256,256]{2,1,0:T(8,128)(2,1)S(1)}, u32[]{:S(2)}, u32[]{:S(2)}) async-start(bf16[4,256,256]{2,1,0:T(8,128)(2,1)} %get-tuple-element.27), calls=%async_computation.3 | async-start | bytes 1048576 | tf_op jit(solution)/shard_map/all_to_all | solution.py:308
  93.2 37.3 %copy-start.5 = (bf16[4,128,448]{2,1,0:T(8,128)(2,1)}, bf16[4,128,448]{2,1,0:T(8,128)(2,1)S(1)}, u32[]{:S(2)}) copy-start(bf16[4,128,448]{2,1,0:T(8,128)(2,1)S(1)} %copy.18.feats_ref) | copy-start | bytes 1376260
  93.2 37.3 %collective-permute-start.2 = (bf16[4,128,448]{2,1,0:T(8,128)(2,1)S(1)}, bf16[4,128,448]{2,1,0:T(8,128)(2,1)S(1)}, u32[]{:S(2)}, u32[]{:S(2)}) collective-permute-start(bf16[4,128,448]{2,1,0:T(8,128)(2,1)S(1)} %copy.18.feats_ref), channel_id=1, source_target_pairs={{0,1},{1,0},{2,3},{3,2},{4,5},{5,4},{6,7},{7,6},{8,9},{9,8},{10,11... | collective-permute-start | bytes 1376264 | tf_op jit(solution)/shard_map/ppermute | solution.py:48
  106.9 23.6 %copy-start.4 = (bf16[4,256,256]{2,1,0:T(8,128)(2,1)}, bf16[4,256,256]{2,1,0:T(8,128)(2,1)S(1)}, u32[]{:S(2)}) copy-start(bf16[4,256,256]{2,1,0:T(8,128)(2,1)S(1)} %all-to-all-done.3) | copy-start | bytes 1572868
  106.9 32.1 %collective-permute-start.3 = (bf16[4,256,256]{2,1,0:T(8,128)(2,1)S(1)}, bf16[4,256,256]{2,1,0:T(8,128)(2,1)S(1)}, u32[]{:S(2)}, u32[]{:S(2)}) collective-permute-start(bf16[4,256,256]{2,1,0:T(8,128)(2,1)S(1)} %all-to-all-done.3), channel_id=1, source_target_pairs={{0,8},{8,16},{16,24},{24,32},{32,40},{40,48},{48,56},{56,64},{64,7... | collective-permute-start | bytes 1572872 | tf_op jit(solution)/shard_map/ppermute | solution.py:44
  108.8 31.1 %collective-permute-start.4 = (bf16[4,256,256]{2,1,0:T(8,128)(2,1)S(1)}, bf16[4,256,256]{2,1,0:T(8,128)(2,1)S(1)}, u32[]{:S(2)}, u32[]{:S(2)}) collective-permute-start(bf16[4,256,256]{2,1,0:T(8,128)(2,1)S(1)} %all-to-all-done.3), channel_id=1, source_target_pairs={{8,0},{16,8},{24,16},{32,24},{40,32},{48,40},{56,48},{64,56},{72,6... | collective-permute-start | bytes 1572872 | tf_op jit(solution)/shard_map/ppermute | solution.py:44
  130.5 9.4 %copy-start.9 = (bf16[4,128,448]{2,1,0:T(8,128)(2,1)}, bf16[4,128,448]{2,1,0:T(8,128)(2,1)S(1)}, u32[]{:S(2)}) copy-start(bf16[4,128,448]{2,1,0:T(8,128)(2,1)S(1)} %collective-permute-done.2.feats_other_ref) | copy-start | bytes 1376260
  139.0 0.9 copy-start.10
  139.9 0.8 copy-start.11
  147.6 26.8 %all-to-all-start.5 = ((bf16[64,16,128]{2,1,0:T(8,128)(2,1)}), bf16[64,16,128]{2,1,0:T(8,128)(2,1)S(1)}, u32[]{:S(2)}, u32[]{:S(2)}) async-start(bf16[64,16,128]{2,1,0:T(8,128)(2,1)} %get-tuple-element.29), calls=%async_computation.5 | async-start | bytes 524288 | tf_op jit(solution)/shard_map/all_to_all | solution.py:315
  192.8 20.7 %copy-start.13 = (bf16[256,256]{1,0:T(8,128)(2,1)S(1)}, bf16[256,256]{1,0:T(8,128)(2,1)}, u32[]{:S(2)}) copy-start(bf16[256,256]{1,0:T(8,128)(2,1)} %get-tuple-element.25) | copy-start | bytes 393220
  192.8 20.7 %copy-start.14 = (bf16[2,128,256]{2,1,0:T(8,128)(2,1)S(1)}, bf16[2,128,256]{2,1,0:T(8,128)(2,1)}, u32[]{:S(2)}) copy-start(bf16[2,128,256]{2,1,0:T(8,128)(2,1)} %get-tuple-element.28) | copy-start | bytes 393220
  193.0 24.9 %copy-start = (bf16[1792,512]{1,0:T(8,128)(2,1)S(1)}, bf16[1792,512]{1,0:T(8,128)(2,1)}, u32[]{:S(2)}) copy-start(bf16[1792,512]{1,0:T(8,128)(2,1)} %weight_ref.1) | copy-start | bytes 5505028
  207.0 12.4 %copy-start.1 = (bf16[4,64,16,128]{3,2,1,0:T(8,128)(2,1)}, bf16[4,64,16,128]{3,2,1,0:T(8,128)(2,1)S(1)}, u32[]{:S(2)}) copy-start(bf16[4,64,16,128]{3,2,1,0:T(8,128)(2,1)S(1)} %all_to_all.41.mine_ref) | copy-start | bytes 3145732
  207.0 12.4 %collective-permute-start.5 = (bf16[4,64,16,128]{3,2,1,0:T(8,128)(2,1)S(1)}, bf16[4,64,16,128]{3,2,1,0:T(8,128)(2,1)S(1)}, u32[]{:S(2)}, u32[]{:S(2)}) collective-permute-start(bf16[4,64,16,128]{3,2,1,0:T(8,128)(2,1)S(1)} %all_to_all.41.mine_ref), channel_id=1, source_target_pairs={{0,1},{1,0},{2,3},{3,2},{4,5},{5,4},{6,7},{7,6},{8,9},{9,8},{10,11... | collective-permute-start | bytes 3145736 | tf_op jit(solution)/shard_map/ppermute | solution.py:48
  219.3 1.0 copy-start.6

commit v4 on v3

--- a/solution.py
+++ b/solution.py
@@ -18,6 +18,7 @@
 RUN = 4
 MEMBERS = 8
 REACH = 3
+PIECES = 7
 WINDOW = REACH * MEMBERS * TILE
 BLOCKS = 512
 DEAD = 31
@@ -38,8 +39,52 @@
     return lax.all_to_all(jnp.broadcast_to(shard[None], (count,) + shard.shape), axes, 0, 0)
 
 
+FAR = ((31, 32), (63, 0), (32, 31), (0, 63))
+
+
+def device(group, run, core):
+    return (group * RUN + run) * 2 + core
+
+
+def across(same, cross):
+    pairs = [(a, b, r, c) for a, b in FAR for r in range(RUN) for c in range(2)]
+    straight = [(device(a, r, c), device(b, r, c)) for a, b, r, c in pairs]
+    turned = [(device(a, r, c), device(b, r, 1 - c)) for a, b, r, c in pairs]
+    got = lax.ppermute(same, AXES, straight)
+    return got if cross is None else (got, lax.ppermute(cross, AXES, turned))
+
+
+def along_run(block):
+    parts = [block]
+    for step in range(1, RUN):
+        pairs = [
+            (device(a, r, c), device(a, r ^ step, c))
+            for a, _ in FAR for r in range(RUN) for c in range(2)
+        ]
+        parts.append(lax.ppermute(block, AXES, pairs))
+    return tuple(parts)
+
+
+def block_of(ids_ref, pieces, reach, member):
+    own, low, high = pieces[:REACH]
+    if reach == 1:
+        return own[member, :TILE, :]
+    near = (low, high)[reach // 2][member, :TILE, :]
+    far = pieces[REACH + member // 2][member % 2, :TILE, :]
+    return jnp.where(ids_ref[3 + reach // 2] > 0, far, near)
+
+
+def keys_of(ids_ref, pieces, reach, member):
+    own, low, high = pieces[:REACH]
+    if reach == 1:
+        return own[member, TILE:, :].astype(f32)
+    near = (low, high)[reach // 2][member, TILE:, :].astype(f32)
+    far = pieces[REACH + member // 2][member % 2, TILE:, :].astype(f32)
+    return jnp.where(ids_ref[3 + reach // 2] > 0, far, near)
+
+
 def neighbours(block):
-    forward = [(i, (i + 1) % GROUPS) for i in range(GROUPS)]
+    forward = [(i, (i + 1) % GROUPS) for i in range(GROUPS) if i % 32 != 31]
     backward = [(target, source) for source, target in forward]
     return lax.ppermute(block, WIDE, forward), lax.ppermute(block, WIDE, backward)
 
@@ -49,7 +94,7 @@
 
 
 def project_kernel(ids_ref, count_ref, tiles_ref, slot_ref, col_ref, keep_ref, features_ref, weight_ref,
-                   copies_ref):
+                   copies_ref, same_ref, cross_ref):
     base = (ids_ref[0] - 1) * MEMBERS
     slot = slot_ref[...]
     live = keep_ref[...] * (slot < count_ref[0]).astype(i32)
@@ -72,13 +117,23 @@
         half = (k % 2) * HALF
         copies_ref[k, :TILE, :] = projected[:, half : half + HALF]
         copies_ref[k, TILE:, :] = keys
+    first = ids_ref[2] == 0
+    left, right = projected[:, :HALF], projected[:, HALF:]
+    same_ref[:TILE, :] = jnp.where(first, left, right)
+    same_ref[TILE:, :] = keys
+    cross_ref[:TILE, :] = jnp.where(first, right, left)
+    cross_ref[TILE:, :] = keys
 
 
 def project(ids, tile_count, tile_cols, slot, col, keep, features, weight):
     return pl.pallas_call(
         project_kernel,
         in_specs=[SMEM_SPEC] * 3 + [VMEM_SPEC] * 5,
-        out_shape=jax.ShapeDtypeStruct((MEMBERS, TILE + KEYS, HALF), bf16),
+        out_shape=(
+            jax.ShapeDtypeStruct((MEMBERS, TILE + KEYS, HALF), bf16),
+            jax.ShapeDtypeStruct((TILE + KEYS, HALF), bf16),
+            jax.ShapeDtypeStruct((TILE + KEYS, HALF), bf16),
+        ),
         name="project",
     )(ids, tile_count, tile_cols, slot, col, keep, features, weight)
 
@@ -96,6 +151,10 @@
         block, cells = keys[:TILE, :], keys[TILE:, :]
         live = jnp.where(block < DEAD, 1.0, 0.0)
         degree_ref[core * TILE : core * TILE + TILE, :] = 1.0 + jnp.sum(live, axis=1, keepdims=True)
+        reach_of = lax.shift_right_logical(block, 3)
+        low_twist = jnp.where(reach_of == 0, ids_ref[3] * run * 2, 0)
+        twist = low_twist + jnp.where(reach_of == 2, ids_ref[4] * run * 2, 0)
+        block = jnp.bitwise_xor(block, twist)
         digits = [digits_of(block, reach) for reach in range(REACH)]
         lanes = lax.broadcasted_iota(i32, (16, 128), 1)
         for step in range(TILE // 16):
@@ -125,15 +184,14 @@
     )(ids, own)
 
 
-def backward_counts_kernel(*refs):
-    pieces, out_ref = refs[:REACH], refs[REACH]
-
-    def source(member, carry):
+def backward_counts_kernel(ids_ref, *refs):
+    pieces, out_ref = refs[:PIECES], refs[PIECES]
+    for member in range(MEMBERS):
         for reach in range(REACH):
-            keys = pieces[reach][member, TILE:, :].astype(f32).astype(i32)
+            keys = keys_of(ids_ref, pieces, reach, member).astype(i32)
             digits = digits_of(keys[:, :TILE], REACH - 1 - reach)
             cells = keys[:, TILE:]
-            lanes = pl.ds(reach * MEMBERS * TILE + member * TILE, TILE)
+            lane = (reach * MEMBERS + member) * TILE
             for step in range(TILE // 16):
                 rows = lax.broadcasted_iota(i32, (16, 128), 0) + step * 16
                 total = jnp.zeros((16, 128), i32)
@@ -142,74 +200,83 @@
                 for k in range(MEMBERS):
                     count = jnp.bitwise_and(lax.shift_right_logical(total, 4 * k), 15)
                     at = k * TILE + step * 16
-                    out_ref[at : at + 16, lanes] = count.astype(f32).astype(bf16)
-        return carry
-
-    lax.fori_loop(0, MEMBERS, source, 0)
-
-
-def backward_counts(pieces):
+                    out_ref[at : at + 16, lane : lane + TILE] = count.astype(f32).astype(bf16)
+
+
+def backward_counts(ids, pieces):
     return pl.pallas_call(
         backward_counts_kernel,
-        in_specs=[VMEM_SPEC] * REACH,
+        in_specs=[SMEM_SPEC] + [VMEM_SPEC] * PIECES,
         out_shape=jax.ShapeDtypeStruct((MEMBERS * TILE, WINDOW), bf16),
         cost_estimate=EAGER,
         name="backward_counts",
-    )(*pieces)
-
-
-def forward_kernel(ids_ref, counts_ref, degree_ref, bias_ref, up_ref, *refs):
-    pieces, (hidden_ref, copies_ref, bias_out_ref) = refs[:REACH], refs[REACH:]
-    run = ids_ref[1]
+    )(ids, *pieces)
+
+
+def forward_kernel(ids_ref, counts_ref, degree_ref, bias_ref, up_ref, up_other_ref, *refs):
+    pieces = refs[:PIECES]
+    hidden_ref, hidden_other_ref, copies_ref, scaled_ref, bias_out_ref = refs[PIECES:]
+    run, first = ids_ref[1], ids_ref[2] == 0
     total = jnp.concatenate(
-        [pieces[1][run * 2 + core, :TILE, :].astype(f32) for core in range(2)], axis=0
+        [pieces[0][run * 2 + core, :TILE, :].astype(f32) for core in range(2)], axis=0
     )
     for reach in range(REACH):
         for member in range(MEMBERS):
             lane = (reach * MEMBERS + member) * TILE
             total = total + jnp.dot(
                 counts_ref[:, lane : lane + TILE],
-                pieces[reach][member, :TILE, :],
+                block_of(ids_ref, pieces, reach, member),
                 preferred_element_type=f32,
             )
     degree = degree_ref[...]
     pre = total / degree + bias_ref[...]
     sigma = jax.nn.sigmoid(pre)
-    hidden_ref[...] = (pre * sigma).astype(bf16)
-    grad_pre = up_ref[...].astype(f32) * sigma * (1.0 + pre * (1.0 - sigma))
-    scaled = (grad_pre / degree).astype(bf16)
+    hidden = (pre * sigma).astype(bf16)
+    hidden_ref[...] = jnp.where(first, hidden[:TILE], hidden[TILE:])
+    hidden_other_ref[...] = jnp.where(first, hidden[TILE:], hidden[:TILE])
+    up_mine = jnp.where(first, up_ref[:, :HALF], up_ref[:, HALF:])
+    up_other = up_other_ref[...]
+    up = jnp.concatenate(
+        [jnp.where(first, up_mine, up_other), jnp.where(first, up_other, up_mine)], axis=0
+    )
+    grad_pre = up.astype(f32) * sigma * (1.0 + pre * (1.0 - sigma))
+    scaled = (grad_pre / degree).astype(bf16).reshape(2, TILE, HALF)
+    scaled_ref[...] = scaled
     for k in range(RUN):
         copies_ref[k] = scaled
     bias_out_ref[...] = jnp.sum(grad_pre, axis=0, keepdims=True)
 
 
-def forward_math(ids, counts, degree, bias, upstream, pieces):
+def forward_math(ids, counts, degree, bias, upstream, up_other, pieces):
     return pl.pallas_call(
         forward_kernel,
-        in_specs=[SMEM_SPEC] + [VMEM_SPEC] * (4 + REACH),
+        in_specs=[SMEM_SPEC] + [VMEM_SPEC] * (5 + PIECES),
         out_shape=(
-            jax.ShapeDtypeStruct((2 * TILE, HALF), bf16),
-            jax.ShapeDtypeStruct((RUN, 2 * TILE, HALF), bf16),
+            jax.ShapeDtypeStruct((TILE, HALF), bf16),
+            jax.ShapeDtypeStruct((TILE, HALF), bf16),
+            jax.ShapeDtypeStruct((RUN, 2, TILE, HALF), bf16),
+            jax.ShapeDtypeStruct((2, TILE, HALF), bf16),
             jax.ShapeDtypeStruct((1, HALF), f32),
         ),
         name="forward_math",
-    )(ids, counts, degree, bias, upstream, *pieces)
+    )(ids, counts, degree, bias, upstream, up_other, *pieces)
 
 
 def backward_kernel(ids_ref, counts_ref, bias_ref, feats_ref, feats_other_ref, *refs):
-    pieces, (own_ref, slab_ref, round_ref) = refs[:REACH], refs[REACH:]
+    pieces, (own_ref, other_ref, slab_ref, round_ref) = refs[:PIECES], refs[PIECES:]
     run, core = ids_ref[1], ids_ref[2]
     group = MEMBERS * TILE
-    total = pieces[1][...].reshape(group, HALF).astype(f32)
+    total = pieces[0][...].reshape(group, HALF).astype(f32)
     for reach in range(REACH):
+        rows = [block_of(ids_ref, pieces, reach, member) for member in range(MEMBERS)]
         total = total + jnp.dot(
             counts_ref[:, reach * group : reach * group + group],
-            pieces[reach][...].reshape(group, HALF),
+            jnp.concatenate(rows, axis=0),
             preferred_element_type=f32,
         )
     round_ref[...] = total.astype(bf16).reshape(MEMBERS, TILE, HALF)
-    for k in range(2):
-        own_ref[k] = round_ref[run * 2 + k]
+    own_ref[...] = round_ref[run * 2 + core]
+    other_ref[...] = round_ref[run * 2 + 1 - core]
     part = jnp.zeros((F_RUN, HALF), f32)
     for feats, side in ((feats_ref, core), (feats_other_ref, 1 - core)):
         rows = jnp.concatenate([round_ref[k * 2 + side] for k in range(RUN)], axis=0)
@@ -231,9 +298,10 @@
 def backward_math(ids, counts, bias_rows, feats, feats_other, pieces):
     return pl.pallas_call(
         backward_kernel,
-        in_specs=[SMEM_SPEC] + [VMEM_SPEC] * (4 + REACH),
+        in_specs=[SMEM_SPEC] + [VMEM_SPEC] * (4 + PIECES),
         out_shape=(
-            jax.ShapeDtypeStruct((2, TILE, HALF), bf16),
+            jax.ShapeDtypeStruct((TILE, HALF), bf16),
+            jax.ShapeDtypeStruct((TILE, HALF), bf16),
             jax.ShapeDtypeStruct((SLABS, 16, 128), bf16),
         ),
         scratch_shapes=[pltpu.VMEM((MEMBERS, TILE, HALF), bf16)],
@@ -284,48 +352,68 @@
 def on_device(features, weight, bias, tile_cols, tile_count, nbr_slot, nbr_col, nbr_keep, upstream):
     group = (lax.axis_index("yh") * 4 + lax.axis_index("x")) * 8 + lax.axis_index("z")
     core = lax.axis_index("c")
-    ids = jnp.stack([group, lax.axis_index("yl"), core]).astype(i32)
-
-    copies = project(
+    first = core == 0
+    far_low, far_high = group % 32 == 0, group % 32 == 31
+    ids = jnp.stack([group, lax.axis_index("yl"), core, far_low, far_high]).astype(i32)
+
+    copies, same, cross = project(
         ids, tile_count, tile_cols, nbr_slot.T, nbr_col.T, nbr_keep.T, features, weight
     )
+    straight, turned = across(same, cross)
     own = lax.all_to_all(copies, ("yl", "c"), 0, 0)
-    up_halves = jnp.stack([upstream[:, :HALF], upstream[:, HALF:]])
-    up_halves = lax.all_to_all(up_halves, "c", 0, 0).reshape(2 * TILE, HALF)
+    tied, _ = lax.optimization_barrier((upstream, copies))
+    up_other = swap_core(jnp.where(first, tied[:, HALF:], tied[:, :HALF]))
+    slices = jnp.stack([features[:, k * F_RUN : (k + 1) * F_RUN] for k in range(RUN)])
+    straight, turned, own, up_other, slices = lax.optimization_barrier(
+        (straight, turned, own, up_other, slices)
+    )
+    received = jnp.stack([jnp.where(first, straight, turned), jnp.where(first, turned, straight)])
     low, high = neighbours(own)
+    parts = along_run(received)
     counts, degree = forward_counts(ids, own)
-    low, high, counts, degree, up_halves = lax.optimization_barrier(
-        (low, high, counts, degree, up_halves)
-    )
-    first = (low, own, high)
-    slices = jnp.stack([features[:, k * F_RUN : (k + 1) * F_RUN] for k in range(RUN)])
     feats = lax.all_to_all(slices, "yl", 0, 0)
     feats_other = swap_core(feats)
-    bias_half = lax.dynamic_slice(bias, (core * HALF,), (HALF,))[None]
-    hidden_halves, scaled, bias_part = forward_math(
-        ids, counts, degree, bias_half, up_halves, first
-    )
-    own = lax.all_to_all(scaled, "yl", 0, 0)
-    counts_back = backward_counts(first)
+    pieces = (own, low, high) + parts
+    bias_half = jnp.where(first, bias[:HALF], bias[HALF:])[None]
+    hidden_mine, hidden_send, scaled_copies, scaled, bias_part = forward_math(
+        ids, counts, degree, bias_half, upstream, up_other, pieces
+    )
+
+    received = across(scaled, None)
+    own = lax.all_to_all(scaled_copies, "yl", 0, 0)
+    hidden_got = swap_core(hidden_send)
+    counts_back = backward_counts(ids, pieces)
+    received, own, counts_back = lax.optimization_barrier((received, own, counts_back))
+    own = own.reshape(MEMBERS, TILE, HALF)
     low, high = neighbours(own)
-    rounds, slabs = backward_math(
+    parts = along_run(received)
+    round_mine, round_send, slabs = backward_math(
         ids, counts_back, high_low(bias_part.reshape(2, 128)), feats, feats_other,
-        tuple(block.reshape(MEMBERS, TILE, HALF) for block in (low, own, high)),
-    )
-    reduced = jnp.sum(lax.all_to_all(slabs, WIDE, 0, 0).astype(f32), axis=0)
+        (own, low, high) + parts,
+    )
+    round_got = swap_core(round_send)
+    own_round = jnp.where(
+        first,
+        jnp.concatenate([round_mine, round_got], axis=1),
+        jnp.concatenate([round_got, round_mine], axis=1),
+    )
+    grad_features = lax.dot_general(
+        own_round, weight, (((1,), (1,)), ((), ())), preferred_element_type=f32
+    ).astype(bf16)
+    hidden = jnp.where(
+        first,
+        jnp.concatenate([hidden_mine, hidden_got], axis=1),
+        jnp.concatenate([hidden_got, hidden_mine], axis=1),
+    )
+    terms = lax.all_to_all(slabs, WIDE, 0, 0)
+    terms, grad_features, hidden = lax.optimization_barrier((terms, grad_features, hidden))
+    reduced = jnp.sum(terms.astype(f32), axis=0)
     piece = jnp.where(
         group == BIAS_SLAB, high_low(reduced[:2] + reduced[2:4]), reduced.astype(bf16)
     )
     column = spread_to(piece, ("yh", "yl", "z"), 64)
     plane = spread_to(column, "x", 4)
     weight_grad, bias_grad = assemble(ids, plane, swap_core(plane))
-    rows = jnp.concatenate([hidden_halves.reshape(2, TILE, HALF), rounds], axis=1)
-    rows = lax.all_to_all(rows, "c", 0, 0)
-    hidden = jnp.concatenate([rows[0, :TILE], rows[1, :TILE]], axis=1)
-    own_round = jnp.concatenate([rows[0, TILE:], rows[1, TILE:]], axis=1)
-    grad_features = lax.dot_general(
-        own_round, weight, (((1,), (1,)), ((), ())), preferred_element_type=f32
-    ).astype(bf16)
     return hidden, grad_features, weight_grad, bias_grad.reshape(HID)
 
 

time: 224 us -> 210 us (0.938)
  waiting for transfers between devices: 71.2 us -> 26.7 us
  starting transfers between devices: 72.6 us -> 98 us
  blocking collectives: 35.9 us -> 39.4 us
    ppermute x0 -> x9, starting transfers between devices: none -> 38.6 us  [the longest x6 20.3 us: along_run(): parts.append(lax.ppermute(block, AXES, pairs))]
    ppermute x2, waiting for transfers between devices: 31.9 us -> 0.01 us  [neighbours(): lax.ppermute(block, WIDE, forward)]
    ppermute x2, starting transfers between devices: 24.2 us -> 2.58 us  [neighbours(): lax.ppermute(block, WIDE, backward)]
    ppermute x0 -> x9, waiting for transfers between devices: none -> 19.1 us  [the longest x6 10.8 us: along_run(): parts.append(lax.ppermute(block, AXES, pairs))]
    all_to_all x3 -> x2, waiting for transfers between devices: 24 us -> 5.29 us  [the longest x1 3.04 us: on_device(): own = lax.all_to_all(scaled_copies, 'yl', 0, 0)]
    all_to_all x1, waiting for transfers between devices: 14.3 us -> 0.01 us  [on_device(): own = lax.all_to_all(copies, ('yl', 'c'), 0, 0)]
    all_to_all x3 -> x2, starting transfers between devices: 27.3 us -> 16.2 us  [the longest x1 10.4 us: on_device(): terms = lax.all_to_all(slabs, WIDE, 0, 0)]
    ppermute x2 -> x5, starting transfers between devices: 10.3 us -> 20.2 us  [swap_core(): return lax.ppermute(block, 'c', [(0, 1), (1, 0)])]
  transfers between devices with their start and end apart: 11 -> 22, of which waited for: 6 -> 7; matrix products, arithmetic and copies ran while one was open for 3% -> 3% of each run, Pallas kernels for 10% -> 9%
where the time goes in v4:
time: 210 us; the launch traced here: 209 us
  starting transfers between devices  98 us (47%)
  blocking collectives  39.4 us (19%)
  Pallas kernels  31.1 us (15%)
  waiting for transfers between devices  26.7 us (13%)
  local copies, waits for them, and re-layouts  5.42 us (3%)
  other arithmetic  3.86 us (2%)
  matrix products  2.4 us (1%)
    all_to_all x2, blocking collectives, spread_to(): lax.all_to_all(jnp.broadcast_to(shard[None], (count,) + shard.shape), axe...  39.4 us
    ppermute x6, starting transfers between devices, along_run(): parts.append(lax.ppermute(block, AXES, pairs))  20.3 us
    ppermute x5, starting transfers between devices, swap_core(): return lax.ppermute(block, 'c', [(0, 1), (1, 0)])  20.2 us
    ppermute x2, starting transfers between devices, across(): got = lax.ppermute(same, AXES, straight)  16.4 us
    ppermute x6, waiting for transfers between devices, along_run(): parts.append(lax.ppermute(block, AXES, pairs))  10.8 us
    all_to_all x1, starting transfers between devices, on_device(): own = lax.all_to_all(copies, ('yl', 'c'), 0, 0)  10.4 us
    all_to_all x1, starting transfers between devices, on_device(): terms = lax.all_to_all(slabs, WIDE, 0, 0)  10.4 us
    pallas_call x1, Pallas kernels, backward_counts(): pl.pallas_call(backward_counts_kernel, in_specs=[SMEM_SPEC] + [VMEM_SPEC]...  8.72 us
  transfers between devices with their start and end apart: 22, of which 7 were waited for; matrix products, arithmetic and copies ran while one was open for 3% of the time, Pallas kernels for 9%

profile of v4, /device:TPU:1, one launch (start us, length us, event | category | flops | bytes accessed | tf_op | source)
XLA Modules:
  0.0 208.7 jit_solution(9082352764512127787)
XLA Ops:
  0.6 0.0 copy-start.12
  1.3 0.6 stack.55.ids_ref
  1.9 3.0 %project.1 = (bf16[8,144,256]{2,1,0:T(8,128)(2,1)}, bf16[144,256]{1,0:T(8,128)(2,1)}, bf16[144,256]{1,0:T(8,128)(2,1)}) custom-call(s32[5]{0:T(128)} %stack.55.ids_ref, s32[1]{0:T(128)S(6)} %copy.23.count_ref, s32[1,24]{1,0:T(1,128)} %tiles_ref.1, s32[15,128]{1,0:T(8,128)} %bitcast.28, s32[15,128]{1,0:T(8,128)} %bitcast.29, s32[15,128]{1,0:T(8,128)} %bitcast.30, ...), custom_call_target="tpu_custom_call" | custom-call | tf_op jit(solution)/shard_map/project/pallas_call | solution.py:129
  5.0 10.4 %all-to-all-start = ((bf16[8,144,256]{2,1,0:T(8,128)(2,1)}), bf16[8,144,256]{2,1,0:T(8,128)(2,1)S(1)}, u32[]{:S(2)}, u32[]{:S(2)}) async-start(bf16[8,144,256]{2,1,0:T(8,128)(2,1)} %get-tuple-element.33), calls=%async_computation | async-start | bytes 1179648 | tf_op jit(solution)/shard_map/all_to_all | solution.py:363
  15.4 12.7 %collective-permute-start = (bf16[144,256]{1,0:T(8,128)(2,1)}, bf16[144,256]{1,0:T(8,128)(2,1)S(1)}, u32[]{:S(2)}, u32[]{:S(2)}) collective-permute-start(bf16[144,256]{1,0:T(8,128)(2,1)} %get-tuple-element.31), channel_id=1, source_target_pairs={{248,256},{249,257},{250,258},{251,259},{252,260},{253,261},{254,2... | collective-permute-start | bytes 221192 | tf_op jit(solution)/shard_map/ppermute | solution.py:53
  28.2 2.0 collective-permute-start.1
  30.2 2.3 %collective-permute-start.2 = (bf16[128,256]{1,0:T(8,128)(2,1)S(1)}, bf16[128,256]{1,0:T(8,128)(2,1)S(1)}, u32[]{:S(2)}, u32[]{:S(2)}) collective-permute-start(bf16[128,256]{1,0:T(8,128)(2,1)S(1)} %slice_select_fusion), channel_id=1, source_target_pairs={{0,1},{1,0},{2,3},{3,2},{4,5},{5,4},{6,7},{7,6},{8,9},{9,8},{10,11... | collective-permute-start | bytes 196616 | tf_op jit(solution)/shard_map/ppermute | solution.py:93
  32.5 0.1 fusion.9
  32.6 0.1 copy.22
  32.8 0.1 copy.21
  32.9 0.1 copy.20
  33.0 0.1 copy.19
  33.2 0.6 slice_select_fusion.1
  33.8 0.8 pad_maximum_fusion
  34.6 0.0 collective-permute-done.2.up_other_ref
  34.6 5.6 %collective-permute-done = bf16[144,256]{1,0:T(8,128)(2,1)S(1)} collective-permute-done((bf16[144,256]{1,0:T(8,128)(2,1)}, bf16[144,256]{1,0:T(8,128)(2,1)S(1)}, u32[]{:S(2)}, u32[]{:S(2)}) %collective-permute-start) | collective-permute-done | bytes 73760 | tf_op jit(solution)/shard_map/ppermute | solution.py:53
  40.2 2.7 %collective-permute-done.1 = bf16[144,256]{1,0:T(8,128)(2,1)S(1)} collective-permute-done((bf16[144,256]{1,0:T(8,128)(2,1)}, bf16[144,256]{1,0:T(8,128)(2,1)S(1)}, u32[]{:S(2)}, u32[]{:S(2)}) %collective-permute-start.1) | collective-permute-done | bytes 73760 | tf_op jit(solution)/shard_map/ppermute | solution.py:54
  42.9 1.3 collective-permute-start.3
  44.2 1.3 collective-permute-start.4
  45.5 7.3 %all-to-all-start.2 = ((bf16[4,128,448]{1,2,0:T(8,128)(2,1)}), bf16[4,128,448]{1,2,0:T(8,128)(2,1)S(1)}, u32[]{:S(2)}, u32[]{:S(2)}) async-start(bf16[4,128,448]{1,2,0:T(8,128)(2,1)} %pad_maximum_fusion), calls=%async_computation.2 | async-start | bytes 917504 | tf_op jit(solution)/shard_map/all_to_all | solution.py:374
  52.8 4.1 %collective-permute-start.5 = (bf16[2,144,256]{2,1,0:T(8,128)(2,1)S(1)}, bf16[2,144,256]{2,1,0:T(8,128)(2,1)S(1)}, u32[]{:S(2)}, u32[]{:S(2)}) collective-permute-start(bf16[2,144,256]{2,1,0:T(8,128)(2,1)S(1)} %pad_maximum_fusion.1.refs_3_), channel_id=1, source_target_pairs={{248,250},{249,251},{250,248},{251,249},{252,254},{253,255},{254,2... | collective-permute-start | bytes 442376 | tf_op jit(solution)/shard_map/ppermute | solution.py:64
  57.0 3.3 %collective-permute-start.6 = (bf16[2,144,256]{2,1,0:T(8,128)(2,1)S(1)}, bf16[2,144,256]{2,1,0:T(8,128)(2,1)S(1)}, u32[]{:S(2)}, u32[]{:S(2)}) collective-permute-start(bf16[2,144,256]{2,1,0:T(8,128)(2,1)S(1)} %pad_maximum_fusion.1.refs_3_), channel_id=1, source_target_pairs={{248,252},{249,253},{250,254},{251,255},{252,248},{253,249},{254,2... | collective-permute-start | bytes 442376 | tf_op jit(solution)/shard_map/ppermute | solution.py:64
  60.2 2.7 %collective-permute-start.7 = (bf16[2,144,256]{2,1,0:T(8,128)(2,1)S(1)}, bf16[2,144,256]{2,1,0:T(8,128)(2,1)S(1)}, u32[]{:S(2)}, u32[]{:S(2)}) collective-permute-start(bf16[2,144,256]{2,1,0:T(8,128)(2,1)S(1)} %pad_maximum_fusion.1.refs_3_), channel_id=1, source_target_pairs={{248,254},{249,255},{250,252},{251,253},{252,250},{253,251},{254,2... | collective-permute-start | bytes 442376 | tf_op jit(solution)/shard_map/ppermute | solution.py:64
  62.9 5.1 %forward_counts.1 = (bf16[256,3072]{1,0:T(8,128)(2,1)}, f32[256,1]{1,0:T(8,128)}) custom-call(s32[5]{0:T(128)} %stack.55.ids_ref, bf16[8,144,256]{2,1,0:T(8,128)(2,1)} %copy-done.2), custom_call_target="tpu_custom_call" | custom-call | flops 4000000000 | bytes 8000000 | tf_op jit(solution)/shard_map/forward_counts/pallas_call | solution.py:175
  68.0 6.9 %collective-permute-done.6.refs_5_ = bf16[2,144,256]{2,1,0:T(8,128)(2,1)S(1)} collective-permute-done((bf16[2,144,256]{2,1,0:T(8,128)(2,1)S(1)}, bf16[2,144,256]{2,1,0:T(8,128)(2,1)S(1)}, u32[]{:S(2)}, u32[]{:S(2)}) %collective-permute-start.6) | collective-permute-done | bytes 147488 | tf_op jit(solution)/shard_map/ppermute | solution.py:64
  75.0 0.6 copy-done.14
  75.6 0.0 copy-done.15
  75.6 0.2 copy-done.7
  75.8 0.3 copy-done.8
  76.1 4.2 %forward_math.1 = (bf16[128,256]{1,0:T(8,128)(2,1)}, bf16[128,256]{1,0:T(8,128)(2,1)}, bf16[4,2,128,256]{3,2,1,0:T(8,128)(2,1)}, bf16[2,128,256]{2,1,0:T(8,128)(2,1)}, f32[1,256]{1,0:T(1,128)}) custom-call(s32[5]{0:T(128)} %stack.55.ids_ref, bf16[256,3072]{1,0:T(8,128)(2,1)} %get-tuple-element.36.counts_ref, f32[256,1]{1,0:T(8,128)} %get-tuple-element.37.degree_ref, ...), custom_call_target="tpu_custom_call" | custom-call | tf_op jit(solution)/shard_map/forward_math/pallas_call | solution.py:251
  80.4 5.9 %all-to-all-start.1 = ((bf16[4,2,128,256]{3,2,1,0:T(8,128)(2,1)}), bf16[4,2,128,256]{3,2,1,0:T(8,128)(2,1)S(1)}, u32[]{:S(2)}, u32[]{:S(2)}) async-start(bf16[4,2,128,256]{3,2,1,0:T(8,128)(2,1)} %get-tuple-element.42), calls=%async_computation.1 | async-start | bytes 1048576 | tf_op jit(solution)/shard_map/all_to_all | solution.py:383
  86.2 3.6 %collective-permute-start.8 = (bf16[2,128,256]{2,1,0:T(8,128)(2,1)}, bf16[2,128,256]{2,1,0:T(8,128)(2,1)S(1)}, u32[]{:S(2)}, u32[]{:S(2)}) collective-permute-start(bf16[2,128,256]{2,1,0:T(8,128)(2,1)} %get-tuple-element.41), channel_id=1, source_target_pairs={{248,256},{249,257},{250,258},{251,259},{252,260},{253,261},{254,2... | collective-permute-start | bytes 393224 | tf_op jit(solution)/shard_map/ppermute | solution.py:53
  89.9 0.2 copy.18.feats_ref
  90.1 0.0 copy-start.5
  90.1 3.9 %collective-permute-start.9 = (bf16[4,128,448]{2,1,0:T(8,128)(2,1)S(1)}, bf16[4,128,448]{2,1,0:T(8,128)(2,1)S(1)}, u32[]{:S(2)}, u32[]{:S(2)}) collective-permute-start(bf16[4,128,448]{2,1,0:T(8,128)(2,1)S(1)} %copy.18.feats_ref), channel_id=1, source_target_pairs={{0,1},{1,0},{2,3},{3,2},{4,5},{5,4},{6,7},{7,6},{8,9},{9,8},{10,11... | collective-permute-start | bytes 1376264 | tf_op jit(solution)/shard_map/ppermute | solution.py:93
  94.1 8.7 %backward_counts.1.counts_ref = bf16[1024,3072]{1,0:T(8,128)(2,1)} custom-call(s32[5]{0:T(128)} %stack.55.ids_ref, bf16[8,144,256]{2,1,0:T(8,128)(2,1)} %copy-done.2, bf16[8,144,256]{2,1,0:T(8,128)(2,1)} %copy-done.7, bf16[8,144,256]{2,1,0:T(8,128)(2,1)} %copy-done.8, bf16[2,144,256]{2,1,0:T(8,128)(2,1)} %copy-done.9, bf16[2,144,256]{2,1,0:T(8,128)(2,1)} %copy-done.13, ...), custom_call_target="tpu_custom_call" | custom-call | flops 4000000000 | bytes 8000000 | tf_op jit(solution)/shard_map/backward_counts/pallas_call | solution.py:207
  102.8 0.0 copy-start.16
  102.8 3.0 %all-to-all-done.1 = bf16[4,2,128,256]{3,2,1,0:T(8,128)(2,1)S(1)} async-done(((bf16[4,2,128,256]{3,2,1,0:T(8,128)(2,1)}), bf16[4,2,128,256]{3,2,1,0:T(8,128)(2,1)S(1)}, u32[]{:S(2)}, u32[]{:S(2)}) %all-to-all-start.1) | async-done | bytes 524320 | tf_op jit(solution)/shard_map/all_to_all | solution.py:383
  105.8 1.3 collective-permute-start.10
  107.2 1.3 collective-permute-start.11
  108.5 0.1 pad.13.clone
  108.6 1.9 collective-permute-start.12
  110.5 5.1 %collective-permute-start.13 = (bf16[2,128,256]{2,1,0:T(8,128)(2,1)S(1)}, bf16[2,128,256]{2,1,0:T(8,128)(2,1)S(1)}, u32[]{:S(2)}, u32[]{:S(2)}) collective-permute-start(bf16[2,128,256]{2,1,0:T(8,128)(2,1)S(1)} %collective-permute-done.8.refs_3_), channel_id=1, source_target_pairs={{248,252},{249,253},{250,254},{251,255},{252,248},{253,249},{254,2... | collective-permute-start | bytes 393224 | tf_op jit(solution)/shard_map/ppermute | solution.py:64
  115.6 3.3 %collective-permute-start.14 = (bf16[2,128,256]{2,1,0:T(8,128)(2,1)S(1)}, bf16[2,128,256]{2,1,0:T(8,128)(2,1)S(1)}, u32[]{:S(2)}, u32[]{:S(2)}) collective-permute-start(bf16[2,128,256]{2,1,0:T(8,128)(2,1)S(1)} %collective-permute-done.8.refs_3_), channel_id=1, source_target_pairs={{248,254},{249,255},{250,252},{251,253},{252,250},{253,251},{254,2... | collective-permute-start | bytes 393224 | tf_op jit(solution)/shard_map/ppermute | solution.py:64
  118.9 0.7 maximum_maximum_fusion.bias_ref
  119.6 3.9 %collective-permute-done.14.refs_6_ = bf16[2,128,256]{2,1,0:T(8,128)(2,1)S(1)} collective-permute-done((bf16[2,128,256]{2,1,0:T(8,128)(2,1)S(1)}, bf16[2,128,256]{2,1,0:T(8,128)(2,1)S(1)}, u32[]{:S(2)}, u32[]{:S(2)}) %collective-permute-start.14) | collective-permute-done | bytes 131104 | tf_op jit(solution)/shard_map/ppermute | solution.py:64
  123.5 0.6 copy-done.19
  124.1 0.8 copy-done.11
  125.0 7.0 %backward_math.1 = (bf16[128,256]{1,0:T(8,128)(2,1)}, bf16[128,256]{1,0:T(8,128)(2,1)}, bf16[64,16,128]{2,1,0:T(8,128)(2,1)}) custom-call(s32[5]{0:T(128)} %stack.55.ids_ref, bf16[1024,3072]{1,0:T(8,128)(2,1)} %backward_counts.1.counts_ref, bf16[16,128]{1,0:T(8,128)(2,1)} %maximum_maximum_fusion.bias_ref, bf16[4,128,448]{2,1,0:T(8,128)(2,1)} %copy-done.5, ...), custom_call_target="tpu_custom_call" | custom-call | tf_op jit(solution)/shard_map/backward_math/pallas_call | solution.py:299
  131.9 10.4 %all-to-all-start.3 = ((bf16[64,16,128]{2,1,0:T(8,128)(2,1)}), bf16[64,16,128]{2,1,0:T(8,128)(2,1)S(1)}, u32[]{:S(2)}, u32[]{:S(2)}) async-start(bf16[64,16,128]{2,1,0:T(8,128)(2,1)} %get-tuple-element.48), calls=%async_computation.3 | async-start | bytes 524288 | tf_op jit(solution)/shard_map/all_to_all | solution.py:408
  142.3 5.9 %collective-permute-start.16 = (bf16[128,256]{1,0:T(8,128)(2,1)}, bf16[128,256]{1,0:T(8,128)(2,1)S(1)}, u32[]{:S(2)}, u32[]{:S(2)}) collective-permute-start(bf16[128,256]{1,0:T(8,128)(2,1)} %get-tuple-element.52), channel_id=1, source_target_pairs={{0,1},{1,0},{2,3},{3,2},{4,5},{5,4},{6,7},{7,6},{8,9},{9,8},{10,11... | collective-permute-start | bytes 196616 | tf_op jit(solution)/shard_map/ppermute | solution.py:93
  148.2 1.9 collective-permute-start.15
  150.2 1.6 maximum_select_fusion.2
  151.8 2.4 %convolution_convert_fusion = bf16[128,1792]{1,0:T(8,128)(2,1)} fusion(bf16[1792,512]{1,0:T(8,128)(2,1)S(1)} %copy-done, bf16[128,256]{1,0:T(8,128)(2,1)S(1)} %collective-permute-done.15, bf16[128,256]{1,0:T(8,128)(2,1)} %get-tuple-element.49, pred[]{:T(512)S(6)} %eq.17), kind=kOutput, calls=%fused_computation | convolution fusion | flops 235700224 | bytes 2424833 | tf_op jit(solution)/shard_map/dot_general | solution.py:400
  154.2 2.2 %all-to-all-done.3 = bf16[64,16,128]{2,1,0:T(8,128)(2,1)S(1)} async-done(((bf16[64,16,128]{2,1,0:T(8,128)(2,1)}), bf16[64,16,128]{2,1,0:T(8,128)(2,1)S(1)}, u32[]{:S(2)}, u32[]{:S(2)}) %all-to-all-start.3) | async-done | bytes 262176 | tf_op jit(solution)/shard_map/all_to_all | solution.py:408
  156.4 0.1 convert_reduce_fusion
  156.5 0.1 maximum_select_fusion.3
  156.6 23.7 %all_to_all.30 = bf16[64,16,128]{2,1,0:T(8,128)(2,1)S(1)} all-to-all(bf16[64,16,128]{2,1,0:T(8,128)(2,1)S(1)} %broadcast_in_dim.7), channel_id=1, replica_groups=mesh['yh'=2,'x'=4,'z'=8,'yl'=4,'c'=2] {'yh','yl','z'}, dimensions={0} | all-to-all | bytes 524288 | tf_op jit(solution)/shard_map/all_to_all | solution.py:39
  180.4 0.1 broadcast_in_dim.8
  180.5 15.7 %all_to_all.31.mine_ref = bf16[4,64,16,128]{3,2,1,0:T(8,128)(2,1)S(1)} all-to-all(bf16[4,64,16,128]{3,2,1,0:T(8,128)(2,1)S(1)} %broadcast_in_dim.8), channel_id=1, replica_groups=mesh['yh'=2,'x'=4,'z'=8,'yl'=4,'c'=2] {'x'}, dimensions={0} | all-to-all | bytes 2097152 | tf_op jit(solution)/shard_map/all_to_all | solution.py:39
  196.2 6.1 %collective-permute-start.17 = (bf16[4,64,16,128]{3,2,1,0:T(8,128)(2,1)S(1)}, bf16[4,64,16,128]{3,2,1,0:T(8,128)(2,1)S(1)}, u32[]{:S(2)}, u32[]{:S(2)}) collective-permute-start(bf16[4,64,16,128]{3,2,1,0:T(8,128)(2,1)S(1)} %all_to_all.31.mine_ref), channel_id=1, source_target_pairs={{0,1},{1,0},{2,3},{3,2},{4,5},{5,4},{6,7},{7,6},{8,9},{9,8},{10,11... | collective-permute-start | bytes 3145736 | tf_op jit(solution)/shard_map/ppermute | solution.py:93
  202.3 2.3 %collective-permute-done.17.other_ref = bf16[4,64,16,128]{3,2,1,0:T(8,128)(2,1)S(1)} collective-permute-done((bf16[4,64,16,128]{3,2,1,0:T(8,128)(2,1)S(1)}, bf16[4,64,16,128]{3,2,1,0:T(8,128)(2,1)S(1)}, u32[]{:S(2)}, u32[]{:S(2)}) %collective-permute-start.17) | collective-permute-done | bytes 1048608 | tf_op jit(solution)/shard_map/ppermute | solution.py:93
  204.6 1.0 copy-done.6
  205.6 3.1 %assemble.1 = (bf16[1792,512]{1,0:T(8,128)(2,1)}, f32[4,128]{1,0:T(4,128)}) custom-call(s32[5]{0:T(128)} %stack.55.ids_ref, bf16[4,64,16,128]{3,2,1,0:T(8,128)(2,1)} %copy-done.1, bf16[4,64,16,128]{3,2,1,0:T(8,128)(2,1)} %copy-done.6), custom_call_target="tpu_custom_call" | custom-call | tf_op jit(solution)/shard_map/assemble/pallas_call | solution.py:336
  (57 shorter events, 0.2 us)
Async XLA Ops:
  0.6 29.5 %copy-start.12 = (bf16[128,512]{1,0:T(8,128)(2,1)S(1)}, bf16[128,512]{1,0:T(8,128)(2,1)}, u32[]{:S(2)}) copy-start(bf16[128,512]{1,0:T(8,128)(2,1)} %up_ref.1) | copy-start | bytes 393220
  1.9 30.5 %copy-start.3 = (bf16[128,1792]{1,0:T(8,128)(2,1)S(1)}, bf16[128,1792]{1,0:T(8,128)(2,1)}, u32[]{:S(2)}) copy-start(bf16[128,1792]{1,0:T(8,128)(2,1)} %features_ref.1) | copy-start | bytes 1376260
  5.0 28.2 %copy-start.21 = (f32[512]{0:T(512)S(1)}, f32[512]{0:T(512)}, u32[]{:S(2)}) copy-start(f32[512]{0:T(512)} %param.11) | copy-start | bytes 6148
  5.0 37.9 %all-to-all-start = ((bf16[8,144,256]{2,1,0:T(8,128)(2,1)}), bf16[8,144,256]{2,1,0:T(8,128)(2,1)S(1)}, u32[]{:S(2)}, u32[]{:S(2)}) async-start(bf16[8,144,256]{2,1,0:T(8,128)(2,1)} %get-tuple-element.33), calls=%async_computation | async-start | bytes 1179648 | tf_op jit(solution)/shard_map/all_to_all | solution.py:363
  15.4 24.8 %collective-permute-start = (bf16[144,256]{1,0:T(8,128)(2,1)}, bf16[144,256]{1,0:T(8,128)(2,1)S(1)}, u32[]{:S(2)}, u32[]{:S(2)}) collective-permute-start(bf16[144,256]{1,0:T(8,128)(2,1)} %get-tuple-element.31), channel_id=1, source_target_pairs={{248,256},{249,257},{250,258},{251,259},{252,260},{253,261},{254,2... | collective-permute-start | bytes 221192 | tf_op jit(solution)/shard_map/ppermute | solution.py:53
  28.2 14.7 %collective-permute-start.1 = (bf16[144,256]{1,0:T(8,128)(2,1)}, bf16[144,256]{1,0:T(8,128)(2,1)S(1)}, u32[]{:S(2)}, u32[]{:S(2)}) collective-permute-start(bf16[144,256]{1,0:T(8,128)(2,1)} %get-tuple-element.32), channel_id=1, source_target_pairs={{248,257},{249,256},{250,259},{251,258},{252,261},{253,260},{254,2... | collective-permute-start | bytes 221192 | tf_op jit(solution)/shard_map/ppermute | solution.py:54
  30.2 4.4 %collective-permute-start.2 = (bf16[128,256]{1,0:T(8,128)(2,1)S(1)}, bf16[128,256]{1,0:T(8,128)(2,1)S(1)}, u32[]{:S(2)}, u32[]{:S(2)}) collective-permute-start(bf16[128,256]{1,0:T(8,128)(2,1)S(1)} %slice_select_fusion), channel_id=1, source_target_pairs={{0,1},{1,0},{2,3},{3,2},{4,5},{5,4},{6,7},{7,6},{8,9},{9,8},{10,11... | collective-permute-start | bytes 196616 | tf_op jit(solution)/shard_map/ppermute | solution.py:93
  34.6 33.4 %copy-start.20 = (bf16[128,256]{1,0:T(8,128)(2,1)}, bf16[128,256]{1,0:T(8,128)(2,1)S(1)}, u32[]{:S(2)}) copy-start(bf16[128,256]{1,0:T(8,128)(2,1)S(1)} %collective-permute-done.2.up_other_ref) | copy-start | bytes 196612
  42.9 20.0 %copy-start.2 = (bf16[8,144,256]{2,1,0:T(8,128)(2,1)}, bf16[8,144,256]{2,1,0:T(8,128)(2,1)S(1)}, u32[]{:S(2)}) copy-start(bf16[8,144,256]{2,1,0:T(8,128)(2,1)S(1)} %all-to-all-done.own_ref.refs_0_) | copy-start | bytes 1769476
  42.9 32.0 %collective-permute-start.3 = (bf16[8,144,256]{2,1,0:T(8,128)(2,1)S(1)}, bf16[8,144,256]{2,1,0:T(8,128)(2,1)S(1)}, u32[]{:S(2)}, u32[]{:S(2)}) collective-permute-start(bf16[8,144,256]{2,1,0:T(8,128)(2,1)S(1)} %all-to-all-done.own_ref.refs_0_), channel_id=1, source_target_pairs={{0,8},{8,16},{16,24},{24,32},{32,40},{40,48},{48,56},{56,64},{64,7... | collective-permute-start | bytes 1769480 | tf_op jit(solution)/shard_map/ppermute | solution.py:89
  44.2 30.7 %collective-permute-start.4 = (bf16[8,144,256]{2,1,0:T(8,128)(2,1)S(1)}, bf16[8,144,256]{2,1,0:T(8,128)(2,1)S(1)}, u32[]{:S(2)}, u32[]{:S(2)}) collective-permute-start(bf16[8,144,256]{2,1,0:T(8,128)(2,1)S(1)} %all-to-all-done.own_ref.refs_0_), channel_id=1, source_target_pairs={{8,0},{16,8},{24,16},{32,24},{40,32},{48,40},{56,48},{64,56},{72,6... | collective-permute-start | bytes 1769480 | tf_op jit(solution)/shard_map/ppermute | solution.py:89
  45.5 34.8 %all-to-all-start.2 = ((bf16[4,128,448]{1,2,0:T(8,128)(2,1)}), bf16[4,128,448]{1,2,0:T(8,128)(2,1)S(1)}, u32[]{:S(2)}, u32[]{:S(2)}) async-start(bf16[4,128,448]{1,2,0:T(8,128)(2,1)} %pad_maximum_fusion), calls=%async_computation.2 | async-start | bytes 917504 | tf_op jit(solution)/shard_map/all_to_all | solution.py:374
  52.8 15.2 %copy-start.9 = (bf16[2,144,256]{2,1,0:T(8,128)(2,1)}, bf16[2,144,256]{2,1,0:T(8,128)(2,1)S(1)}, u32[]{:S(2)}) copy-start(bf16[2,144,256]{2,1,0:T(8,128)(2,1)S(1)} %pad_maximum_fusion.1.refs_3_) | copy-start | bytes 442372
  52.8 15.2 %collective-permute-start.5 = (bf16[2,144,256]{2,1,0:T(8,128)(2,1)S(1)}, bf16[2,144,256]{2,1,0:T(8,128)(2,1)S(1)}, u32[]{:S(2)}, u32[]{:S(2)}) collective-permute-start(bf16[2,144,256]{2,1,0:T(8,128)(2,1)S(1)} %pad_maximum_fusion.1.refs_3_), channel_id=1, source_target_pairs={{248,250},{249,251},{250,248},{251,249},{252,254},{253,255},{254,2... | collective-permute-start | bytes 442376 | tf_op jit(solution)/shard_map/ppermute | solution.py:64
  57.0 17.9 %collective-permute-start.6 = (bf16[2,144,256]{2,1,0:T(8,128)(2,1)S(1)}, bf16[2,144,256]{2,1,0:T(8,128)(2,1)S(1)}, u32[]{:S(2)}, u32[]{:S(2)}) collective-permute-start(bf16[2,144,256]{2,1,0:T(8,128)(2,1)S(1)} %pad_maximum_fusion.1.refs_3_), channel_id=1, source_target_pairs={{248,252},{249,253},{250,254},{251,255},{252,248},{253,249},{254,2... | collective-permute-start | bytes 442376 | tf_op jit(solution)/shard_map/ppermute | solution.py:64
  60.2 14.7 %collective-permute-start.7 = (bf16[2,144,256]{2,1,0:T(8,128)(2,1)S(1)}, bf16[2,144,256]{2,1,0:T(8,128)(2,1)S(1)}, u32[]{:S(2)}, u32[]{:S(2)}) collective-permute-start(bf16[2,144,256]{2,1,0:T(8,128)(2,1)S(1)} %pad_maximum_fusion.1.refs_3_), channel_id=1, source_target_pairs={{248,254},{249,255},{250,252},{251,253},{252,250},{253,251},{254,2... | collective-permute-start | bytes 442376 | tf_op jit(solution)/shard_map/ppermute | solution.py:64
  68.0 6.9 %copy-start.13 = (bf16[2,144,256]{2,1,0:T(8,128)(2,1)}, bf16[2,144,256]{2,1,0:T(8,128)(2,1)S(1)}, u32[]{:S(2)}) copy-start(bf16[2,144,256]{2,1,0:T(8,128)(2,1)S(1)} %collective-permute-done.5.refs_4_) | copy-start | bytes 442372
  74.9 0.7 copy-start.14
  74.9 0.7 copy-start.15
  74.9 0.9 copy-start.7
  74.9 1.2 copy-start.8
  80.4 25.5 %all-to-all-start.1 = ((bf16[4,2,128,256]{3,2,1,0:T(8,128)(2,1)}), bf16[4,2,128,256]{3,2,1,0:T(8,128)(2,1)S(1)}, u32[]{:S(2)}, u32[]{:S(2)}) async-start(bf16[4,2,128,256]{3,2,1,0:T(8,128)(2,1)} %get-tuple-element.42), calls=%async_computation.1 | async-start | bytes 1048576 | tf_op jit(solution)/shard_map/all_to_all | solution.py:383
  86.2 16.5 %collective-permute-start.8 = (bf16[2,128,256]{2,1,0:T(8,128)(2,1)}, bf16[2,128,256]{2,1,0:T(8,128)(2,1)S(1)}, u32[]{:S(2)}, u32[]{:S(2)}) collective-permute-start(bf16[2,128,256]{2,1,0:T(8,128)(2,1)} %get-tuple-element.41), channel_id=1, source_target_pairs={{248,256},{249,257},{250,258},{251,259},{252,260},{253,261},{254,2... | collective-permute-start | bytes 393224 | tf_op jit(solution)/shard_map/ppermute | solution.py:53
  90.1 12.7 %copy-start.5 = (bf16[4,128,448]{2,1,0:T(8,128)(2,1)}, bf16[4,128,448]{2,1,0:T(8,128)(2,1)S(1)}, u32[]{:S(2)}) copy-start(bf16[4,128,448]{2,1,0:T(8,128)(2,1)S(1)} %copy.18.feats_ref) | copy-start | bytes 1376260
  90.1 18.4 %copy-start.22 = (f32[1,256]{1,0:T(1,128)S(1)}, f32[1,256]{1,0:T(1,128)}, u32[]{:S(2)}) copy-start(f32[1,256]{1,0:T(1,128)} %get-tuple-element.44) | copy-start | bytes 3076
  90.1 25.5 %collective-permute-start.9 = (bf16[4,128,448]{2,1,0:T(8,128)(2,1)S(1)}, bf16[4,128,448]{2,1,0:T(8,128)(2,1)S(1)}, u32[]{:S(2)}, u32[]{:S(2)}) collective-permute-start(bf16[4,128,448]{2,1,0:T(8,128)(2,1)S(1)} %copy.18.feats_ref), channel_id=1, source_target_pairs={{0,1},{1,0},{2,3},{3,2},{4,5},{5,4},{6,7},{7,6},{8,9},{9,8},{10,11... | collective-permute-start | bytes 1376264 | tf_op jit(solution)/shard_map/ppermute | solution.py:93
  102.8 21.4 %copy-start.16 = (bf16[2,128,256]{2,1,0:T(8,128)(2,1)}, bf16[2,128,256]{2,1,0:T(8,128)(2,1)S(1)}, u32[]{:S(2)}) copy-start(bf16[2,128,256]{2,1,0:T(8,128)(2,1)S(1)} %collective-permute-done.8.refs_3_) | copy-start | bytes 393220
  105.8 18.3 %copy-start.4 = (bf16[4,2,128,256]{3,2,1,0:T(8,128)(2,1)}, bf16[4,2,128,256]{3,2,1,0:T(8,128)(2,1)S(1)}, u32[]{:S(2)}) copy-start(bf16[4,2,128,256]{3,2,1,0:T(8,128)(2,1)S(1)} %all-to-all-done.1) | copy-start | bytes 1572868
  105.8 17.6 %collective-permute-start.10 = (bf16[8,128,256]{2,1,0:T(8,128)(2,1)S(1)}, bf16[8,128,256]{2,1,0:T(8,128)(2,1)S(1)}, u32[]{:S(2)}, u32[]{:S(2)}) collective-permute-start(bf16[8,128,256]{2,1,0:T(8,128)(2,1)S(1)} %bitcast.21), channel_id=1, source_target_pairs={{0,8},{8,16},{16,24},{24,32},{32,40},{40,48},{48,56},{56,64},{64,7... | collective-permute-start | bytes 1572872 | tf_op jit(solution)/shard_map/ppermute | solution.py:89
  107.2 17.0 %collective-permute-start.11 = (bf16[8,128,256]{2,1,0:T(8,128)(2,1)S(1)}, bf16[8,128,256]{2,1,0:T(8,128)(2,1)}, u32[]{:S(2)}, u32[]{:S(2)}) collective-permute-start(bf16[8,128,256]{2,1,0:T(8,128)(2,1)S(1)} %bitcast.22), channel_id=1, source_target_pairs={{8,0},{16,8},{24,16},{32,24},{40,32},{48,40},{56,48},{64,56},{72,6... | collective-permute-start | bytes 1572872 | tf_op jit(solution)/shard_map/ppermute | solution.py:89
  108.6 11.0 %collective-permute-start.12 = (bf16[2,128,256]{2,1,0:T(8,128)(2,1)S(1)}, bf16[2,128,256]{2,1,0:T(8,128)(2,1)S(1)}, u32[]{:S(2)}, u32[]{:S(2)}) collective-permute-start(bf16[2,128,256]{2,1,0:T(8,128)(2,1)S(1)} %collective-permute-done.8.refs_3_), channel_id=1, source_target_pairs={{248,250},{249,251},{250,248},{251,249},{252,254},{253,255},{254,2... | collective-permute-start | bytes 393224 | tf_op jit(solution)/shard_map/ppermute | solution.py:64
  110.5 9.1 %collective-permute-start.13 = (bf16[2,128,256]{2,1,0:T(8,128)(2,1)S(1)}, bf16[2,128,256]{2,1,0:T(8,128)(2,1)S(1)}, u32[]{:S(2)}, u32[]{:S(2)}) collective-permute-start(bf16[2,128,256]{2,1,0:T(8,128)(2,1)S(1)} %collective-permute-done.8.refs_3_), channel_id=1, source_target_pairs={{248,252},{249,253},{250,254},{251,255},{252,248},{253,249},{254,2... | collective-permute-start | bytes 393224 | tf_op jit(solution)/shard_map/ppermute | solution.py:64
  115.6 8.6 %copy-start.10 = (bf16[4,128,448]{2,1,0:T(8,128)(2,1)}, bf16[4,128,448]{2,1,0:T(8,128)(2,1)S(1)}, u32[]{:S(2)}) copy-start(bf16[4,128,448]{2,1,0:T(8,128)(2,1)S(1)} %collective-permute-done.9.feats_other_ref) | copy-start | bytes 1376260
  115.6 7.9 %collective-permute-start.14 = (bf16[2,128,256]{2,1,0:T(8,128)(2,1)S(1)}, bf16[2,128,256]{2,1,0:T(8,128)(2,1)S(1)}, u32[]{:S(2)}, u32[]{:S(2)}) collective-permute-start(bf16[2,128,256]{2,1,0:T(8,128)(2,1)S(1)} %collective-permute-done.8.refs_3_), channel_id=1, source_target_pairs={{248,254},{249,255},{250,252},{251,253},{252,250},{253,251},{254,2... | collective-permute-start | bytes 393224 | tf_op jit(solution)/shard_map/ppermute | solution.py:64
  119.5 32.2 %copy-start = (bf16[1792,512]{1,0:T(8,128)(2,1)S(1)}, bf16[1792,512]{1,0:T(8,128)(2,1)}, u32[]{:S(2)}) copy-start(bf16[1792,512]{1,0:T(8,128)(2,1)} %weight_ref.1) | copy-start | bytes 5505028
  119.5 3.9 %copy-start.17 = (bf16[2,128,256]{2,1,0:T(8,128)(2,1)}, bf16[2,128,256]{2,1,0:T(8,128)(2,1)S(1)}, u32[]{:S(2)}) copy-start(bf16[2,128,256]{2,1,0:T(8,128)(2,1)S(1)} %collective-permute-done.12.refs_4_) | copy-start | bytes 393220
  119.5 3.9 %copy-start.18 = (bf16[2,128,256]{2,1,0:T(8,128)(2,1)}, bf16[2,128,256]{2,1,0:T(8,128)(2,1)S(1)}, u32[]{:S(2)}) copy-start(bf16[2,128,256]{2,1,0:T(8,128)(2,1)S(1)} %collective-permute-done.13.refs_5_) | copy-start | bytes 393220
  123.5 0.6 copy-start.19
  124.1 0.9 copy-start.11
  131.9 24.5 %all-to-all-start.3 = ((bf16[64,16,128]{2,1,0:T(8,128)(2,1)}), bf16[64,16,128]{2,1,0:T(8,128)(2,1)S(1)}, u32[]{:S(2)}, u32[]{:S(2)}) async-start(bf16[64,16,128]{2,1,0:T(8,128)(2,1)} %get-tuple-element.48), calls=%async_computation.3 | async-start | bytes 524288 | tf_op jit(solution)/shard_map/all_to_all | solution.py:408
  142.3 7.8 %collective-permute-start.16 = (bf16[128,256]{1,0:T(8,128)(2,1)}, bf16[128,256]{1,0:T(8,128)(2,1)S(1)}, u32[]{:S(2)}, u32[]{:S(2)}) collective-permute-start(bf16[128,256]{1,0:T(8,128)(2,1)} %get-tuple-element.52), channel_id=1, source_target_pairs={{0,1},{1,0},{2,3},{3,2},{4,5},{5,4},{6,7},{7,6},{8,9},{9,8},{10,11... | collective-permute-start | bytes 196616 | tf_op jit(solution)/shard_map/ppermute | solution.py:93
  148.2 3.5 %collective-permute-start.15 = (bf16[128,256]{1,0:T(8,128)(2,1)}, bf16[128,256]{1,0:T(8,128)(2,1)S(1)}, u32[]{:S(2)}, u32[]{:S(2)}) collective-permute-start(bf16[128,256]{1,0:T(8,128)(2,1)} %get-tuple-element.50), channel_id=1, source_target_pairs={{0,1},{1,0},{2,3},{3,2},{4,5},{5,4},{6,7},{7,6},{8,9},{9,8},{10,11... | collective-permute-start | bytes 196616 | tf_op jit(solution)/shard_map/ppermute | solution.py:93
  196.2 8.4 %copy-start.1 = (bf16[4,64,16,128]{3,2,1,0:T(8,128)(2,1)}, bf16[4,64,16,128]{3,2,1,0:T(8,128)(2,1)S(1)}, u32[]{:S(2)}) copy-start(bf16[4,64,16,128]{3,2,1,0:T(8,128)(2,1)S(1)} %all_to_all.31.mine_ref) | copy-start | bytes 3145732
  196.2 8.4 %collective-permute-start.17 = (bf16[4,64,16,128]{3,2,1,0:T(8,128)(2,1)S(1)}, bf16[4,64,16,128]{3,2,1,0:T(8,128)(2,1)S(1)}, u32[]{:S(2)}, u32[]{:S(2)}) collective-permute-start(bf16[4,64,16,128]{3,2,1,0:T(8,128)(2,1)S(1)} %all_to_all.31.mine_ref), channel_id=1, source_target_pairs={{0,1},{1,0},{2,3},{3,2},{4,5},{5,4},{6,7},{7,6},{8,9},{9,8},{10,11... | collective-permute-start | bytes 3145736 | tf_op jit(solution)/shard_map/ppermute | solution.py:93
  204.6 1.0 copy-start.6

commit v5 on v4

--- a/solution.py
+++ b/solution.py
@@ -213,14 +213,57 @@
     )(ids, *pieces)
 
 
-def forward_kernel(ids_ref, counts_ref, degree_ref, bias_ref, up_ref, up_other_ref, *refs):
-    pieces = refs[:PIECES]
-    hidden_ref, hidden_other_ref, copies_ref, scaled_ref, bias_out_ref = refs[PIECES:]
-    run, first = ids_ref[1], ids_ref[2] == 0
+def forward_own_kernel(ids_ref, counts_ref, own_ref, total_ref):
+    run = ids_ref[1]
     total = jnp.concatenate(
-        [pieces[0][run * 2 + core, :TILE, :].astype(f32) for core in range(2)], axis=0
-    )
-    for reach in range(REACH):
+        [own_ref[run * 2 + core, :TILE, :].astype(f32) for core in range(2)], axis=0
+    )
+    for member in range(MEMBERS):
+        lane = (MEMBERS + member) * TILE
+        total = total + jnp.dot(
+            counts_ref[:, lane : lane + TILE],
+            own_ref[member, :TILE, :],
+            preferred_element_type=f32,
+        )
+    total_ref[...] = total
+
+
+def forward_own(ids, counts, own):
+    return pl.pallas_call(
+        forward_own_kernel,
+        in_specs=[SMEM_SPEC] + [VMEM_SPEC] * 2,
+        out_shape=jax.ShapeDtypeStruct((2 * TILE, HALF), f32),
+        cost_estimate=EAGER,
+        name="forward_own",
+    )(ids, counts, own)
+
+
+def backward_own_kernel(counts_ref, own_ref, total_ref):
+    group = MEMBERS * TILE
+    own = own_ref[...].reshape(group, HALF)
+    total_ref[...] = own.astype(f32) + jnp.dot(
+        counts_ref[:, group : 2 * group], own, preferred_element_type=f32
+    )
+
+
+def backward_own(counts, own):
+    return pl.pallas_call(
+        backward_own_kernel,
+        in_specs=[VMEM_SPEC] * 2,
+        out_shape=jax.ShapeDtypeStruct((MEMBERS * TILE, HALF), f32),
+        cost_estimate=EAGER,
+        name="backward_own",
+    )(counts, own)
+
+
+def forward_kernel(
+    ids_ref, counts_ref, total_ref, degree_ref, bias_ref, up_ref, up_other_ref, *refs
+):
+    pieces = (None,) + refs[: PIECES - 1]
+    hidden_ref, hidden_other_ref, copies_ref, scaled_ref, bias_out_ref = refs[PIECES - 1 :]
+    first = ids_ref[2] == 0
+    total = total_ref[...]
+    for reach in (0, 2):
         for member in range(MEMBERS):
             lane = (reach * MEMBERS + member) * TILE
             total = total + jnp.dot(
@@ -247,7 +290,7 @@
     bias_out_ref[...] = jnp.sum(grad_pre, axis=0, keepdims=True)
 
 
-def forward_math(ids, counts, degree, bias, upstream, up_other, pieces):
+def forward_math(ids, counts, total, degree, bias, upstream, up_other, pieces):
     return pl.pallas_call(
         forward_kernel,
         in_specs=[SMEM_SPEC] + [VMEM_SPEC] * (5 + PIECES),
@@ -259,15 +302,16 @@
             jax.ShapeDtypeStruct((1, HALF), f32),
         ),
         name="forward_math",
-    )(ids, counts, degree, bias, upstream, up_other, *pieces)
-
-
-def backward_kernel(ids_ref, counts_ref, bias_ref, feats_ref, feats_other_ref, *refs):
-    pieces, (own_ref, other_ref, slab_ref, round_ref) = refs[:PIECES], refs[PIECES:]
+    )(ids, counts, total, degree, bias, upstream, up_other, *pieces)
+
+
+def backward_kernel(ids_ref, counts_ref, total_ref, bias_ref, feats_ref, feats_other_ref, *refs):
+    pieces = (None,) + refs[: PIECES - 1]
+    own_ref, other_ref, slab_ref, round_ref = refs[PIECES - 1 :]
     run, core = ids_ref[1], ids_ref[2]
     group = MEMBERS * TILE
-    total = pieces[0][...].reshape(group, HALF).astype(f32)
-    for reach in range(REACH):
+    total = total_ref[...]
+    for reach in (0, 2):
         rows = [block_of(ids_ref, pieces, reach, member) for member in range(MEMBERS)]
         total = total + jnp.dot(
             counts_ref[:, reach * group : reach * group + group],
@@ -295,7 +339,7 @@
         slab_ref[rest] = jnp.zeros((16, 128), bf16)
 
 
-def backward_math(ids, counts, bias_rows, feats, feats_other, pieces):
+def backward_math(ids, counts, total, bias_rows, feats, feats_other, pieces):
     return pl.pallas_call(
         backward_kernel,
         in_specs=[SMEM_SPEC] + [VMEM_SPEC] * (4 + PIECES),
@@ -306,7 +350,7 @@
         ),
         scratch_shapes=[pltpu.VMEM((MEMBERS, TILE, HALF), bf16)],
         name="backward_math",
-    )(ids, counts, bias_rows, feats, feats_other, *pieces)
+    )(ids, counts, total, bias_rows, feats, feats_other, *pieces)
 
 
 def assemble_kernel(ids_ref, mine_ref, other_ref, weight_ref, bias_ref):
@@ -364,9 +408,8 @@
     tied, _ = lax.optimization_barrier((upstream, copies))
     up_other = swap_core(jnp.where(first, tied[:, HALF:], tied[:, :HALF]))
     slices = jnp.stack([features[:, k * F_RUN : (k + 1) * F_RUN] for k in range(RUN)])
-    straight, turned, own, up_other, slices = lax.optimization_barrier(
-        (straight, turned, own, up_other, slices)
-    )
+    own, up_other, slices = lax.optimization_barrier((own, up_other, slices))
+    straight, turned, _ = lax.optimization_barrier((straight, turned, own))
     received = jnp.stack([jnp.where(first, straight, turned), jnp.where(first, turned, straight)])
     low, high = neighbours(own)
     parts = along_run(received)
@@ -376,7 +419,8 @@
     pieces = (own, low, high) + parts
     bias_half = jnp.where(first, bias[:HALF], bias[HALF:])[None]
     hidden_mine, hidden_send, scaled_copies, scaled, bias_part = forward_math(
-        ids, counts, degree, bias_half, upstream, up_other, pieces
+        ids, counts, forward_own(ids, counts, own), degree, bias_half, upstream, up_other,
+        pieces[1:],
     )
 
     received = across(scaled, None)
@@ -388,8 +432,8 @@
     low, high = neighbours(own)
     parts = along_run(received)
     round_mine, round_send, slabs = backward_math(
-        ids, counts_back, high_low(bias_part.reshape(2, 128)), feats, feats_other,
-        (own, low, high) + parts,
+        ids, counts_back, backward_own(counts_back, own), high_low(bias_part.reshape(2, 128)),
+        feats, feats_other, (low, high) + parts,
     )
     round_got = swap_core(round_send)
     own_round = jnp.where(

time: 210 us -> 205 us (0.976)
  waiting for transfers between devices: 26.7 us -> 18.8 us
  Pallas kernels: 31.1 us -> 37.5 us
  starting transfers between devices: 98 us -> 94.3 us
    ppermute x6, waiting for transfers between devices: 10.8 us -> 0.02 us  [along_run(): parts.append(lax.ppermute(block, AXES, pairs))]
    pallas_call x0 -> x2, Pallas kernels: none -> 7.22 us  [the longest x1 4.54 us: backward_own(): pl.pallas_call(backward_own_kernel, in_specs=[VMEM_SPEC] * 2, out_shape=j...]
    all_to_all x1, waiting for transfers between devices: 0.01 us -> 3.55 us  [on_device(): feats = lax.all_to_all(slices, 'yl', 0, 0)]
    all_to_all x1, starting transfers between devices: 7.26 us -> 4.25 us  [on_device(): feats = lax.all_to_all(slices, 'yl', 0, 0)]
    ppermute x2, waiting for transfers between devices: 5.56 us -> 2.95 us  [across(): got = lax.ppermute(same, AXES, straight)]
    ppermute x1, waiting for transfers between devices: 2.73 us -> 5.14 us  [across(): return got if cross is None else (got, lax.ppermute(cross, AXES, turned))]
    unnamed x50 -> x48, local copies, waits for them, and re-layouts: 4.22 us -> 4.41 us
  transfers between devices with their start and end apart: 22 -> 22, of which waited for: 7 -> 7; matrix products, arithmetic and copies ran while one was open for 3% -> 3% of each run, Pallas kernels for 9% -> 12%
where the time goes in v5:
time: 205 us; the launch traced here: 203 us
  starting transfers between devices  94.3 us (46%)
  blocking collectives  40 us (20%)
  Pallas kernels  37.5 us (18%)
  waiting for transfers between devices  18.8 us (9%)
  local copies, waits for them, and re-layouts  5.69 us (3%)
  other arithmetic  2.95 us (1%)
  matrix products  2.4 us (1%)
    all_to_all x2, blocking collectives, spread_to(): lax.all_to_all(jnp.broadcast_to(shard[None], (count,) + shard.shape), axe...  40 us
    ppermute x6, starting transfers between devices, along_run(): parts.append(lax.ppermute(block, AXES, pairs))  20.8 us
    ppermute x5, starting transfers between devices, swap_core(): return lax.ppermute(block, 'c', [(0, 1), (1, 0)])  19.2 us
    ppermute x2, starting transfers between devices, across(): got = lax.ppermute(same, AXES, straight)  18.1 us
    all_to_all x1, starting transfers between devices, on_device(): own = lax.all_to_all(copies, ('yl', 'c'), 0, 0)  10.5 us
    all_to_all x1, starting transfers between devices, on_device(): terms = lax.all_to_all(slabs, WIDE, 0, 0)  9.91 us
    pallas_call x1, Pallas kernels, backward_counts(): pl.pallas_call(backward_counts_kernel, in_specs=[SMEM_SPEC] + [VMEM_SPEC]...  8.72 us
    pallas_call x1, Pallas kernels, backward_math(): pl.pallas_call(backward_kernel, in_specs=[SMEM_SPEC] + [VMEM_SPEC] * (4 +...  6.58 us
  transfers between devices with their start and end apart: 22, of which 7 were waited for; matrix products, arithmetic and copies ran while one was open for 3% of the time, Pallas kernels for 12%

profile of v5, /device:TPU:1, one launch (start us, length us, event | category | flops | bytes accessed | tf_op | source)
XLA Modules:
  0.0 203.4 jit_solution(8549484034318052398)
XLA Ops:
  0.6 0.0 copy-start.12
  1.3 0.7 stack.55.ids_ref
  2.0 3.0 %project.1 = (bf16[8,144,256]{2,1,0:T(8,128)(2,1)}, bf16[144,256]{1,0:T(8,128)(2,1)}, bf16[144,256]{1,0:T(8,128)(2,1)}) custom-call(s32[5]{0:T(128)} %stack.55.ids_ref, s32[1]{0:T(128)S(6)} %copy.23.count_ref, s32[1,24]{1,0:T(1,128)} %tiles_ref.1, s32[15,128]{1,0:T(8,128)} %bitcast.25, s32[15,128]{1,0:T(8,128)} %bitcast.26, s32[15,128]{1,0:T(8,128)} %bitcast.27, ...), custom_call_target="tpu_custom_call" | custom-call | tf_op jit(solution)/shard_map/project/pallas_call | solution.py:129
  5.0 10.5 %all-to-all-start = ((bf16[8,144,256]{2,1,0:T(8,128)(2,1)}), bf16[8,144,256]{2,1,0:T(8,128)(2,1)S(1)}, u32[]{:S(2)}, u32[]{:S(2)}) async-start(bf16[8,144,256]{2,1,0:T(8,128)(2,1)} %get-tuple-element.31), calls=%async_computation | async-start | bytes 1179648 | tf_op jit(solution)/shard_map/all_to_all | solution.py:407
  15.5 2.0 collective-permute-start
  17.6 12.7 %collective-permute-start.3 = (bf16[144,256]{1,0:T(8,128)(2,1)}, bf16[144,256]{1,0:T(8,128)(2,1)S(1)}, u32[]{:S(2)}, u32[]{:S(2)}) collective-permute-start(bf16[144,256]{1,0:T(8,128)(2,1)} %get-tuple-element.37), channel_id=1, source_target_pairs={{248,256},{249,257},{250,258},{251,259},{252,260},{253,261},{254,2... | collective-permute-start | bytes 221192 | tf_op jit(solution)/shard_map/ppermute | solution.py:53
  30.3 2.2 %collective-permute-start.4 = (bf16[144,256]{1,0:T(8,128)(2,1)}, bf16[144,256]{1,0:T(8,128)(2,1)S(1)}, u32[]{:S(2)}, u32[]{:S(2)}) collective-permute-start(bf16[144,256]{1,0:T(8,128)(2,1)} %get-tuple-element.38), channel_id=1, source_target_pairs={{248,257},{249,256},{250,259},{251,258},{252,261},{253,260},{254,2... | collective-permute-start | bytes 221192 | tf_op jit(solution)/shard_map/ppermute | solution.py:54
  32.5 0.1 fusion.9
  32.7 0.1 copy.22
  32.8 0.1 copy.21
  32.9 0.1 copy.20
  33.1 0.1 copy.19
  33.2 0.6 slice_select_fusion.1
  33.8 0.8 pad_maximum_fusion
  34.7 1.3 collective-permute-start.1
  36.0 1.3 collective-permute-start.2
  37.3 3.0 %collective-permute-done.3 = bf16[144,256]{1,0:T(8,128)(2,1)S(1)} collective-permute-done((bf16[144,256]{1,0:T(8,128)(2,1)}, bf16[144,256]{1,0:T(8,128)(2,1)S(1)}, u32[]{:S(2)}, u32[]{:S(2)}) %collective-permute-start.3) | collective-permute-done | bytes 73760 | tf_op jit(solution)/shard_map/ppermute | solution.py:53
  40.2 5.1 %collective-permute-done.4 = bf16[144,256]{1,0:T(8,128)(2,1)S(1)} collective-permute-done((bf16[144,256]{1,0:T(8,128)(2,1)}, bf16[144,256]{1,0:T(8,128)(2,1)S(1)}, u32[]{:S(2)}, u32[]{:S(2)}) %collective-permute-start.4) | collective-permute-done | bytes 73760 | tf_op jit(solution)/shard_map/ppermute | solution.py:54
  45.4 4.0 %collective-permute-start.5 = (bf16[2,144,256]{2,1,0:T(8,128)(2,1)S(1)}, bf16[2,144,256]{2,1,0:T(8,128)(2,1)S(1)}, u32[]{:S(2)}, u32[]{:S(2)}) collective-permute-start(bf16[2,144,256]{2,1,0:T(8,128)(2,1)S(1)} %pad_maximum_fusion.1.refs_2_.refs_3_), channel_id=1, source_target_pairs={{248,250},{249,251},{250,248},{251,249},{252,254},{253,255},{254,2... | collective-permute-start | bytes 442376 | tf_op jit(solution)/shard_map/ppermute | solution.py:64
  49.5 4.3 %collective-permute-start.6 = (bf16[2,144,256]{2,1,0:T(8,128)(2,1)S(1)}, bf16[2,144,256]{2,1,0:T(8,128)(2,1)S(1)}, u32[]{:S(2)}, u32[]{:S(2)}) collective-permute-start(bf16[2,144,256]{2,1,0:T(8,128)(2,1)S(1)} %pad_maximum_fusion.1.refs_2_.refs_3_), channel_id=1, source_target_pairs={{248,252},{249,253},{250,254},{251,255},{252,248},{253,249},{254,2... | collective-permute-start | bytes 442376 | tf_op jit(solution)/shard_map/ppermute | solution.py:64
  53.8 2.2 %collective-permute-start.7 = (bf16[2,144,256]{2,1,0:T(8,128)(2,1)S(1)}, bf16[2,144,256]{2,1,0:T(8,128)(2,1)S(1)}, u32[]{:S(2)}, u32[]{:S(2)}) collective-permute-start(bf16[2,144,256]{2,1,0:T(8,128)(2,1)S(1)} %pad_maximum_fusion.1.refs_2_.refs_3_), channel_id=1, source_target_pairs={{248,254},{249,255},{250,252},{251,253},{252,250},{253,251},{254,2... | collective-permute-start | bytes 442376 | tf_op jit(solution)/shard_map/ppermute | solution.py:64
  56.0 4.3 %all-to-all-start.2 = ((bf16[4,128,448]{1,2,0:T(8,128)(2,1)}), bf16[4,128,448]{1,2,0:T(8,128)(2,1)S(1)}, u32[]{:S(2)}, u32[]{:S(2)}) async-start(bf16[4,128,448]{1,2,0:T(8,128)(2,1)} %pad_maximum_fusion), calls=%async_computation.2 | async-start | bytes 917504 | tf_op jit(solution)/shard_map/all_to_all | solution.py:417
  60.3 5.1 %forward_counts.1 = (bf16[256,3072]{1,0:T(8,128)(2,1)}, f32[256,1]{1,0:T(8,128)}) custom-call(s32[5]{0:T(128)} %stack.55.ids_ref, bf16[8,144,256]{2,1,0:T(8,128)(2,1)} %copy-done.8), custom_call_target="tpu_custom_call" | custom-call | flops 4000000000 | bytes 8000000 | tf_op jit(solution)/shard_map/forward_counts/pallas_call | solution.py:175
  65.4 2.7 %forward_own.1.total_ref = f32[256,256]{1,0:T(8,128)} custom-call(s32[5]{0:T(128)} %stack.55.ids_ref, bf16[256,3072]{1,0:T(8,128)(2,1)} %get-tuple-element.34.counts_ref, bf16[8,144,256]{2,1,0:T(8,128)(2,1)} %copy-done.8), custom_call_target="tpu_custom_call" | custom-call | flops 4000000000 | bytes 8000000 | tf_op jit(solution)/shard_map/forward_own/pallas_call | solution.py:232
  68.1 0.6 copy-done.13
  68.7 0.1 copy-done.14
  68.8 0.1 copy-done.15
  68.9 0.2 copy-done.5
  69.1 0.3 copy-done.6
  69.3 3.8 %forward_math.1 = (bf16[128,256]{1,0:T(8,128)(2,1)}, bf16[128,256]{1,0:T(8,128)(2,1)}, bf16[4,2,128,256]{3,2,1,0:T(8,128)(2,1)}, bf16[2,128,256]{2,1,0:T(8,128)(2,1)}, f32[1,256]{1,0:T(1,128)}) custom-call(s32[5]{0:T(128)} %stack.55.ids_ref, bf16[256,3072]{1,0:T(8,128)(2,1)} %get-tuple-element.34.counts_ref, f32[256,256]{1,0:T(8,128)} %forward_own.1.total_ref, ...), custom_call_target="tpu_custom_call" | custom-call | tf_op jit(solution)/shard_map/forward_math/pallas_call | solution.py:294
  73.1 3.6 %all-to-all-done.2 = bf16[4,128,448]{1,2,0:T(8,128)(2,1)S(1)} async-done(((bf16[4,128,448]{1,2,0:T(8,128)(2,1)}), bf16[4,128,448]{1,2,0:T(8,128)(2,1)S(1)}, u32[]{:S(2)}, u32[]{:S(2)}) %all-to-all-start.2) | async-done | bytes 458784 | tf_op jit(solution)/shard_map/all_to_all | solution.py:417
  76.6 4.2 %all-to-all-start.1 = ((bf16[4,2,128,256]{3,2,1,0:T(8,128)(2,1)}), bf16[4,2,128,256]{3,2,1,0:T(8,128)(2,1)}, u32[]{:S(2)}, u32[]{:S(2)}) async-start(bf16[4,2,128,256]{3,2,1,0:T(8,128)(2,1)} %get-tuple-element.42), calls=%async_computation.1 | async-start | bytes 1048576 | tf_op jit(solution)/shard_map/all_to_all | solution.py:427
  80.8 0.1 pad.13.clone
  80.9 5.4 %collective-permute-start.8 = (bf16[2,128,256]{2,1,0:T(8,128)(2,1)}, bf16[2,128,256]{2,1,0:T(8,128)(2,1)S(1)}, u32[]{:S(2)}, u32[]{:S(2)}) collective-permute-start(bf16[2,128,256]{2,1,0:T(8,128)(2,1)} %get-tuple-element.41), channel_id=1, source_target_pairs={{248,256},{249,257},{250,258},{251,259},{252,260},{253,261},{254,2... | collective-permute-start | bytes 393224 | tf_op jit(solution)/shard_map/ppermute | solution.py:53
  86.2 0.2 copy.18.feats_ref
  86.5 3.7 %collective-permute-start.9 = (bf16[4,128,448]{2,1,0:T(8,128)(2,1)S(1)}, bf16[4,128,448]{2,1,0:T(8,128)(2,1)S(1)}, u32[]{:S(2)}, u32[]{:S(2)}) collective-permute-start(bf16[4,128,448]{2,1,0:T(8,128)(2,1)S(1)} %copy.18.feats_ref), channel_id=1, source_target_pairs={{0,1},{1,0},{2,3},{3,2},{4,5},{5,4},{6,7},{7,6},{8,9},{9,8},{10,11... | collective-permute-start | bytes 1376264 | tf_op jit(solution)/shard_map/ppermute | solution.py:93
  90.2 8.7 %backward_counts.1.counts_ref = bf16[1024,3072]{1,0:T(8,128)(2,1)} custom-call(s32[5]{0:T(128)} %stack.55.ids_ref, bf16[8,144,256]{2,1,0:T(8,128)(2,1)} %copy-done.8, bf16[8,144,256]{2,1,0:T(8,128)(2,1)} %copy-done.5, bf16[8,144,256]{2,1,0:T(8,128)(2,1)} %copy-done.6, bf16[2,144,256]{2,1,0:T(8,128)(2,1)} %copy-done.7, bf16[2,144,256]{2,1,0:T(8,128)(2,1)} %copy-done.13, ...), custom_call_target="tpu_custom_call" | custom-call | flops 4000000000 | bytes 8000000 | tf_op jit(solution)/shard_map/backward_counts/pallas_call | solution.py:207
  99.0 1.5 all-to-all-done.1
  100.4 1.3 collective-permute-start.10
  101.8 1.3 collective-permute-start.11
  103.1 0.7 maximum_maximum_fusion.bias_ref
  103.7 2.1 %collective-permute-start.12 = (bf16[2,128,256]{2,1,0:T(8,128)(2,1)S(1)}, bf16[2,128,256]{2,1,0:T(8,128)(2,1)}, u32[]{:S(2)}, u32[]{:S(2)}) collective-permute-start(bf16[2,128,256]{2,1,0:T(8,128)(2,1)S(1)} %collective-permute-done.8.refs_2_), channel_id=1, source_target_pairs={{248,250},{249,251},{250,248},{251,249},{252,254},{253,255},{254,2... | collective-permute-start | bytes 393224 | tf_op jit(solution)/shard_map/ppermute | solution.py:64
  105.9 4.9 %collective-permute-start.13 = (bf16[2,128,256]{2,1,0:T(8,128)(2,1)S(1)}, bf16[2,128,256]{2,1,0:T(8,128)(2,1)}, u32[]{:S(2)}, u32[]{:S(2)}) collective-permute-start(bf16[2,128,256]{2,1,0:T(8,128)(2,1)S(1)} %collective-permute-done.8.refs_2_), channel_id=1, source_target_pairs={{248,252},{249,253},{250,254},{251,255},{252,248},{253,249},{254,2... | collective-permute-start | bytes 393224 | tf_op jit(solution)/shard_map/ppermute | solution.py:64
  110.8 3.3 %collective-permute-start.14 = (bf16[2,128,256]{2,1,0:T(8,128)(2,1)S(1)}, bf16[2,128,256]{2,1,0:T(8,128)(2,1)}, u32[]{:S(2)}, u32[]{:S(2)}) collective-permute-start(bf16[2,128,256]{2,1,0:T(8,128)(2,1)S(1)} %collective-permute-done.8.refs_2_), channel_id=1, source_target_pairs={{248,254},{249,255},{250,252},{251,253},{252,250},{253,251},{254,2... | collective-permute-start | bytes 393224 | tf_op jit(solution)/shard_map/ppermute | solution.py:64
  114.1 4.5 %backward_own.1.total_ref = f32[1024,256]{1,0:T(8,128)} custom-call(bf16[1024,3072]{1,0:T(8,128)(2,1)} %backward_counts.1.counts_ref, bf16[8,128,256]{2,1,0:T(8,128)(2,1)} %bitcast.15.own_ref), custom_call_target="tpu_custom_call" | custom-call | flops 4000000000 | bytes 8000000 | tf_op jit(solution)/shard_map/backward_own/pallas_call | solution.py:250
  118.7 0.8 copy-done.10
  119.5 0.8 copy-done.11
  120.3 6.6 %backward_math.1 = (bf16[128,256]{1,0:T(8,128)(2,1)}, bf16[128,256]{1,0:T(8,128)(2,1)}, bf16[64,16,128]{2,1,0:T(8,128)(2,1)}) custom-call(s32[5]{0:T(128)} %stack.55.ids_ref, bf16[1024,3072]{1,0:T(8,128)(2,1)} %backward_counts.1.counts_ref, f32[1024,256]{1,0:T(8,128)} %backward_own.1.total_ref, bf16[16,128]{1,0:T(8,128)(2,1)} %maximum_maximum_fusion.bias_ref, ...), custom_call_target="tpu_custom_call" | custom-call | tf_op jit(solution)/shard_map/backward_math/pallas_call | solution.py:343
  126.9 9.9 %all-to-all-start.3 = ((bf16[64,16,128]{2,1,0:T(8,128)(2,1)}), bf16[64,16,128]{2,1,0:T(8,128)(2,1)S(1)}, u32[]{:S(2)}, u32[]{:S(2)}) async-start(bf16[64,16,128]{2,1,0:T(8,128)(2,1)} %get-tuple-element.48), calls=%async_computation.3 | async-start | bytes 524288 | tf_op jit(solution)/shard_map/all_to_all | solution.py:452
  136.8 5.7 %collective-permute-start.16 = (bf16[128,256]{1,0:T(8,128)(2,1)S(1)}, bf16[128,256]{1,0:T(8,128)(2,1)S(1)}, u32[]{:S(2)}, u32[]{:S(2)}) collective-permute-start(bf16[128,256]{1,0:T(8,128)(2,1)S(1)} %copy-done.21), channel_id=1, source_target_pairs={{0,1},{1,0},{2,3},{3,2},{4,5},{5,4},{6,7},{7,6},{8,9},{9,8},{10,11... | collective-permute-start | bytes 196616 | tf_op jit(solution)/shard_map/ppermute | solution.py:93
  142.5 1.9 collective-permute-start.15
  144.5 0.7 maximum_select_fusion.2
  145.1 0.7 collective-permute-done.15
  145.9 2.4 %convolution_convert_fusion = bf16[128,1792]{1,0:T(8,128)(2,1)} fusion(bf16[1792,512]{1,0:T(8,128)(2,1)S(1)} %copy-done, bf16[128,256]{1,0:T(8,128)(2,1)S(1)} %collective-permute-done.15, bf16[128,256]{1,0:T(8,128)(2,1)} %get-tuple-element.49, pred[]{:T(512)S(6)} %eq.17), kind=kOutput, calls=%fused_computation | convolution fusion | flops 235700224 | bytes 2424833 | tf_op jit(solution)/shard_map/dot_general | solution.py:444
  148.3 2.6 %all-to-all-done.3 = bf16[64,16,128]{2,1,0:T(8,128)(2,1)S(1)} async-done(((bf16[64,16,128]{2,1,0:T(8,128)(2,1)}), bf16[64,16,128]{2,1,0:T(8,128)(2,1)S(1)}, u32[]{:S(2)}, u32[]{:S(2)}) %all-to-all-start.3) | async-done | bytes 262176 | tf_op jit(solution)/shard_map/all_to_all | solution.py:452
  150.9 0.1 convert_reduce_fusion
  151.0 0.1 maximum_select_fusion.3
  151.1 23.1 %all_to_all.30 = bf16[64,16,128]{2,1,0:T(8,128)(2,1)S(1)} all-to-all(bf16[64,16,128]{2,1,0:T(8,128)(2,1)S(1)} %broadcast_in_dim.7), channel_id=1, replica_groups=mesh['yh'=2,'x'=4,'z'=8,'yl'=4,'c'=2] {'yh','yl','z'}, dimensions={0} | all-to-all | bytes 524288 | tf_op jit(solution)/shard_map/all_to_all | solution.py:39
  174.2 0.1 broadcast_in_dim.8
  174.4 16.9 %all_to_all.31.mine_ref = bf16[4,64,16,128]{3,2,1,0:T(8,128)(2,1)S(1)} all-to-all(bf16[4,64,16,128]{3,2,1,0:T(8,128)(2,1)S(1)} %broadcast_in_dim.8), channel_id=1, replica_groups=mesh['yh'=2,'x'=4,'z'=8,'yl'=4,'c'=2] {'x'}, dimensions={0} | all-to-all | bytes 2097152 | tf_op jit(solution)/shard_map/all_to_all | solution.py:39
  191.3 5.8 %collective-permute-start.17 = (bf16[4,64,16,128]{3,2,1,0:T(8,128)(2,1)S(1)}, bf16[4,64,16,128]{3,2,1,0:T(8,128)(2,1)S(1)}, u32[]{:S(2)}, u32[]{:S(2)}) collective-permute-start(bf16[4,64,16,128]{3,2,1,0:T(8,128)(2,1)S(1)} %all_to_all.31.mine_ref), channel_id=1, source_target_pairs={{0,1},{1,0},{2,3},{3,2},{4,5},{5,4},{6,7},{7,6},{8,9},{9,8},{10,11... | collective-permute-start | bytes 3145736 | tf_op jit(solution)/shard_map/ppermute | solution.py:93
  197.1 2.3 %collective-permute-done.17.other_ref = bf16[4,64,16,128]{3,2,1,0:T(8,128)(2,1)S(1)} collective-permute-done((bf16[4,64,16,128]{3,2,1,0:T(8,128)(2,1)S(1)}, bf16[4,64,16,128]{3,2,1,0:T(8,128)(2,1)S(1)}, u32[]{:S(2)}, u32[]{:S(2)}) %collective-permute-start.17) | collective-permute-done | bytes 1048608 | tf_op jit(solution)/shard_map/ppermute | solution.py:93
  199.4 1.0 copy-done.4
  200.3 3.1 %assemble.1 = (bf16[1792,512]{1,0:T(8,128)(2,1)}, f32[4,128]{1,0:T(4,128)}) custom-call(s32[5]{0:T(128)} %stack.55.ids_ref, bf16[4,64,16,128]{3,2,1,0:T(8,128)(2,1)} %copy-done.1, bf16[4,64,16,128]{3,2,1,0:T(8,128)(2,1)} %copy-done.4), custom_call_target="tpu_custom_call" | custom-call | tf_op jit(solution)/shard_map/assemble/pallas_call | solution.py:380
  (57 shorter events, 0.2 us)
Async XLA Ops:
  0.6 14.9 %copy-start.12 = (bf16[128,512]{1,0:T(8,128)(2,1)S(1)}, bf16[128,512]{1,0:T(8,128)(2,1)}, u32[]{:S(2)}) copy-start(bf16[128,512]{1,0:T(8,128)(2,1)} %up_ref.1) | copy-start | bytes 393220
  2.0 30.5 %copy-start.2 = (bf16[128,1792]{1,0:T(8,128)(2,1)S(1)}, bf16[128,1792]{1,0:T(8,128)(2,1)}, u32[]{:S(2)}) copy-start(bf16[128,1792]{1,0:T(8,128)(2,1)} %features_ref.1) | copy-start | bytes 1376260
  5.0 28.2 %copy-start.19 = (f32[512]{0:T(512)S(1)}, f32[512]{0:T(512)}, u32[]{:S(2)}) copy-start(f32[512]{0:T(512)} %param.11) | copy-start | bytes 6148
  5.0 29.6 %all-to-all-start = ((bf16[8,144,256]{2,1,0:T(8,128)(2,1)}), bf16[8,144,256]{2,1,0:T(8,128)(2,1)S(1)}, u32[]{:S(2)}, u32[]{:S(2)}) async-start(bf16[8,144,256]{2,1,0:T(8,128)(2,1)} %get-tuple-element.31), calls=%async_computation | async-start | bytes 1179648 | tf_op jit(solution)/shard_map/all_to_all | solution.py:407
  15.5 19.1 %collective-permute-start = (bf16[128,256]{1,0:T(8,128)(2,1)S(1)}, bf16[128,256]{1,0:T(8,128)(2,1)S(1)}, u32[]{:S(2)}, u32[]{:S(2)}) collective-permute-start(bf16[128,256]{1,0:T(8,128)(2,1)S(1)} %slice_select_fusion), channel_id=1, source_target_pairs={{0,1},{1,0},{2,3},{3,2},{4,5},{5,4},{6,7},{7,6},{8,9},{9,8},{10,11... | collective-permute-start | bytes 196616 | tf_op jit(solution)/shard_map/ppermute | solution.py:93
  17.6 22.7 %collective-permute-start.3 = (bf16[144,256]{1,0:T(8,128)(2,1)}, bf16[144,256]{1,0:T(8,128)(2,1)S(1)}, u32[]{:S(2)}, u32[]{:S(2)}) collective-permute-start(bf16[144,256]{1,0:T(8,128)(2,1)} %get-tuple-element.37), channel_id=1, source_target_pairs={{248,256},{249,257},{250,258},{251,259},{252,260},{253,261},{254,2... | collective-permute-start | bytes 221192 | tf_op jit(solution)/shard_map/ppermute | solution.py:53
  30.3 15.1 %collective-permute-start.4 = (bf16[144,256]{1,0:T(8,128)(2,1)}, bf16[144,256]{1,0:T(8,128)(2,1)S(1)}, u32[]{:S(2)}, u32[]{:S(2)}) collective-permute-start(bf16[144,256]{1,0:T(8,128)(2,1)} %get-tuple-element.38), channel_id=1, source_target_pairs={{248,257},{249,256},{250,259},{251,258},{252,261},{253,260},{254,2... | collective-permute-start | bytes 221192 | tf_op jit(solution)/shard_map/ppermute | solution.py:54
  34.6 30.7 %copy-start.17 = (bf16[128,256]{1,0:T(8,128)(2,1)}, bf16[128,256]{1,0:T(8,128)(2,1)S(1)}, u32[]{:S(2)}) copy-start(bf16[128,256]{1,0:T(8,128)(2,1)S(1)} %collective-permute-done.up_other_ref) | copy-start | bytes 196612
  34.6 25.6 %copy-start.8 = (bf16[8,144,256]{2,1,0:T(8,128)(2,1)}, bf16[8,144,256]{2,1,0:T(8,128)(2,1)S(1)}, u32[]{:S(2)}) copy-start(bf16[8,144,256]{2,1,0:T(8,128)(2,1)S(1)} %all-to-all-done.own_ref.refs_0_) | copy-start | bytes 1769476
  34.7 33.4 %collective-permute-start.1 = (bf16[8,144,256]{2,1,0:T(8,128)(2,1)S(1)}, bf16[8,144,256]{2,1,0:T(8,128)(2,1)S(1)}, u32[]{:S(2)}, u32[]{:S(2)}) collective-permute-start(bf16[8,144,256]{2,1,0:T(8,128)(2,1)S(1)} %all-to-all-done.own_ref.refs_0_), channel_id=1, source_target_pairs={{0,8},{8,16},{16,24},{24,32},{32,40},{40,48},{48,56},{56,64},{64,7... | collective-permute-start | bytes 1769480 | tf_op jit(solution)/shard_map/ppermute | solution.py:89
  36.0 32.1 %collective-permute-start.2 = (bf16[8,144,256]{2,1,0:T(8,128)(2,1)S(1)}, bf16[8,144,256]{2,1,0:T(8,128)(2,1)S(1)}, u32[]{:S(2)}, u32[]{:S(2)}) collective-permute-start(bf16[8,144,256]{2,1,0:T(8,128)(2,1)S(1)} %all-to-all-done.own_ref.refs_0_), channel_id=1, source_target_pairs={{8,0},{16,8},{24,16},{32,24},{40,32},{48,40},{56,48},{64,56},{72,6... | collective-permute-start | bytes 1769480 | tf_op jit(solution)/shard_map/ppermute | solution.py:89
  45.4 19.9 %copy-start.7 = (bf16[2,144,256]{2,1,0:T(8,128)(2,1)}, bf16[2,144,256]{2,1,0:T(8,128)(2,1)S(1)}, u32[]{:S(2)}) copy-start(bf16[2,144,256]{2,1,0:T(8,128)(2,1)S(1)} %pad_maximum_fusion.1.refs_2_.refs_3_) | copy-start | bytes 442372
  45.4 22.6 %collective-permute-start.5 = (bf16[2,144,256]{2,1,0:T(8,128)(2,1)S(1)}, bf16[2,144,256]{2,1,0:T(8,128)(2,1)S(1)}, u32[]{:S(2)}, u32[]{:S(2)}) collective-permute-start(bf16[2,144,256]{2,1,0:T(8,128)(2,1)S(1)} %pad_maximum_fusion.1.refs_2_.refs_3_), channel_id=1, source_target_pairs={{248,250},{249,251},{250,248},{251,249},{252,254},{253,255},{254,2... | collective-permute-start | bytes 442376 | tf_op jit(solution)/shard_map/ppermute | solution.py:64
  49.5 18.6 %collective-permute-start.6 = (bf16[2,144,256]{2,1,0:T(8,128)(2,1)S(1)}, bf16[2,144,256]{2,1,0:T(8,128)(2,1)S(1)}, u32[]{:S(2)}, u32[]{:S(2)}) collective-permute-start(bf16[2,144,256]{2,1,0:T(8,128)(2,1)S(1)} %pad_maximum_fusion.1.refs_2_.refs_3_), channel_id=1, source_target_pairs={{248,252},{249,253},{250,254},{251,255},{252,248},{253,249},{254,2... | collective-permute-start | bytes 442376 | tf_op jit(solution)/shard_map/ppermute | solution.py:64
  53.8 14.3 %collective-permute-start.7 = (bf16[2,144,256]{2,1,0:T(8,128)(2,1)S(1)}, bf16[2,144,256]{2,1,0:T(8,128)(2,1)S(1)}, u32[]{:S(2)}, u32[]{:S(2)}) collective-permute-start(bf16[2,144,256]{2,1,0:T(8,128)(2,1)S(1)} %pad_maximum_fusion.1.refs_2_.refs_3_), channel_id=1, source_target_pairs={{248,254},{249,255},{250,252},{251,253},{252,250},{253,251},{254,2... | collective-permute-start | bytes 442376 | tf_op jit(solution)/shard_map/ppermute | solution.py:64
  56.0 20.6 %all-to-all-start.2 = ((bf16[4,128,448]{1,2,0:T(8,128)(2,1)}), bf16[4,128,448]{1,2,0:T(8,128)(2,1)S(1)}, u32[]{:S(2)}, u32[]{:S(2)}) async-start(bf16[4,128,448]{1,2,0:T(8,128)(2,1)} %pad_maximum_fusion), calls=%async_computation.2 | async-start | bytes 917504 | tf_op jit(solution)/shard_map/all_to_all | solution.py:417
  68.1 0.7 copy-start.13
  68.1 0.7 copy-start.14
  68.1 0.8 copy-start.15
  68.1 1.0 copy-start.5
  68.1 1.2 copy-start.6
  76.6 23.8 %all-to-all-start.1 = ((bf16[4,2,128,256]{3,2,1,0:T(8,128)(2,1)}), bf16[4,2,128,256]{3,2,1,0:T(8,128)(2,1)}, u32[]{:S(2)}, u32[]{:S(2)}) async-start(bf16[4,2,128,256]{3,2,1,0:T(8,128)(2,1)} %get-tuple-element.42), calls=%async_computation.1 | async-start | bytes 1048576 | tf_op jit(solution)/shard_map/all_to_all | solution.py:427
  80.9 18.1 %collective-permute-start.8 = (bf16[2,128,256]{2,1,0:T(8,128)(2,1)}, bf16[2,128,256]{2,1,0:T(8,128)(2,1)S(1)}, u32[]{:S(2)}, u32[]{:S(2)}) collective-permute-start(bf16[2,128,256]{2,1,0:T(8,128)(2,1)} %get-tuple-element.41), channel_id=1, source_target_pairs={{248,256},{249,257},{250,258},{251,259},{252,260},{253,261},{254,2... | collective-permute-start | bytes 393224 | tf_op jit(solution)/shard_map/ppermute | solution.py:53
  86.5 12.5 %copy-start.3 = (bf16[4,128,448]{2,1,0:T(8,128)(2,1)}, bf16[4,128,448]{2,1,0:T(8,128)(2,1)S(1)}, u32[]{:S(2)}) copy-start(bf16[4,128,448]{2,1,0:T(8,128)(2,1)S(1)} %copy.18.feats_ref) | copy-start | bytes 1376260
  86.5 12.5 %copy-start.20 = (f32[1,256]{1,0:T(1,128)S(1)}, f32[1,256]{1,0:T(1,128)}, u32[]{:S(2)}) copy-start(f32[1,256]{1,0:T(1,128)} %get-tuple-element.45) | copy-start | bytes 3076
  86.5 24.3 %collective-permute-start.9 = (bf16[4,128,448]{2,1,0:T(8,128)(2,1)S(1)}, bf16[4,128,448]{2,1,0:T(8,128)(2,1)S(1)}, u32[]{:S(2)}, u32[]{:S(2)}) collective-permute-start(bf16[4,128,448]{2,1,0:T(8,128)(2,1)S(1)} %copy.18.feats_ref), channel_id=1, source_target_pairs={{0,1},{1,0},{2,3},{3,2},{4,5},{5,4},{6,7},{7,6},{8,9},{9,8},{10,11... | collective-permute-start | bytes 1376264 | tf_op jit(solution)/shard_map/ppermute | solution.py:93
  99.0 19.6 %copy-start.16 = (bf16[2,128,256]{2,1,0:T(8,128)(2,1)}, bf16[2,128,256]{2,1,0:T(8,128)(2,1)S(1)}, u32[]{:S(2)}) copy-start(bf16[2,128,256]{2,1,0:T(8,128)(2,1)S(1)} %collective-permute-done.8.refs_2_) | copy-start | bytes 393220
  100.4 18.2 %collective-permute-start.10 = (bf16[8,128,256]{2,1,0:T(8,128)(2,1)}, bf16[8,128,256]{2,1,0:T(8,128)(2,1)S(1)}, u32[]{:S(2)}, u32[]{:S(2)}) collective-permute-start(bf16[8,128,256]{2,1,0:T(8,128)(2,1)} %bitcast.15.own_ref), channel_id=1, source_target_pairs={{0,8},{8,16},{16,24},{24,32},{32,40},{40,48},{48,56},{56,64},{64,7... | collective-permute-start | bytes 1572872 | tf_op jit(solution)/shard_map/ppermute | solution.py:89
  101.8 16.9 %collective-permute-start.11 = (bf16[8,128,256]{2,1,0:T(8,128)(2,1)}, bf16[8,128,256]{2,1,0:T(8,128)(2,1)S(1)}, u32[]{:S(2)}, u32[]{:S(2)}) collective-permute-start(bf16[8,128,256]{2,1,0:T(8,128)(2,1)} %bitcast.15.own_ref), channel_id=1, source_target_pairs={{8,0},{16,8},{24,16},{32,24},{40,32},{48,40},{56,48},{64,56},{72,6... | collective-permute-start | bytes 1572872 | tf_op jit(solution)/shard_map/ppermute | solution.py:89
  103.7 14.9 %collective-permute-start.12 = (bf16[2,128,256]{2,1,0:T(8,128)(2,1)S(1)}, bf16[2,128,256]{2,1,0:T(8,128)(2,1)}, u32[]{:S(2)}, u32[]{:S(2)}) collective-permute-start(bf16[2,128,256]{2,1,0:T(8,128)(2,1)S(1)} %collective-permute-done.8.refs_2_), channel_id=1, source_target_pairs={{248,250},{249,251},{250,248},{251,249},{252,254},{253,255},{254,2... | collective-permute-start | bytes 393224 | tf_op jit(solution)/shard_map/ppermute | solution.py:64
  105.9 12.8 %collective-permute-start.13 = (bf16[2,128,256]{2,1,0:T(8,128)(2,1)S(1)}, bf16[2,128,256]{2,1,0:T(8,128)(2,1)}, u32[]{:S(2)}, u32[]{:S(2)}) collective-permute-start(bf16[2,128,256]{2,1,0:T(8,128)(2,1)S(1)} %collective-permute-done.8.refs_2_), channel_id=1, source_target_pairs={{248,252},{249,253},{250,254},{251,255},{252,248},{253,249},{254,2... | collective-permute-start | bytes 393224 | tf_op jit(solution)/shard_map/ppermute | solution.py:64
  110.8 7.8 %copy-start.9 = (bf16[4,128,448]{2,1,0:T(8,128)(2,1)}, bf16[4,128,448]{2,1,0:T(8,128)(2,1)S(1)}, u32[]{:S(2)}) copy-start(bf16[4,128,448]{2,1,0:T(8,128)(2,1)S(1)} %collective-permute-done.9.feats_other_ref) | copy-start | bytes 1376260
  110.8 7.9 %collective-permute-start.14 = (bf16[2,128,256]{2,1,0:T(8,128)(2,1)S(1)}, bf16[2,128,256]{2,1,0:T(8,128)(2,1)}, u32[]{:S(2)}, u32[]{:S(2)}) collective-permute-start(bf16[2,128,256]{2,1,0:T(8,128)(2,1)S(1)} %collective-permute-done.8.refs_2_), channel_id=1, source_target_pairs={{248,254},{249,255},{250,252},{251,253},{252,250},{253,251},{254,2... | collective-permute-start | bytes 393224 | tf_op jit(solution)/shard_map/ppermute | solution.py:64
  118.6 27.3 %copy-start = (bf16[1792,512]{1,0:T(8,128)(2,1)S(1)}, bf16[1792,512]{1,0:T(8,128)(2,1)}, u32[]{:S(2)}) copy-start(bf16[1792,512]{1,0:T(8,128)(2,1)} %weight_ref.1) | copy-start | bytes 5505028
  118.6 18.2 %copy-start.21 = (bf16[128,256]{1,0:T(8,128)(2,1)S(1)}, bf16[128,256]{1,0:T(8,128)(2,1)}, u32[]{:S(2)}) copy-start(bf16[128,256]{1,0:T(8,128)(2,1)} %get-tuple-element.52) | copy-start | bytes 196612
  118.6 25.8 %copy-start.18 = (bf16[128,256]{1,0:T(8,128)(2,1)S(1)}, bf16[128,256]{1,0:T(8,128)(2,1)}, u32[]{:S(2)}) copy-start(bf16[128,256]{1,0:T(8,128)(2,1)} %get-tuple-element.51) | copy-start | bytes 196612
  118.7 0.8 copy-start.10
  119.5 0.8 copy-start.11
  126.9 24.0 %all-to-all-start.3 = ((bf16[64,16,128]{2,1,0:T(8,128)(2,1)}), bf16[64,16,128]{2,1,0:T(8,128)(2,1)S(1)}, u32[]{:S(2)}, u32[]{:S(2)}) async-start(bf16[64,16,128]{2,1,0:T(8,128)(2,1)} %get-tuple-element.48), calls=%async_computation.3 | async-start | bytes 524288 | tf_op jit(solution)/shard_map/all_to_all | solution.py:452
  136.8 7.6 %collective-permute-start.16 = (bf16[128,256]{1,0:T(8,128)(2,1)S(1)}, bf16[128,256]{1,0:T(8,128)(2,1)S(1)}, u32[]{:S(2)}, u32[]{:S(2)}) collective-permute-start(bf16[128,256]{1,0:T(8,128)(2,1)S(1)} %copy-done.21), channel_id=1, source_target_pairs={{0,1},{1,0},{2,3},{3,2},{4,5},{5,4},{6,7},{7,6},{8,9},{9,8},{10,11... | collective-permute-start | bytes 196616 | tf_op jit(solution)/shard_map/ppermute | solution.py:93
  142.5 3.4 %collective-permute-start.15 = (bf16[128,256]{1,0:T(8,128)(2,1)}, bf16[128,256]{1,0:T(8,128)(2,1)S(1)}, u32[]{:S(2)}, u32[]{:S(2)}) collective-permute-start(bf16[128,256]{1,0:T(8,128)(2,1)} %get-tuple-element.50), channel_id=1, source_target_pairs={{0,1},{1,0},{2,3},{3,2},{4,5},{5,4},{6,7},{7,6},{8,9},{9,8},{10,11... | collective-permute-start | bytes 196616 | tf_op jit(solution)/shard_map/ppermute | solution.py:93
  191.3 8.1 %copy-start.1 = (bf16[4,64,16,128]{3,2,1,0:T(8,128)(2,1)}, bf16[4,64,16,128]{3,2,1,0:T(8,128)(2,1)S(1)}, u32[]{:S(2)}) copy-start(bf16[4,64,16,128]{3,2,1,0:T(8,128)(2,1)S(1)} %all_to_all.31.mine_ref) | copy-start | bytes 3145732
  191.3 8.1 %collective-permute-start.17 = (bf16[4,64,16,128]{3,2,1,0:T(8,128)(2,1)S(1)}, bf16[4,64,16,128]{3,2,1,0:T(8,128)(2,1)S(1)}, u32[]{:S(2)}, u32[]{:S(2)}) collective-permute-start(bf16[4,64,16,128]{3,2,1,0:T(8,128)(2,1)S(1)} %all_to_all.31.mine_ref), channel_id=1, source_target_pairs={{0,1},{1,0},{2,3},{3,2},{4,5},{5,4},{6,7},{7,6},{8,9},{9,8},{10,11... | collective-permute-start | bytes 3145736 | tf_op jit(solution)/shard_map/ppermute | solution.py:93
  199.4 1.0 copy-start.4

commit v6 on v5

--- a/solution.py
+++ b/solution.py
@@ -353,39 +353,52 @@
     )(ids, counts, total, bias_rows, feats, feats_other, *pieces)
 
 
-def assemble_kernel(ids_ref, mine_ref, other_ref, weight_ref, bias_ref):
+def assemble_kernel(ids_ref, *refs):
+    mine, other, (weight_ref, bias_ref) = refs[:4], refs[4:8], refs[8:]
     first = ids_ref[2] == 0
-    bias = [jnp.zeros((2, 128), f32), jnp.zeros((2, 128), f32)]
-    for x in range(4):
-        for column in range(64):
-            yh, run, z = column // 32, (column // 8) % 4, column % 8
-            slab = (yh * 4 + x) * 8 + z
-            if slab > BIAS_SLAB:
-                continue
-            mine, other = mine_ref[x, column], other_ref[x, column]
-            for core in range(2):
-                keep = first if core == 0 else jnp.logical_not(first)
-                value = jnp.where(keep, mine, other)
-                if slab == BIAS_SLAB:
-                    rows = value.astype(f32)
-                    bias[core] = bias[core] + (rows[:2] + rows[2:4])
-                else:
-                    row, lane = run * F_RUN + (slab // 2) * 16, core * HALF + (slab % 2) * 128
-                    weight_ref[row : row + 16, lane : lane + 128] = value
-    bias_ref[:2, :] = bias[0]
-    bias_ref[2:, :] = bias[1]
+    for k in range(4):
+        x = jnp.bitwise_xor(ids_ref[5], k)
+        for yh in range(2):
+
+            def place(k=k, yh=yh):
+                for run in range(RUN):
+                    for z in range(8):
+                        column = (yh * RUN + run) * 8 + z
+                        row = run * F_RUN + yh * 256 + (z // 2) * 16
+                        here = pl.ds(pl.multiple_of(row + x * 64, 16), 16)
+                        for core in range(2):
+                            keep = first if core == 0 else jnp.logical_not(first)
+                            value = jnp.where(keep, mine[k][column], other[k][column])
+                            lane = core * HALF + (z % 2) * 128
+                            weight_ref[here, lane : lane + 128] = value
+
+            def total(k=k, yh=yh):
+                for core in range(2):
+                    keep = first if core == 0 else jnp.logical_not(first)
+                    bias = jnp.zeros((2, 128), f32)
+                    for run in range(RUN):
+                        column = (yh * RUN + run) * 8
+                        rows = jnp.where(keep, mine[k][column], other[k][column]).astype(f32)
+                        bias = bias + (rows[:2] + rows[2:4])
+                    bias_ref[core * 2 : core * 2 + 2, :] = bias
+
+            if yh == 0:
+                place()
+            else:
+                pl.when(x != 3)(place)
+                pl.when(x == 3)(total)
 
 
 def assemble(ids, mine, other):
     return pl.pallas_call(
         assemble_kernel,
-        in_specs=[SMEM_SPEC] + [VMEM_SPEC] * 2,
+        in_specs=[SMEM_SPEC] + [VMEM_SPEC] * 8,
         out_shape=(
             jax.ShapeDtypeStruct((RUN * F_RUN, HID), bf16),
             jax.ShapeDtypeStruct((4, 128), f32),
         ),
         name="assemble",
-    )(ids, mine, other)
+    )(ids, *mine, *other)
 
 
 def high_low(value):
@@ -398,29 +411,29 @@
     core = lax.axis_index("c")
     first = core == 0
     far_low, far_high = group % 32 == 0, group % 32 == 31
-    ids = jnp.stack([group, lax.axis_index("yl"), core, far_low, far_high]).astype(i32)
+    ids = jnp.stack([group, lax.axis_index("yl"), core, far_low, far_high, lax.axis_index("x")]).astype(i32)
 
     copies, same, cross = project(
         ids, tile_count, tile_cols, nbr_slot.T, nbr_col.T, nbr_keep.T, features, weight
     )
     straight, turned = across(same, cross)
     own = lax.all_to_all(copies, ("yl", "c"), 0, 0)
+    slices = jnp.stack([features[:, k * F_RUN : (k + 1) * F_RUN] for k in range(RUN)])
     tied, _ = lax.optimization_barrier((upstream, copies))
     up_other = swap_core(jnp.where(first, tied[:, HALF:], tied[:, :HALF]))
-    slices = jnp.stack([features[:, k * F_RUN : (k + 1) * F_RUN] for k in range(RUN)])
     own, up_other, slices = lax.optimization_barrier((own, up_other, slices))
-    straight, turned, _ = lax.optimization_barrier((straight, turned, own))
+    low, high = neighbours(own)
+    counts, degree = forward_counts(ids, own)
+    own_total = forward_own(ids, counts, own)
+    straight, turned, own_total = lax.optimization_barrier((straight, turned, own_total))
     received = jnp.stack([jnp.where(first, straight, turned), jnp.where(first, turned, straight)])
-    low, high = neighbours(own)
     parts = along_run(received)
-    counts, degree = forward_counts(ids, own)
     feats = lax.all_to_all(slices, "yl", 0, 0)
     feats_other = swap_core(feats)
     pieces = (own, low, high) + parts
     bias_half = jnp.where(first, bias[:HALF], bias[HALF:])[None]
     hidden_mine, hidden_send, scaled_copies, scaled, bias_part = forward_math(
-        ids, counts, forward_own(ids, counts, own), degree, bias_half, upstream, up_other,
-        pieces[1:],
+        ids, counts, own_total, degree, bias_half, upstream, up_other, pieces[1:]
     )
 
     received = across(scaled, None)
@@ -456,8 +469,11 @@
         group == BIAS_SLAB, high_low(reduced[:2] + reduced[2:4]), reduced.astype(bf16)
     )
     column = spread_to(piece, ("yh", "yl", "z"), 64)
-    plane = spread_to(column, "x", 4)
-    weight_grad, bias_grad = assemble(ids, plane, swap_core(plane))
+    columns = [column]
+    for step in (2, 1, 3):
+        columns.append(lax.ppermute(column, "x", [(i, i ^ step) for i in range(4)]))
+    columns = [columns[0], columns[2], columns[1], columns[3]]
+    weight_grad, bias_grad = assemble(ids, columns, [swap_core(block) for block in columns])
     return hidden, grad_features, weight_grad, bias_grad.reshape(HID)
 
 

time: 205 us -> 212 us (1.034)
  starting transfers between devices: 94.3 us -> 119 us
  blocking collectives: 40 us -> 23.2 us
    all_to_all x2 -> x1, blocking collectives: 40 us -> 23.2 us  [spread_to(): lax.all_to_all(jnp.broadcast_to(shard[None], (count,) + shard.shape), axe...]
    ppermute x6, waiting for transfers between devices: 0.02 us -> 12.5 us  [along_run(): parts.append(lax.ppermute(block, AXES, pairs))]
    ppermute x0 -> x3, starting transfers between devices: none -> 10.2 us  [on_device(): columns.append(lax.ppermute(column, 'x', [(i, i ^ step) for i in range(4)]))]
    ppermute x2, starting transfers between devices: 18.1 us -> 27.9 us  [across(): got = lax.ppermute(same, AXES, straight)]
    ppermute x5 -> x8, starting transfers between devices: 19.2 us -> 27.9 us  [swap_core(): return lax.ppermute(block, 'c', [(0, 1), (1, 0)])]
    ppermute x1, waiting for transfers between devices: 5.14 us -> 0.01 us  [across(): return got if cross is None else (got, lax.ppermute(cross, AXES, turned))]
    all_to_all x1, waiting for transfers between devices: 3.55 us -> 0.01 us  [on_device(): feats = lax.all_to_all(slices, 'yl', 0, 0)]
    all_to_all x1, starting transfers between devices: 9.91 us -> 6.38 us  [on_device(): terms = lax.all_to_all(slabs, WIDE, 0, 0)]
  transfers between devices with their start and end apart: 22 -> 28, of which waited for: 7 -> 6; matrix products, arithmetic and copies ran while one was open for 3% -> 3% of each run, Pallas kernels for 12% -> 12%
where the time goes in v6:
time: 212 us; the launch traced here: 211 us
  starting transfers between devices  119 us (56%)
  Pallas kernels  37.6 us (18%)
  blocking collectives  23.2 us (11%)
  waiting for transfers between devices  17.7 us (8%)
  local copies, waits for them, and re-layouts  6.06 us (3%)
  other arithmetic  2.96 us (1%)
  matrix products  2.4 us (1%)
    ppermute x8, starting transfers between devices, swap_core(): return lax.ppermute(block, 'c', [(0, 1), (1, 0)])  27.9 us
    ppermute x2, starting transfers between devices, across(): got = lax.ppermute(same, AXES, straight)  27.9 us
    all_to_all x1, blocking collectives, spread_to(): lax.all_to_all(jnp.broadcast_to(shard[None], (count,) + shard.shape), axe...  23.2 us
    ppermute x6, starting transfers between devices, along_run(): parts.append(lax.ppermute(block, AXES, pairs))  19.9 us
    ppermute x6, waiting for transfers between devices, along_run(): parts.append(lax.ppermute(block, AXES, pairs))  12.5 us
    all_to_all x1, starting transfers between devices, on_device(): own = lax.all_to_all(copies, ('yl', 'c'), 0, 0)  10.3 us
    ppermute x3, starting transfers between devices, on_device(): columns.append(lax.ppermute(column, 'x', [(i, i ^ step) for i in range(4)]))  10.2 us
    pallas_call x1, Pallas kernels, backward_counts(): pl.pallas_call(backward_counts_kernel, in_specs=[SMEM_SPEC] + [VMEM_SPEC]...  8.68 us
  transfers between devices with their start and end apart: 28, of which 6 were waited for; matrix products, arithmetic and copies ran while one was open for 3% of the time, Pallas kernels for 12%

profile of v6, /device:TPU:1, one launch (start us, length us, event | category | flops | bytes accessed | tf_op | source)
XLA Modules:
  0.0 211.0 jit_solution(7853589229533932728)
XLA Ops:
  1.3 0.6 stack.59.ids_ref
  2.0 3.0 %project.1 = (bf16[8,144,256]{2,1,0:T(8,128)(2,1)}, bf16[144,256]{1,0:T(8,128)(2,1)}, bf16[144,256]{1,0:T(8,128)(2,1)}) custom-call(s32[6]{0:T(128)} %stack.59.ids_ref, s32[1]{0:T(128)S(6)} %copy.23.count_ref, s32[1,24]{1,0:T(1,128)} %tiles_ref.1, s32[15,128]{1,0:T(8,128)} %bitcast.26, s32[15,128]{1,0:T(8,128)} %bitcast.27, s32[15,128]{1,0:T(8,128)} %bitcast.28, ...), custom_call_target="tpu_custom_call" | custom-call | tf_op jit(solution)/shard_map/project/pallas_call | solution.py:129
  5.0 10.3 %all-to-all-start = ((bf16[8,144,256]{2,1,0:T(8,128)(2,1)}), bf16[8,144,256]{2,1,0:T(8,128)(2,1)S(1)}, u32[]{:S(2)}, u32[]{:S(2)}) async-start(bf16[8,144,256]{2,1,0:T(8,128)(2,1)} %get-tuple-element.32), calls=%async_computation | async-start | bytes 1179648 | tf_op jit(solution)/shard_map/all_to_all | solution.py:420
  15.3 2.0 collective-permute-start
  17.4 12.7 %collective-permute-start.1 = (bf16[144,256]{1,0:T(8,128)(2,1)}, bf16[144,256]{1,0:T(8,128)(2,1)S(1)}, u32[]{:S(2)}, u32[]{:S(2)}) collective-permute-start(bf16[144,256]{1,0:T(8,128)(2,1)} %get-tuple-element.36), channel_id=1, source_target_pairs={{248,256},{249,257},{250,258},{251,259},{252,260},{253,261},{254,2... | collective-permute-start | bytes 221192 | tf_op jit(solution)/shard_map/ppermute | solution.py:53
  30.1 2.2 %collective-permute-start.2 = (bf16[144,256]{1,0:T(8,128)(2,1)}, bf16[144,256]{1,0:T(8,128)(2,1)S(1)}, u32[]{:S(2)}, u32[]{:S(2)}) collective-permute-start(bf16[144,256]{1,0:T(8,128)(2,1)} %get-tuple-element.37), channel_id=1, source_target_pairs={{248,257},{249,256},{250,259},{251,258},{252,261},{253,260},{254,2... | collective-permute-start | bytes 221192 | tf_op jit(solution)/shard_map/ppermute | solution.py:54
  32.3 0.1 fusion.9
  32.5 0.1 copy.22
  32.6 0.1 copy.21
  32.8 0.1 copy.20
  32.9 0.1 copy.19
  33.0 0.8 pad_maximum_fusion
  33.9 0.8 copy-done.7
  34.7 5.1 %forward_counts.1 = (bf16[256,3072]{1,0:T(8,128)(2,1)}, f32[256,1]{1,0:T(8,128)}) custom-call(s32[6]{0:T(128)} %stack.59.ids_ref, bf16[8,144,256]{2,1,0:T(8,128)(2,1)} %copy-done.7), custom_call_target="tpu_custom_call" | custom-call | flops 4000000000 | bytes 8000000 | tf_op jit(solution)/shard_map/forward_counts/pallas_call | solution.py:175
  39.8 1.3 collective-permute-start.3
  41.1 1.3 collective-permute-start.4
  42.4 4.5 %all-to-all-start.2 = ((bf16[4,128,448]{1,2,0:T(8,128)(2,1)}), bf16[4,128,448]{1,2,0:T(8,128)(2,1)S(1)}, u32[]{:S(2)}, u32[]{:S(2)}) async-start(bf16[4,128,448]{1,2,0:T(8,128)(2,1)} %pad_maximum_fusion), calls=%async_computation.2 | async-start | bytes 917504 | tf_op jit(solution)/shard_map/all_to_all | solution.py:431
  46.9 2.7 %forward_own.1.total_ref = f32[256,256]{1,0:T(8,128)} custom-call(s32[6]{0:T(128)} %stack.59.ids_ref, bf16[256,3072]{1,0:T(8,128)(2,1)} %get-tuple-element.35.counts_ref, bf16[8,144,256]{2,1,0:T(8,128)(2,1)} %copy-done.7), custom_call_target="tpu_custom_call" | custom-call | flops 4000000000 | bytes 8000000 | tf_op jit(solution)/shard_map/forward_own/pallas_call | solution.py:232
  49.7 3.4 %collective-permute-start.5 = (bf16[2,144,256]{2,1,0:T(8,128)(2,1)S(1)}, bf16[2,144,256]{2,1,0:T(8,128)(2,1)S(1)}, u32[]{:S(2)}, u32[]{:S(2)}) collective-permute-start(bf16[2,144,256]{2,1,0:T(8,128)(2,1)S(1)} %pad_maximum_fusion.1.refs_2_.refs_3_), channel_id=1, source_target_pairs={{248,250},{249,251},{250,248},{251,249},{252,254},{253,255},{254,2... | collective-permute-start | bytes 442376 | tf_op jit(solution)/shard_map/ppermute | solution.py:64
  53.1 4.0 %collective-permute-start.6 = (bf16[2,144,256]{2,1,0:T(8,128)(2,1)S(1)}, bf16[2,144,256]{2,1,0:T(8,128)(2,1)S(1)}, u32[]{:S(2)}, u32[]{:S(2)}) collective-permute-start(bf16[2,144,256]{2,1,0:T(8,128)(2,1)S(1)} %pad_maximum_fusion.1.refs_2_.refs_3_), channel_id=1, source_target_pairs={{248,252},{249,253},{250,254},{251,255},{252,248},{253,249},{254,2... | collective-permute-start | bytes 442376 | tf_op jit(solution)/shard_map/ppermute | solution.py:64
  57.1 1.9 collective-permute-start.7
  59.0 0.6 slice_select_fusion.1
  59.6 9.4 %collective-permute-done.6.refs_4_.refs_5_ = bf16[2,144,256]{2,1,0:T(8,128)(2,1)S(1)} collective-permute-done((bf16[2,144,256]{2,1,0:T(8,128)(2,1)S(1)}, bf16[2,144,256]{2,1,0:T(8,128)(2,1)S(1)}, u32[]{:S(2)}, u32[]{:S(2)}) %collective-permute-start.6) | collective-permute-done | bytes 147488 | tf_op jit(solution)/shard_map/ppermute | solution.py:64
  69.1 0.6 copy-done.20
  69.8 0.2 copy-done.4
  70.0 0.2 copy-done.5
  70.2 3.7 %forward_math.1 = (bf16[128,256]{1,0:T(8,128)(2,1)}, bf16[128,256]{1,0:T(8,128)(2,1)}, bf16[4,2,128,256]{3,2,1,0:T(8,128)(2,1)}, bf16[2,128,256]{2,1,0:T(8,128)(2,1)}, f32[1,256]{1,0:T(1,128)}) custom-call(s32[6]{0:T(128)} %stack.59.ids_ref, bf16[256,3072]{1,0:T(8,128)(2,1)} %get-tuple-element.35.counts_ref, f32[256,256]{1,0:T(8,128)} %forward_own.1.total_ref, ...), custom_call_target="tpu_custom_call" | custom-call | tf_op jit(solution)/shard_map/forward_math/pallas_call | solution.py:294
  74.0 4.7 %all-to-all-start.1 = ((bf16[4,2,128,256]{3,2,1,0:T(8,128)(2,1)}), bf16[4,2,128,256]{3,2,1,0:T(8,128)(2,1)}, u32[]{:S(2)}, u32[]{:S(2)}) async-start(bf16[4,2,128,256]{3,2,1,0:T(8,128)(2,1)} %get-tuple-element.44), calls=%async_computation.1 | async-start | bytes 1048576 | tf_op jit(solution)/shard_map/all_to_all | solution.py:440
  78.7 0.1 pad.13.clone
  78.8 15.1 %collective-permute-start.8 = (bf16[2,128,256]{2,1,0:T(8,128)(2,1)}, bf16[2,128,256]{2,1,0:T(8,128)(2,1)S(1)}, u32[]{:S(2)}, u32[]{:S(2)}) collective-permute-start(bf16[2,128,256]{2,1,0:T(8,128)(2,1)} %get-tuple-element.43), channel_id=1, source_target_pairs={{248,256},{249,257},{250,258},{251,259},{252,260},{253,261},{254,2... | collective-permute-start | bytes 393224 | tf_op jit(solution)/shard_map/ppermute | solution.py:53
  93.9 0.2 copy.18.feats_ref
  94.2 3.6 %collective-permute-start.9 = (bf16[4,128,448]{2,1,0:T(8,128)(2,1)S(1)}, bf16[4,128,448]{2,1,0:T(8,128)(2,1)S(1)}, u32[]{:S(2)}, u32[]{:S(2)}) collective-permute-start(bf16[4,128,448]{2,1,0:T(8,128)(2,1)S(1)} %copy.18.feats_ref), channel_id=1, source_target_pairs={{0,1},{1,0},{2,3},{3,2},{4,5},{5,4},{6,7},{7,6},{8,9},{9,8},{10,11... | collective-permute-start | bytes 1376264 | tf_op jit(solution)/shard_map/ppermute | solution.py:93
  97.7 8.7 %backward_counts.1.counts_ref = bf16[1024,3072]{1,0:T(8,128)(2,1)} custom-call(s32[6]{0:T(128)} %stack.59.ids_ref, bf16[8,144,256]{2,1,0:T(8,128)(2,1)} %copy-done.7, bf16[8,144,256]{2,1,0:T(8,128)(2,1)} %copy-done.4, bf16[8,144,256]{2,1,0:T(8,128)(2,1)} %copy-done.5, bf16[2,144,256]{2,1,0:T(8,128)(2,1)} %copy-done.6, bf16[2,144,256]{2,1,0:T(8,128)(2,1)} %copy-done.19, ...), custom_call_target="tpu_custom_call" | custom-call | flops 4000000000 | bytes 8000000 | tf_op jit(solution)/shard_map/backward_counts/pallas_call | solution.py:207
  106.5 1.3 collective-permute-start.10
  107.8 1.3 collective-permute-start.11
  109.1 0.7 maximum_maximum_fusion.bias_ref
  109.8 4.5 %collective-permute-start.12 = (bf16[2,128,256]{2,1,0:T(8,128)(2,1)S(1)}, bf16[2,128,256]{2,1,0:T(8,128)(2,1)}, u32[]{:S(2)}, u32[]{:S(2)}) collective-permute-start(bf16[2,128,256]{2,1,0:T(8,128)(2,1)S(1)} %collective-permute-done.8.refs_2_), channel_id=1, source_target_pairs={{248,250},{249,251},{250,248},{251,249},{252,254},{253,255},{254,2... | collective-permute-start | bytes 393224 | tf_op jit(solution)/shard_map/ppermute | solution.py:64
  114.3 3.1 %collective-permute-start.13 = (bf16[2,128,256]{2,1,0:T(8,128)(2,1)S(1)}, bf16[2,128,256]{2,1,0:T(8,128)(2,1)}, u32[]{:S(2)}, u32[]{:S(2)}) collective-permute-start(bf16[2,128,256]{2,1,0:T(8,128)(2,1)S(1)} %collective-permute-done.8.refs_2_), channel_id=1, source_target_pairs={{248,252},{249,253},{250,254},{251,255},{252,248},{253,249},{254,2... | collective-permute-start | bytes 393224 | tf_op jit(solution)/shard_map/ppermute | solution.py:64
  117.4 3.0 %collective-permute-start.14 = (bf16[2,128,256]{2,1,0:T(8,128)(2,1)S(1)}, bf16[2,128,256]{2,1,0:T(8,128)(2,1)}, u32[]{:S(2)}, u32[]{:S(2)}) collective-permute-start(bf16[2,128,256]{2,1,0:T(8,128)(2,1)S(1)} %collective-permute-done.8.refs_2_), channel_id=1, source_target_pairs={{248,254},{249,255},{250,252},{251,253},{252,250},{253,251},{254,2... | collective-permute-start | bytes 393224 | tf_op jit(solution)/shard_map/ppermute | solution.py:64
  120.4 4.5 %backward_own.1.total_ref = f32[1024,256]{1,0:T(8,128)} custom-call(bf16[1024,3072]{1,0:T(8,128)(2,1)} %backward_counts.1.counts_ref, bf16[8,128,256]{2,1,0:T(8,128)(2,1)} %bitcast.16.own_ref), custom_call_target="tpu_custom_call" | custom-call | flops 4000000000 | bytes 8000000 | tf_op jit(solution)/shard_map/backward_own/pallas_call | solution.py:250
  125.0 3.0 %collective-permute-done.13.refs_4_ = bf16[2,128,256]{2,1,0:T(8,128)(2,1)} collective-permute-done((bf16[2,128,256]{2,1,0:T(8,128)(2,1)S(1)}, bf16[2,128,256]{2,1,0:T(8,128)(2,1)}, u32[]{:S(2)}, u32[]{:S(2)}) %collective-permute-start.13) | collective-permute-done | bytes 131104 | tf_op jit(solution)/shard_map/ppermute | solution.py:64
  128.0 0.8 copy-done.9
  128.8 0.8 copy-done.10
  129.7 6.7 %backward_math.1 = (bf16[128,256]{1,0:T(8,128)(2,1)}, bf16[128,256]{1,0:T(8,128)(2,1)}, bf16[64,16,128]{2,1,0:T(8,128)(2,1)}) custom-call(s32[6]{0:T(128)} %stack.59.ids_ref, bf16[1024,3072]{1,0:T(8,128)(2,1)} %backward_counts.1.counts_ref, f32[1024,256]{1,0:T(8,128)} %backward_own.1.total_ref, bf16[16,128]{1,0:T(8,128)(2,1)} %maximum_maximum_fusion.bias_ref, ...), custom_call_target="tpu_custom_call" | custom-call | tf_op jit(solution)/shard_map/backward_math/pallas_call | solution.py:343
  136.3 6.4 %all-to-all-start.3 = ((bf16[64,16,128]{2,1,0:T(8,128)(2,1)}), bf16[64,16,128]{2,1,0:T(8,128)(2,1)S(1)}, u32[]{:S(2)}, u32[]{:S(2)}) async-start(bf16[64,16,128]{2,1,0:T(8,128)(2,1)} %get-tuple-element.50), calls=%async_computation.3 | async-start | bytes 524288 | tf_op jit(solution)/shard_map/all_to_all | solution.py:465
  142.7 5.9 %collective-permute-start.16 = (bf16[128,256]{1,0:T(8,128)(2,1)S(1)}, bf16[128,256]{1,0:T(8,128)(2,1)S(1)}, u32[]{:S(2)}, u32[]{:S(2)}) collective-permute-start(bf16[128,256]{1,0:T(8,128)(2,1)S(1)} %copy-done.27), channel_id=1, source_target_pairs={{0,1},{1,0},{2,3},{3,2},{4,5},{5,4},{6,7},{7,6},{8,9},{9,8},{10,11... | collective-permute-start | bytes 196616 | tf_op jit(solution)/shard_map/ppermute | solution.py:93
  148.7 1.9 collective-permute-start.15
  150.6 0.7 maximum_select_fusion.2
  151.3 0.7 collective-permute-done.15
  152.0 2.4 %convolution_convert_fusion = bf16[128,1792]{1,0:T(8,128)(2,1)} fusion(bf16[1792,512]{1,0:T(8,128)(2,1)S(1)} %copy-done, bf16[128,256]{1,0:T(8,128)(2,1)S(1)} %collective-permute-done.15, bf16[128,256]{1,0:T(8,128)(2,1)} %get-tuple-element.51, pred[]{:T(512)S(6)} %eq.17), kind=kOutput, calls=%fused_computation | convolution fusion | flops 235700224 | bytes 2424833 | tf_op jit(solution)/shard_map/dot_general | solution.py:457
  154.4 2.4 %all-to-all-done.3 = bf16[64,16,128]{2,1,0:T(8,128)(2,1)S(1)} async-done(((bf16[64,16,128]{2,1,0:T(8,128)(2,1)}), bf16[64,16,128]{2,1,0:T(8,128)(2,1)S(1)}, u32[]{:S(2)}, u32[]{:S(2)}) %all-to-all-start.3) | async-done | bytes 262176 | tf_op jit(solution)/shard_map/all_to_all | solution.py:465
  156.9 0.1 maximum_select_fusion.3
  157.0 23.2 %all_to_all.25.refs_0_ = bf16[64,16,128]{2,1,0:T(8,128)(2,1)S(1)} all-to-all(bf16[64,16,128]{2,1,0:T(8,128)(2,1)S(1)} %broadcast_in_dim.10), channel_id=1, replica_groups=mesh['yh'=2,'x'=4,'z'=8,'yl'=4,'c'=2] {'yh','yl','z'}, dimensions={0} | all-to-all | bytes 524288 | tf_op jit(solution)/shard_map/all_to_all | solution.py:39
  180.2 3.9 %collective-permute-start.17 = (bf16[64,16,128]{2,1,0:T(8,128)(2,1)S(1)}, bf16[64,16,128]{2,1,0:T(8,128)(2,1)S(1)}, u32[]{:S(2)}, u32[]{:S(2)}) collective-permute-start(bf16[64,16,128]{2,1,0:T(8,128)(2,1)S(1)} %all_to_all.25.refs_0_), channel_id=1, source_target_pairs={{0,64},{64,0},{128,192},{192,128},{1,65},{65,1},{129,193},{193,129... | collective-permute-start | bytes 786440 | tf_op jit(solution)/shard_map/ppermute | solution.py:474
  184.1 4.4 %collective-permute-start.18 = (bf16[64,16,128]{2,1,0:T(8,128)(2,1)S(1)}, bf16[64,16,128]{2,1,0:T(8,128)(2,1)S(1)}, u32[]{:S(2)}, u32[]{:S(2)}) collective-permute-start(bf16[64,16,128]{2,1,0:T(8,128)(2,1)S(1)} %all_to_all.25.refs_0_), channel_id=1, source_target_pairs={{0,128},{64,192},{128,0},{192,64},{1,129},{65,193},{129,1},{193,65... | collective-permute-start | bytes 786440 | tf_op jit(solution)/shard_map/ppermute | solution.py:474
  188.5 1.9 collective-permute-start.19
  190.5 5.5 %collective-permute-start.20 = (bf16[64,16,128]{2,1,0:T(8,128)(2,1)S(1)}, bf16[64,16,128]{2,1,0:T(8,128)(2,1)S(1)}, u32[]{:S(2)}, u32[]{:S(2)}) collective-permute-start(bf16[64,16,128]{2,1,0:T(8,128)(2,1)S(1)} %all_to_all.25.refs_0_), channel_id=1, source_target_pairs={{0,1},{1,0},{2,3},{3,2},{4,5},{5,4},{6,7},{7,6},{8,9},{9,8},{10,11... | collective-permute-start | bytes 786440 | tf_op jit(solution)/shard_map/ppermute | solution.py:93
  195.9 1.9 collective-permute-start.21
  197.9 3.6 %collective-permute-start.22 = (bf16[64,16,128]{2,1,0:T(8,128)(2,1)S(1)}, bf16[64,16,128]{2,1,0:T(8,128)(2,1)S(1)}, u32[]{:S(2)}, u32[]{:S(2)}) collective-permute-start(bf16[64,16,128]{2,1,0:T(8,128)(2,1)S(1)} %collective-permute-done.18.refs_2_), channel_id=1, source_target_pairs={{0,1},{1,0},{2,3},{3,2},{4,5},{5,4},{6,7},{7,6},{8,9},{9,8},{10,11... | collective-permute-start | bytes 786440 | tf_op jit(solution)/shard_map/ppermute | solution.py:93
  201.5 1.0 collective-permute-done.19.refs_3_
  202.5 3.5 %collective-permute-start.23 = (bf16[64,16,128]{2,1,0:T(8,128)(2,1)S(1)}, bf16[64,16,128]{2,1,0:T(8,128)(2,1)S(1)}, u32[]{:S(2)}, u32[]{:S(2)}) collective-permute-start(bf16[64,16,128]{2,1,0:T(8,128)(2,1)S(1)} %collective-permute-done.19.refs_3_), channel_id=1, source_target_pairs={{0,1},{1,0},{2,3},{3,2},{4,5},{5,4},{6,7},{7,6},{8,9},{9,8},{10,11... | collective-permute-start | bytes 786440 | tf_op jit(solution)/shard_map/ppermute | solution.py:93
  206.0 1.1 collective-permute-done.23.refs_7_
  207.1 0.7 copy-done.18
  207.9 3.1 %assemble.1 = (bf16[1792,512]{1,0:T(8,128)(2,1)}, f32[4,128]{1,0:T(4,128)}) custom-call(s32[6]{0:T(128)} %stack.59.ids_ref, bf16[64,16,128]{2,1,0:T(8,128)(2,1)} %copy-done.3, bf16[64,16,128]{2,1,0:T(8,128)(2,1)} %copy-done.12, bf16[64,16,128]{2,1,0:T(8,128)(2,1)} %copy-done.13, bf16[64,16,128]{2,1,0:T(8,128)(2,1)} %copy-done.14, ...), custom_call_target="tpu_custom_call" | custom-call | tf_op jit(solution)/shard_map/assemble/pallas_call | solution.py:393
  (79 shorter events, 0.4 us)
Async XLA Ops:
  0.6 14.7 %copy-start.11 = (bf16[128,512]{1,0:T(8,128)(2,1)S(1)}, bf16[128,512]{1,0:T(8,128)(2,1)}, u32[]{:S(2)}) copy-start(bf16[128,512]{1,0:T(8,128)(2,1)} %up_ref.1) | copy-start | bytes 393220
  2.0 30.4 %copy-start.1 = (bf16[128,1792]{1,0:T(8,128)(2,1)S(1)}, bf16[128,1792]{1,0:T(8,128)(2,1)}, u32[]{:S(2)}) copy-start(bf16[128,1792]{1,0:T(8,128)(2,1)} %features_ref.1) | copy-start | bytes 1376260
  5.0 28.9 %all-to-all-start = ((bf16[8,144,256]{2,1,0:T(8,128)(2,1)}), bf16[8,144,256]{2,1,0:T(8,128)(2,1)S(1)}, u32[]{:S(2)}, u32[]{:S(2)}) async-start(bf16[8,144,256]{2,1,0:T(8,128)(2,1)} %get-tuple-element.32), calls=%async_computation | async-start | bytes 1179648 | tf_op jit(solution)/shard_map/all_to_all | solution.py:420
  15.3 18.6 %collective-permute-start = (bf16[128,256]{1,0:T(8,128)(2,1)S(1)}, bf16[128,256]{1,0:T(8,128)(2,1)S(1)}, u32[]{:S(2)}, u32[]{:S(2)}) collective-permute-start(bf16[128,256]{1,0:T(8,128)(2,1)S(1)} %slice_select_fusion), channel_id=1, source_target_pairs={{0,1},{1,0},{2,3},{3,2},{4,5},{5,4},{6,7},{7,6},{8,9},{9,8},{10,11... | collective-permute-start | bytes 196616 | tf_op jit(solution)/shard_map/ppermute | solution.py:93
  17.4 32.3 %collective-permute-start.1 = (bf16[144,256]{1,0:T(8,128)(2,1)}, bf16[144,256]{1,0:T(8,128)(2,1)S(1)}, u32[]{:S(2)}, u32[]{:S(2)}) collective-permute-start(bf16[144,256]{1,0:T(8,128)(2,1)} %get-tuple-element.36), channel_id=1, source_target_pairs={{248,256},{249,257},{250,258},{251,259},{252,260},{253,261},{254,2... | collective-permute-start | bytes 221192 | tf_op jit(solution)/shard_map/ppermute | solution.py:53
  30.1 19.5 %collective-permute-start.2 = (bf16[144,256]{1,0:T(8,128)(2,1)}, bf16[144,256]{1,0:T(8,128)(2,1)S(1)}, u32[]{:S(2)}, u32[]{:S(2)}) collective-permute-start(bf16[144,256]{1,0:T(8,128)(2,1)} %get-tuple-element.37), channel_id=1, source_target_pairs={{248,257},{249,256},{250,259},{251,258},{252,261},{253,260},{254,2... | collective-permute-start | bytes 221192 | tf_op jit(solution)/shard_map/ppermute | solution.py:54
  33.9 5.9 %copy-start.23 = (bf16[128,256]{1,0:T(8,128)(2,1)}, bf16[128,256]{1,0:T(8,128)(2,1)S(1)}, u32[]{:S(2)}) copy-start(bf16[128,256]{1,0:T(8,128)(2,1)S(1)} %collective-permute-done.up_other_ref) | copy-start | bytes 196612
  33.9 0.8 copy-start.7
  39.8 29.3 %collective-permute-start.3 = (bf16[8,144,256]{2,1,0:T(8,128)(2,1)}, bf16[8,144,256]{2,1,0:T(8,128)(2,1)S(1)}, u32[]{:S(2)}, u32[]{:S(2)}) collective-permute-start(bf16[8,144,256]{2,1,0:T(8,128)(2,1)} %copy-done.7), channel_id=1, source_target_pairs={{0,8},{8,16},{16,24},{24,32},{32,40},{40,48},{48,56},{56,64},{64,7... | collective-permute-start | bytes 1769480 | tf_op jit(solution)/shard_map/ppermute | solution.py:89
  41.1 28.0 %collective-permute-start.4 = (bf16[8,144,256]{2,1,0:T(8,128)(2,1)}, bf16[8,144,256]{2,1,0:T(8,128)(2,1)S(1)}, u32[]{:S(2)}, u32[]{:S(2)}) collective-permute-start(bf16[8,144,256]{2,1,0:T(8,128)(2,1)} %copy-done.7), channel_id=1, source_target_pairs={{8,0},{16,8},{24,16},{32,24},{40,32},{48,40},{56,48},{64,56},{72,6... | collective-permute-start | bytes 1769480 | tf_op jit(solution)/shard_map/ppermute | solution.py:89
  42.4 31.6 %all-to-all-start.2 = ((bf16[4,128,448]{1,2,0:T(8,128)(2,1)}), bf16[4,128,448]{1,2,0:T(8,128)(2,1)S(1)}, u32[]{:S(2)}, u32[]{:S(2)}) async-start(bf16[4,128,448]{1,2,0:T(8,128)(2,1)} %pad_maximum_fusion), calls=%async_computation.2 | async-start | bytes 917504 | tf_op jit(solution)/shard_map/all_to_all | solution.py:431
  46.9 12.1 %copy-start.25 = (f32[512]{0:T(512)S(1)}, f32[512]{0:T(512)}, u32[]{:S(2)}) copy-start(f32[512]{0:T(512)} %param.11) | copy-start | bytes 6148
  49.7 19.4 %copy-start.6 = (bf16[2,144,256]{2,1,0:T(8,128)(2,1)}, bf16[2,144,256]{2,1,0:T(8,128)(2,1)S(1)}, u32[]{:S(2)}) copy-start(bf16[2,144,256]{2,1,0:T(8,128)(2,1)S(1)} %pad_maximum_fusion.1.refs_2_.refs_3_) | copy-start | bytes 442372
  49.7 9.9 %collective-permute-start.5 = (bf16[2,144,256]{2,1,0:T(8,128)(2,1)S(1)}, bf16[2,144,256]{2,1,0:T(8,128)(2,1)S(1)}, u32[]{:S(2)}, u32[]{:S(2)}) collective-permute-start(bf16[2,144,256]{2,1,0:T(8,128)(2,1)S(1)} %pad_maximum_fusion.1.refs_2_.refs_3_), channel_id=1, source_target_pairs={{248,250},{249,251},{250,248},{251,249},{252,254},{253,255},{254,2... | collective-permute-start | bytes 442376 | tf_op jit(solution)/shard_map/ppermute | solution.py:64
  53.1 16.0 %collective-permute-start.6 = (bf16[2,144,256]{2,1,0:T(8,128)(2,1)S(1)}, bf16[2,144,256]{2,1,0:T(8,128)(2,1)S(1)}, u32[]{:S(2)}, u32[]{:S(2)}) collective-permute-start(bf16[2,144,256]{2,1,0:T(8,128)(2,1)S(1)} %pad_maximum_fusion.1.refs_2_.refs_3_), channel_id=1, source_target_pairs={{248,252},{249,253},{250,254},{251,255},{252,248},{253,249},{254,2... | collective-permute-start | bytes 442376 | tf_op jit(solution)/shard_map/ppermute | solution.py:64
  57.1 12.0 %collective-permute-start.7 = (bf16[2,144,256]{2,1,0:T(8,128)(2,1)S(1)}, bf16[2,144,256]{2,1,0:T(8,128)(2,1)S(1)}, u32[]{:S(2)}, u32[]{:S(2)}) collective-permute-start(bf16[2,144,256]{2,1,0:T(8,128)(2,1)S(1)} %pad_maximum_fusion.1.refs_2_.refs_3_), channel_id=1, source_target_pairs={{248,254},{249,255},{250,252},{251,253},{252,250},{253,251},{254,2... | collective-permute-start | bytes 442376 | tf_op jit(solution)/shard_map/ppermute | solution.py:64
  59.6 9.5 %copy-start.19 = (bf16[2,144,256]{2,1,0:T(8,128)(2,1)}, bf16[2,144,256]{2,1,0:T(8,128)(2,1)S(1)}, u32[]{:S(2)}) copy-start(bf16[2,144,256]{2,1,0:T(8,128)(2,1)S(1)} %collective-permute-done.5.refs_3_.refs_4_) | copy-start | bytes 442372
  69.0 0.7 copy-start.20
  69.1 0.7 copy-start.21
  69.1 1.0 copy-start.4
  69.1 1.2 copy-start.5
  74.0 32.5 %all-to-all-start.1 = ((bf16[4,2,128,256]{3,2,1,0:T(8,128)(2,1)}), bf16[4,2,128,256]{3,2,1,0:T(8,128)(2,1)}, u32[]{:S(2)}, u32[]{:S(2)}) async-start(bf16[4,2,128,256]{3,2,1,0:T(8,128)(2,1)} %get-tuple-element.44), calls=%async_computation.1 | async-start | bytes 1048576 | tf_op jit(solution)/shard_map/all_to_all | solution.py:440
  78.8 27.6 %collective-permute-start.8 = (bf16[2,128,256]{2,1,0:T(8,128)(2,1)}, bf16[2,128,256]{2,1,0:T(8,128)(2,1)S(1)}, u32[]{:S(2)}, u32[]{:S(2)}) collective-permute-start(bf16[2,128,256]{2,1,0:T(8,128)(2,1)} %get-tuple-element.43), channel_id=1, source_target_pairs={{248,256},{249,257},{250,258},{251,259},{252,260},{253,261},{254,2... | collective-permute-start | bytes 393224 | tf_op jit(solution)/shard_map/ppermute | solution.py:53
  94.1 12.3 %copy-start.2 = (bf16[4,128,448]{2,1,0:T(8,128)(2,1)}, bf16[4,128,448]{2,1,0:T(8,128)(2,1)S(1)}, u32[]{:S(2)}) copy-start(bf16[4,128,448]{2,1,0:T(8,128)(2,1)S(1)} %copy.18.feats_ref) | copy-start | bytes 1376260
  94.2 12.3 %copy-start.26 = (f32[1,256]{1,0:T(1,128)S(1)}, f32[1,256]{1,0:T(1,128)}, u32[]{:S(2)}) copy-start(f32[1,256]{1,0:T(1,128)} %get-tuple-element.47) | copy-start | bytes 3076
  94.2 23.3 %collective-permute-start.9 = (bf16[4,128,448]{2,1,0:T(8,128)(2,1)S(1)}, bf16[4,128,448]{2,1,0:T(8,128)(2,1)S(1)}, u32[]{:S(2)}, u32[]{:S(2)}) collective-permute-start(bf16[4,128,448]{2,1,0:T(8,128)(2,1)S(1)} %copy.18.feats_ref), channel_id=1, source_target_pairs={{0,1},{1,0},{2,3},{3,2},{4,5},{5,4},{6,7},{7,6},{8,9},{9,8},{10,11... | collective-permute-start | bytes 1376264 | tf_op jit(solution)/shard_map/ppermute | solution.py:93
  106.4 18.5 %copy-start.22 = (bf16[2,128,256]{2,1,0:T(8,128)(2,1)}, bf16[2,128,256]{2,1,0:T(8,128)(2,1)S(1)}, u32[]{:S(2)}) copy-start(bf16[2,128,256]{2,1,0:T(8,128)(2,1)S(1)} %collective-permute-done.8.refs_2_) | copy-start | bytes 393220
  106.5 21.5 %collective-permute-start.10 = (bf16[8,128,256]{2,1,0:T(8,128)(2,1)}, bf16[8,128,256]{2,1,0:T(8,128)(2,1)S(1)}, u32[]{:S(2)}, u32[]{:S(2)}) collective-permute-start(bf16[8,128,256]{2,1,0:T(8,128)(2,1)} %bitcast.16.own_ref), channel_id=1, source_target_pairs={{0,8},{8,16},{16,24},{24,32},{32,40},{40,48},{48,56},{56,64},{64,7... | collective-permute-start | bytes 1572872 | tf_op jit(solution)/shard_map/ppermute | solution.py:89
  107.8 20.2 %collective-permute-start.11 = (bf16[8,128,256]{2,1,0:T(8,128)(2,1)}, bf16[8,128,256]{2,1,0:T(8,128)(2,1)S(1)}, u32[]{:S(2)}, u32[]{:S(2)}) collective-permute-start(bf16[8,128,256]{2,1,0:T(8,128)(2,1)} %bitcast.16.own_ref), channel_id=1, source_target_pairs={{8,0},{16,8},{24,16},{32,24},{40,32},{48,40},{56,48},{64,56},{72,6... | collective-permute-start | bytes 1572872 | tf_op jit(solution)/shard_map/ppermute | solution.py:89
  109.8 15.2 %collective-permute-start.12 = (bf16[2,128,256]{2,1,0:T(8,128)(2,1)S(1)}, bf16[2,128,256]{2,1,0:T(8,128)(2,1)}, u32[]{:S(2)}, u32[]{:S(2)}) collective-permute-start(bf16[2,128,256]{2,1,0:T(8,128)(2,1)S(1)} %collective-permute-done.8.refs_2_), channel_id=1, source_target_pairs={{248,250},{249,251},{250,248},{251,249},{252,254},{253,255},{254,2... | collective-permute-start | bytes 393224 | tf_op jit(solution)/shard_map/ppermute | solution.py:64
  114.3 13.7 %collective-permute-start.13 = (bf16[2,128,256]{2,1,0:T(8,128)(2,1)S(1)}, bf16[2,128,256]{2,1,0:T(8,128)(2,1)}, u32[]{:S(2)}, u32[]{:S(2)}) collective-permute-start(bf16[2,128,256]{2,1,0:T(8,128)(2,1)S(1)} %collective-permute-done.8.refs_2_), channel_id=1, source_target_pairs={{248,252},{249,253},{250,254},{251,255},{252,248},{253,249},{254,2... | collective-permute-start | bytes 393224 | tf_op jit(solution)/shard_map/ppermute | solution.py:64
  117.4 7.5 %copy-start.8 = (bf16[4,128,448]{2,1,0:T(8,128)(2,1)}, bf16[4,128,448]{2,1,0:T(8,128)(2,1)S(1)}, u32[]{:S(2)}) copy-start(bf16[4,128,448]{2,1,0:T(8,128)(2,1)S(1)} %collective-permute-done.9.feats_other_ref) | copy-start | bytes 1376260
  117.4 10.6 %collective-permute-start.14 = (bf16[2,128,256]{2,1,0:T(8,128)(2,1)S(1)}, bf16[2,128,256]{2,1,0:T(8,128)(2,1)}, u32[]{:S(2)}, u32[]{:S(2)}) collective-permute-start(bf16[2,128,256]{2,1,0:T(8,128)(2,1)S(1)} %collective-permute-done.8.refs_2_), channel_id=1, source_target_pairs={{248,254},{249,255},{250,252},{251,253},{252,250},{253,251},{254,2... | collective-permute-start | bytes 393224 | tf_op jit(solution)/shard_map/ppermute | solution.py:64
  125.0 27.1 %copy-start = (bf16[1792,512]{1,0:T(8,128)(2,1)S(1)}, bf16[1792,512]{1,0:T(8,128)(2,1)}, u32[]{:S(2)}) copy-start(bf16[1792,512]{1,0:T(8,128)(2,1)} %weight_ref.1) | copy-start | bytes 5505028
  125.0 17.8 %copy-start.27 = (bf16[128,256]{1,0:T(8,128)(2,1)S(1)}, bf16[128,256]{1,0:T(8,128)(2,1)}, u32[]{:S(2)}) copy-start(bf16[128,256]{1,0:T(8,128)(2,1)} %get-tuple-element.54) | copy-start | bytes 196612
  125.0 25.6 %copy-start.24 = (bf16[128,256]{1,0:T(8,128)(2,1)S(1)}, bf16[128,256]{1,0:T(8,128)(2,1)}, u32[]{:S(2)}) copy-start(bf16[128,256]{1,0:T(8,128)(2,1)} %get-tuple-element.53) | copy-start | bytes 196612
  128.0 0.8 copy-start.9
  128.8 0.8 copy-start.10
  136.3 20.5 %all-to-all-start.3 = ((bf16[64,16,128]{2,1,0:T(8,128)(2,1)}), bf16[64,16,128]{2,1,0:T(8,128)(2,1)S(1)}, u32[]{:S(2)}, u32[]{:S(2)}) async-start(bf16[64,16,128]{2,1,0:T(8,128)(2,1)} %get-tuple-element.50), calls=%async_computation.3 | async-start | bytes 524288 | tf_op jit(solution)/shard_map/all_to_all | solution.py:465
  142.7 7.9 %collective-permute-start.16 = (bf16[128,256]{1,0:T(8,128)(2,1)S(1)}, bf16[128,256]{1,0:T(8,128)(2,1)S(1)}, u32[]{:S(2)}, u32[]{:S(2)}) collective-permute-start(bf16[128,256]{1,0:T(8,128)(2,1)S(1)} %copy-done.27), channel_id=1, source_target_pairs={{0,1},{1,0},{2,3},{3,2},{4,5},{5,4},{6,7},{7,6},{8,9},{9,8},{10,11... | collective-permute-start | bytes 196616 | tf_op jit(solution)/shard_map/ppermute | solution.py:93
  148.7 3.4 %collective-permute-start.15 = (bf16[128,256]{1,0:T(8,128)(2,1)}, bf16[128,256]{1,0:T(8,128)(2,1)S(1)}, u32[]{:S(2)}, u32[]{:S(2)}) collective-permute-start(bf16[128,256]{1,0:T(8,128)(2,1)} %get-tuple-element.52), channel_id=1, source_target_pairs={{0,1},{1,0},{2,3},{3,2},{4,5},{5,4},{6,7},{7,6},{8,9},{9,8},{10,11... | collective-permute-start | bytes 196616 | tf_op jit(solution)/shard_map/ppermute | solution.py:93
  180.2 26.9 %copy-start.3 = (bf16[64,16,128]{2,1,0:T(8,128)(2,1)}, bf16[64,16,128]{2,1,0:T(8,128)(2,1)S(1)}, u32[]{:S(2)}) copy-start(bf16[64,16,128]{2,1,0:T(8,128)(2,1)S(1)} %all_to_all.25.refs_0_) | copy-start | bytes 786436
  180.2 15.7 %collective-permute-start.17 = (bf16[64,16,128]{2,1,0:T(8,128)(2,1)S(1)}, bf16[64,16,128]{2,1,0:T(8,128)(2,1)S(1)}, u32[]{:S(2)}, u32[]{:S(2)}) collective-permute-start(bf16[64,16,128]{2,1,0:T(8,128)(2,1)S(1)} %all_to_all.25.refs_0_), channel_id=1, source_target_pairs={{0,64},{64,0},{128,192},{192,128},{1,65},{65,1},{129,193},{193,129... | collective-permute-start | bytes 786440 | tf_op jit(solution)/shard_map/ppermute | solution.py:474
  184.1 13.8 %collective-permute-start.18 = (bf16[64,16,128]{2,1,0:T(8,128)(2,1)S(1)}, bf16[64,16,128]{2,1,0:T(8,128)(2,1)S(1)}, u32[]{:S(2)}, u32[]{:S(2)}) collective-permute-start(bf16[64,16,128]{2,1,0:T(8,128)(2,1)S(1)} %all_to_all.25.refs_0_), channel_id=1, source_target_pairs={{0,128},{64,192},{128,0},{192,64},{1,129},{65,193},{129,1},{193,65... | collective-permute-start | bytes 786440 | tf_op jit(solution)/shard_map/ppermute | solution.py:474
  188.5 13.9 %collective-permute-start.19 = (bf16[64,16,128]{2,1,0:T(8,128)(2,1)S(1)}, bf16[64,16,128]{2,1,0:T(8,128)(2,1)S(1)}, u32[]{:S(2)}, u32[]{:S(2)}) collective-permute-start(bf16[64,16,128]{2,1,0:T(8,128)(2,1)S(1)} %all_to_all.25.refs_0_), channel_id=1, source_target_pairs={{0,192},{64,128},{128,64},{192,0},{1,193},{65,129},{129,65},{193,1... | collective-permute-start | bytes 786440 | tf_op jit(solution)/shard_map/ppermute | solution.py:474
  190.5 15.5 %collective-permute-start.20 = (bf16[64,16,128]{2,1,0:T(8,128)(2,1)S(1)}, bf16[64,16,128]{2,1,0:T(8,128)(2,1)S(1)}, u32[]{:S(2)}, u32[]{:S(2)}) collective-permute-start(bf16[64,16,128]{2,1,0:T(8,128)(2,1)S(1)} %all_to_all.25.refs_0_), channel_id=1, source_target_pairs={{0,1},{1,0},{2,3},{3,2},{4,5},{5,4},{6,7},{7,6},{8,9},{9,8},{10,11... | collective-permute-start | bytes 786440 | tf_op jit(solution)/shard_map/ppermute | solution.py:93
  195.9 11.2 %copy-start.12 = (bf16[64,16,128]{2,1,0:T(8,128)(2,1)}, bf16[64,16,128]{2,1,0:T(8,128)(2,1)S(1)}, u32[]{:S(2)}) copy-start(bf16[64,16,128]{2,1,0:T(8,128)(2,1)S(1)} %collective-permute-done.17.refs_1_) | copy-start | bytes 786436
  195.9 10.0 %collective-permute-start.21 = (bf16[64,16,128]{2,1,0:T(8,128)(2,1)S(1)}, bf16[64,16,128]{2,1,0:T(8,128)(2,1)S(1)}, u32[]{:S(2)}, u32[]{:S(2)}) collective-permute-start(bf16[64,16,128]{2,1,0:T(8,128)(2,1)S(1)} %collective-permute-done.17.refs_1_), channel_id=1, source_target_pairs={{0,1},{1,0},{2,3},{3,2},{4,5},{5,4},{6,7},{7,6},{8,9},{9,8},{10,11... | collective-permute-start | bytes 786440 | tf_op jit(solution)/shard_map/ppermute | solution.py:93
  197.9 9.2 %copy-start.13 = (bf16[64,16,128]{2,1,0:T(8,128)(2,1)}, bf16[64,16,128]{2,1,0:T(8,128)(2,1)S(1)}, u32[]{:S(2)}) copy-start(bf16[64,16,128]{2,1,0:T(8,128)(2,1)S(1)} %collective-permute-done.18.refs_2_) | copy-start | bytes 786436
  197.9 8.1 %collective-permute-start.22 = (bf16[64,16,128]{2,1,0:T(8,128)(2,1)S(1)}, bf16[64,16,128]{2,1,0:T(8,128)(2,1)S(1)}, u32[]{:S(2)}, u32[]{:S(2)}) collective-permute-start(bf16[64,16,128]{2,1,0:T(8,128)(2,1)S(1)} %collective-permute-done.18.refs_2_), channel_id=1, source_target_pairs={{0,1},{1,0},{2,3},{3,2},{4,5},{5,4},{6,7},{7,6},{8,9},{9,8},{10,11... | collective-permute-start | bytes 786440 | tf_op jit(solution)/shard_map/ppermute | solution.py:93
  202.5 4.6 %copy-start.14 = (bf16[64,16,128]{2,1,0:T(8,128)(2,1)}, bf16[64,16,128]{2,1,0:T(8,128)(2,1)S(1)}, u32[]{:S(2)}) copy-start(bf16[64,16,128]{2,1,0:T(8,128)(2,1)S(1)} %collective-permute-done.19.refs_3_) | copy-start | bytes 786436
  202.5 4.6 %collective-permute-start.23 = (bf16[64,16,128]{2,1,0:T(8,128)(2,1)S(1)}, bf16[64,16,128]{2,1,0:T(8,128)(2,1)S(1)}, u32[]{:S(2)}, u32[]{:S(2)}) collective-permute-start(bf16[64,16,128]{2,1,0:T(8,128)(2,1)S(1)} %collective-permute-done.19.refs_3_), channel_id=1, source_target_pairs={{0,1},{1,0},{2,3},{3,2},{4,5},{5,4},{6,7},{7,6},{8,9},{9,8},{10,11... | collective-permute-start | bytes 786440 | tf_op jit(solution)/shard_map/ppermute | solution.py:93
  206.0 1.1 copy-start.15
  206.0 1.1 copy-start.16
  206.0 1.1 copy-start.17
  207.1 0.7 copy-start.18

commit v7 on v5

--- a/solution.py
+++ b/solution.py
@@ -323,13 +323,10 @@
     other_ref[...] = round_ref[run * 2 + 1 - core]
     part = jnp.zeros((F_RUN, HALF), f32)
     for feats, side in ((feats_ref, core), (feats_other_ref, 1 - core)):
-        rows = jnp.concatenate([round_ref[k * 2 + side] for k in range(RUN)], axis=0)
-        part = part + lax.dot_general(
-            feats[...].reshape(RUN * TILE, F_RUN),
-            rows,
-            (((0,), (0,)), ((), ())),
-            preferred_element_type=f32,
-        )
+        for k in range(RUN):
+            part = part + jnp.dot(
+                feats[k], round_ref[k * 2 + side], preferred_element_type=f32
+            )
     part = part.astype(bf16)
     for row in range(F_RUN // 16):
         for lane in range(2):
@@ -407,7 +404,7 @@
     own = lax.all_to_all(copies, ("yl", "c"), 0, 0)
     tied, _ = lax.optimization_barrier((upstream, copies))
     up_other = swap_core(jnp.where(first, tied[:, HALF:], tied[:, :HALF]))
-    slices = jnp.stack([features[:, k * F_RUN : (k + 1) * F_RUN] for k in range(RUN)])
+    slices = features.T.reshape(RUN, F_RUN, TILE)
     own, up_other, slices = lax.optimization_barrier((own, up_other, slices))
     straight, turned, _ = lax.optimization_barrier((straight, turned, own))
     received = jnp.stack([jnp.where(first, straight, turned), jnp.where(first, turned, straight)])

time: 205 us -> 205 us (level)
    unnamed x48 -> x42, local copies, waits for them, and re-layouts: 4.41 us -> 3.84 us
where the time goes in v7:
time: 205 us; the launch traced here: 203 us
  starting transfers between devices  93.8 us (46%)
  blocking collectives  39.4 us (19%)
  Pallas kernels  38.2 us (19%)
  waiting for transfers between devices  19.3 us (9%)
  local copies, waits for them, and re-layouts  5.64 us (3%)
  other arithmetic  3.03 us (1%)
  matrix products  2.4 us (1%)
    all_to_all x2, blocking collectives, spread_to(): lax.all_to_all(jnp.broadcast_to(shard[None], (count,) + shard.shape), axe...  39.4 us
    ppermute x6, starting transfers between devices, along_run(): parts.append(lax.ppermute(block, AXES, pairs))  20.5 us
    ppermute x5, starting transfers between devices, swap_core(): return lax.ppermute(block, 'c', [(0, 1), (1, 0)])  20 us
    ppermute x2, starting transfers between devices, across(): got = lax.ppermute(same, AXES, straight)  17 us
    all_to_all x1, starting transfers between devices, on_device(): own = lax.all_to_all(copies, ('yl', 'c'), 0, 0)  10.3 us
    all_to_all x1, starting transfers between devices, on_device(): terms = lax.all_to_all(slabs, WIDE, 0, 0)  10.2 us
    pallas_call x1, Pallas kernels, backward_counts(): pl.pallas_call(backward_counts_kernel, in_specs=[SMEM_SPEC] + [VMEM_SPEC]...  8.72 us
    pallas_call x1, Pallas kernels, backward_math(): pl.pallas_call(backward_kernel, in_specs=[SMEM_SPEC] + [VMEM_SPEC] * (4 +...  7.21 us
  transfers between devices with their start and end apart: 22, of which 7 were waited for; matrix products, arithmetic and copies ran while one was open for 3% of the time, Pallas kernels for 12%

profile of v7, /device:TPU:1, one launch (start us, length us, event | category | flops | bytes accessed | tf_op | source)
XLA Modules:
  0.0 203.4 jit_solution(14321142680230861189)
XLA Ops:
  0.6 0.0 copy-start.11
  1.3 0.6 stack.40.ids_ref
  1.9 3.0 %project.1 = (bf16[8,144,256]{2,1,0:T(8,128)(2,1)}, bf16[144,256]{1,0:T(8,128)(2,1)}, bf16[144,256]{1,0:T(8,128)(2,1)}) custom-call(s32[5]{0:T(128)} %stack.40.ids_ref, s32[1]{0:T(128)S(6)} %copy.14.count_ref, s32[1,24]{1,0:T(1,128)} %tiles_ref.1, s32[15,128]{1,0:T(8,128)} %bitcast.23, s32[15,128]{1,0:T(8,128)} %bitcast.24, s32[15,128]{1,0:T(8,128)} %bitcast.25, ...), custom_call_target="tpu_custom_call" | custom-call | tf_op jit(solution)/shard_map/project/pallas_call | solution.py:129
  4.9 10.3 %all-to-all-start = ((bf16[8,144,256]{2,1,0:T(8,128)(2,1)}), bf16[8,144,256]{2,1,0:T(8,128)(2,1)S(1)}, u32[]{:S(2)}, u32[]{:S(2)}) async-start(bf16[8,144,256]{2,1,0:T(8,128)(2,1)} %get-tuple-element.31), calls=%async_computation | async-start | bytes 1179648 | tf_op jit(solution)/shard_map/all_to_all | solution.py:404
  15.3 2.0 collective-permute-start
  17.3 12.8 %collective-permute-start.3 = (bf16[144,256]{1,0:T(8,128)(2,1)}, bf16[144,256]{1,0:T(8,128)(2,1)S(1)}, u32[]{:S(2)}, u32[]{:S(2)}) collective-permute-start(bf16[144,256]{1,0:T(8,128)(2,1)} %get-tuple-element.37), channel_id=1, source_target_pairs={{248,256},{249,257},{250,258},{251,259},{252,260},{253,261},{254,2... | collective-permute-start | bytes 221192 | tf_op jit(solution)/shard_map/ppermute | solution.py:53
  30.1 2.2 %collective-permute-start.4 = (bf16[144,256]{1,0:T(8,128)(2,1)}, bf16[144,256]{1,0:T(8,128)(2,1)S(1)}, u32[]{:S(2)}, u32[]{:S(2)}) collective-permute-start(bf16[144,256]{1,0:T(8,128)(2,1)} %get-tuple-element.38), channel_id=1, source_target_pairs={{248,257},{249,256},{250,259},{251,258},{252,261},{253,260},{254,2... | collective-permute-start | bytes 221192 | tf_op jit(solution)/shard_map/ppermute | solution.py:54
  32.3 0.6 slice_select_fusion.1
  32.9 1.0 copy.13
  33.8 0.0 collective-permute-done.up_other_ref
  33.8 0.0 all-to-all-done.own_ref.refs_0_
  33.8 1.3 collective-permute-start.1
  35.2 1.3 collective-permute-start.2
  36.5 3.5 %collective-permute-done.3 = bf16[144,256]{1,0:T(8,128)(2,1)S(1)} collective-permute-done((bf16[144,256]{1,0:T(8,128)(2,1)}, bf16[144,256]{1,0:T(8,128)(2,1)S(1)}, u32[]{:S(2)}, u32[]{:S(2)}) %collective-permute-start.3) | collective-permute-done | bytes 73760 | tf_op jit(solution)/shard_map/ppermute | solution.py:53
  40.0 5.1 %collective-permute-done.4 = bf16[144,256]{1,0:T(8,128)(2,1)S(1)} collective-permute-done((bf16[144,256]{1,0:T(8,128)(2,1)}, bf16[144,256]{1,0:T(8,128)(2,1)S(1)}, u32[]{:S(2)}, u32[]{:S(2)}) %collective-permute-start.4) | collective-permute-done | bytes 73760 | tf_op jit(solution)/shard_map/ppermute | solution.py:54
  45.2 4.0 %collective-permute-start.5 = (bf16[2,144,256]{2,1,0:T(8,128)(2,1)S(1)}, bf16[2,144,256]{2,1,0:T(8,128)(2,1)S(1)}, u32[]{:S(2)}, u32[]{:S(2)}) collective-permute-start(bf16[2,144,256]{2,1,0:T(8,128)(2,1)S(1)} %pad_maximum_fusion.refs_2_.refs_3_), channel_id=1, source_target_pairs={{248,250},{249,251},{250,248},{251,249},{252,254},{253,255},{254,2... | collective-permute-start | bytes 442376 | tf_op jit(solution)/shard_map/ppermute | solution.py:64
  49.2 4.3 %collective-permute-start.6 = (bf16[2,144,256]{2,1,0:T(8,128)(2,1)S(1)}, bf16[2,144,256]{2,1,0:T(8,128)(2,1)S(1)}, u32[]{:S(2)}, u32[]{:S(2)}) collective-permute-start(bf16[2,144,256]{2,1,0:T(8,128)(2,1)S(1)} %pad_maximum_fusion.refs_2_.refs_3_), channel_id=1, source_target_pairs={{248,252},{249,253},{250,254},{251,255},{252,248},{253,249},{254,2... | collective-permute-start | bytes 442376 | tf_op jit(solution)/shard_map/ppermute | solution.py:64
  53.6 2.2 %collective-permute-start.7 = (bf16[2,144,256]{2,1,0:T(8,128)(2,1)S(1)}, bf16[2,144,256]{2,1,0:T(8,128)(2,1)S(1)}, u32[]{:S(2)}, u32[]{:S(2)}) collective-permute-start(bf16[2,144,256]{2,1,0:T(8,128)(2,1)S(1)} %pad_maximum_fusion.refs_2_.refs_3_), channel_id=1, source_target_pairs={{248,254},{249,255},{250,252},{251,253},{252,250},{253,251},{254,2... | collective-permute-start | bytes 442376 | tf_op jit(solution)/shard_map/ppermute | solution.py:64
  55.8 4.3 %all-to-all-start.2 = ((bf16[4,448,128]{2,1,0:T(8,128)(2,1)}), bf16[4,448,128]{2,1,0:T(8,128)(2,1)S(1)}, u32[]{:S(2)}, u32[]{:S(2)}) async-start(bf16[4,448,128]{2,1,0:T(8,128)(2,1)} %bitcast.9), calls=%async_computation.2 | async-start | bytes 917504 | tf_op jit(solution)/shard_map/all_to_all | solution.py:414
  60.0 5.1 %forward_counts.1 = (bf16[256,3072]{1,0:T(8,128)(2,1)}, f32[256,1]{1,0:T(8,128)}) custom-call(s32[5]{0:T(128)} %stack.40.ids_ref, bf16[8,144,256]{2,1,0:T(8,128)(2,1)} %copy-done.8), custom_call_target="tpu_custom_call" | custom-call | flops 4000000000 | bytes 8000000 | tf_op jit(solution)/shard_map/forward_counts/pallas_call | solution.py:175
  65.1 2.7 %forward_own.1.total_ref = f32[256,256]{1,0:T(8,128)} custom-call(s32[5]{0:T(128)} %stack.40.ids_ref, bf16[256,3072]{1,0:T(8,128)(2,1)} %get-tuple-element.34.counts_ref, bf16[8,144,256]{2,1,0:T(8,128)(2,1)} %copy-done.8), custom_call_target="tpu_custom_call" | custom-call | flops 4000000000 | bytes 8000000 | tf_op jit(solution)/shard_map/forward_own/pallas_call | solution.py:232
  67.8 0.0 collective-permute-done.7.refs_5_.refs_6_
  67.9 0.0 collective-permute-done.2.refs_1_.refs_2_
  67.9 0.6 copy-done.14
  68.5 0.1 copy-done.15
  68.5 0.1 copy-done.16
  68.6 0.2 copy-done.5
  68.8 0.3 copy-done.6
  69.1 3.8 %forward_math.1 = (bf16[128,256]{1,0:T(8,128)(2,1)}, bf16[128,256]{1,0:T(8,128)(2,1)}, bf16[4,2,128,256]{3,2,1,0:T(8,128)(2,1)}, bf16[2,128,256]{2,1,0:T(8,128)(2,1)}, f32[1,256]{1,0:T(1,128)}) custom-call(s32[5]{0:T(128)} %stack.40.ids_ref, bf16[256,3072]{1,0:T(8,128)(2,1)} %get-tuple-element.34.counts_ref, f32[256,256]{1,0:T(8,128)} %forward_own.1.total_ref, ...), custom_call_target="tpu_custom_call" | custom-call | tf_op jit(solution)/shard_map/forward_math/pallas_call | solution.py:294
  72.9 3.5 %all-to-all-done.2.feats_ref = bf16[4,448,128]{2,1,0:T(8,128)(2,1)S(1)} async-done(((bf16[4,448,128]{2,1,0:T(8,128)(2,1)}), bf16[4,448,128]{2,1,0:T(8,128)(2,1)S(1)}, u32[]{:S(2)}, u32[]{:S(2)}) %all-to-all-start.2) | async-done | bytes 458784 | tf_op jit(solution)/shard_map/all_to_all | solution.py:414
  76.4 4.1 %all-to-all-start.1 = ((bf16[4,2,128,256]{3,2,1,0:T(8,128)(2,1)}), bf16[4,2,128,256]{3,2,1,0:T(8,128)(2,1)S(1)}, u32[]{:S(2)}, u32[]{:S(2)}) async-start(bf16[4,2,128,256]{3,2,1,0:T(8,128)(2,1)} %get-tuple-element.42), calls=%async_computation.1 | async-start | bytes 1048576 | tf_op jit(solution)/shard_map/all_to_all | solution.py:424
  80.5 0.1 pad.13.clone
  80.6 4.3 %collective-permute-start.8 = (bf16[2,128,256]{2,1,0:T(8,128)(2,1)}, bf16[2,128,256]{2,1,0:T(8,128)(2,1)S(1)}, u32[]{:S(2)}, u32[]{:S(2)}) collective-permute-start(bf16[2,128,256]{2,1,0:T(8,128)(2,1)} %get-tuple-element.41), channel_id=1, source_target_pairs={{248,256},{249,257},{250,258},{251,259},{252,260},{253,261},{254,2... | collective-permute-start | bytes 393224 | tf_op jit(solution)/shard_map/ppermute | solution.py:53
  84.8 4.2 %collective-permute-start.9 = (bf16[4,448,128]{2,1,0:T(8,128)(2,1)S(1)}, bf16[4,448,128]{2,1,0:T(8,128)(2,1)S(1)}, u32[]{:S(2)}, u32[]{:S(2)}) collective-permute-start(bf16[4,448,128]{2,1,0:T(8,128)(2,1)S(1)} %all-to-all-done.2.feats_ref), channel_id=1, source_target_pairs={{0,1},{1,0},{2,3},{3,2},{4,5},{5,4},{6,7},{7,6},{8,9},{9,8},{10,11... | collective-permute-start | bytes 1376264 | tf_op jit(solution)/shard_map/ppermute | solution.py:93
  89.0 8.7 %backward_counts.1.counts_ref = bf16[1024,3072]{1,0:T(8,128)(2,1)} custom-call(s32[5]{0:T(128)} %stack.40.ids_ref, bf16[8,144,256]{2,1,0:T(8,128)(2,1)} %copy-done.8, bf16[8,144,256]{2,1,0:T(8,128)(2,1)} %copy-done.5, bf16[8,144,256]{2,1,0:T(8,128)(2,1)} %copy-done.6, bf16[2,144,256]{2,1,0:T(8,128)(2,1)} %copy-done.7, bf16[2,144,256]{2,1,0:T(8,128)(2,1)} %copy-done.14, ...), custom_call_target="tpu_custom_call" | custom-call | flops 4000000000 | bytes 8000000 | tf_op jit(solution)/shard_map/backward_counts/pallas_call | solution.py:207
  97.8 0.0 copy-start.17
  97.8 2.3 %all-to-all-done.1 = bf16[4,2,128,256]{3,2,1,0:T(8,128)(2,1)S(1)} async-done(((bf16[4,2,128,256]{3,2,1,0:T(8,128)(2,1)}), bf16[4,2,128,256]{3,2,1,0:T(8,128)(2,1)S(1)}, u32[]{:S(2)}, u32[]{:S(2)}) %all-to-all-start.1) | async-done | bytes 524320 | tf_op jit(solution)/shard_map/all_to_all | solution.py:424
  100.1 1.3 collective-permute-start.10
  101.4 1.3 collective-permute-start.11
  102.7 0.7 maximum_maximum_fusion.bias_ref
  103.4 1.9 collective-permute-start.12
  105.3 4.7 %collective-permute-start.13 = (bf16[2,128,256]{2,1,0:T(8,128)(2,1)S(1)}, bf16[2,128,256]{2,1,0:T(8,128)(2,1)}, u32[]{:S(2)}, u32[]{:S(2)}) collective-permute-start(bf16[2,128,256]{2,1,0:T(8,128)(2,1)S(1)} %collective-permute-done.8.refs_2_), channel_id=1, source_target_pairs={{248,252},{249,253},{250,254},{251,255},{252,248},{253,249},{254,2... | collective-permute-start | bytes 393224 | tf_op jit(solution)/shard_map/ppermute | solution.py:64
  110.1 3.3 %collective-permute-start.14 = (bf16[2,128,256]{2,1,0:T(8,128)(2,1)S(1)}, bf16[2,128,256]{2,1,0:T(8,128)(2,1)}, u32[]{:S(2)}, u32[]{:S(2)}) collective-permute-start(bf16[2,128,256]{2,1,0:T(8,128)(2,1)S(1)} %collective-permute-done.8.refs_2_), channel_id=1, source_target_pairs={{248,254},{249,255},{250,252},{251,253},{252,250},{253,251},{254,2... | collective-permute-start | bytes 393224 | tf_op jit(solution)/shard_map/ppermute | solution.py:64
  113.4 4.5 %backward_own.1.total_ref = f32[1024,256]{1,0:T(8,128)} custom-call(bf16[1024,3072]{1,0:T(8,128)(2,1)} %backward_counts.1.counts_ref, bf16[8,128,256]{2,1,0:T(8,128)(2,1)} %bitcast.22), custom_call_target="tpu_custom_call" | custom-call | flops 4000000000 | bytes 8000000 | tf_op jit(solution)/shard_map/backward_own/pallas_call | solution.py:250
  117.9 0.0 collective-permute-done.12.refs_3_
  117.9 0.1 collective-permute-done.14.refs_5_
  118.0 0.8 copy-done.9
  118.8 0.8 copy-done.10
  119.6 7.2 %backward_math.1 = (bf16[128,256]{1,0:T(8,128)(2,1)}, bf16[128,256]{1,0:T(8,128)(2,1)}, bf16[64,16,128]{2,1,0:T(8,128)(2,1)}) custom-call(s32[5]{0:T(128)} %stack.40.ids_ref, bf16[1024,3072]{1,0:T(8,128)(2,1)} %backward_counts.1.counts_ref, f32[1024,256]{1,0:T(8,128)} %backward_own.1.total_ref, bf16[16,128]{1,0:T(8,128)(2,1)} %maximum_maximum_fusion.bias_ref, ...), custom_call_target="tpu_custom_call" | custom-call | tf_op jit(solution)/shard_map/backward_math/pallas_call | solution.py:340
  126.8 10.2 %all-to-all-start.3 = ((bf16[64,16,128]{2,1,0:T(8,128)(2,1)}), bf16[64,16,128]{2,1,0:T(8,128)(2,1)S(1)}, u32[]{:S(2)}, u32[]{:S(2)}) async-start(bf16[64,16,128]{2,1,0:T(8,128)(2,1)} %get-tuple-element.48), calls=%async_computation.3 | async-start | bytes 524288 | tf_op jit(solution)/shard_map/all_to_all | solution.py:449
  137.1 5.8 %collective-permute-start.16 = (bf16[128,256]{1,0:T(8,128)(2,1)}, bf16[128,256]{1,0:T(8,128)(2,1)S(1)}, u32[]{:S(2)}, u32[]{:S(2)}) collective-permute-start(bf16[128,256]{1,0:T(8,128)(2,1)} %get-tuple-element.52), channel_id=1, source_target_pairs={{0,1},{1,0},{2,3},{3,2},{4,5},{5,4},{6,7},{7,6},{8,9},{9,8},{10,11... | collective-permute-start | bytes 196616 | tf_op jit(solution)/shard_map/ppermute | solution.py:93
  142.9 1.9 collective-permute-start.15
  144.8 1.6 maximum_select_fusion.2
  146.4 2.4 %convolution_convert_fusion = bf16[128,1792]{1,0:T(8,128)(2,1)} fusion(bf16[1792,512]{1,0:T(8,128)(2,1)S(1)} %copy-done, bf16[128,256]{1,0:T(8,128)(2,1)S(1)} %collective-permute-done.15, bf16[128,256]{1,0:T(8,128)(2,1)} %get-tuple-element.49, pred[]{:T(512)S(6)} %eq.17), kind=kOutput, calls=%fused_computation | convolution fusion | flops 235700224 | bytes 2424833 | tf_op jit(solution)/shard_map/dot_general | solution.py:441
  148.8 2.4 %all-to-all-done.3 = bf16[64,16,128]{2,1,0:T(8,128)(2,1)S(1)} async-done(((bf16[64,16,128]{2,1,0:T(8,128)(2,1)}), bf16[64,16,128]{2,1,0:T(8,128)(2,1)S(1)}, u32[]{:S(2)}, u32[]{:S(2)}) %all-to-all-start.3) | async-done | bytes 262176 | tf_op jit(solution)/shard_map/all_to_all | solution.py:449
  151.2 0.1 convert_reduce_fusion
  151.3 0.1 maximum_select_fusion.3
  151.4 23.7 %all_to_all.30 = bf16[64,16,128]{2,1,0:T(8,128)(2,1)S(1)} all-to-all(bf16[64,16,128]{2,1,0:T(8,128)(2,1)S(1)} %broadcast_in_dim.7), channel_id=1, replica_groups=mesh['yh'=2,'x'=4,'z'=8,'yl'=4,'c'=2] {'yh','yl','z'}, dimensions={0} | all-to-all | bytes 524288 | tf_op jit(solution)/shard_map/all_to_all | solution.py:39
  175.1 0.1 broadcast_in_dim.8
  175.3 15.7 %all_to_all.31.mine_ref = bf16[4,64,16,128]{3,2,1,0:T(8,128)(2,1)S(1)} all-to-all(bf16[4,64,16,128]{3,2,1,0:T(8,128)(2,1)S(1)} %broadcast_in_dim.8), channel_id=1, replica_groups=mesh['yh'=2,'x'=4,'z'=8,'yl'=4,'c'=2] {'x'}, dimensions={0} | all-to-all | bytes 2097152 | tf_op jit(solution)/shard_map/all_to_all | solution.py:39
  191.0 6.1 %collective-permute-start.17 = (bf16[4,64,16,128]{3,2,1,0:T(8,128)(2,1)S(1)}, bf16[4,64,16,128]{3,2,1,0:T(8,128)(2,1)S(1)}, u32[]{:S(2)}, u32[]{:S(2)}) collective-permute-start(bf16[4,64,16,128]{3,2,1,0:T(8,128)(2,1)S(1)} %all_to_all.31.mine_ref), channel_id=1, source_target_pairs={{0,1},{1,0},{2,3},{3,2},{4,5},{5,4},{6,7},{7,6},{8,9},{9,8},{10,11... | collective-permute-start | bytes 3145736 | tf_op jit(solution)/shard_map/ppermute | solution.py:93
  197.1 2.3 %collective-permute-done.17.other_ref = bf16[4,64,16,128]{3,2,1,0:T(8,128)(2,1)S(1)} collective-permute-done((bf16[4,64,16,128]{3,2,1,0:T(8,128)(2,1)S(1)}, bf16[4,64,16,128]{3,2,1,0:T(8,128)(2,1)S(1)}, u32[]{:S(2)}, u32[]{:S(2)}) %collective-permute-start.17) | collective-permute-done | bytes 1048608 | tf_op jit(solution)/shard_map/ppermute | solution.py:93
  199.4 1.0 copy-done.4
  200.4 3.1 %assemble.1 = (bf16[1792,512]{1,0:T(8,128)(2,1)}, f32[4,128]{1,0:T(4,128)}) custom-call(s32[5]{0:T(128)} %stack.40.ids_ref, bf16[4,64,16,128]{3,2,1,0:T(8,128)(2,1)} %copy-done.1, bf16[4,64,16,128]{3,2,1,0:T(8,128)(2,1)} %copy-done.4), custom_call_target="tpu_custom_call" | custom-call | tf_op jit(solution)/shard_map/assemble/pallas_call | solution.py:377
  (49 shorter events, 0.2 us)
Async XLA Ops:
  0.6 14.6 %copy-start.11 = (bf16[128,512]{1,0:T(8,128)(2,1)S(1)}, bf16[128,512]{1,0:T(8,128)(2,1)}, u32[]{:S(2)}) copy-start(bf16[128,512]{1,0:T(8,128)(2,1)} %up_ref.1) | copy-start | bytes 393220
  1.9 30.4 %copy-start.19 = (f32[512]{0:T(512)S(1)}, f32[512]{0:T(512)}, u32[]{:S(2)}) copy-start(f32[512]{0:T(512)} %param.11) | copy-start | bytes 6148
  1.9 30.9 %copy-start.2 = (bf16[128,1792]{1,0:T(8,128)(2,1)S(1)}, bf16[128,1792]{1,0:T(8,128)(2,1)}, u32[]{:S(2)}) copy-start(bf16[128,1792]{1,0:T(8,128)(2,1)} %features_ref.1) | copy-start | bytes 1376260
  4.9 28.9 %all-to-all-start = ((bf16[8,144,256]{2,1,0:T(8,128)(2,1)}), bf16[8,144,256]{2,1,0:T(8,128)(2,1)S(1)}, u32[]{:S(2)}, u32[]{:S(2)}) async-start(bf16[8,144,256]{2,1,0:T(8,128)(2,1)} %get-tuple-element.31), calls=%async_computation | async-start | bytes 1179648 | tf_op jit(solution)/shard_map/all_to_all | solution.py:404
  15.3 18.6 %collective-permute-start = (bf16[128,256]{1,0:T(8,128)(2,1)S(1)}, bf16[128,256]{1,0:T(8,128)(2,1)S(1)}, u32[]{:S(2)}, u32[]{:S(2)}) collective-permute-start(bf16[128,256]{1,0:T(8,128)(2,1)S(1)} %slice_select_fusion), channel_id=1, source_target_pairs={{0,1},{1,0},{2,3},{3,2},{4,5},{5,4},{6,7},{7,6},{8,9},{9,8},{10,11... | collective-permute-start | bytes 196616 | tf_op jit(solution)/shard_map/ppermute | solution.py:93
  17.3 22.7 %collective-permute-start.3 = (bf16[144,256]{1,0:T(8,128)(2,1)}, bf16[144,256]{1,0:T(8,128)(2,1)S(1)}, u32[]{:S(2)}, u32[]{:S(2)}) collective-permute-start(bf16[144,256]{1,0:T(8,128)(2,1)} %get-tuple-element.37), channel_id=1, source_target_pairs={{248,256},{249,257},{250,258},{251,259},{252,260},{253,261},{254,2... | collective-permute-start | bytes 221192 | tf_op jit(solution)/shard_map/ppermute | solution.py:53
  30.1 15.1 %collective-permute-start.4 = (bf16[144,256]{1,0:T(8,128)(2,1)}, bf16[144,256]{1,0:T(8,128)(2,1)S(1)}, u32[]{:S(2)}, u32[]{:S(2)}) collective-permute-start(bf16[144,256]{1,0:T(8,128)(2,1)} %get-tuple-element.38), channel_id=1, source_target_pairs={{248,257},{249,256},{250,259},{251,258},{252,261},{253,260},{254,2... | collective-permute-start | bytes 221192 | tf_op jit(solution)/shard_map/ppermute | solution.py:54
  33.8 31.3 %copy-start.18 = (bf16[128,256]{1,0:T(8,128)(2,1)}, bf16[128,256]{1,0:T(8,128)(2,1)S(1)}, u32[]{:S(2)}) copy-start(bf16[128,256]{1,0:T(8,128)(2,1)S(1)} %collective-permute-done.up_other_ref) | copy-start | bytes 196612
  33.8 26.2 %copy-start.8 = (bf16[8,144,256]{2,1,0:T(8,128)(2,1)}, bf16[8,144,256]{2,1,0:T(8,128)(2,1)S(1)}, u32[]{:S(2)}) copy-start(bf16[8,144,256]{2,1,0:T(8,128)(2,1)S(1)} %all-to-all-done.own_ref.refs_0_) | copy-start | bytes 1769476
  33.8 34.0 %collective-permute-start.1 = (bf16[8,144,256]{2,1,0:T(8,128)(2,1)S(1)}, bf16[8,144,256]{2,1,0:T(8,128)(2,1)S(1)}, u32[]{:S(2)}, u32[]{:S(2)}) collective-permute-start(bf16[8,144,256]{2,1,0:T(8,128)(2,1)S(1)} %all-to-all-done.own_ref.refs_0_), channel_id=1, source_target_pairs={{0,8},{8,16},{16,24},{24,32},{32,40},{40,48},{48,56},{56,64},{64,7... | collective-permute-start | bytes 1769480 | tf_op jit(solution)/shard_map/ppermute | solution.py:89
  35.2 32.7 %collective-permute-start.2 = (bf16[8,144,256]{2,1,0:T(8,128)(2,1)S(1)}, bf16[8,144,256]{2,1,0:T(8,128)(2,1)S(1)}, u32[]{:S(2)}, u32[]{:S(2)}) collective-permute-start(bf16[8,144,256]{2,1,0:T(8,128)(2,1)S(1)} %all-to-all-done.own_ref.refs_0_), channel_id=1, source_target_pairs={{8,0},{16,8},{24,16},{32,24},{40,32},{48,40},{56,48},{64,56},{72,6... | collective-permute-start | bytes 1769480 | tf_op jit(solution)/shard_map/ppermute | solution.py:89
  45.2 19.9 %copy-start.7 = (bf16[2,144,256]{2,1,0:T(8,128)(2,1)}, bf16[2,144,256]{2,1,0:T(8,128)(2,1)S(1)}, u32[]{:S(2)}) copy-start(bf16[2,144,256]{2,1,0:T(8,128)(2,1)S(1)} %pad_maximum_fusion.refs_2_.refs_3_) | copy-start | bytes 442372
  45.2 22.6 %collective-permute-start.5 = (bf16[2,144,256]{2,1,0:T(8,128)(2,1)S(1)}, bf16[2,144,256]{2,1,0:T(8,128)(2,1)S(1)}, u32[]{:S(2)}, u32[]{:S(2)}) collective-permute-start(bf16[2,144,256]{2,1,0:T(8,128)(2,1)S(1)} %pad_maximum_fusion.refs_2_.refs_3_), channel_id=1, source_target_pairs={{248,250},{249,251},{250,248},{251,249},{252,254},{253,255},{254,2... | collective-permute-start | bytes 442376 | tf_op jit(solution)/shard_map/ppermute | solution.py:64
  49.2 18.6 %collective-permute-start.6 = (bf16[2,144,256]{2,1,0:T(8,128)(2,1)S(1)}, bf16[2,144,256]{2,1,0:T(8,128)(2,1)S(1)}, u32[]{:S(2)}, u32[]{:S(2)}) collective-permute-start(bf16[2,144,256]{2,1,0:T(8,128)(2,1)S(1)} %pad_maximum_fusion.refs_2_.refs_3_), channel_id=1, source_target_pairs={{248,252},{249,253},{250,254},{251,255},{252,248},{253,249},{254,2... | collective-permute-start | bytes 442376 | tf_op jit(solution)/shard_map/ppermute | solution.py:64
  53.6 14.3 %collective-permute-start.7 = (bf16[2,144,256]{2,1,0:T(8,128)(2,1)S(1)}, bf16[2,144,256]{2,1,0:T(8,128)(2,1)S(1)}, u32[]{:S(2)}, u32[]{:S(2)}) collective-permute-start(bf16[2,144,256]{2,1,0:T(8,128)(2,1)S(1)} %pad_maximum_fusion.refs_2_.refs_3_), channel_id=1, source_target_pairs={{248,254},{249,255},{250,252},{251,253},{252,250},{253,251},{254,2... | collective-permute-start | bytes 442376 | tf_op jit(solution)/shard_map/ppermute | solution.py:64
  55.8 20.6 %all-to-all-start.2 = ((bf16[4,448,128]{2,1,0:T(8,128)(2,1)}), bf16[4,448,128]{2,1,0:T(8,128)(2,1)S(1)}, u32[]{:S(2)}, u32[]{:S(2)}) async-start(bf16[4,448,128]{2,1,0:T(8,128)(2,1)} %bitcast.9), calls=%async_computation.2 | async-start | bytes 917504 | tf_op jit(solution)/shard_map/all_to_all | solution.py:414
  67.8 0.7 copy-start.14
  67.8 0.7 copy-start.15
  67.8 0.7 copy-start.16
  67.9 0.9 copy-start.5
  67.9 1.2 copy-start.6
  76.4 21.3 %copy-start.3 = (bf16[4,448,128]{2,1,0:T(8,128)(2,1)}, bf16[4,448,128]{2,1,0:T(8,128)(2,1)S(1)}, u32[]{:S(2)}) copy-start(bf16[4,448,128]{2,1,0:T(8,128)(2,1)S(1)} %all-to-all-done.2.feats_ref) | copy-start | bytes 1376260
  76.4 23.7 %all-to-all-start.1 = ((bf16[4,2,128,256]{3,2,1,0:T(8,128)(2,1)}), bf16[4,2,128,256]{3,2,1,0:T(8,128)(2,1)S(1)}, u32[]{:S(2)}, u32[]{:S(2)}) async-start(bf16[4,2,128,256]{3,2,1,0:T(8,128)(2,1)} %get-tuple-element.42), calls=%async_computation.1 | async-start | bytes 1048576 | tf_op jit(solution)/shard_map/all_to_all | solution.py:424
  80.6 17.2 %copy-start.20 = (f32[1,256]{1,0:T(1,128)S(1)}, f32[1,256]{1,0:T(1,128)}, u32[]{:S(2)}) copy-start(f32[1,256]{1,0:T(1,128)} %get-tuple-element.45) | copy-start | bytes 3076
  80.6 17.2 %collective-permute-start.8 = (bf16[2,128,256]{2,1,0:T(8,128)(2,1)}, bf16[2,128,256]{2,1,0:T(8,128)(2,1)S(1)}, u32[]{:S(2)}, u32[]{:S(2)}) collective-permute-start(bf16[2,128,256]{2,1,0:T(8,128)(2,1)} %get-tuple-element.41), channel_id=1, source_target_pairs={{248,256},{249,257},{250,258},{251,259},{252,260},{253,261},{254,2... | collective-permute-start | bytes 393224 | tf_op jit(solution)/shard_map/ppermute | solution.py:53
  84.8 25.2 %collective-permute-start.9 = (bf16[4,448,128]{2,1,0:T(8,128)(2,1)S(1)}, bf16[4,448,128]{2,1,0:T(8,128)(2,1)S(1)}, u32[]{:S(2)}, u32[]{:S(2)}) collective-permute-start(bf16[4,448,128]{2,1,0:T(8,128)(2,1)S(1)} %all-to-all-done.2.feats_ref), channel_id=1, source_target_pairs={{0,1},{1,0},{2,3},{3,2},{4,5},{5,4},{6,7},{7,6},{8,9},{9,8},{10,11... | collective-permute-start | bytes 1376264 | tf_op jit(solution)/shard_map/ppermute | solution.py:93
  97.8 20.1 %copy-start.17 = (bf16[2,128,256]{2,1,0:T(8,128)(2,1)}, bf16[2,128,256]{2,1,0:T(8,128)(2,1)S(1)}, u32[]{:S(2)}) copy-start(bf16[2,128,256]{2,1,0:T(8,128)(2,1)S(1)} %collective-permute-done.8.refs_2_) | copy-start | bytes 393220
  100.1 13.2 %copy-start.12 = (bf16[4,2,128,256]{3,2,1,0:T(8,128)(2,1)}, bf16[4,2,128,256]{3,2,1,0:T(8,128)(2,1)S(1)}, u32[]{:S(2)}) copy-start(bf16[4,2,128,256]{3,2,1,0:T(8,128)(2,1)S(1)} %all-to-all-done.1) | copy-start | bytes 1572868
  100.1 17.9 %collective-permute-start.10 = (bf16[8,128,256]{2,1,0:T(8,128)(2,1)S(1)}, bf16[8,128,256]{2,1,0:T(8,128)(2,1)S(1)}, u32[]{:S(2)}, u32[]{:S(2)}) collective-permute-start(bf16[8,128,256]{2,1,0:T(8,128)(2,1)S(1)} %bitcast.20), channel_id=1, source_target_pairs={{0,8},{8,16},{16,24},{24,32},{32,40},{40,48},{48,56},{56,64},{64,7... | collective-permute-start | bytes 1572872 | tf_op jit(solution)/shard_map/ppermute | solution.py:89
  101.4 16.6 %collective-permute-start.11 = (bf16[8,128,256]{2,1,0:T(8,128)(2,1)S(1)}, bf16[8,128,256]{2,1,0:T(8,128)(2,1)S(1)}, u32[]{:S(2)}, u32[]{:S(2)}) collective-permute-start(bf16[8,128,256]{2,1,0:T(8,128)(2,1)S(1)} %bitcast.21), channel_id=1, source_target_pairs={{8,0},{16,8},{24,16},{32,24},{40,32},{48,40},{56,48},{64,56},{72,6... | collective-permute-start | bytes 1572872 | tf_op jit(solution)/shard_map/ppermute | solution.py:89
  103.4 14.5 %collective-permute-start.12 = (bf16[2,128,256]{2,1,0:T(8,128)(2,1)S(1)}, bf16[2,128,256]{2,1,0:T(8,128)(2,1)}, u32[]{:S(2)}, u32[]{:S(2)}) collective-permute-start(bf16[2,128,256]{2,1,0:T(8,128)(2,1)S(1)} %collective-permute-done.8.refs_2_), channel_id=1, source_target_pairs={{248,250},{249,251},{250,248},{251,249},{252,254},{253,255},{254,2... | collective-permute-start | bytes 393224 | tf_op jit(solution)/shard_map/ppermute | solution.py:64
  105.3 12.6 %collective-permute-start.13 = (bf16[2,128,256]{2,1,0:T(8,128)(2,1)S(1)}, bf16[2,128,256]{2,1,0:T(8,128)(2,1)}, u32[]{:S(2)}, u32[]{:S(2)}) collective-permute-start(bf16[2,128,256]{2,1,0:T(8,128)(2,1)S(1)} %collective-permute-done.8.refs_2_), channel_id=1, source_target_pairs={{248,252},{249,253},{250,254},{251,255},{252,248},{253,249},{254,2... | collective-permute-start | bytes 393224 | tf_op jit(solution)/shard_map/ppermute | solution.py:64
  110.0 3.3 %copy-start.13 = (bf16[4,448,128]{2,1,0:T(8,128)(2,1)}, bf16[4,448,128]{2,1,0:T(8,128)(2,1)S(1)}, u32[]{:S(2)}) copy-start(bf16[4,448,128]{2,1,0:T(8,128)(2,1)S(1)} %collective-permute-done.9.feats_other_ref) | copy-start | bytes 1376260
  110.1 7.9 %collective-permute-start.14 = (bf16[2,128,256]{2,1,0:T(8,128)(2,1)S(1)}, bf16[2,128,256]{2,1,0:T(8,128)(2,1)}, u32[]{:S(2)}, u32[]{:S(2)}) collective-permute-start(bf16[2,128,256]{2,1,0:T(8,128)(2,1)S(1)} %collective-permute-done.8.refs_2_), channel_id=1, source_target_pairs={{248,254},{249,255},{250,252},{251,253},{252,250},{253,251},{254,2... | collective-permute-start | bytes 393224 | tf_op jit(solution)/shard_map/ppermute | solution.py:64
  117.9 28.5 %copy-start = (bf16[1792,512]{1,0:T(8,128)(2,1)S(1)}, bf16[1792,512]{1,0:T(8,128)(2,1)}, u32[]{:S(2)}) copy-start(bf16[1792,512]{1,0:T(8,128)(2,1)} %weight_ref.1) | copy-start | bytes 5505028
  118.0 0.8 copy-start.9
  118.8 0.8 copy-start.10
  126.8 24.4 %all-to-all-start.3 = ((bf16[64,16,128]{2,1,0:T(8,128)(2,1)}), bf16[64,16,128]{2,1,0:T(8,128)(2,1)S(1)}, u32[]{:S(2)}, u32[]{:S(2)}) async-start(bf16[64,16,128]{2,1,0:T(8,128)(2,1)} %get-tuple-element.48), calls=%async_computation.3 | async-start | bytes 524288 | tf_op jit(solution)/shard_map/all_to_all | solution.py:449
  137.1 7.7 %collective-permute-start.16 = (bf16[128,256]{1,0:T(8,128)(2,1)}, bf16[128,256]{1,0:T(8,128)(2,1)S(1)}, u32[]{:S(2)}, u32[]{:S(2)}) collective-permute-start(bf16[128,256]{1,0:T(8,128)(2,1)} %get-tuple-element.52), channel_id=1, source_target_pairs={{0,1},{1,0},{2,3},{3,2},{4,5},{5,4},{6,7},{7,6},{8,9},{9,8},{10,11... | collective-permute-start | bytes 196616 | tf_op jit(solution)/shard_map/ppermute | solution.py:93
  142.9 3.5 %collective-permute-start.15 = (bf16[128,256]{1,0:T(8,128)(2,1)}, bf16[128,256]{1,0:T(8,128)(2,1)S(1)}, u32[]{:S(2)}, u32[]{:S(2)}) collective-permute-start(bf16[128,256]{1,0:T(8,128)(2,1)} %get-tuple-element.50), channel_id=1, source_target_pairs={{0,1},{1,0},{2,3},{3,2},{4,5},{5,4},{6,7},{7,6},{8,9},{9,8},{10,11... | collective-permute-start | bytes 196616 | tf_op jit(solution)/shard_map/ppermute | solution.py:93
  191.0 8.4 %copy-start.1 = (bf16[4,64,16,128]{3,2,1,0:T(8,128)(2,1)}, bf16[4,64,16,128]{3,2,1,0:T(8,128)(2,1)S(1)}, u32[]{:S(2)}) copy-start(bf16[4,64,16,128]{3,2,1,0:T(8,128)(2,1)S(1)} %all_to_all.31.mine_ref) | copy-start | bytes 3145732
  191.0 8.4 %collective-permute-start.17 = (bf16[4,64,16,128]{3,2,1,0:T(8,128)(2,1)S(1)}, bf16[4,64,16,128]{3,2,1,0:T(8,128)(2,1)S(1)}, u32[]{:S(2)}, u32[]{:S(2)}) collective-permute-start(bf16[4,64,16,128]{3,2,1,0:T(8,128)(2,1)S(1)} %all_to_all.31.mine_ref), channel_id=1, source_target_pairs={{0,1},{1,0},{2,3},{3,2},{4,5},{5,4},{6,7},{7,6},{8,9},{9,8},{10,11... | collective-permute-start | bytes 3145736 | tf_op jit(solution)/shard_map/ppermute | solution.py:93
  199.4 1.0 copy-start.4

commit v8 on v7

--- a/solution.py
+++ b/solution.py
@@ -48,8 +48,8 @@
 
 def across(same, cross):
     pairs = [(a, b, r, c) for a, b in FAR for r in range(RUN) for c in range(2)]
-    straight = [(device(a, r, c), device(b, r, c)) for a, b, r, c in pairs]
-    turned = [(device(a, r, c), device(b, r, 1 - c)) for a, b, r, c in pairs]
+    straight = [(device(a, r, c), device(b, 3 - r, c)) for a, b, r, c in pairs]
+    turned = [(device(a, r, c), device(b, 3 - r, 1 - c)) for a, b, r, c in pairs]
     got = lax.ppermute(same, AXES, straight)
     return got if cross is None else (got, lax.ppermute(cross, AXES, turned))
 
@@ -152,8 +152,9 @@
         live = jnp.where(block < DEAD, 1.0, 0.0)
         degree_ref[core * TILE : core * TILE + TILE, :] = 1.0 + jnp.sum(live, axis=1, keepdims=True)
         reach_of = lax.shift_right_logical(block, 3)
-        low_twist = jnp.where(reach_of == 0, ids_ref[3] * run * 2, 0)
-        twist = low_twist + jnp.where(reach_of == 2, ids_ref[4] * run * 2, 0)
+        turn = jnp.bitwise_xor(run, 3) * 2
+        low_twist = jnp.where(reach_of == 0, ids_ref[3] * turn, 0)
+        twist = low_twist + jnp.where(reach_of == 2, ids_ref[4] * turn, 0)
         block = jnp.bitwise_xor(block, twist)
         digits = [digits_of(block, reach) for reach in range(REACH)]
         lanes = lax.broadcasted_iota(i32, (16, 128), 1)
@@ -323,10 +324,11 @@
     other_ref[...] = round_ref[run * 2 + 1 - core]
     part = jnp.zeros((F_RUN, HALF), f32)
     for feats, side in ((feats_ref, core), (feats_other_ref, 1 - core)):
-        for k in range(RUN):
-            part = part + jnp.dot(
-                feats[k], round_ref[k * 2 + side], preferred_element_type=f32
-            )
+        part = part + jnp.dot(
+            jnp.concatenate([feats[k] for k in range(RUN)], axis=1),
+            jnp.concatenate([round_ref[k * 2 + side] for k in range(RUN)], axis=0),
+            preferred_element_type=f32,
+        )
     part = part.astype(bf16)
     for row in range(F_RUN // 16):
         for lane in range(2):

time: 205 us -> 201 us (0.980)
  starting transfers between devices: 93.8 us -> 90.7 us
  waiting for transfers between devices: 19.3 us -> 22 us
  blocking collectives: 39.4 us -> 37 us
    ppermute x5, starting transfers between devices: 20 us -> 16.3 us  [swap_core(): return lax.ppermute(block, 'c', [(0, 1), (1, 0)])]
    ppermute x2, waiting for transfers between devices: 3.53 us -> 0.01 us  [across(): got = lax.ppermute(same, AXES, straight)]
    all_to_all x1, waiting for transfers between devices: 2.39 us -> 5.58 us  [on_device(): terms = lax.all_to_all(slabs, WIDE, 0, 0)]
    ppermute x6, waiting for transfers between devices: 0.1 us -> 3.01 us  [along_run(): parts.append(lax.ppermute(block, AXES, pairs))]
    ppermute x2, starting transfers between devices: 17 us -> 19.6 us  [across(): got = lax.ppermute(same, AXES, straight)]
    all_to_all x2, blocking collectives: 39.4 us -> 37 us  [spread_to(): lax.all_to_all(jnp.broadcast_to(shard[None], (count,) + shard.shape), axe...]
    all_to_all x1, waiting for transfers between devices: 2.32 us -> 0.01 us  [on_device(): own = lax.all_to_all(scaled_copies, 'yl', 0, 0)]
  transfers between devices with their start and end apart: 22 -> 22, of which waited for: 7 -> 5; matrix products, arithmetic and copies ran while one was open for 3% -> 3% of each run, Pallas kernels for 12% -> 12%
where the time goes in v8:
time: 201 us; the launch traced here: 200 us
  starting transfers between devices  90.7 us (45%)
  Pallas kernels  37.5 us (19%)
  blocking collectives  37 us (18%)
  waiting for transfers between devices  22 us (11%)
  local copies, waits for them, and re-layouts  5.63 us (3%)
  other arithmetic  3.03 us (2%)
  matrix products  2.4 us (1%)
    all_to_all x2, blocking collectives, spread_to(): lax.all_to_all(jnp.broadcast_to(shard[None], (count,) + shard.shape), axe...  37 us
    ppermute x6, starting transfers between devices, along_run(): parts.append(lax.ppermute(block, AXES, pairs))  20.2 us
    ppermute x2, starting transfers between devices, across(): got = lax.ppermute(same, AXES, straight)  19.6 us
    ppermute x5, starting transfers between devices, swap_core(): return lax.ppermute(block, 'c', [(0, 1), (1, 0)])  16.3 us
    all_to_all x1, starting transfers between devices, on_device(): own = lax.all_to_all(copies, ('yl', 'c'), 0, 0)  10.3 us
    all_to_all x1, starting transfers between devices, on_device(): terms = lax.all_to_all(slabs, WIDE, 0, 0)  10.2 us
    pallas_call x1, Pallas kernels, backward_counts(): pl.pallas_call(backward_counts_kernel, in_specs=[SMEM_SPEC] + [VMEM_SPEC]...  8.72 us
    pallas_call x1, Pallas kernels, backward_math(): pl.pallas_call(backward_kernel, in_specs=[SMEM_SPEC] + [VMEM_SPEC] * (4 +...  6.54 us
  transfers between devices with their start and end apart: 22, of which 5 were waited for; matrix products, arithmetic and copies ran while one was open for 3% of the time, Pallas kernels for 12%

profile of v8, /device:TPU:1, one launch (start us, length us, event | category | flops | bytes accessed | tf_op | source)
XLA Modules:
  0.0 200.0 jit_solution(12339786851772503696)
XLA Ops:
  0.6 0.0 copy-start.11
  1.3 0.6 stack.40.ids_ref
  1.9 3.0 %project.1 = (bf16[8,144,256]{2,1,0:T(8,128)(2,1)}, bf16[144,256]{1,0:T(8,128)(2,1)}, bf16[144,256]{1,0:T(8,128)(2,1)}) custom-call(s32[5]{0:T(128)} %stack.40.ids_ref, s32[1]{0:T(128)S(6)} %copy.14.count_ref, s32[1,24]{1,0:T(1,128)} %tiles_ref.1, s32[15,128]{1,0:T(8,128)} %bitcast.23, s32[15,128]{1,0:T(8,128)} %bitcast.24, s32[15,128]{1,0:T(8,128)} %bitcast.25, ...), custom_call_target="tpu_custom_call" | custom-call | tf_op jit(solution)/shard_map/project/pallas_call | solution.py:129
  4.9 10.3 %all-to-all-start = ((bf16[8,144,256]{2,1,0:T(8,128)(2,1)}), bf16[8,144,256]{2,1,0:T(8,128)(2,1)S(1)}, u32[]{:S(2)}, u32[]{:S(2)}) async-start(bf16[8,144,256]{2,1,0:T(8,128)(2,1)} %get-tuple-element.31), calls=%async_computation | async-start | bytes 1179648 | tf_op jit(solution)/shard_map/all_to_all | solution.py:406
  15.3 2.0 %collective-permute-start = (bf16[128,256]{1,0:T(8,128)(2,1)S(1)}, bf16[128,256]{1,0:T(8,128)(2,1)S(1)}, u32[]{:S(2)}, u32[]{:S(2)}) collective-permute-start(bf16[128,256]{1,0:T(8,128)(2,1)S(1)} %slice_select_fusion), channel_id=1, source_target_pairs={{0,1},{1,0},{2,3},{3,2},{4,5},{5,4},{6,7},{7,6},{8,9},{9,8},{10,11... | collective-permute-start | bytes 196616 | tf_op jit(solution)/shard_map/ppermute | solution.py:93
  17.3 13.2 %collective-permute-start.3 = (bf16[144,256]{1,0:T(8,128)(2,1)}, bf16[144,256]{1,0:T(8,128)(2,1)S(1)}, u32[]{:S(2)}, u32[]{:S(2)}) collective-permute-start(bf16[144,256]{1,0:T(8,128)(2,1)} %get-tuple-element.37), channel_id=1, source_target_pairs={{248,262},{249,263},{250,260},{251,261},{252,258},{253,259},{254,2... | collective-permute-start | bytes 221192 | tf_op jit(solution)/shard_map/ppermute | solution.py:53
  30.5 2.0 collective-permute-start.4
  32.5 0.6 slice_select_fusion.1
  33.1 1.0 copy.13
  34.1 1.3 collective-permute-start.1
  35.4 1.3 collective-permute-start.2
  36.7 0.0 collective-permute-done.3
  36.7 5.7 %collective-permute-done.4 = bf16[144,256]{1,0:T(8,128)(2,1)S(1)} collective-permute-done((bf16[144,256]{1,0:T(8,128)(2,1)}, bf16[144,256]{1,0:T(8,128)(2,1)S(1)}, u32[]{:S(2)}, u32[]{:S(2)}) %collective-permute-start.4) | collective-permute-done | bytes 73760 | tf_op jit(solution)/shard_map/ppermute | solution.py:54
  42.5 4.9 %collective-permute-start.5 = (bf16[2,144,256]{2,1,0:T(8,128)(2,1)S(1)}, bf16[2,144,256]{2,1,0:T(8,128)(2,1)S(1)}, u32[]{:S(2)}, u32[]{:S(2)}) collective-permute-start(bf16[2,144,256]{2,1,0:T(8,128)(2,1)S(1)} %pad_maximum_fusion.refs_2_.refs_3_), channel_id=1, source_target_pairs={{248,250},{249,251},{250,248},{251,249},{252,254},{253,255},{254,2... | collective-permute-start | bytes 442376 | tf_op jit(solution)/shard_map/ppermute | solution.py:64
  47.4 1.9 collective-permute-start.6
  49.3 4.0 %collective-permute-start.7 = (bf16[2,144,256]{2,1,0:T(8,128)(2,1)S(1)}, bf16[2,144,256]{2,1,0:T(8,128)(2,1)S(1)}, u32[]{:S(2)}, u32[]{:S(2)}) collective-permute-start(bf16[2,144,256]{2,1,0:T(8,128)(2,1)S(1)} %pad_maximum_fusion.refs_2_.refs_3_), channel_id=1, source_target_pairs={{248,254},{249,255},{250,252},{251,253},{252,250},{253,251},{254,2... | collective-permute-start | bytes 442376 | tf_op jit(solution)/shard_map/ppermute | solution.py:64
  53.3 3.5 %all-to-all-start.2 = ((bf16[4,448,128]{2,1,0:T(8,128)(2,1)}), bf16[4,448,128]{2,1,0:T(8,128)(2,1)S(1)}, u32[]{:S(2)}, u32[]{:S(2)}) async-start(bf16[4,448,128]{2,1,0:T(8,128)(2,1)} %bitcast.9), calls=%async_computation.2 | async-start | bytes 917504 | tf_op jit(solution)/shard_map/all_to_all | solution.py:416
  56.8 5.1 %forward_counts.1 = (bf16[256,3072]{1,0:T(8,128)(2,1)}, f32[256,1]{1,0:T(8,128)}) custom-call(s32[5]{0:T(128)} %stack.40.ids_ref, bf16[8,144,256]{2,1,0:T(8,128)(2,1)} %copy-done.8), custom_call_target="tpu_custom_call" | custom-call | flops 4000000000 | bytes 8000000 | tf_op jit(solution)/shard_map/forward_counts/pallas_call | solution.py:176
  61.9 2.7 %forward_own.1.total_ref = f32[256,256]{1,0:T(8,128)} custom-call(s32[5]{0:T(128)} %stack.40.ids_ref, bf16[256,3072]{1,0:T(8,128)(2,1)} %get-tuple-element.34.counts_ref, bf16[8,144,256]{2,1,0:T(8,128)(2,1)} %copy-done.8), custom_call_target="tpu_custom_call" | custom-call | flops 4000000000 | bytes 8000000 | tf_op jit(solution)/shard_map/forward_own/pallas_call | solution.py:233
  64.6 0.0 collective-permute-done.5.refs_3_.refs_4_
  64.6 0.0 collective-permute-done.6.refs_4_.refs_5_
  64.6 0.0 collective-permute-done.1.refs_0_.refs_1_
  64.6 0.0 collective-permute-done.2.refs_1_.refs_2_
  64.7 0.6 copy-done.14
  65.2 0.1 copy-done.15
  65.3 0.1 copy-done.16
  65.3 0.2 copy-done.5
  65.6 0.3 copy-done.6
  65.8 3.8 %forward_math.1 = (bf16[128,256]{1,0:T(8,128)(2,1)}, bf16[128,256]{1,0:T(8,128)(2,1)}, bf16[4,2,128,256]{3,2,1,0:T(8,128)(2,1)}, bf16[2,128,256]{2,1,0:T(8,128)(2,1)}, f32[1,256]{1,0:T(1,128)}) custom-call(s32[5]{0:T(128)} %stack.40.ids_ref, bf16[256,3072]{1,0:T(8,128)(2,1)} %get-tuple-element.34.counts_ref, f32[256,256]{1,0:T(8,128)} %forward_own.1.total_ref, ...), custom_call_target="tpu_custom_call" | custom-call | tf_op jit(solution)/shard_map/forward_math/pallas_call | solution.py:295
  69.7 5.4 %all-to-all-done.2.feats_ref = bf16[4,448,128]{2,1,0:T(8,128)(2,1)S(1)} async-done(((bf16[4,448,128]{2,1,0:T(8,128)(2,1)}), bf16[4,448,128]{2,1,0:T(8,128)(2,1)S(1)}, u32[]{:S(2)}, u32[]{:S(2)}) %all-to-all-start.2) | async-done | bytes 458784 | tf_op jit(solution)/shard_map/all_to_all | solution.py:416
  75.0 3.5 %all-to-all-start.1 = ((bf16[4,2,128,256]{3,2,1,0:T(8,128)(2,1)}), bf16[4,2,128,256]{3,2,1,0:T(8,128)(2,1)S(1)}, u32[]{:S(2)}, u32[]{:S(2)}) async-start(bf16[4,2,128,256]{3,2,1,0:T(8,128)(2,1)} %get-tuple-element.42), calls=%async_computation.1 | async-start | bytes 1048576 | tf_op jit(solution)/shard_map/all_to_all | solution.py:426
  78.5 0.1 pad.13.clone
  78.6 6.3 %collective-permute-start.8 = (bf16[2,128,256]{2,1,0:T(8,128)(2,1)}, bf16[2,128,256]{2,1,0:T(8,128)(2,1)S(1)}, u32[]{:S(2)}, u32[]{:S(2)}) collective-permute-start(bf16[2,128,256]{2,1,0:T(8,128)(2,1)} %get-tuple-element.41), channel_id=1, source_target_pairs={{248,262},{249,263},{250,260},{251,261},{252,258},{253,259},{254,2... | collective-permute-start | bytes 393224 | tf_op jit(solution)/shard_map/ppermute | solution.py:53
  85.0 3.4 %collective-permute-start.9 = (bf16[4,448,128]{2,1,0:T(8,128)(2,1)S(1)}, bf16[4,448,128]{2,1,0:T(8,128)(2,1)S(1)}, u32[]{:S(2)}, u32[]{:S(2)}) collective-permute-start(bf16[4,448,128]{2,1,0:T(8,128)(2,1)S(1)} %all-to-all-done.2.feats_ref), channel_id=1, source_target_pairs={{0,1},{1,0},{2,3},{3,2},{4,5},{5,4},{6,7},{7,6},{8,9},{9,8},{10,11... | collective-permute-start | bytes 1376264 | tf_op jit(solution)/shard_map/ppermute | solution.py:93
  88.4 8.7 %backward_counts.1.counts_ref = bf16[1024,3072]{1,0:T(8,128)(2,1)} custom-call(s32[5]{0:T(128)} %stack.40.ids_ref, bf16[8,144,256]{2,1,0:T(8,128)(2,1)} %copy-done.8, bf16[8,144,256]{2,1,0:T(8,128)(2,1)} %copy-done.5, bf16[8,144,256]{2,1,0:T(8,128)(2,1)} %copy-done.6, bf16[2,144,256]{2,1,0:T(8,128)(2,1)} %copy-done.7, bf16[2,144,256]{2,1,0:T(8,128)(2,1)} %copy-done.14, ...), custom_call_target="tpu_custom_call" | custom-call | flops 4000000000 | bytes 8000000 | tf_op jit(solution)/shard_map/backward_counts/pallas_call | solution.py:208
  97.1 0.0 copy-start.17
  97.1 0.0 all-to-all-done.1
  97.1 1.3 collective-permute-start.10
  98.5 1.3 collective-permute-start.11
  99.8 0.7 maximum_maximum_fusion.bias_ref
  100.4 3.1 %collective-permute-start.12 = (bf16[2,128,256]{2,1,0:T(8,128)(2,1)S(1)}, bf16[2,128,256]{2,1,0:T(8,128)(2,1)}, u32[]{:S(2)}, u32[]{:S(2)}) collective-permute-start(bf16[2,128,256]{2,1,0:T(8,128)(2,1)S(1)} %collective-permute-done.8.refs_2_), channel_id=1, source_target_pairs={{248,250},{249,251},{250,248},{251,249},{252,254},{253,255},{254,2... | collective-permute-start | bytes 393224 | tf_op jit(solution)/shard_map/ppermute | solution.py:64
  103.5 1.9 collective-permute-start.13
  105.5 4.4 %collective-permute-start.14 = (bf16[2,128,256]{2,1,0:T(8,128)(2,1)S(1)}, bf16[2,128,256]{2,1,0:T(8,128)(2,1)}, u32[]{:S(2)}, u32[]{:S(2)}) collective-permute-start(bf16[2,128,256]{2,1,0:T(8,128)(2,1)S(1)} %collective-permute-done.8.refs_2_), channel_id=1, source_target_pairs={{248,254},{249,255},{250,252},{251,253},{252,250},{253,251},{254,2... | collective-permute-start | bytes 393224 | tf_op jit(solution)/shard_map/ppermute | solution.py:64
  109.9 4.5 %backward_own.1.total_ref = f32[1024,256]{1,0:T(8,128)} custom-call(bf16[1024,3072]{1,0:T(8,128)(2,1)} %backward_counts.1.counts_ref, bf16[8,128,256]{2,1,0:T(8,128)(2,1)} %bitcast.22), custom_call_target="tpu_custom_call" | custom-call | flops 4000000000 | bytes 8000000 | tf_op jit(solution)/shard_map/backward_own/pallas_call | solution.py:251
  114.5 3.0 %collective-permute-done.13.refs_4_ = bf16[2,128,256]{2,1,0:T(8,128)(2,1)} collective-permute-done((bf16[2,128,256]{2,1,0:T(8,128)(2,1)S(1)}, bf16[2,128,256]{2,1,0:T(8,128)(2,1)}, u32[]{:S(2)}, u32[]{:S(2)}) %collective-permute-start.13) | collective-permute-done | bytes 131104 | tf_op jit(solution)/shard_map/ppermute | solution.py:64
  117.5 0.0 collective-permute-done.10.refs_0_
  117.5 0.8 copy-done.9
  118.3 0.8 copy-done.10
  119.1 6.5 %backward_math.1 = (bf16[128,256]{1,0:T(8,128)(2,1)}, bf16[128,256]{1,0:T(8,128)(2,1)}, bf16[64,16,128]{2,1,0:T(8,128)(2,1)}) custom-call(s32[5]{0:T(128)} %stack.40.ids_ref, bf16[1024,3072]{1,0:T(8,128)(2,1)} %backward_counts.1.counts_ref, f32[1024,256]{1,0:T(8,128)} %backward_own.1.total_ref, bf16[16,128]{1,0:T(8,128)(2,1)} %maximum_maximum_fusion.bias_ref, ...), custom_call_target="tpu_custom_call" | custom-call | tf_op jit(solution)/shard_map/backward_math/pallas_call | solution.py:342
  125.7 10.2 %all-to-all-start.3 = ((bf16[64,16,128]{2,1,0:T(8,128)(2,1)}), bf16[64,16,128]{2,1,0:T(8,128)(2,1)S(1)}, u32[]{:S(2)}, u32[]{:S(2)}) async-start(bf16[64,16,128]{2,1,0:T(8,128)(2,1)} %get-tuple-element.48), calls=%async_computation.3 | async-start | bytes 524288 | tf_op jit(solution)/shard_map/all_to_all | solution.py:451
  135.8 2.8 %collective-permute-start.16 = (bf16[128,256]{1,0:T(8,128)(2,1)}, bf16[128,256]{1,0:T(8,128)(2,1)S(1)}, u32[]{:S(2)}, u32[]{:S(2)}) collective-permute-start(bf16[128,256]{1,0:T(8,128)(2,1)} %get-tuple-element.52), channel_id=1, source_target_pairs={{0,1},{1,0},{2,3},{3,2},{4,5},{5,4},{6,7},{7,6},{8,9},{9,8},{10,11... | collective-permute-start | bytes 196616 | tf_op jit(solution)/shard_map/ppermute | solution.py:93
  138.6 1.9 collective-permute-start.15
  140.6 1.6 maximum_select_fusion.2
  142.2 2.4 %convolution_convert_fusion = bf16[128,1792]{1,0:T(8,128)(2,1)} fusion(bf16[1792,512]{1,0:T(8,128)(2,1)S(1)} %copy-done, bf16[128,256]{1,0:T(8,128)(2,1)S(1)} %collective-permute-done.15, bf16[128,256]{1,0:T(8,128)(2,1)} %get-tuple-element.49, pred[]{:T(512)S(6)} %eq.17), kind=kOutput, calls=%fused_computation | convolution fusion | flops 235700224 | bytes 2424833 | tf_op jit(solution)/shard_map/dot_general | solution.py:443
  144.6 5.6 %all-to-all-done.3 = bf16[64,16,128]{2,1,0:T(8,128)(2,1)S(1)} async-done(((bf16[64,16,128]{2,1,0:T(8,128)(2,1)}), bf16[64,16,128]{2,1,0:T(8,128)(2,1)S(1)}, u32[]{:S(2)}, u32[]{:S(2)}) %all-to-all-start.3) | async-done | bytes 262176 | tf_op jit(solution)/shard_map/all_to_all | solution.py:451
  150.2 0.1 convert_reduce_fusion
  150.3 0.1 maximum_select_fusion.3
  150.4 21.1 %all_to_all.30 = bf16[64,16,128]{2,1,0:T(8,128)(2,1)S(1)} all-to-all(bf16[64,16,128]{2,1,0:T(8,128)(2,1)S(1)} %broadcast_in_dim.7), channel_id=1, replica_groups=mesh['yh'=2,'x'=4,'z'=8,'yl'=4,'c'=2] {'yh','yl','z'}, dimensions={0} | all-to-all | bytes 524288 | tf_op jit(solution)/shard_map/all_to_all | solution.py:39
  171.5 0.1 broadcast_in_dim.8
  171.6 15.9 %all_to_all.31.mine_ref = bf16[4,64,16,128]{3,2,1,0:T(8,128)(2,1)S(1)} all-to-all(bf16[4,64,16,128]{3,2,1,0:T(8,128)(2,1)S(1)} %broadcast_in_dim.8), channel_id=1, replica_groups=mesh['yh'=2,'x'=4,'z'=8,'yl'=4,'c'=2] {'x'}, dimensions={0} | all-to-all | bytes 2097152 | tf_op jit(solution)/shard_map/all_to_all | solution.py:39
  187.5 6.1 %collective-permute-start.17 = (bf16[4,64,16,128]{3,2,1,0:T(8,128)(2,1)S(1)}, bf16[4,64,16,128]{3,2,1,0:T(8,128)(2,1)S(1)}, u32[]{:S(2)}, u32[]{:S(2)}) collective-permute-start(bf16[4,64,16,128]{3,2,1,0:T(8,128)(2,1)S(1)} %all_to_all.31.mine_ref), channel_id=1, source_target_pairs={{0,1},{1,0},{2,3},{3,2},{4,5},{5,4},{6,7},{7,6},{8,9},{9,8},{10,11... | collective-permute-start | bytes 3145736 | tf_op jit(solution)/shard_map/ppermute | solution.py:93
  193.7 2.3 %collective-permute-done.17.other_ref = bf16[4,64,16,128]{3,2,1,0:T(8,128)(2,1)S(1)} collective-permute-done((bf16[4,64,16,128]{3,2,1,0:T(8,128)(2,1)S(1)}, bf16[4,64,16,128]{3,2,1,0:T(8,128)(2,1)S(1)}, u32[]{:S(2)}, u32[]{:S(2)}) %collective-permute-start.17) | collective-permute-done | bytes 1048608 | tf_op jit(solution)/shard_map/ppermute | solution.py:93
  195.9 1.0 copy-done.4
  196.9 3.1 %assemble.1 = (bf16[1792,512]{1,0:T(8,128)(2,1)}, f32[4,128]{1,0:T(4,128)}) custom-call(s32[5]{0:T(128)} %stack.40.ids_ref, bf16[4,64,16,128]{3,2,1,0:T(8,128)(2,1)} %copy-done.1, bf16[4,64,16,128]{3,2,1,0:T(8,128)(2,1)} %copy-done.4), custom_call_target="tpu_custom_call" | custom-call | tf_op jit(solution)/shard_map/assemble/pallas_call | solution.py:379
  (49 shorter events, 0.2 us)
Async XLA Ops:
  0.6 14.6 %copy-start.11 = (bf16[128,512]{1,0:T(8,128)(2,1)S(1)}, bf16[128,512]{1,0:T(8,128)(2,1)}, u32[]{:S(2)}) copy-start(bf16[128,512]{1,0:T(8,128)(2,1)} %up_ref.1) | copy-start | bytes 393220
  1.9 30.6 %copy-start.19 = (f32[512]{0:T(512)S(1)}, f32[512]{0:T(512)}, u32[]{:S(2)}) copy-start(f32[512]{0:T(512)} %param.11) | copy-start | bytes 6148
  1.9 31.2 %copy-start.2 = (bf16[128,1792]{1,0:T(8,128)(2,1)S(1)}, bf16[128,1792]{1,0:T(8,128)(2,1)}, u32[]{:S(2)}) copy-start(bf16[128,1792]{1,0:T(8,128)(2,1)} %features_ref.1) | copy-start | bytes 1376260
  4.9 29.1 %all-to-all-start = ((bf16[8,144,256]{2,1,0:T(8,128)(2,1)}), bf16[8,144,256]{2,1,0:T(8,128)(2,1)S(1)}, u32[]{:S(2)}, u32[]{:S(2)}) async-start(bf16[8,144,256]{2,1,0:T(8,128)(2,1)} %get-tuple-element.31), calls=%async_computation | async-start | bytes 1179648 | tf_op jit(solution)/shard_map/all_to_all | solution.py:406
  15.3 18.8 %collective-permute-start = (bf16[128,256]{1,0:T(8,128)(2,1)S(1)}, bf16[128,256]{1,0:T(8,128)(2,1)S(1)}, u32[]{:S(2)}, u32[]{:S(2)}) collective-permute-start(bf16[128,256]{1,0:T(8,128)(2,1)S(1)} %slice_select_fusion), channel_id=1, source_target_pairs={{0,1},{1,0},{2,3},{3,2},{4,5},{5,4},{6,7},{7,6},{8,9},{9,8},{10,11... | collective-permute-start | bytes 196616 | tf_op jit(solution)/shard_map/ppermute | solution.py:93
  17.3 19.4 %collective-permute-start.3 = (bf16[144,256]{1,0:T(8,128)(2,1)}, bf16[144,256]{1,0:T(8,128)(2,1)S(1)}, u32[]{:S(2)}, u32[]{:S(2)}) collective-permute-start(bf16[144,256]{1,0:T(8,128)(2,1)} %get-tuple-element.37), channel_id=1, source_target_pairs={{248,262},{249,263},{250,260},{251,261},{252,258},{253,259},{254,2... | collective-permute-start | bytes 221192 | tf_op jit(solution)/shard_map/ppermute | solution.py:53
  30.5 11.9 %collective-permute-start.4 = (bf16[144,256]{1,0:T(8,128)(2,1)}, bf16[144,256]{1,0:T(8,128)(2,1)S(1)}, u32[]{:S(2)}, u32[]{:S(2)}) collective-permute-start(bf16[144,256]{1,0:T(8,128)(2,1)} %get-tuple-element.38), channel_id=1, source_target_pairs={{248,263},{249,262},{250,261},{251,260},{252,259},{253,258},{254,2... | collective-permute-start | bytes 221192 | tf_op jit(solution)/shard_map/ppermute | solution.py:54
  34.1 27.8 %copy-start.18 = (bf16[128,256]{1,0:T(8,128)(2,1)}, bf16[128,256]{1,0:T(8,128)(2,1)S(1)}, u32[]{:S(2)}) copy-start(bf16[128,256]{1,0:T(8,128)(2,1)S(1)} %collective-permute-done.up_other_ref) | copy-start | bytes 196612
  34.1 22.7 %copy-start.8 = (bf16[8,144,256]{2,1,0:T(8,128)(2,1)}, bf16[8,144,256]{2,1,0:T(8,128)(2,1)S(1)}, u32[]{:S(2)}) copy-start(bf16[8,144,256]{2,1,0:T(8,128)(2,1)S(1)} %all-to-all-done.own_ref.refs_0_) | copy-start | bytes 1769476
  34.1 30.5 %collective-permute-start.1 = (bf16[8,144,256]{2,1,0:T(8,128)(2,1)S(1)}, bf16[8,144,256]{2,1,0:T(8,128)(2,1)S(1)}, u32[]{:S(2)}, u32[]{:S(2)}) collective-permute-start(bf16[8,144,256]{2,1,0:T(8,128)(2,1)S(1)} %all-to-all-done.own_ref.refs_0_), channel_id=1, source_target_pairs={{0,8},{8,16},{16,24},{24,32},{32,40},{40,48},{48,56},{56,64},{64,7... | collective-permute-start | bytes 1769480 | tf_op jit(solution)/shard_map/ppermute | solution.py:89
  35.4 29.2 %collective-permute-start.2 = (bf16[8,144,256]{2,1,0:T(8,128)(2,1)S(1)}, bf16[8,144,256]{2,1,0:T(8,128)(2,1)S(1)}, u32[]{:S(2)}, u32[]{:S(2)}) collective-permute-start(bf16[8,144,256]{2,1,0:T(8,128)(2,1)S(1)} %all-to-all-done.own_ref.refs_0_), channel_id=1, source_target_pairs={{8,0},{16,8},{24,16},{32,24},{40,32},{48,40},{56,48},{64,56},{72,6... | collective-permute-start | bytes 1769480 | tf_op jit(solution)/shard_map/ppermute | solution.py:89
  42.5 19.4 %copy-start.7 = (bf16[2,144,256]{2,1,0:T(8,128)(2,1)}, bf16[2,144,256]{2,1,0:T(8,128)(2,1)S(1)}, u32[]{:S(2)}) copy-start(bf16[2,144,256]{2,1,0:T(8,128)(2,1)S(1)} %pad_maximum_fusion.refs_2_.refs_3_) | copy-start | bytes 442372
  42.5 22.1 %collective-permute-start.5 = (bf16[2,144,256]{2,1,0:T(8,128)(2,1)S(1)}, bf16[2,144,256]{2,1,0:T(8,128)(2,1)S(1)}, u32[]{:S(2)}, u32[]{:S(2)}) collective-permute-start(bf16[2,144,256]{2,1,0:T(8,128)(2,1)S(1)} %pad_maximum_fusion.refs_2_.refs_3_), channel_id=1, source_target_pairs={{248,250},{249,251},{250,248},{251,249},{252,254},{253,255},{254,2... | collective-permute-start | bytes 442376 | tf_op jit(solution)/shard_map/ppermute | solution.py:64
  47.4 17.2 %collective-permute-start.6 = (bf16[2,144,256]{2,1,0:T(8,128)(2,1)S(1)}, bf16[2,144,256]{2,1,0:T(8,128)(2,1)S(1)}, u32[]{:S(2)}, u32[]{:S(2)}) collective-permute-start(bf16[2,144,256]{2,1,0:T(8,128)(2,1)S(1)} %pad_maximum_fusion.refs_2_.refs_3_), channel_id=1, source_target_pairs={{248,252},{249,253},{250,254},{251,255},{252,248},{253,249},{254,2... | collective-permute-start | bytes 442376 | tf_op jit(solution)/shard_map/ppermute | solution.py:64
  49.3 15.3 %collective-permute-start.7 = (bf16[2,144,256]{2,1,0:T(8,128)(2,1)S(1)}, bf16[2,144,256]{2,1,0:T(8,128)(2,1)S(1)}, u32[]{:S(2)}, u32[]{:S(2)}) collective-permute-start(bf16[2,144,256]{2,1,0:T(8,128)(2,1)S(1)} %pad_maximum_fusion.refs_2_.refs_3_), channel_id=1, source_target_pairs={{248,254},{249,255},{250,252},{251,253},{252,250},{253,251},{254,2... | collective-permute-start | bytes 442376 | tf_op jit(solution)/shard_map/ppermute | solution.py:64
  53.3 21.7 %all-to-all-start.2 = ((bf16[4,448,128]{2,1,0:T(8,128)(2,1)}), bf16[4,448,128]{2,1,0:T(8,128)(2,1)S(1)}, u32[]{:S(2)}, u32[]{:S(2)}) async-start(bf16[4,448,128]{2,1,0:T(8,128)(2,1)} %bitcast.9), calls=%async_computation.2 | async-start | bytes 917504 | tf_op jit(solution)/shard_map/all_to_all | solution.py:416
  64.6 0.7 copy-start.14
  64.6 0.7 copy-start.15
  64.6 0.7 copy-start.16
  64.6 0.9 copy-start.5
  64.7 1.2 copy-start.6
  75.0 22.0 %copy-start.3 = (bf16[4,448,128]{2,1,0:T(8,128)(2,1)}, bf16[4,448,128]{2,1,0:T(8,128)(2,1)S(1)}, u32[]{:S(2)}) copy-start(bf16[4,448,128]{2,1,0:T(8,128)(2,1)S(1)} %all-to-all-done.2.feats_ref) | copy-start | bytes 1376260
  75.0 22.1 %all-to-all-start.1 = ((bf16[4,2,128,256]{3,2,1,0:T(8,128)(2,1)}), bf16[4,2,128,256]{3,2,1,0:T(8,128)(2,1)S(1)}, u32[]{:S(2)}, u32[]{:S(2)}) async-start(bf16[4,2,128,256]{3,2,1,0:T(8,128)(2,1)} %get-tuple-element.42), calls=%async_computation.1 | async-start | bytes 1048576 | tf_op jit(solution)/shard_map/all_to_all | solution.py:426
  78.6 18.5 %copy-start.20 = (f32[1,256]{1,0:T(1,128)S(1)}, f32[1,256]{1,0:T(1,128)}, u32[]{:S(2)}) copy-start(f32[1,256]{1,0:T(1,128)} %get-tuple-element.45) | copy-start | bytes 3076
  78.6 18.5 %collective-permute-start.8 = (bf16[2,128,256]{2,1,0:T(8,128)(2,1)}, bf16[2,128,256]{2,1,0:T(8,128)(2,1)S(1)}, u32[]{:S(2)}, u32[]{:S(2)}) collective-permute-start(bf16[2,128,256]{2,1,0:T(8,128)(2,1)} %get-tuple-element.41), channel_id=1, source_target_pairs={{248,262},{249,263},{250,260},{251,261},{252,258},{253,259},{254,2... | collective-permute-start | bytes 393224 | tf_op jit(solution)/shard_map/ppermute | solution.py:53
  85.0 20.5 %collective-permute-start.9 = (bf16[4,448,128]{2,1,0:T(8,128)(2,1)S(1)}, bf16[4,448,128]{2,1,0:T(8,128)(2,1)S(1)}, u32[]{:S(2)}, u32[]{:S(2)}) collective-permute-start(bf16[4,448,128]{2,1,0:T(8,128)(2,1)S(1)} %all-to-all-done.2.feats_ref), channel_id=1, source_target_pairs={{0,1},{1,0},{2,3},{3,2},{4,5},{5,4},{6,7},{7,6},{8,9},{9,8},{10,11... | collective-permute-start | bytes 1376264 | tf_op jit(solution)/shard_map/ppermute | solution.py:93
  97.1 17.4 %copy-start.17 = (bf16[2,128,256]{2,1,0:T(8,128)(2,1)}, bf16[2,128,256]{2,1,0:T(8,128)(2,1)S(1)}, u32[]{:S(2)}) copy-start(bf16[2,128,256]{2,1,0:T(8,128)(2,1)S(1)} %collective-permute-done.8.refs_2_) | copy-start | bytes 393220
  97.1 12.8 %copy-start.12 = (bf16[4,2,128,256]{3,2,1,0:T(8,128)(2,1)}, bf16[4,2,128,256]{3,2,1,0:T(8,128)(2,1)S(1)}, u32[]{:S(2)}) copy-start(bf16[4,2,128,256]{3,2,1,0:T(8,128)(2,1)S(1)} %all-to-all-done.1) | copy-start | bytes 1572868
  97.1 20.3 %collective-permute-start.10 = (bf16[8,128,256]{2,1,0:T(8,128)(2,1)S(1)}, bf16[8,128,256]{2,1,0:T(8,128)(2,1)S(1)}, u32[]{:S(2)}, u32[]{:S(2)}) collective-permute-start(bf16[8,128,256]{2,1,0:T(8,128)(2,1)S(1)} %bitcast.20), channel_id=1, source_target_pairs={{0,8},{8,16},{16,24},{24,32},{32,40},{40,48},{48,56},{56,64},{64,7... | collective-permute-start | bytes 1572872 | tf_op jit(solution)/shard_map/ppermute | solution.py:89
  98.5 19.0 %collective-permute-start.11 = (bf16[8,128,256]{2,1,0:T(8,128)(2,1)S(1)}, bf16[8,128,256]{2,1,0:T(8,128)(2,1)S(1)}, u32[]{:S(2)}, u32[]{:S(2)}) collective-permute-start(bf16[8,128,256]{2,1,0:T(8,128)(2,1)S(1)} %bitcast.21), channel_id=1, source_target_pairs={{8,0},{16,8},{24,16},{32,24},{40,32},{48,40},{56,48},{64,56},{72,6... | collective-permute-start | bytes 1572872 | tf_op jit(solution)/shard_map/ppermute | solution.py:89
  100.4 14.1 %collective-permute-start.12 = (bf16[2,128,256]{2,1,0:T(8,128)(2,1)S(1)}, bf16[2,128,256]{2,1,0:T(8,128)(2,1)}, u32[]{:S(2)}, u32[]{:S(2)}) collective-permute-start(bf16[2,128,256]{2,1,0:T(8,128)(2,1)S(1)} %collective-permute-done.8.refs_2_), channel_id=1, source_target_pairs={{248,250},{249,251},{250,248},{251,249},{252,254},{253,255},{254,2... | collective-permute-start | bytes 393224 | tf_op jit(solution)/shard_map/ppermute | solution.py:64
  103.5 14.0 %collective-permute-start.13 = (bf16[2,128,256]{2,1,0:T(8,128)(2,1)S(1)}, bf16[2,128,256]{2,1,0:T(8,128)(2,1)}, u32[]{:S(2)}, u32[]{:S(2)}) collective-permute-start(bf16[2,128,256]{2,1,0:T(8,128)(2,1)S(1)} %collective-permute-done.8.refs_2_), channel_id=1, source_target_pairs={{248,252},{249,253},{250,254},{251,255},{252,248},{253,249},{254,2... | collective-permute-start | bytes 393224 | tf_op jit(solution)/shard_map/ppermute | solution.py:64
  105.5 4.5 %copy-start.13 = (bf16[4,448,128]{2,1,0:T(8,128)(2,1)}, bf16[4,448,128]{2,1,0:T(8,128)(2,1)S(1)}, u32[]{:S(2)}) copy-start(bf16[4,448,128]{2,1,0:T(8,128)(2,1)S(1)} %collective-permute-done.9.feats_other_ref) | copy-start | bytes 1376260
  105.5 12.0 %collective-permute-start.14 = (bf16[2,128,256]{2,1,0:T(8,128)(2,1)S(1)}, bf16[2,128,256]{2,1,0:T(8,128)(2,1)}, u32[]{:S(2)}, u32[]{:S(2)}) collective-permute-start(bf16[2,128,256]{2,1,0:T(8,128)(2,1)S(1)} %collective-permute-done.8.refs_2_), channel_id=1, source_target_pairs={{248,254},{249,255},{250,252},{251,253},{252,250},{253,251},{254,2... | collective-permute-start | bytes 393224 | tf_op jit(solution)/shard_map/ppermute | solution.py:64
  114.5 27.7 %copy-start = (bf16[1792,512]{1,0:T(8,128)(2,1)S(1)}, bf16[1792,512]{1,0:T(8,128)(2,1)}, u32[]{:S(2)}) copy-start(bf16[1792,512]{1,0:T(8,128)(2,1)} %weight_ref.1) | copy-start | bytes 5505028
  117.5 0.8 copy-start.9
  118.3 0.8 copy-start.10
  125.7 24.5 %all-to-all-start.3 = ((bf16[64,16,128]{2,1,0:T(8,128)(2,1)}), bf16[64,16,128]{2,1,0:T(8,128)(2,1)S(1)}, u32[]{:S(2)}, u32[]{:S(2)}) async-start(bf16[64,16,128]{2,1,0:T(8,128)(2,1)} %get-tuple-element.48), calls=%async_computation.3 | async-start | bytes 524288 | tf_op jit(solution)/shard_map/all_to_all | solution.py:451
  135.8 4.7 %collective-permute-start.16 = (bf16[128,256]{1,0:T(8,128)(2,1)}, bf16[128,256]{1,0:T(8,128)(2,1)S(1)}, u32[]{:S(2)}, u32[]{:S(2)}) collective-permute-start(bf16[128,256]{1,0:T(8,128)(2,1)} %get-tuple-element.52), channel_id=1, source_target_pairs={{0,1},{1,0},{2,3},{3,2},{4,5},{5,4},{6,7},{7,6},{8,9},{9,8},{10,11... | collective-permute-start | bytes 196616 | tf_op jit(solution)/shard_map/ppermute | solution.py:93
  138.6 3.5 %collective-permute-start.15 = (bf16[128,256]{1,0:T(8,128)(2,1)}, bf16[128,256]{1,0:T(8,128)(2,1)S(1)}, u32[]{:S(2)}, u32[]{:S(2)}) collective-permute-start(bf16[128,256]{1,0:T(8,128)(2,1)} %get-tuple-element.50), channel_id=1, source_target_pairs={{0,1},{1,0},{2,3},{3,2},{4,5},{5,4},{6,7},{7,6},{8,9},{9,8},{10,11... | collective-permute-start | bytes 196616 | tf_op jit(solution)/shard_map/ppermute | solution.py:93
  187.5 8.4 %copy-start.1 = (bf16[4,64,16,128]{3,2,1,0:T(8,128)(2,1)}, bf16[4,64,16,128]{3,2,1,0:T(8,128)(2,1)S(1)}, u32[]{:S(2)}) copy-start(bf16[4,64,16,128]{3,2,1,0:T(8,128)(2,1)S(1)} %all_to_all.31.mine_ref) | copy-start | bytes 3145732
  187.5 8.4 %collective-permute-start.17 = (bf16[4,64,16,128]{3,2,1,0:T(8,128)(2,1)S(1)}, bf16[4,64,16,128]{3,2,1,0:T(8,128)(2,1)S(1)}, u32[]{:S(2)}, u32[]{:S(2)}) collective-permute-start(bf16[4,64,16,128]{3,2,1,0:T(8,128)(2,1)S(1)} %all_to_all.31.mine_ref), channel_id=1, source_target_pairs={{0,1},{1,0},{2,3},{3,2},{4,5},{5,4},{6,7},{7,6},{8,9},{9,8},{10,11... | collective-permute-start | bytes 3145736 | tf_op jit(solution)/shard_map/ppermute | solution.py:93
  195.9 1.0 copy-start.4

commit v9 on v8

--- a/solution.py
+++ b/solution.py
@@ -234,7 +234,6 @@
         forward_own_kernel,
         in_specs=[SMEM_SPEC] + [VMEM_SPEC] * 2,
         out_shape=jax.ShapeDtypeStruct((2 * TILE, HALF), f32),
-        cost_estimate=EAGER,
         name="forward_own",
     )(ids, counts, own)
 

time: 201 us -> 203 us (level)
  starting transfers between devices: 90.7 us -> 93.7 us
    all_to_all x1, waiting for transfers between devices: 5.38 us -> 0.01 us  [on_device(): feats = lax.all_to_all(slices, 'yl', 0, 0)]
    ppermute x6, waiting for transfers between devices: 3.01 us -> 7.23 us  [along_run(): parts.append(lax.ppermute(block, AXES, pairs))]
    all_to_all x1, starting transfers between devices: 3.47 us -> 5.88 us  [on_device(): own = lax.all_to_all(scaled_copies, 'yl', 0, 0)]
where the time goes in v9:
time: 203 us; the launch traced here: 202 us
  starting transfers between devices  93.7 us (46%)
  Pallas kernels  37.5 us (18%)
  blocking collectives  37 us (18%)
  waiting for transfers between devices  20.8 us (10%)
  local copies, waits for them, and re-layouts  5.61 us (3%)
  other arithmetic  3.03 us (1%)
  matrix products  2.4 us (1%)
    all_to_all x2, blocking collectives, spread_to(): lax.all_to_all(jnp.broadcast_to(shard[None], (count,) + shard.shape), axe...  37 us
    ppermute x6, starting transfers between devices, along_run(): parts.append(lax.ppermute(block, AXES, pairs))  19.5 us
    ppermute x2, starting transfers between devices, across(): got = lax.ppermute(same, AXES, straight)  19.4 us
    ppermute x5, starting transfers between devices, swap_core(): return lax.ppermute(block, 'c', [(0, 1), (1, 0)])  17 us
    all_to_all x1, starting transfers between devices, on_device(): own = lax.all_to_all(copies, ('yl', 'c'), 0, 0)  10.3 us
    all_to_all x1, starting transfers between devices, on_device(): terms = lax.all_to_all(slabs, WIDE, 0, 0)  10.2 us
    pallas_call x1, Pallas kernels, backward_counts(): pl.pallas_call(backward_counts_kernel, in_specs=[SMEM_SPEC] + [VMEM_SPEC]...  8.72 us
    ppermute x6, waiting for transfers between devices, along_run(): parts.append(lax.ppermute(block, AXES, pairs))  7.23 us
  transfers between devices with their start and end apart: 22, of which 5 were waited for; matrix products, arithmetic and copies ran while one was open for 3% of the time, Pallas kernels for 12%

profile of v9, /device:TPU:1, one launch (start us, length us, event | category | flops | bytes accessed | tf_op | source)
XLA Modules:
  0.0 201.8 jit_solution(17833559163517039499)
XLA Ops:
  0.6 0.0 copy-start.11
  1.3 0.6 stack.40.ids_ref
  1.9 3.0 %project.1 = (bf16[8,144,256]{2,1,0:T(8,128)(2,1)}, bf16[144,256]{1,0:T(8,128)(2,1)}, bf16[144,256]{1,0:T(8,128)(2,1)}) custom-call(s32[5]{0:T(128)} %stack.40.ids_ref, s32[1]{0:T(128)S(6)} %copy.14.count_ref, s32[1,24]{1,0:T(1,128)} %tiles_ref.1, s32[15,128]{1,0:T(8,128)} %bitcast.23, s32[15,128]{1,0:T(8,128)} %bitcast.24, s32[15,128]{1,0:T(8,128)} %bitcast.25, ...), custom_call_target="tpu_custom_call" | custom-call | tf_op jit(solution)/shard_map/project/pallas_call | solution.py:129
  4.9 10.3 %all-to-all-start = ((bf16[8,144,256]{2,1,0:T(8,128)(2,1)}), bf16[8,144,256]{2,1,0:T(8,128)(2,1)S(1)}, u32[]{:S(2)}, u32[]{:S(2)}) async-start(bf16[8,144,256]{2,1,0:T(8,128)(2,1)} %get-tuple-element.31), calls=%async_computation | async-start | bytes 1179648 | tf_op jit(solution)/shard_map/all_to_all | solution.py:405
  15.3 2.0 %collective-permute-start = (bf16[128,256]{1,0:T(8,128)(2,1)S(1)}, bf16[128,256]{1,0:T(8,128)(2,1)S(1)}, u32[]{:S(2)}, u32[]{:S(2)}) collective-permute-start(bf16[128,256]{1,0:T(8,128)(2,1)S(1)} %slice_select_fusion), channel_id=1, source_target_pairs={{0,1},{1,0},{2,3},{3,2},{4,5},{5,4},{6,7},{7,6},{8,9},{9,8},{10,11... | collective-permute-start | bytes 196616 | tf_op jit(solution)/shard_map/ppermute | solution.py:93
  17.3 13.2 %collective-permute-start.3 = (bf16[144,256]{1,0:T(8,128)(2,1)}, bf16[144,256]{1,0:T(8,128)(2,1)S(1)}, u32[]{:S(2)}, u32[]{:S(2)}) collective-permute-start(bf16[144,256]{1,0:T(8,128)(2,1)} %get-tuple-element.37), channel_id=1, source_target_pairs={{248,262},{249,263},{250,260},{251,261},{252,258},{253,259},{254,2... | collective-permute-start | bytes 221192 | tf_op jit(solution)/shard_map/ppermute | solution.py:53
  30.5 2.0 collective-permute-start.4
  32.5 0.6 slice_select_fusion.1
  33.1 1.0 copy.13
  34.1 1.3 collective-permute-start.1
  35.4 1.3 collective-permute-start.2
  36.7 0.0 collective-permute-done.3
  36.7 5.7 %collective-permute-done.4 = bf16[144,256]{1,0:T(8,128)(2,1)S(1)} collective-permute-done((bf16[144,256]{1,0:T(8,128)(2,1)}, bf16[144,256]{1,0:T(8,128)(2,1)S(1)}, u32[]{:S(2)}, u32[]{:S(2)}) %collective-permute-start.4) | collective-permute-done | bytes 73760 | tf_op jit(solution)/shard_map/ppermute | solution.py:54
  42.5 4.2 %all-to-all-start.2 = ((bf16[4,448,128]{2,1,0:T(8,128)(2,1)}), bf16[4,448,128]{2,1,0:T(8,128)(2,1)S(1)}, u32[]{:S(2)}, u32[]{:S(2)}) async-start(bf16[4,448,128]{2,1,0:T(8,128)(2,1)} %bitcast.9), calls=%async_computation.2 | async-start | bytes 917504 | tf_op jit(solution)/shard_map/all_to_all | solution.py:415
  46.7 4.1 %collective-permute-start.5 = (bf16[2,144,256]{2,1,0:T(8,128)(2,1)S(1)}, bf16[2,144,256]{2,1,0:T(8,128)(2,1)S(1)}, u32[]{:S(2)}, u32[]{:S(2)}) collective-permute-start(bf16[2,144,256]{2,1,0:T(8,128)(2,1)S(1)} %pad_maximum_fusion.refs_2_.refs_3_), channel_id=1, source_target_pairs={{248,250},{249,251},{250,248},{251,249},{252,254},{253,255},{254,2... | collective-permute-start | bytes 442376 | tf_op jit(solution)/shard_map/ppermute | solution.py:64
  50.9 3.3 %collective-permute-start.6 = (bf16[2,144,256]{2,1,0:T(8,128)(2,1)S(1)}, bf16[2,144,256]{2,1,0:T(8,128)(2,1)S(1)}, u32[]{:S(2)}, u32[]{:S(2)}) collective-permute-start(bf16[2,144,256]{2,1,0:T(8,128)(2,1)S(1)} %pad_maximum_fusion.refs_2_.refs_3_), channel_id=1, source_target_pairs={{248,252},{249,253},{250,254},{251,255},{252,248},{253,249},{254,2... | collective-permute-start | bytes 442376 | tf_op jit(solution)/shard_map/ppermute | solution.py:64
  54.1 2.7 %collective-permute-start.7 = (bf16[2,144,256]{2,1,0:T(8,128)(2,1)S(1)}, bf16[2,144,256]{2,1,0:T(8,128)(2,1)S(1)}, u32[]{:S(2)}, u32[]{:S(2)}) collective-permute-start(bf16[2,144,256]{2,1,0:T(8,128)(2,1)S(1)} %pad_maximum_fusion.refs_2_.refs_3_), channel_id=1, source_target_pairs={{248,254},{249,255},{250,252},{251,253},{252,250},{253,251},{254,2... | collective-permute-start | bytes 442376 | tf_op jit(solution)/shard_map/ppermute | solution.py:64
  56.8 5.1 %forward_counts.1 = (bf16[256,3072]{1,0:T(8,128)(2,1)}, f32[256,1]{1,0:T(8,128)}) custom-call(s32[5]{0:T(128)} %stack.40.ids_ref, bf16[8,144,256]{2,1,0:T(8,128)(2,1)} %copy-done.2), custom_call_target="tpu_custom_call" | custom-call | flops 4000000000 | bytes 8000000 | tf_op jit(solution)/shard_map/forward_counts/pallas_call | solution.py:176
  61.9 2.7 %forward_own.1.total_ref = f32[256,256]{1,0:T(8,128)} custom-call(s32[5]{0:T(128)} %stack.40.ids_ref, bf16[256,3072]{1,0:T(8,128)(2,1)} %get-tuple-element.34.counts_ref, bf16[8,144,256]{2,1,0:T(8,128)(2,1)} %copy-done.2), custom_call_target="tpu_custom_call" | custom-call | tf_op jit(solution)/shard_map/forward_own/pallas_call | solution.py:233
  64.6 0.0 collective-permute-done.5.refs_3_.refs_4_
  64.6 4.2 %collective-permute-done.6.refs_4_.refs_5_ = bf16[2,144,256]{2,1,0:T(8,128)(2,1)S(1)} collective-permute-done((bf16[2,144,256]{2,1,0:T(8,128)(2,1)S(1)}, bf16[2,144,256]{2,1,0:T(8,128)(2,1)S(1)}, u32[]{:S(2)}, u32[]{:S(2)}) %collective-permute-start.6) | collective-permute-done | bytes 147488 | tf_op jit(solution)/shard_map/ppermute | solution.py:64
  68.8 0.0 collective-permute-done.7.refs_5_.refs_6_
  68.8 0.0 collective-permute-done.1.refs_0_.refs_1_
  68.8 0.0 collective-permute-done.2.refs_1_.refs_2_
  68.9 0.6 copy-done.15
  69.4 0.1 copy-done.16
  69.5 0.2 copy-done.6
  69.7 0.3 copy-done.7
  70.0 3.8 %forward_math.1 = (bf16[128,256]{1,0:T(8,128)(2,1)}, bf16[128,256]{1,0:T(8,128)(2,1)}, bf16[4,2,128,256]{3,2,1,0:T(8,128)(2,1)}, bf16[2,128,256]{2,1,0:T(8,128)(2,1)}, f32[1,256]{1,0:T(1,128)}) custom-call(s32[5]{0:T(128)} %stack.40.ids_ref, bf16[256,3072]{1,0:T(8,128)(2,1)} %get-tuple-element.34.counts_ref, f32[256,256]{1,0:T(8,128)} %forward_own.1.total_ref, ...), custom_call_target="tpu_custom_call" | custom-call | tf_op jit(solution)/shard_map/forward_math/pallas_call | solution.py:294
  73.8 0.0 all-to-all-done.2.feats_ref
  73.8 0.0 copy-start.4
  73.8 5.9 %all-to-all-start.1 = ((bf16[4,2,128,256]{3,2,1,0:T(8,128)(2,1)}), bf16[4,2,128,256]{3,2,1,0:T(8,128)(2,1)S(1)}, u32[]{:S(2)}, u32[]{:S(2)}) async-start(bf16[4,2,128,256]{3,2,1,0:T(8,128)(2,1)} %get-tuple-element.42), calls=%async_computation.1 | async-start | bytes 1048576 | tf_op jit(solution)/shard_map/all_to_all | solution.py:425
  79.7 0.1 pad.13.clone
  79.8 6.1 %collective-permute-start.8 = (bf16[2,128,256]{2,1,0:T(8,128)(2,1)}, bf16[2,128,256]{2,1,0:T(8,128)(2,1)S(1)}, u32[]{:S(2)}, u32[]{:S(2)}) collective-permute-start(bf16[2,128,256]{2,1,0:T(8,128)(2,1)} %get-tuple-element.41), channel_id=1, source_target_pairs={{248,262},{249,263},{250,260},{251,261},{252,258},{253,259},{254,2... | collective-permute-start | bytes 393224 | tf_op jit(solution)/shard_map/ppermute | solution.py:53
  86.0 4.2 %collective-permute-start.9 = (bf16[4,448,128]{2,1,0:T(8,128)(2,1)S(1)}, bf16[4,448,128]{2,1,0:T(8,128)(2,1)S(1)}, u32[]{:S(2)}, u32[]{:S(2)}) collective-permute-start(bf16[4,448,128]{2,1,0:T(8,128)(2,1)S(1)} %all-to-all-done.2.feats_ref), channel_id=1, source_target_pairs={{0,1},{1,0},{2,3},{3,2},{4,5},{5,4},{6,7},{7,6},{8,9},{9,8},{10,11... | collective-permute-start | bytes 1376264 | tf_op jit(solution)/shard_map/ppermute | solution.py:93
  90.2 8.7 %backward_counts.1.counts_ref = bf16[1024,3072]{1,0:T(8,128)(2,1)} custom-call(s32[5]{0:T(128)} %stack.40.ids_ref, bf16[8,144,256]{2,1,0:T(8,128)(2,1)} %copy-done.2, bf16[8,144,256]{2,1,0:T(8,128)(2,1)} %copy-done.6, bf16[8,144,256]{2,1,0:T(8,128)(2,1)} %copy-done.7, bf16[2,144,256]{2,1,0:T(8,128)(2,1)} %copy-done.8, bf16[2,144,256]{2,1,0:T(8,128)(2,1)} %copy-done.14, ...), custom_call_target="tpu_custom_call" | custom-call | flops 4000000000 | bytes 8000000 | tf_op jit(solution)/shard_map/backward_counts/pallas_call | solution.py:208
  98.9 0.0 copy-start.17
  98.9 0.0 all-to-all-done.1
  98.9 1.3 collective-permute-start.10
  100.3 1.3 collective-permute-start.11
  101.6 0.7 maximum_maximum_fusion.bias_ref
  102.2 3.1 %collective-permute-start.12 = (bf16[2,128,256]{2,1,0:T(8,128)(2,1)S(1)}, bf16[2,128,256]{2,1,0:T(8,128)(2,1)}, u32[]{:S(2)}, u32[]{:S(2)}) collective-permute-start(bf16[2,128,256]{2,1,0:T(8,128)(2,1)S(1)} %collective-permute-done.8.refs_2_), channel_id=1, source_target_pairs={{248,250},{249,251},{250,248},{251,249},{252,254},{253,255},{254,2... | collective-permute-start | bytes 393224 | tf_op jit(solution)/shard_map/ppermute | solution.py:64
  105.3 2.1 %collective-permute-start.13 = (bf16[2,128,256]{2,1,0:T(8,128)(2,1)S(1)}, bf16[2,128,256]{2,1,0:T(8,128)(2,1)}, u32[]{:S(2)}, u32[]{:S(2)}) collective-permute-start(bf16[2,128,256]{2,1,0:T(8,128)(2,1)S(1)} %collective-permute-done.8.refs_2_), channel_id=1, source_target_pairs={{248,252},{249,253},{250,254},{251,255},{252,248},{253,249},{254,2... | collective-permute-start | bytes 393224 | tf_op jit(solution)/shard_map/ppermute | solution.py:64
  107.4 4.3 %collective-permute-start.14 = (bf16[2,128,256]{2,1,0:T(8,128)(2,1)S(1)}, bf16[2,128,256]{2,1,0:T(8,128)(2,1)}, u32[]{:S(2)}, u32[]{:S(2)}) collective-permute-start(bf16[2,128,256]{2,1,0:T(8,128)(2,1)S(1)} %collective-permute-done.8.refs_2_), channel_id=1, source_target_pairs={{248,254},{249,255},{250,252},{251,253},{252,250},{253,251},{254,2... | collective-permute-start | bytes 393224 | tf_op jit(solution)/shard_map/ppermute | solution.py:64
  111.7 4.5 %backward_own.1.total_ref = f32[1024,256]{1,0:T(8,128)} custom-call(bf16[1024,3072]{1,0:T(8,128)(2,1)} %backward_counts.1.counts_ref, bf16[8,128,256]{2,1,0:T(8,128)(2,1)} %bitcast.22), custom_call_target="tpu_custom_call" | custom-call | flops 4000000000 | bytes 8000000 | tf_op jit(solution)/shard_map/backward_own/pallas_call | solution.py:250
  116.3 3.0 %collective-permute-done.13.refs_4_ = bf16[2,128,256]{2,1,0:T(8,128)(2,1)} collective-permute-done((bf16[2,128,256]{2,1,0:T(8,128)(2,1)S(1)}, bf16[2,128,256]{2,1,0:T(8,128)(2,1)}, u32[]{:S(2)}, u32[]{:S(2)}) %collective-permute-start.13) | collective-permute-done | bytes 131104 | tf_op jit(solution)/shard_map/ppermute | solution.py:64
  119.3 0.8 copy-done.9
  120.1 0.8 copy-done.10
  120.9 6.5 %backward_math.1 = (bf16[128,256]{1,0:T(8,128)(2,1)}, bf16[128,256]{1,0:T(8,128)(2,1)}, bf16[64,16,128]{2,1,0:T(8,128)(2,1)}) custom-call(s32[5]{0:T(128)} %stack.40.ids_ref, bf16[1024,3072]{1,0:T(8,128)(2,1)} %backward_counts.1.counts_ref, f32[1024,256]{1,0:T(8,128)} %backward_own.1.total_ref, bf16[16,128]{1,0:T(8,128)(2,1)} %maximum_maximum_fusion.bias_ref, ...), custom_call_target="tpu_custom_call" | custom-call | tf_op jit(solution)/shard_map/backward_math/pallas_call | solution.py:341
  127.4 10.2 %all-to-all-start.3 = ((bf16[64,16,128]{2,1,0:T(8,128)(2,1)}), bf16[64,16,128]{2,1,0:T(8,128)(2,1)S(1)}, u32[]{:S(2)}, u32[]{:S(2)}) async-start(bf16[64,16,128]{2,1,0:T(8,128)(2,1)} %get-tuple-element.48), calls=%async_computation.3 | async-start | bytes 524288 | tf_op jit(solution)/shard_map/all_to_all | solution.py:450
  137.6 2.8 %collective-permute-start.16 = (bf16[128,256]{1,0:T(8,128)(2,1)}, bf16[128,256]{1,0:T(8,128)(2,1)S(1)}, u32[]{:S(2)}, u32[]{:S(2)}) collective-permute-start(bf16[128,256]{1,0:T(8,128)(2,1)} %get-tuple-element.52), channel_id=1, source_target_pairs={{0,1},{1,0},{2,3},{3,2},{4,5},{5,4},{6,7},{7,6},{8,9},{9,8},{10,11... | collective-permute-start | bytes 196616 | tf_op jit(solution)/shard_map/ppermute | solution.py:93
  140.4 1.9 collective-permute-start.15
  142.3 1.6 maximum_select_fusion.2
  144.0 2.4 %convolution_convert_fusion = bf16[128,1792]{1,0:T(8,128)(2,1)} fusion(bf16[1792,512]{1,0:T(8,128)(2,1)S(1)} %copy-done, bf16[128,256]{1,0:T(8,128)(2,1)S(1)} %collective-permute-done.15, bf16[128,256]{1,0:T(8,128)(2,1)} %get-tuple-element.49, pred[]{:T(512)S(6)} %eq.17), kind=kOutput, calls=%fused_computation | convolution fusion | flops 235700224 | bytes 2424833 | tf_op jit(solution)/shard_map/dot_general | solution.py:442
  146.4 5.6 %all-to-all-done.3 = bf16[64,16,128]{2,1,0:T(8,128)(2,1)S(1)} async-done(((bf16[64,16,128]{2,1,0:T(8,128)(2,1)}), bf16[64,16,128]{2,1,0:T(8,128)(2,1)S(1)}, u32[]{:S(2)}, u32[]{:S(2)}) %all-to-all-start.3) | async-done | bytes 262176 | tf_op jit(solution)/shard_map/all_to_all | solution.py:450
  151.9 0.1 convert_reduce_fusion
  152.0 0.1 maximum_select_fusion.3
  152.2 21.1 %all_to_all.30 = bf16[64,16,128]{2,1,0:T(8,128)(2,1)S(1)} all-to-all(bf16[64,16,128]{2,1,0:T(8,128)(2,1)S(1)} %broadcast_in_dim.7), channel_id=1, replica_groups=mesh['yh'=2,'x'=4,'z'=8,'yl'=4,'c'=2] {'yh','yl','z'}, dimensions={0} | all-to-all | bytes 524288 | tf_op jit(solution)/shard_map/all_to_all | solution.py:39
  173.2 0.1 broadcast_in_dim.8
  173.4 15.9 %all_to_all.31.mine_ref = bf16[4,64,16,128]{3,2,1,0:T(8,128)(2,1)S(1)} all-to-all(bf16[4,64,16,128]{3,2,1,0:T(8,128)(2,1)S(1)} %broadcast_in_dim.8), channel_id=1, replica_groups=mesh['yh'=2,'x'=4,'z'=8,'yl'=4,'c'=2] {'x'}, dimensions={0} | all-to-all | bytes 2097152 | tf_op jit(solution)/shard_map/all_to_all | solution.py:39
  189.3 6.1 %collective-permute-start.17 = (bf16[4,64,16,128]{3,2,1,0:T(8,128)(2,1)S(1)}, bf16[4,64,16,128]{3,2,1,0:T(8,128)(2,1)S(1)}, u32[]{:S(2)}, u32[]{:S(2)}) collective-permute-start(bf16[4,64,16,128]{3,2,1,0:T(8,128)(2,1)S(1)} %all_to_all.31.mine_ref), channel_id=1, source_target_pairs={{0,1},{1,0},{2,3},{3,2},{4,5},{5,4},{6,7},{7,6},{8,9},{9,8},{10,11... | collective-permute-start | bytes 3145736 | tf_op jit(solution)/shard_map/ppermute | solution.py:93
  195.4 2.3 %collective-permute-done.17.other_ref = bf16[4,64,16,128]{3,2,1,0:T(8,128)(2,1)S(1)} collective-permute-done((bf16[4,64,16,128]{3,2,1,0:T(8,128)(2,1)S(1)}, bf16[4,64,16,128]{3,2,1,0:T(8,128)(2,1)S(1)}, u32[]{:S(2)}, u32[]{:S(2)}) %collective-permute-start.17) | collective-permute-done | bytes 1048608 | tf_op jit(solution)/shard_map/ppermute | solution.py:93
  197.7 1.0 copy-done.5
  198.7 3.1 %assemble.1 = (bf16[1792,512]{1,0:T(8,128)(2,1)}, f32[4,128]{1,0:T(4,128)}) custom-call(s32[5]{0:T(128)} %stack.40.ids_ref, bf16[4,64,16,128]{3,2,1,0:T(8,128)(2,1)} %copy-done.1, bf16[4,64,16,128]{3,2,1,0:T(8,128)(2,1)} %copy-done.5), custom_call_target="tpu_custom_call" | custom-call | tf_op jit(solution)/shard_map/assemble/pallas_call | solution.py:378
  (49 shorter events, 0.2 us)
Async XLA Ops:
  0.6 14.6 %copy-start.11 = (bf16[128,512]{1,0:T(8,128)(2,1)S(1)}, bf16[128,512]{1,0:T(8,128)(2,1)}, u32[]{:S(2)}) copy-start(bf16[128,512]{1,0:T(8,128)(2,1)} %up_ref.1) | copy-start | bytes 393220
  1.9 30.6 %copy-start.19 = (f32[512]{0:T(512)S(1)}, f32[512]{0:T(512)}, u32[]{:S(2)}) copy-start(f32[512]{0:T(512)} %param.11) | copy-start | bytes 6148
  1.9 31.2 %copy-start.3 = (bf16[128,1792]{1,0:T(8,128)(2,1)S(1)}, bf16[128,1792]{1,0:T(8,128)(2,1)}, u32[]{:S(2)}) copy-start(bf16[128,1792]{1,0:T(8,128)(2,1)} %features_ref.1) | copy-start | bytes 1376260
  4.9 29.1 %all-to-all-start = ((bf16[8,144,256]{2,1,0:T(8,128)(2,1)}), bf16[8,144,256]{2,1,0:T(8,128)(2,1)S(1)}, u32[]{:S(2)}, u32[]{:S(2)}) async-start(bf16[8,144,256]{2,1,0:T(8,128)(2,1)} %get-tuple-element.31), calls=%async_computation | async-start | bytes 1179648 | tf_op jit(solution)/shard_map/all_to_all | solution.py:405
  15.3 18.8 %collective-permute-start = (bf16[128,256]{1,0:T(8,128)(2,1)S(1)}, bf16[128,256]{1,0:T(8,128)(2,1)S(1)}, u32[]{:S(2)}, u32[]{:S(2)}) collective-permute-start(bf16[128,256]{1,0:T(8,128)(2,1)S(1)} %slice_select_fusion), channel_id=1, source_target_pairs={{0,1},{1,0},{2,3},{3,2},{4,5},{5,4},{6,7},{7,6},{8,9},{9,8},{10,11... | collective-permute-start | bytes 196616 | tf_op jit(solution)/shard_map/ppermute | solution.py:93
  17.3 19.4 %collective-permute-start.3 = (bf16[144,256]{1,0:T(8,128)(2,1)}, bf16[144,256]{1,0:T(8,128)(2,1)S(1)}, u32[]{:S(2)}, u32[]{:S(2)}) collective-permute-start(bf16[144,256]{1,0:T(8,128)(2,1)} %get-tuple-element.37), channel_id=1, source_target_pairs={{248,262},{249,263},{250,260},{251,261},{252,258},{253,259},{254,2... | collective-permute-start | bytes 221192 | tf_op jit(solution)/shard_map/ppermute | solution.py:53
  30.5 11.9 %collective-permute-start.4 = (bf16[144,256]{1,0:T(8,128)(2,1)}, bf16[144,256]{1,0:T(8,128)(2,1)S(1)}, u32[]{:S(2)}, u32[]{:S(2)}) collective-permute-start(bf16[144,256]{1,0:T(8,128)(2,1)} %get-tuple-element.38), channel_id=1, source_target_pairs={{248,263},{249,262},{250,261},{251,260},{252,259},{253,258},{254,2... | collective-permute-start | bytes 221192 | tf_op jit(solution)/shard_map/ppermute | solution.py:54
  34.1 27.8 %copy-start.18 = (bf16[128,256]{1,0:T(8,128)(2,1)}, bf16[128,256]{1,0:T(8,128)(2,1)S(1)}, u32[]{:S(2)}) copy-start(bf16[128,256]{1,0:T(8,128)(2,1)S(1)} %collective-permute-done.up_other_ref) | copy-start | bytes 196612
  34.1 22.7 %copy-start.2 = (bf16[8,144,256]{2,1,0:T(8,128)(2,1)}, bf16[8,144,256]{2,1,0:T(8,128)(2,1)S(1)}, u32[]{:S(2)}) copy-start(bf16[8,144,256]{2,1,0:T(8,128)(2,1)S(1)} %all-to-all-done.own_ref.refs_0_) | copy-start | bytes 1769476
  34.1 34.7 %collective-permute-start.1 = (bf16[8,144,256]{2,1,0:T(8,128)(2,1)S(1)}, bf16[8,144,256]{2,1,0:T(8,128)(2,1)S(1)}, u32[]{:S(2)}, u32[]{:S(2)}) collective-permute-start(bf16[8,144,256]{2,1,0:T(8,128)(2,1)S(1)} %all-to-all-done.own_ref.refs_0_), channel_id=1, source_target_pairs={{0,8},{8,16},{16,24},{24,32},{32,40},{40,48},{48,56},{56,64},{64,7... | collective-permute-start | bytes 1769480 | tf_op jit(solution)/shard_map/ppermute | solution.py:89
  35.4 33.4 %collective-permute-start.2 = (bf16[8,144,256]{2,1,0:T(8,128)(2,1)S(1)}, bf16[8,144,256]{2,1,0:T(8,128)(2,1)S(1)}, u32[]{:S(2)}, u32[]{:S(2)}) collective-permute-start(bf16[8,144,256]{2,1,0:T(8,128)(2,1)S(1)} %all-to-all-done.own_ref.refs_0_), channel_id=1, source_target_pairs={{8,0},{16,8},{24,16},{32,24},{40,32},{48,40},{56,48},{64,56},{72,6... | collective-permute-start | bytes 1769480 | tf_op jit(solution)/shard_map/ppermute | solution.py:89
  42.5 31.4 %all-to-all-start.2 = ((bf16[4,448,128]{2,1,0:T(8,128)(2,1)}), bf16[4,448,128]{2,1,0:T(8,128)(2,1)S(1)}, u32[]{:S(2)}, u32[]{:S(2)}) async-start(bf16[4,448,128]{2,1,0:T(8,128)(2,1)} %bitcast.9), calls=%async_computation.2 | async-start | bytes 917504 | tf_op jit(solution)/shard_map/all_to_all | solution.py:415
  46.7 15.2 %copy-start.8 = (bf16[2,144,256]{2,1,0:T(8,128)(2,1)}, bf16[2,144,256]{2,1,0:T(8,128)(2,1)S(1)}, u32[]{:S(2)}) copy-start(bf16[2,144,256]{2,1,0:T(8,128)(2,1)S(1)} %pad_maximum_fusion.refs_2_.refs_3_) | copy-start | bytes 442372
  46.7 17.8 %collective-permute-start.5 = (bf16[2,144,256]{2,1,0:T(8,128)(2,1)S(1)}, bf16[2,144,256]{2,1,0:T(8,128)(2,1)S(1)}, u32[]{:S(2)}, u32[]{:S(2)}) collective-permute-start(bf16[2,144,256]{2,1,0:T(8,128)(2,1)S(1)} %pad_maximum_fusion.refs_2_.refs_3_), channel_id=1, source_target_pairs={{248,250},{249,251},{250,248},{251,249},{252,254},{253,255},{254,2... | collective-permute-start | bytes 442376 | tf_op jit(solution)/shard_map/ppermute | solution.py:64
  50.9 17.9 %collective-permute-start.6 = (bf16[2,144,256]{2,1,0:T(8,128)(2,1)S(1)}, bf16[2,144,256]{2,1,0:T(8,128)(2,1)S(1)}, u32[]{:S(2)}, u32[]{:S(2)}) collective-permute-start(bf16[2,144,256]{2,1,0:T(8,128)(2,1)S(1)} %pad_maximum_fusion.refs_2_.refs_3_), channel_id=1, source_target_pairs={{248,252},{249,253},{250,254},{251,255},{252,248},{253,249},{254,2... | collective-permute-start | bytes 442376 | tf_op jit(solution)/shard_map/ppermute | solution.py:64
  54.1 14.7 %collective-permute-start.7 = (bf16[2,144,256]{2,1,0:T(8,128)(2,1)S(1)}, bf16[2,144,256]{2,1,0:T(8,128)(2,1)S(1)}, u32[]{:S(2)}, u32[]{:S(2)}) collective-permute-start(bf16[2,144,256]{2,1,0:T(8,128)(2,1)S(1)} %pad_maximum_fusion.refs_2_.refs_3_), channel_id=1, source_target_pairs={{248,254},{249,255},{250,252},{251,253},{252,250},{253,251},{254,2... | collective-permute-start | bytes 442376 | tf_op jit(solution)/shard_map/ppermute | solution.py:64
  64.6 4.3 %copy-start.14 = (bf16[2,144,256]{2,1,0:T(8,128)(2,1)}, bf16[2,144,256]{2,1,0:T(8,128)(2,1)S(1)}, u32[]{:S(2)}) copy-start(bf16[2,144,256]{2,1,0:T(8,128)(2,1)S(1)} %collective-permute-done.5.refs_3_.refs_4_) | copy-start | bytes 442372
  68.8 0.6 copy-start.15
  68.8 0.7 copy-start.16
  68.8 0.9 copy-start.6
  68.8 1.2 copy-start.7
  73.8 25.0 %copy-start.4 = (bf16[4,448,128]{2,1,0:T(8,128)(2,1)}, bf16[4,448,128]{2,1,0:T(8,128)(2,1)S(1)}, u32[]{:S(2)}) copy-start(bf16[4,448,128]{2,1,0:T(8,128)(2,1)S(1)} %all-to-all-done.2.feats_ref) | copy-start | bytes 1376260
  73.8 25.1 %all-to-all-start.1 = ((bf16[4,2,128,256]{3,2,1,0:T(8,128)(2,1)}), bf16[4,2,128,256]{3,2,1,0:T(8,128)(2,1)S(1)}, u32[]{:S(2)}, u32[]{:S(2)}) async-start(bf16[4,2,128,256]{3,2,1,0:T(8,128)(2,1)} %get-tuple-element.42), calls=%async_computation.1 | async-start | bytes 1048576 | tf_op jit(solution)/shard_map/all_to_all | solution.py:425
  79.8 19.1 %copy-start.20 = (f32[1,256]{1,0:T(1,128)S(1)}, f32[1,256]{1,0:T(1,128)}, u32[]{:S(2)}) copy-start(f32[1,256]{1,0:T(1,128)} %get-tuple-element.45) | copy-start | bytes 3076
  79.8 19.1 %collective-permute-start.8 = (bf16[2,128,256]{2,1,0:T(8,128)(2,1)}, bf16[2,128,256]{2,1,0:T(8,128)(2,1)S(1)}, u32[]{:S(2)}, u32[]{:S(2)}) collective-permute-start(bf16[2,128,256]{2,1,0:T(8,128)(2,1)} %get-tuple-element.41), channel_id=1, source_target_pairs={{248,262},{249,263},{250,260},{251,261},{252,258},{253,259},{254,2... | collective-permute-start | bytes 393224 | tf_op jit(solution)/shard_map/ppermute | solution.py:53
  86.0 21.5 %collective-permute-start.9 = (bf16[4,448,128]{2,1,0:T(8,128)(2,1)S(1)}, bf16[4,448,128]{2,1,0:T(8,128)(2,1)S(1)}, u32[]{:S(2)}, u32[]{:S(2)}) collective-permute-start(bf16[4,448,128]{2,1,0:T(8,128)(2,1)S(1)} %all-to-all-done.2.feats_ref), channel_id=1, source_target_pairs={{0,1},{1,0},{2,3},{3,2},{4,5},{5,4},{6,7},{7,6},{8,9},{9,8},{10,11... | collective-permute-start | bytes 1376264 | tf_op jit(solution)/shard_map/ppermute | solution.py:93
  98.9 17.4 %copy-start.17 = (bf16[2,128,256]{2,1,0:T(8,128)(2,1)}, bf16[2,128,256]{2,1,0:T(8,128)(2,1)S(1)}, u32[]{:S(2)}) copy-start(bf16[2,128,256]{2,1,0:T(8,128)(2,1)S(1)} %collective-permute-done.8.refs_2_) | copy-start | bytes 393220
  98.9 12.8 %copy-start.12 = (bf16[4,2,128,256]{3,2,1,0:T(8,128)(2,1)}, bf16[4,2,128,256]{3,2,1,0:T(8,128)(2,1)S(1)}, u32[]{:S(2)}) copy-start(bf16[4,2,128,256]{3,2,1,0:T(8,128)(2,1)S(1)} %all-to-all-done.1) | copy-start | bytes 1572868
  98.9 20.3 %collective-permute-start.10 = (bf16[8,128,256]{2,1,0:T(8,128)(2,1)S(1)}, bf16[8,128,256]{2,1,0:T(8,128)(2,1)S(1)}, u32[]{:S(2)}, u32[]{:S(2)}) collective-permute-start(bf16[8,128,256]{2,1,0:T(8,128)(2,1)S(1)} %bitcast.20), channel_id=1, source_target_pairs={{0,8},{8,16},{16,24},{24,32},{32,40},{40,48},{48,56},{56,64},{64,7... | collective-permute-start | bytes 1572872 | tf_op jit(solution)/shard_map/ppermute | solution.py:89
  100.3 19.0 %collective-permute-start.11 = (bf16[8,128,256]{2,1,0:T(8,128)(2,1)S(1)}, bf16[8,128,256]{2,1,0:T(8,128)(2,1)S(1)}, u32[]{:S(2)}, u32[]{:S(2)}) collective-permute-start(bf16[8,128,256]{2,1,0:T(8,128)(2,1)S(1)} %bitcast.21), channel_id=1, source_target_pairs={{8,0},{16,8},{24,16},{32,24},{40,32},{48,40},{56,48},{64,56},{72,6... | collective-permute-start | bytes 1572872 | tf_op jit(solution)/shard_map/ppermute | solution.py:89
  102.2 14.1 %collective-permute-start.12 = (bf16[2,128,256]{2,1,0:T(8,128)(2,1)S(1)}, bf16[2,128,256]{2,1,0:T(8,128)(2,1)}, u32[]{:S(2)}, u32[]{:S(2)}) collective-permute-start(bf16[2,128,256]{2,1,0:T(8,128)(2,1)S(1)} %collective-permute-done.8.refs_2_), channel_id=1, source_target_pairs={{248,250},{249,251},{250,248},{251,249},{252,254},{253,255},{254,2... | collective-permute-start | bytes 393224 | tf_op jit(solution)/shard_map/ppermute | solution.py:64
  105.3 14.0 %collective-permute-start.13 = (bf16[2,128,256]{2,1,0:T(8,128)(2,1)S(1)}, bf16[2,128,256]{2,1,0:T(8,128)(2,1)}, u32[]{:S(2)}, u32[]{:S(2)}) collective-permute-start(bf16[2,128,256]{2,1,0:T(8,128)(2,1)S(1)} %collective-permute-done.8.refs_2_), channel_id=1, source_target_pairs={{248,252},{249,253},{250,254},{251,255},{252,248},{253,249},{254,2... | collective-permute-start | bytes 393224 | tf_op jit(solution)/shard_map/ppermute | solution.py:64
  107.4 4.3 %copy-start.13 = (bf16[4,448,128]{2,1,0:T(8,128)(2,1)}, bf16[4,448,128]{2,1,0:T(8,128)(2,1)S(1)}, u32[]{:S(2)}) copy-start(bf16[4,448,128]{2,1,0:T(8,128)(2,1)S(1)} %collective-permute-done.9.feats_other_ref) | copy-start | bytes 1376260
  107.4 11.8 %collective-permute-start.14 = (bf16[2,128,256]{2,1,0:T(8,128)(2,1)S(1)}, bf16[2,128,256]{2,1,0:T(8,128)(2,1)}, u32[]{:S(2)}, u32[]{:S(2)}) collective-permute-start(bf16[2,128,256]{2,1,0:T(8,128)(2,1)S(1)} %collective-permute-done.8.refs_2_), channel_id=1, source_target_pairs={{248,254},{249,255},{250,252},{251,253},{252,250},{253,251},{254,2... | collective-permute-start | bytes 393224 | tf_op jit(solution)/shard_map/ppermute | solution.py:64
  116.3 27.7 %copy-start = (bf16[1792,512]{1,0:T(8,128)(2,1)S(1)}, bf16[1792,512]{1,0:T(8,128)(2,1)}, u32[]{:S(2)}) copy-start(bf16[1792,512]{1,0:T(8,128)(2,1)} %weight_ref.1) | copy-start | bytes 5505028
  119.3 0.8 copy-start.9
  120.1 0.8 copy-start.10
  127.4 24.5 %all-to-all-start.3 = ((bf16[64,16,128]{2,1,0:T(8,128)(2,1)}), bf16[64,16,128]{2,1,0:T(8,128)(2,1)S(1)}, u32[]{:S(2)}, u32[]{:S(2)}) async-start(bf16[64,16,128]{2,1,0:T(8,128)(2,1)} %get-tuple-element.48), calls=%async_computation.3 | async-start | bytes 524288 | tf_op jit(solution)/shard_map/all_to_all | solution.py:450
  137.6 4.7 %collective-permute-start.16 = (bf16[128,256]{1,0:T(8,128)(2,1)}, bf16[128,256]{1,0:T(8,128)(2,1)S(1)}, u32[]{:S(2)}, u32[]{:S(2)}) collective-permute-start(bf16[128,256]{1,0:T(8,128)(2,1)} %get-tuple-element.52), channel_id=1, source_target_pairs={{0,1},{1,0},{2,3},{3,2},{4,5},{5,4},{6,7},{7,6},{8,9},{9,8},{10,11... | collective-permute-start | bytes 196616 | tf_op jit(solution)/shard_map/ppermute | solution.py:93
  140.4 3.5 %collective-permute-start.15 = (bf16[128,256]{1,0:T(8,128)(2,1)}, bf16[128,256]{1,0:T(8,128)(2,1)S(1)}, u32[]{:S(2)}, u32[]{:S(2)}) collective-permute-start(bf16[128,256]{1,0:T(8,128)(2,1)} %get-tuple-element.50), channel_id=1, source_target_pairs={{0,1},{1,0},{2,3},{3,2},{4,5},{5,4},{6,7},{7,6},{8,9},{9,8},{10,11... | collective-permute-start | bytes 196616 | tf_op jit(solution)/shard_map/ppermute | solution.py:93
  189.3 8.4 %copy-start.1 = (bf16[4,64,16,128]{3,2,1,0:T(8,128)(2,1)}, bf16[4,64,16,128]{3,2,1,0:T(8,128)(2,1)S(1)}, u32[]{:S(2)}) copy-start(bf16[4,64,16,128]{3,2,1,0:T(8,128)(2,1)S(1)} %all_to_all.31.mine_ref) | copy-start | bytes 3145732
  189.3 8.4 %collective-permute-start.17 = (bf16[4,64,16,128]{3,2,1,0:T(8,128)(2,1)S(1)}, bf16[4,64,16,128]{3,2,1,0:T(8,128)(2,1)S(1)}, u32[]{:S(2)}, u32[]{:S(2)}) collective-permute-start(bf16[4,64,16,128]{3,2,1,0:T(8,128)(2,1)S(1)} %all_to_all.31.mine_ref), channel_id=1, source_target_pairs={{0,1},{1,0},{2,3},{3,2},{4,5},{5,4},{6,7},{7,6},{8,9},{9,8},{10,11... | collective-permute-start | bytes 3145736 | tf_op jit(solution)/shard_map/ppermute | solution.py:93
  197.7 1.0 copy-start.5
